TPU v7x, 512 devices: a whole 4x4x16 slice. The times are simulated.
512 devices in a mesh: row: 16 (over x, z_hi), col: 32 (over z_lo, y, core).
Axes of the slice: x: 4, y: 4, z: 16 (z_hi: 4, z_lo: 4; z = z_hi * 4 + z_lo), core: 2. Of those that a mesh axis runs over, the one named last changes fastest.
Arguments:
- inverse_pool: bfloat16 [16384, 16384], P('row', 'col'), as said below
- factor_one: bfloat16 [16384, 256], P(('row', 'col')), may hold values from -0.046875 to 0.046875
- factor_two: bfloat16 [16384, 256], P(('row', 'col')), may hold values from -0.046875 to 0.046875
- diag_inv_one: float32 [256, 256], replicated, may hold values from -3 to 3
- diag_inv_two: float32 [256, 256], replicated, may hold values from -3 to 3
- struct_one: int32 [64], replicated, may hold values 0 or 1
- struct_two: int32 [64], replicated, may hold values 0 or 1
Outputs:
- column_one: bfloat16 [16384, 256], P(('row', 'col'))
- column_two: bfloat16 [16384, 256], P(('row', 'col'))
- diagonal_one: float32 [256, 256], replicated
- diagonal_two: float32 [256, 256], replicated
Inputs may be any that keep to these rules, and one draw needn't show every extreme that they name: inverse_pool is symmetric: entry (i, j) equals entry (j, i).
All inputs are finite; a program needn't handle non-finite values.
Results may differ from a plain program's by a relative error of at most 0.0007.
Values may be sent and summed in bfloat16 or wider, within the bound.
No kernel may reach another device: no remote copies, remote signals or barrier semaphores. Data moves between devices by JAX's collectives and lax.ppermute only.
A program may use at most 64 MiB of HBM per device.

v0:
```python
import jax
import jax.numpy as jnp
from jax import lax
from jax.sharding import PartitionSpec as P

B = 256


def broadcast(block, axis, owner):
    block = jnp.where(lax.axis_index(axis) == owner, block, jnp.zeros_like(block))
    return lax.psum(block, axis)


def local_mask(struct, first_row, row_count):
    spread = jnp.repeat(struct, B)
    return lax.dynamic_slice_in_dim(spread, first_row, row_count, 0)


def per_device(
    inverse_pool, factor_one, factor_two, diag_inv_one, diag_inv_two, struct_one, struct_two
):
    num_row = lax.axis_size("row")
    num_col = lax.axis_size("col")
    row_count = factor_one.shape[0]
    width = factor_one.shape[1]
    col_width = inverse_pool.shape[1]
    linear = lax.axis_index("row") * num_col + lax.axis_index("col")
    first_row = linear * row_count
    mask_one = local_mask(struct_one, first_row, row_count)
    mask_two = local_mask(struct_two, first_row, row_count)
    masked_one = factor_one * mask_one.astype(jnp.bfloat16)[:, None]
    masked_two = factor_two * mask_two.astype(jnp.bfloat16)[:, None]
    strip_one, strip_two = (
        lax.all_gather(masked_one, "col", axis=0, tiled=True),
        lax.all_gather(masked_two, "col", axis=0, tiled=True),
    )
    stacked = jnp.concatenate([strip_one, strip_two], axis=1)
    col_ratio = num_col // num_row
    root_row = lax.axis_index("col") // col_ratio
    offset = lax.axis_index("col") % col_ratio * col_width
    arrived = broadcast(stacked, "row", root_row)
    owned_rows = lax.dynamic_slice_in_dim(arrived, offset, col_width, 0)
    product = lax.psum_scatter(
        jnp.dot(inverse_pool, owned_rows, preferred_element_type=jnp.float32),
        "col",
        scatter_dimension=0,
        tiled=True,
    )
    product_one = product[:, :width]
    product_two = product[:, width:]
    column_one = (-(product_one * mask_one.astype(jnp.float32)[:, None])).astype(jnp.bfloat16)
    column_two = (-(product_two * mask_two.astype(jnp.float32)[:, None])).astype(jnp.bfloat16)
    term_one = jnp.dot(
        masked_one.astype(jnp.float32).T,
        product_one,
        precision=lax.Precision.HIGHEST,
        preferred_element_type=jnp.float32,
    )
    term_two = jnp.dot(
        masked_two.astype(jnp.float32).T,
        product_two,
        precision=lax.Precision.HIGHEST,
        preferred_element_type=jnp.float32,
    )
    total_one, total_two = lax.psum((term_one, term_two), ("row", "col"))
    return (column_one, column_two, diag_inv_one + total_one, diag_inv_two + total_two)


def solution(mesh):
    in_specs = (
        P("row", "col"),
        P(("row", "col"), None),
        P(("row", "col"), None),
        P(),
        P(),
        P(),
        P(),
    )
    out_specs = (P(("row", "col"), None), P(("row", "col"), None), P(), P())
    return jax.shard_map(
        per_device, mesh=mesh, in_specs=in_specs, out_specs=out_specs, check_vma=False
    )
```

profile of v0, /device:TPU:1, one launch (start us, length us, event | category | flops | bytes accessed | tf_op | source)
XLA Modules:
  0.0 932.1 jit_solution(10251943174924167101)
XLA Ops:
  7.2 0.0 copy-start
  7.2 0.0 all-reduce.4.cloned.1.call-start
  7.2 0.8 broadcast_bitcast_fusion.1
  8.1 0.7 broadcast_bitcast_fusion
  8.9 0.1 dynamic-slice_convert_fusion
  8.9 0.8 broadcast_multiply_fusion.1
  9.7 47.3 %all_gather.6 = bf16[1024,256]{1,0:T(8,128)(2,1)S(1)} all-gather(bf16[32,256]{1,0:T(8,128)(2,1)S(1)} %broadcast_multiply_fusion.1), channel_id=1, replica_groups=mesh['row'=16,'col'=32] {'col'}, dimensions={0}, use_global_device_ids=true | all-gather | bytes 540672 | tf_op jit(solution)/shard_map/all_gather | solution.py:34
  57.1 0.8 broadcast_multiply_fusion
  57.9 39.3 %all_gather.7 = bf16[1024,256]{1,0:T(8,128)(2,1)S(1)} all-gather(bf16[32,256]{1,0:T(8,128)(2,1)S(1)} %broadcast_multiply_fusion), channel_id=1, replica_groups=mesh['row'=16,'col'=32] {'col'}, dimensions={0}, use_global_device_ids=true | all-gather | bytes 540672 | tf_op jit(solution)/shard_map/all_gather | solution.py:35
  97.2 1.2 maximum_select_fusion
  98.4 0.0 all-reduce.4.cloned.1.call-update
  98.4 0.0 reduce-scatter.4.cloned.1.call-start
  98.5 207.2 %all-reduce.4.cloned.1.call-done = bf16[1024,512]{1,0:T(8,128)(2,1)} async-done(((bf16[1024,512]{1,0:T(8,128)(2,1)}), bf16[1024,512]{1,0:T(8,128)(2,1)}) %all-reduce.4.cloned.1.call-update) | async-done | bytes 1048592 | tf_op jit(solution)/shard_map/psum | solution.py:11
  305.7 0.0 copy-done
  305.7 1.8 convolution_bitcast_fusion
  307.5 1.9 copy.15
  309.4 0.0 copy-start.1
  309.4 0.0 copy-start.2
  309.4 0.0 reduce-scatter.4.cloned.1.call-update
  309.4 0.0 all-reduce.6.cloned.1.call-start
  309.5 147.7 %reduce-scatter.4.cloned.1.call-done = f32[32,512]{1,0:T(8,128)} async-done(((f32[1024,512]{1,0:T(8,128)}), f32[32,512]{1,0:T(8,128)}) %reduce-scatter.4.cloned.1.call-update) | async-done | bytes 65552
  457.2 0.8 fusion.6
  458.0 0.1 copy.18
  458.1 1.8 fusion.2
  459.8 1.8 fusion.4
  461.6 0.0 all-reduce.6.cloned.1.call-update
  461.7 0.7 copy.14
  462.3 0.1 copy.17
  462.5 0.7 copy.13
  463.2 459.0 %all-reduce.6.cloned.1.call-done = (f32[256,256]{1,0:T(8,128)}, f32[256,256]{1,0:T(8,128)}) async-done(((f32[256,256]{1,0:T(8,128)}, f32[256,256]{1,0:T(8,128)}), (f32[256,256]{1,0:T(8,128)}, f32[256,256]{1,0:T(8,128)})) %all-reduce.6.cloned.1.call-update) | async-done | bytes 524304 | tf_op jit(solution)/shard_map/psum | solution.py:65
  922.1 0.0 copy-done.1
  922.1 1.7 add.33
  923.8 0.0 copy-done.2
  923.8 1.7 add.34
  (4 shorter events, 0.1 us)
Async XLA Ops:
  7.2 298.5 %copy-start = (bf16[1024,512]{1,0:T(8,128)(2,1)S(1)}, bf16[1024,512]{1,0:T(8,128)(2,1)}, u32[]{:S(2)}) copy-start(bf16[1024,512]{1,0:T(8,128)(2,1)} %param.7) | copy-start | bytes 3145732
  7.2 298.5 %all-reduce.4.cloned.1.call-start = ((), (), s32[]{:S(2)}) async-start(), calls=%async_computation.1 | async-start | bytes 2097152 | tf_op jit(solution)/shard_map/psum | solution.py:11
  98.4 358.8 %reduce-scatter.4.cloned.1.call-start = ((), (), s32[]{:S(2)}) async-start(), calls=%async_computation.2 | async-start | bytes 2162688
  309.4 612.8 %copy-start.1 = (f32[256,256]{1,0:T(8,128)S(1)}, f32[256,256]{1,0:T(8,128)}, u32[]{:S(2)}) copy-start(f32[256,256]{1,0:T(8,128)} %param.10) | copy-start | bytes 786436
  309.4 614.5 %copy-start.2 = (f32[256,256]{1,0:T(8,128)S(1)}, f32[256,256]{1,0:T(8,128)}, u32[]{:S(2)}) copy-start(f32[256,256]{1,0:T(8,128)} %param.11) | copy-start | bytes 786436
  309.4 612.7 %all-reduce.6.cloned.1.call-start = ((), (), s32[]{:S(2)}) async-start(), calls=%async_computation.3 | async-start | bytes 1048576 | tf_op jit(solution)/shard_map/psum | solution.py:65
Sparse Core Ops, SparseCore 0:
  98.5 207.1 all-reduce.3
  309.5 147.6 reduce-scatter.3
  463.3 458.8 all-reduce.5
where the time goes:
time: 933 us; the launch traced here: 932 us
  waiting for transfers between devices  814 us (87%)
  blocking collectives  86.6 us (9%)
  between operations  13.8 us (1%)
    psum x1, waiting for transfers between devices, per_device(): total_one, total_two = lax.psum((term_one, term_two), ('row', 'col'))  459 us
    psum x1, waiting for transfers between devices, broadcast(): return lax.psum(block, axis)  207 us
    unnamed x4, waiting for transfers between devices  148 us
    all_gather x1, blocking collectives, per_device(): lax.all_gather(masked_one, 'col', axis=0, tiled=True)  47.3 us
    all_gather x1, blocking collectives, per_device(): lax.all_gather(masked_two, 'col', axis=0, tiled=True)  39.3 us
  transfers between devices with their start and end apart: 3, of which 3 were waited for; matrix products, arithmetic and copies ran while one was open for 0% of the time, Pallas kernels for 0%

commit v1 on v0

v1 whole, which is shorter than its diff:
```python
import jax
import jax.numpy as jnp
from jax import lax
from jax.sharding import Mesh, PartitionSpec as P

B = 256
AXES = ("x", "zh", "zl", "y", "core")
SIZES = (4, 4, 4, 4, 2)
ROWS = 16
COLS = 32


def exchange(parts, axes):
    return lax.all_to_all(parts, axes, 0, 0)


def gather(block, axes, count):
    return exchange(jnp.broadcast_to(block[None], (count, *block.shape)), axes)


def per_device(
    inverse_pool, factor_one, factor_two, diag_inv_one, diag_inv_two, struct_one, struct_two
):
    row_count, width = factor_one.shape
    half = width // 2
    row = lax.axis_index(("x", "zh"))
    col = lax.axis_index(("zl", "y", "core"))
    own_block = (row * COLS + col) * row_count // B
    there_block = (col * ROWS + row) * row_count // B
    masked = jnp.concatenate(
        [
            factor_one * struct_one[own_block].astype(jnp.bfloat16),
            factor_two * struct_two[own_block].astype(jnp.bfloat16),
        ],
        axis=1,
    )
    swap = [(c * ROWS + r, r * COLS + c) for r in range(ROWS) for c in range(COLS)]
    masked_there = lax.ppermute(masked, AXES, swap)

    pair = gather(masked, "core", 2).reshape(2 * row_count, 2 * width)
    strip = gather(pair, ("zl", "y"), 16).reshape(-1, 2 * width)
    partial = lax.dot_general(
        inverse_pool, strip, (((0,), (0,)), ((), ())), preferred_element_type=jnp.float32
    )
    product = jnp.sum(exchange(partial.reshape(4, -1, 2 * width), "x"), axis=0)
    product = jnp.sum(exchange(product.reshape(4, -1, 2 * width), "zh"), axis=0)
    product_one = product[:, :width]
    product_two = product[:, width:]

    mask_one = struct_one[there_block].astype(jnp.float32)
    mask_two = struct_two[there_block].astype(jnp.float32)
    column = jnp.concatenate([-(product_one * mask_one), -(product_two * mask_two)], axis=1)
    column = lax.ppermute(column.astype(jnp.bfloat16), AXES, [(b, a) for a, b in swap])

    def blocks(left, right):
        term = lax.dot_general(
            left.astype(jnp.float32),
            right,
            (((0,), (0,)), ((), ())),
            precision=lax.Precision.HIGHEST,
            preferred_element_type=jnp.float32,
        )
        return [term[:half, :half], term[:half, half:], term[half:, half:]]

    packed = jnp.concatenate(
        blocks(masked_there[:, :width], product_one) + blocks(masked_there[:, width:], product_two),
        axis=0,
    )
    shard = jnp.sum(exchange(packed.reshape(32, -1, half), ("x", "y", "core")), axis=0)
    shard = jnp.sum(gather(shard, ("zh", "zl"), 16), axis=0)
    total = gather(shard, ("x", "y", "core"), 32).reshape(2, 3, half, half)

    def whole(t):
        return jnp.concatenate(
            [
                jnp.concatenate([t[0], t[1]], axis=1),
                jnp.concatenate([t[1].T, t[2]], axis=1),
            ],
            axis=0,
        )

    return (
        column[:, :width],
        column[:, width:],
        diag_inv_one + whole(total[0]),
        diag_inv_two + whole(total[1]),
    )


def solution(mesh):
    fine = Mesh(mesh.devices.reshape(SIZES), AXES)
    rows = P(AXES, None)
    in_specs = (P(("x", "zh"), ("zl", "y", "core")), rows, rows, P(), P(), P(), P())
    out_specs = (rows, rows, P(), P())
    return jax.shard_map(
        per_device, mesh=fine, in_specs=in_specs, out_specs=out_specs, check_vma=False
    )
```

time: 933 us -> 166 us (0.18)
  the two profiles are of different devices: /device:TPU:1 before, /device:TPU:58 now
where the time goes in v1:
time: 166 us
  blocking collectives  72.9 us (44%)
  starting transfers between devices  45.7 us (28%)
  waiting for transfers between devices  32.7 us (20%)
  local copies, waits for them, and re-layouts  7.16 us (4%)
  between operations  3.53 us (2%)
  other arithmetic  2.4 us (1%)
    all_to_all x4, blocking collectives, exchange(): return lax.all_to_all(parts, axes, 0, 0)  72.9 us
    all_to_all x3, starting transfers between devices, exchange(): return lax.all_to_all(parts, axes, 0, 0)  25.9 us
    all_to_all x3, waiting for transfers between devices, exchange(): return lax.all_to_all(parts, axes, 0, 0)  18.8 us
    ppermute x1, starting transfers between devices, per_device(): masked_there = lax.ppermute(masked, AXES, swap)  14.5 us
    ppermute x1, waiting for transfers between devices, per_device(): lax.ppermute(column.astype(jnp.bfloat16), AXES, [(b, a) for a, b in swap])  13.9 us
    ppermute x1, starting transfers between devices, per_device(): lax.ppermute(column.astype(jnp.bfloat16), AXES, [(b, a) for a, b in swap])  5.21 us
  transfers between devices with their start and end apart: 5, of which 3 were waited for; matrix products, arithmetic and copies ran while one was open for 0% of the time, Pallas kernels for 0%

profile of v1, /device:TPU:58, one launch (start us, length us, event | category | flops | bytes accessed | tf_op | source)
XLA Modules:
  0.0 165.7 jit_solution(10139901297331478502)
XLA Ops:
  0.6 0.0 copy-start
  0.7 0.0 copy-start.4
  0.7 0.0 copy-start.6
  0.7 0.0 copy-start.7
  0.7 0.7 copy-done.6
  1.4 0.0 copy-done.7
  1.4 0.6 fusion.8
  3.4 0.0 copy-done.4
  3.4 0.0 copy-start.5
  3.4 0.7 copy-done.5
  4.1 3.8 %all_to_all.35 = bf16[2,32,512]{2,1,0:T(8,128)(2,1)S(1)} all-to-all(bf16[2,32,512]{2,1,0:T(8,128)(2,1)S(1)} %broadcast_in_dim.10), channel_id=1, replica_groups=mesh['x'=4,'zh'=4,'zl'=4,'y'=4,'core'=2] {'core'}, dimensions={0} | all-to-all | bytes 131072 | tf_op jit(solution)/shard_map/all_to_all | solution.py:14
  7.9 0.1 broadcast_in_dim.12
  8.0 33.0 %all_to_all.36 = bf16[16,64,512]{2,1,0:T(8,128)(2,1)S(1)} all-to-all(bf16[16,64,512]{2,1,0:T(8,128)(2,1)S(1)} %broadcast_in_dim.12), channel_id=1, replica_groups=mesh['x'=4,'zh'=4,'zl'=4,'y'=4,'core'=2] {'zl','y'}, dimensions={0} | all-to-all | bytes 2097152 | tf_op jit(solution)/shard_map/all_to_all | solution.py:14
  41.0 0.0 copy-done
  41.0 0.8 fusion.10
  41.7 17.4 %all_to_all.37 = f32[4,128,512]{2,1,0:T(8,128)S(1)} all-to-all(f32[4,128,512]{2,1,0:T(8,128)S(1)} %bitcast.35), channel_id=1, replica_groups=mesh['x'=4,'zh'=4,'zl'=4,'y'=4,'core'=2] {'x'}, dimensions={0} | all-to-all | bytes 2097152 | tf_op jit(solution)/shard_map/all_to_all | solution.py:14
  59.1 0.8 reduce_sum.36
  59.9 12.4 %all-to-all-start.3 = ((f32[4,32,512]{2,1,0:T(8,128)}), f32[4,32,512]{2,1,0:T(8,128)S(1)}, u32[]{:S(2)}, u32[]{:S(2)}) async-start(f32[4,32,512]{2,1,0:T(8,128)} %bitcast.6), calls=%async_computation.3 | async-start | bytes 524288 | tf_op jit(solution)/shard_map/all_to_all | solution.py:14
  72.3 14.5 %collective-permute-start.1 = (bf16[32,512]{1,0:T(8,128)(2,1)S(1)}, bf16[32,512]{1,0:T(8,128)(2,1)S(1)}, u32[]{:S(2)}, u32[]{:S(2)}) collective-permute-start(bf16[32,512]{1,0:T(8,128)(2,1)S(1)} %pad_maximum_fusion.1), channel_id=1, source_target_pairs={{0,0},{16,1},{32,2},{48,3},{64,4},{80,5},{96,6},{112,7},{128,8},{1... | collective-permute-start | bytes 98312 | tf_op jit(solution)/shard_map/ppermute | solution.py:38
  86.8 3.4 %all-to-all-done.3 = f32[4,32,512]{2,1,0:T(8,128)S(1)} async-done(((f32[4,32,512]{2,1,0:T(8,128)}), f32[4,32,512]{2,1,0:T(8,128)S(1)}, u32[]{:S(2)}, u32[]{:S(2)}) %all-to-all-start.3) | async-done | bytes 262176 | tf_op jit(solution)/shard_map/all_to_all | solution.py:14
  90.2 0.0 collective-permute-done.1
  90.2 0.3 fusion
  90.5 0.0 copy-start.1
  90.5 0.7 copy-done.1
  91.2 0.3 fusion.2
  91.6 0.0 slice-start
  91.6 0.9 slice-done
  92.5 18.8 %all_to_all.38 = f32[32,24,128]{2,1,0:T(8,128)S(1)} all-to-all(f32[32,24,128]{2,1,0:T(8,128)S(1)} %bitcast.33), channel_id=1, replica_groups=mesh['x'=4,'zh'=4,'zl'=4,'y'=4,'core'=2] {'x','y','core'}, dimensions={0} | all-to-all | bytes 786432 | tf_op jit(solution)/shard_map/all_to_all | solution.py:14
  111.3 0.7 broadcast_in_dim.13
  112.0 7.2 %all-to-all-start.5 = ((f32[16,24,128]{2,1,0:T(8,128)}), f32[16,24,128]{2,1,0:T(8,128)S(1)}, u32[]{:S(2)}, u32[]{:S(2)}) async-start(f32[16,24,128]{2,1,0:T(8,128)} %broadcast_in_dim.13), calls=%async_computation.5 | async-start | bytes 393216 | tf_op jit(solution)/shard_map/all_to_all | solution.py:14
  120.5 15.4 %all-to-all-done.5 = f32[16,24,128]{2,1,0:T(8,128)S(1)} async-done(((f32[16,24,128]{2,1,0:T(8,128)}), f32[16,24,128]{2,1,0:T(8,128)S(1)}, u32[]{:S(2)}, u32[]{:S(2)}) %all-to-all-start.5) | async-done | bytes 196640 | tf_op jit(solution)/shard_map/all_to_all | solution.py:14
  136.0 0.8 broadcast_in_dim.14
  136.7 6.4 %all-to-all-start.6 = ((f32[32,24,128]{2,1,0:T(8,128)}), f32[32,24,128]{2,1,0:T(8,128)S(1)}, u32[]{:S(2)}, u32[]{:S(2)}) async-start(f32[32,24,128]{2,1,0:T(8,128)} %broadcast_in_dim.14), calls=%async_computation.6 | async-start | bytes 786432 | tf_op jit(solution)/shard_map/all_to_all | solution.py:14
  143.1 5.2 %collective-permute-start = (bf16[32,512]{1,0:T(8,128)(2,1)S(1)}, bf16[32,512]{1,0:T(8,128)(2,1)S(1)}, u32[]{:S(2)}, u32[]{:S(2)}) collective-permute-start(bf16[32,512]{1,0:T(8,128)(2,1)S(1)} %pad_maximum_fusion.2), channel_id=1, source_target_pairs={{0,0},{1,16},{2,32},{3,48},{4,64},{5,80},{6,96},{7,112},{8,128},{9... | collective-permute-start | bytes 98312 | tf_op jit(solution)/shard_map/ppermute | solution.py:53
  148.3 13.9 %collective-permute-done = bf16[32,512]{1,0:T(8,128)(2,1)S(1)} collective-permute-done((bf16[32,512]{1,0:T(8,128)(2,1)S(1)}, bf16[32,512]{1,0:T(8,128)(2,1)S(1)}, u32[]{:S(2)}, u32[]{:S(2)}) %collective-permute-start) | collective-permute-done | bytes 32800 | tf_op jit(solution)/shard_map/ppermute | solution.py:53
  162.2 0.6 fusion.7
  162.9 0.0 all-to-all-done.6
  162.9 0.1 copy.13
  163.0 0.0 copy-start.2
  163.1 0.1 copy.14
  163.2 0.8 copy-done.2
  164.0 0.0 copy-start.3
  164.0 0.7 maximum_add_fusion
  164.7 0.3 copy-done.3
  165.0 0.7 maximum_add_fusion.1
  (16 shorter events, 0.2 us)
Async XLA Ops:
  0.6 40.4 %copy-start = (bf16[1024,512]{1,0:T(8,128)(2,1)S(1)}, bf16[1024,512]{1,0:T(8,128)(2,1)}, u32[]{:S(2)}) copy-start(bf16[1024,512]{1,0:T(8,128)(2,1)} %param.7) | copy-start | bytes 3145732
  0.7 2.7 %copy-start.4 = (bf16[32,256]{1,0:T(8,128)(2,1)S(1)}, bf16[32,256]{1,0:T(8,128)(2,1)}, u32[]{:S(2)}) copy-start(bf16[32,256]{1,0:T(8,128)(2,1)} %param.8) | copy-start | bytes 49156
  0.7 0.7 copy-start.6
  0.7 0.7 copy-start.7
  3.4 0.7 copy-start.5
  59.9 30.3 %all-to-all-start.3 = ((f32[4,32,512]{2,1,0:T(8,128)}), f32[4,32,512]{2,1,0:T(8,128)S(1)}, u32[]{:S(2)}, u32[]{:S(2)}) async-start(f32[4,32,512]{2,1,0:T(8,128)} %bitcast.6), calls=%async_computation.3 | async-start | bytes 524288 | tf_op jit(solution)/shard_map/all_to_all | solution.py:14
  72.3 17.9 %collective-permute-start.1 = (bf16[32,512]{1,0:T(8,128)(2,1)S(1)}, bf16[32,512]{1,0:T(8,128)(2,1)S(1)}, u32[]{:S(2)}, u32[]{:S(2)}) collective-permute-start(bf16[32,512]{1,0:T(8,128)(2,1)S(1)} %pad_maximum_fusion.1), channel_id=1, source_target_pairs={{0,0},{16,1},{32,2},{48,3},{64,4},{80,5},{96,6},{112,7},{128,8},{1... | collective-permute-start | bytes 98312 | tf_op jit(solution)/shard_map/ppermute | solution.py:38
  90.5 0.7 copy-start.1
  91.6 0.9 slice-start
  112.0 23.9 %all-to-all-start.5 = ((f32[16,24,128]{2,1,0:T(8,128)}), f32[16,24,128]{2,1,0:T(8,128)S(1)}, u32[]{:S(2)}, u32[]{:S(2)}) async-start(f32[16,24,128]{2,1,0:T(8,128)} %broadcast_in_dim.13), calls=%async_computation.5 | async-start | bytes 393216 | tf_op jit(solution)/shard_map/all_to_all | solution.py:14
  136.7 26.1 %all-to-all-start.6 = ((f32[32,24,128]{2,1,0:T(8,128)}), f32[32,24,128]{2,1,0:T(8,128)S(1)}, u32[]{:S(2)}, u32[]{:S(2)}) async-start(f32[32,24,128]{2,1,0:T(8,128)} %broadcast_in_dim.14), calls=%async_computation.6 | async-start | bytes 786432 | tf_op jit(solution)/shard_map/all_to_all | solution.py:14
  143.1 19.1 %collective-permute-start = (bf16[32,512]{1,0:T(8,128)(2,1)S(1)}, bf16[32,512]{1,0:T(8,128)(2,1)S(1)}, u32[]{:S(2)}, u32[]{:S(2)}) collective-permute-start(bf16[32,512]{1,0:T(8,128)(2,1)S(1)} %pad_maximum_fusion.2), channel_id=1, source_target_pairs={{0,0},{1,16},{2,32},{3,48},{4,64},{5,80},{6,96},{7,112},{8,128},{9... | collective-permute-start | bytes 98312 | tf_op jit(solution)/shard_map/ppermute | solution.py:53
  163.0 1.0 copy-start.2
  164.0 1.0 copy-start.3

commit v2 on v1

v2 whole, which is shorter than its diff:
```python
import jax
import jax.numpy as jnp
from jax import lax
from jax.sharding import Mesh, PartitionSpec as P

B = 256
AXES = ("x", "zh", "zl", "y", "core")
SIZES = (4, 4, 4, 4, 2)
SWAP = [(0, 1), (1, 0)]


def exchange(parts, axes):
    return lax.all_to_all(parts, axes, 0, 0)


def gather(block, axes, count):
    return exchange(jnp.broadcast_to(block[None], (count, *block.shape)), axes)


def device_id(chip_row, chip_col, core):
    return (chip_row * 16 + chip_col) * 2 + core


def home_chip(chip_row, core):
    x, zh = chip_row // 4, chip_row % 4
    return ((x >> 1) ^ core) * 8 + (x & 1) * 4 + zh


def per_device(
    inverse_pool, factor_one, factor_two, diag_inv_one, diag_inv_two, struct_one, struct_two
):
    row_count, width = factor_one.shape
    half = width // 2
    x = lax.axis_index("x")
    chip_row = lax.axis_index(("x", "zh"))
    chip_col = lax.axis_index(("zl", "y"))
    core = lax.axis_index("core")
    first = core == 0
    struct = jnp.where(first, struct_one, struct_two)
    mask_here = struct[chip_row * 4 + lax.axis_index("zl")]
    mask_there = struct[chip_col * 4 + ((x >> 1) ^ core) * 2 + (x & 1)]

    sibling_pool = lax.ppermute(inverse_pool, "core", SWAP)
    rows = exchange(jnp.stack([factor_one, factor_two]), "core").reshape(2 * row_count, width)
    rows = rows * mask_here.astype(jnp.bfloat16)
    there = [
        (device_id(chip, home_chip(chip_r, k), k), device_id(chip_r, chip, k))
        for chip_r in range(16)
        for chip in range(16)
        for k in range(2)
    ]
    rows_there = lax.ppermute(rows, AXES, there)
    strip = gather(rows, ("zl", "y"), 16).reshape(-1, width)

    partial = lax.dot_general(
        jnp.concatenate([inverse_pool, sibling_pool], axis=1),
        strip,
        (((0,), (0,)), ((), ())),
        preferred_element_type=jnp.float32,
    )
    product = jnp.sum(exchange(partial.reshape(4, -1, width), "x"), axis=0)
    product = jnp.sum(exchange(product.reshape(4, -1, width), "zh"), axis=0)

    column = (-(product * mask_there.astype(jnp.float32))).astype(jnp.bfloat16)
    column = column.reshape(2, row_count, width)
    back = [(b, a) for a, b in there]
    cross = [(b, a ^ 1) for a, b in there]
    mine = lax.ppermute(jnp.where(first, column[0], column[1]), AXES, back)
    other = lax.ppermute(jnp.where(first, column[1], column[0]), AXES, cross)

    def term(left, right):
        return lax.dot_general(
            rows_there[:, left].astype(jnp.float32),
            product[:, right],
            (((0,), (0,)), ((), ())),
            precision=lax.Precision.HIGHEST,
            preferred_element_type=jnp.float32,
        )

    low, high = slice(0, half), slice(half, width)
    packed = jnp.concatenate([term(low, low), term(low, high), term(high, high)], axis=0)
    shard = jnp.sum(exchange(packed.reshape(16, -1, half), ("x", "y")), axis=0)
    shard = jnp.sum(gather(shard, ("zh", "zl"), 16), axis=0)
    total = gather(shard, ("x", "y"), 16).reshape(3, half, half)
    sibling = lax.ppermute(total, "core", SWAP)

    def whole(t):
        return jnp.concatenate(
            [
                jnp.concatenate([t[0], t[1]], axis=1),
                jnp.concatenate([t[1].T, t[2]], axis=1),
            ],
            axis=0,
        )

    return (
        jnp.where(first, mine, other),
        jnp.where(first, other, mine),
        diag_inv_one + whole(jnp.where(first, total, sibling)),
        diag_inv_two + whole(jnp.where(first, sibling, total)),
    )


def solution(mesh):
    fine = Mesh(mesh.devices.reshape(SIZES), AXES)
    rows = P(AXES, None)
    in_specs = (P(("x", "zh"), ("zl", "y", "core")), rows, rows, P(), P(), P(), P())
    out_specs = (rows, rows, P(), P())
    return jax.shard_map(
        per_device, mesh=fine, in_specs=in_specs, out_specs=out_specs, check_vma=False
    )
```

time: 166 us -> 153 us (0.922)
  the two profiles are of different devices: /device:TPU:58 before, /device:TPU:17 now
where the time goes in v2:
time: 153 us; the launch traced here: 152 us
  starting transfers between devices  80.2 us (52%)
  blocking collectives  28 us (18%)
  waiting for transfers between devices  27.6 us (18%)
  other arithmetic  6.74 us (4%)
  local copies, waits for them, and re-layouts  5.9 us (4%)
  between operations  2.14 us (1%)
    all_to_all x5, starting transfers between devices, exchange(): return lax.all_to_all(parts, axes, 0, 0)  37.3 us
    all_to_all x2, blocking collectives, exchange(): return lax.all_to_all(parts, axes, 0, 0)  28 us
    all_to_all x5, waiting for transfers between devices, exchange(): return lax.all_to_all(parts, axes, 0, 0)  16.9 us
    ppermute x1, starting transfers between devices, per_device(): rows_there = lax.ppermute(rows, AXES, there)  14.9 us
    ppermute x1, starting transfers between devices, per_device(): mine = lax.ppermute(jnp.where(first, column[0], column[1]), AXES, back)  13.7 us
    ppermute x1, starting transfers between devices, per_device(): other = lax.ppermute(jnp.where(first, column[1], column[0]), AXES, cross)  10.2 us
    ppermute x1, waiting for transfers between devices, per_device(): rows_there = lax.ppermute(rows, AXES, there)  5.86 us
  transfers between devices with their start and end apart: 10, of which 6 were waited for; matrix products, arithmetic and copies ran while one was open for 4% of the time, Pallas kernels for 0%

profile of v2, /device:TPU:17, one launch (start us, length us, event | category | flops | bytes accessed | tf_op | source)
XLA Modules:
  0.0 152.0 jit_solution(10654611787553515067)
XLA Ops:
  0.6 0.0 copy-start
  0.6 1.4 pad_maximum_fusion.1
  2.1 3.9 %all-to-all-start = ((bf16[2,32,256]{2,1,0:T(8,128)(2,1)}), bf16[2,32,256]{2,1,0:T(8,128)(2,1)S(1)}, u32[]{:S(2)}, u32[]{:S(2)}) async-start(bf16[2,32,256]{2,1,0:T(8,128)(2,1)} %pad_maximum_fusion.1), calls=%async_computation | async-start | bytes 65536 | tf_op jit(solution)/shard_map/all_to_all | solution.py:13
  6.0 0.7 broadcast_select_fusion.6
  6.7 0.6 fusion.9
  7.9 0.0 all-to-all-done
  7.9 0.8 broadcast_in_dim.6
  8.8 8.8 %all-to-all-start.1 = ((bf16[16,64,256]{2,1,0:T(8,128)(2,1)}), bf16[16,64,256]{2,1,0:T(8,128)(2,1)S(1)}, u32[]{:S(2)}, u32[]{:S(2)}) async-start(bf16[16,64,256]{2,1,0:T(8,128)(2,1)} %broadcast_in_dim.6), calls=%async_computation.1 | async-start | bytes 1048576 | tf_op jit(solution)/shard_map/all_to_all | solution.py:13
  17.6 2.2 %collective-permute-start = (bf16[1024,512]{1,0:T(8,128)(2,1)}, bf16[1024,512]{1,0:T(8,128)(2,1)S(1)}, u32[]{:S(2)}, u32[]{:S(2)}) collective-permute-start(bf16[1024,512]{1,0:T(8,128)(2,1)} %param.7), channel_id=1, source_target_pairs={{0,1},{1,0},{2,3},{3,2},{4,5},{5,4},{6,7},{7,6},{8,9},{9,8},{10,11... | collective-permute-start | bytes 3145736 | tf_op jit(solution)/shard_map/ppermute | solution.py:43
  19.8 2.5 %collective-permute-done = bf16[1024,512]{1,0:T(8,128)(2,1)S(1)} collective-permute-done((bf16[1024,512]{1,0:T(8,128)(2,1)}, bf16[1024,512]{1,0:T(8,128)(2,1)S(1)}, u32[]{:S(2)}, u32[]{:S(2)}) %collective-permute-start) | collective-permute-done | bytes 1048608 | tf_op jit(solution)/shard_map/ppermute | solution.py:43
  22.3 0.0 copy-done
  22.3 1.7 %maximum_bitcast_fusion = bf16[1024,1024]{0,1:T(8,128)(2,1)} fusion(bf16[1024,512]{1,0:T(8,128)(2,1)S(1)} %collective-permute-done, bf16[1024,512]{1,0:T(8,128)(2,1)S(1)} %copy-done), kind=kLoop, calls=%fused_computation | loop fusion | flops 4194304 | bytes 4194304 | tf_op jit(solution)/shard_map/dot_general | solution.py:55
  24.0 2.9 %copy.14 = bf16[1024,1024]{1,0:T(8,128)(2,1)S(1)} copy(bf16[1024,1024]{0,1:T(8,128)(2,1)} %maximum_bitcast_fusion) | data formatting | bytes 4194304 | tf_op jit(solution)/shard_map/dot_general | solution.py:55
  26.8 4.0 %all-to-all-done.1 = bf16[16,64,256]{2,1,0:T(8,128)(2,1)S(1)} async-done(((bf16[16,64,256]{2,1,0:T(8,128)(2,1)}), bf16[16,64,256]{2,1,0:T(8,128)(2,1)S(1)}, u32[]{:S(2)}, u32[]{:S(2)}) %all-to-all-start.1) | async-done | bytes 524320 | tf_op jit(solution)/shard_map/all_to_all | solution.py:13
  30.9 0.7 fusion.10
  31.6 14.7 %all_to_all.35 = f32[4,256,256]{2,1,0:T(8,128)S(1)} all-to-all(f32[4,256,256]{2,1,0:T(8,128)S(1)} %fusion.10), channel_id=1, replica_groups=mesh['x'=4,'zh'=4,'zl'=4,'y'=4,'core'=2] {'x'}, dimensions={0} | all-to-all | bytes 2097152 | tf_op jit(solution)/shard_map/all_to_all | solution.py:13
  46.3 0.8 reduce_sum.36
  47.0 12.1 %all-to-all-start.3 = ((f32[4,64,256]{2,1,0:T(8,128)}), f32[4,64,256]{2,1,0:T(8,128)S(1)}, u32[]{:S(2)}, u32[]{:S(2)}) async-start(f32[4,64,256]{2,1,0:T(8,128)} %bitcast.8), calls=%async_computation.3 | async-start | bytes 524288 | tf_op jit(solution)/shard_map/all_to_all | solution.py:13
  59.1 14.9 %collective-permute-start.3 = (bf16[64,256]{1,0:T(8,128)(2,1)S(1)}, bf16[64,256]{1,0:T(8,128)(2,1)S(1)}, u32[]{:S(2)}, u32[]{:S(2)}) collective-permute-start(bf16[64,256]{1,0:T(8,128)(2,1)S(1)} %bitcast.40), channel_id=1, source_target_pairs={{0,0},{17,1},{32,2},{49,3},{64,4},{81,5},{96,6},{113,7},{128,8},{1... | collective-permute-start | bytes 98312 | tf_op jit(solution)/shard_map/ppermute | solution.py:52
  74.0 1.2 all-to-all-done.3
  75.2 5.9 %collective-permute-done.3 = bf16[64,256]{1,0:T(8,128)(2,1)S(1)} collective-permute-done((bf16[64,256]{1,0:T(8,128)(2,1)S(1)}, bf16[64,256]{1,0:T(8,128)(2,1)S(1)}, u32[]{:S(2)}, u32[]{:S(2)}) %collective-permute-start.3) | collective-permute-done | bytes 32800 | tf_op jit(solution)/shard_map/ppermute | solution.py:52
  81.1 0.2 fusion.2
  81.3 0.2 fusion.4
  81.6 0.2 fusion
  81.8 0.0 copy-start.1
  81.8 13.3 %all_to_all.36 = f32[16,24,128]{2,1,0:T(8,128)S(1)} all-to-all(f32[16,24,128]{2,1,0:T(8,128)S(1)} %bitcast.36), channel_id=1, replica_groups=mesh['x'=4,'zh'=4,'zl'=4,'y'=4,'core'=2] {'x','y'}, dimensions={0} | all-to-all | bytes 393216 | tf_op jit(solution)/shard_map/all_to_all | solution.py:13
  95.2 0.7 broadcast_in_dim.7
  95.9 0.0 copy-start.2
  95.9 7.5 %all-to-all-start.5 = ((f32[16,24,128]{2,1,0:T(8,128)}), f32[16,24,128]{2,1,0:T(8,128)S(1)}, u32[]{:S(2)}, u32[]{:S(2)}) async-start(f32[16,24,128]{2,1,0:T(8,128)} %broadcast_in_dim.7), calls=%async_computation.5 | async-start | bytes 393216 | tf_op jit(solution)/shard_map/all_to_all | solution.py:13
  104.0 11.7 %all-to-all-done.5 = f32[16,24,128]{2,1,0:T(8,128)S(1)} async-done(((f32[16,24,128]{2,1,0:T(8,128)}), f32[16,24,128]{2,1,0:T(8,128)S(1)}, u32[]{:S(2)}, u32[]{:S(2)}) %all-to-all-start.5) | async-done | bytes 196640 | tf_op jit(solution)/shard_map/all_to_all | solution.py:13
  115.7 0.7 broadcast_in_dim.8
  116.4 5.0 %all-to-all-start.6 = ((f32[16,24,128]{2,1,0:T(8,128)}), f32[16,24,128]{2,1,0:T(8,128)S(1)}, u32[]{:S(2)}, u32[]{:S(2)}) async-start(f32[16,24,128]{2,1,0:T(8,128)} %broadcast_in_dim.8), calls=%async_computation.6 | async-start | bytes 393216 | tf_op jit(solution)/shard_map/all_to_all | solution.py:13
  121.4 10.2 %collective-permute-start.2 = (bf16[32,256]{1,0:T(8,128)(2,1)S(1)}, bf16[32,256]{1,0:T(8,128)(2,1)S(1)}, u32[]{:S(2)}, u32[]{:S(2)}) collective-permute-start(bf16[32,256]{1,0:T(8,128)(2,1)S(1)} %get-tuple-element.16), channel_id=1, source_target_pairs={{0,1},{1,16},{2,33},{3,48},{4,65},{5,80},{6,97},{7,112},{8,129},{9... | collective-permute-start | bytes 49160 | tf_op jit(solution)/shard_map/ppermute | solution.py:69
  131.6 13.7 %collective-permute-start.1 = (bf16[32,256]{1,0:T(8,128)(2,1)S(1)}, bf16[32,256]{1,0:T(8,128)(2,1)S(1)}, u32[]{:S(2)}, u32[]{:S(2)}) collective-permute-start(bf16[32,256]{1,0:T(8,128)(2,1)S(1)} %get-tuple-element.17), channel_id=1, source_target_pairs={{0,0},{1,17},{2,32},{3,49},{4,64},{5,81},{6,96},{7,113},{8,128},{9... | collective-permute-start | bytes 49160 | tf_op jit(solution)/shard_map/ppermute | solution.py:68
  145.3 0.0 all-to-all-done.6
  145.4 1.9 %collective-permute-start.4 = (f32[3,128,128]{2,1,0:T(8,128)S(1)}, f32[3,128,128]{2,1,0:T(8,128)S(1)}, u32[]{:S(2)}, u32[]{:S(2)}) collective-permute-start(f32[3,128,128]{2,1,0:T(8,128)S(1)} %bitcast.37), channel_id=1, source_target_pairs={{0,1},{1,0},{2,3},{3,2},{4,5},{5,4},{6,7},{7,6},{8,9},{9,8},{10,11... | collective-permute-start | bytes 589832 | tf_op jit(solution)/shard_map/ppermute | solution.py:85
  147.3 0.0 collective-permute-done.2
  147.3 2.3 %collective-permute-done.1 = bf16[32,256]{1,0:T(8,128)(2,1)S(1)} collective-permute-done((bf16[32,256]{1,0:T(8,128)(2,1)S(1)}, bf16[32,256]{1,0:T(8,128)(2,1)S(1)}, u32[]{:S(2)}, u32[]{:S(2)}) %collective-permute-start.1) | collective-permute-done | bytes 16416 | tf_op jit(solution)/shard_map/ppermute | solution.py:68
  149.6 0.6 broadcast_select_fusion.2
  150.2 0.0 collective-permute-done.4
  150.3 0.1 copy.15
  150.4 0.1 copy.16
  150.5 0.0 copy-done.1
  150.5 0.7 maximum_add_fusion
  151.3 0.0 copy-done.2
  151.3 0.7 maximum_add_fusion.1
  (9 shorter events, 0.2 us)
Async XLA Ops:
  0.6 21.7 %copy-start = (bf16[1024,512]{1,0:T(8,128)(2,1)S(1)}, bf16[1024,512]{1,0:T(8,128)(2,1)}, u32[]{:S(2)}) copy-start(bf16[1024,512]{1,0:T(8,128)(2,1)} %param.7) | copy-start | bytes 3145732
  2.1 5.8 %all-to-all-start = ((bf16[2,32,256]{2,1,0:T(8,128)(2,1)}), bf16[2,32,256]{2,1,0:T(8,128)(2,1)S(1)}, u32[]{:S(2)}, u32[]{:S(2)}) async-start(bf16[2,32,256]{2,1,0:T(8,128)(2,1)} %pad_maximum_fusion.1), calls=%async_computation | async-start | bytes 65536 | tf_op jit(solution)/shard_map/all_to_all | solution.py:13
  8.8 22.1 %all-to-all-start.1 = ((bf16[16,64,256]{2,1,0:T(8,128)(2,1)}), bf16[16,64,256]{2,1,0:T(8,128)(2,1)S(1)}, u32[]{:S(2)}, u32[]{:S(2)}) async-start(bf16[16,64,256]{2,1,0:T(8,128)(2,1)} %broadcast_in_dim.6), calls=%async_computation.1 | async-start | bytes 1048576 | tf_op jit(solution)/shard_map/all_to_all | solution.py:13
  17.6 4.8 %collective-permute-start = (bf16[1024,512]{1,0:T(8,128)(2,1)}, bf16[1024,512]{1,0:T(8,128)(2,1)S(1)}, u32[]{:S(2)}, u32[]{:S(2)}) collective-permute-start(bf16[1024,512]{1,0:T(8,128)(2,1)} %param.7), channel_id=1, source_target_pairs={{0,1},{1,0},{2,3},{3,2},{4,5},{5,4},{6,7},{7,6},{8,9},{9,8},{10,11... | collective-permute-start | bytes 3145736 | tf_op jit(solution)/shard_map/ppermute | solution.py:43
  47.0 28.1 %all-to-all-start.3 = ((f32[4,64,256]{2,1,0:T(8,128)}), f32[4,64,256]{2,1,0:T(8,128)S(1)}, u32[]{:S(2)}, u32[]{:S(2)}) async-start(f32[4,64,256]{2,1,0:T(8,128)} %bitcast.8), calls=%async_computation.3 | async-start | bytes 524288 | tf_op jit(solution)/shard_map/all_to_all | solution.py:13
  59.1 21.9 %collective-permute-start.3 = (bf16[64,256]{1,0:T(8,128)(2,1)S(1)}, bf16[64,256]{1,0:T(8,128)(2,1)S(1)}, u32[]{:S(2)}, u32[]{:S(2)}) collective-permute-start(bf16[64,256]{1,0:T(8,128)(2,1)S(1)} %bitcast.40), channel_id=1, source_target_pairs={{0,0},{17,1},{32,2},{49,3},{64,4},{81,5},{96,6},{113,7},{128,8},{1... | collective-permute-start | bytes 98312 | tf_op jit(solution)/shard_map/ppermute | solution.py:52
  81.8 68.7 %copy-start.1 = (f32[256,256]{1,0:T(8,128)S(1)}, f32[256,256]{1,0:T(8,128)}, u32[]{:S(2)}) copy-start(f32[256,256]{1,0:T(8,128)} %param.10) | copy-start | bytes 786436
  95.9 55.4 %copy-start.2 = (f32[256,256]{1,0:T(8,128)S(1)}, f32[256,256]{1,0:T(8,128)}, u32[]{:S(2)}) copy-start(f32[256,256]{1,0:T(8,128)} %param.11) | copy-start | bytes 786436
  95.9 19.8 %all-to-all-start.5 = ((f32[16,24,128]{2,1,0:T(8,128)}), f32[16,24,128]{2,1,0:T(8,128)S(1)}, u32[]{:S(2)}, u32[]{:S(2)}) async-start(f32[16,24,128]{2,1,0:T(8,128)} %broadcast_in_dim.7), calls=%async_computation.5 | async-start | bytes 393216 | tf_op jit(solution)/shard_map/all_to_all | solution.py:13
  116.4 28.9 %all-to-all-start.6 = ((f32[16,24,128]{2,1,0:T(8,128)}), f32[16,24,128]{2,1,0:T(8,128)S(1)}, u32[]{:S(2)}, u32[]{:S(2)}) async-start(f32[16,24,128]{2,1,0:T(8,128)} %broadcast_in_dim.8), calls=%async_computation.6 | async-start | bytes 393216 | tf_op jit(solution)/shard_map/all_to_all | solution.py:13
  121.4 25.9 %collective-permute-start.2 = (bf16[32,256]{1,0:T(8,128)(2,1)S(1)}, bf16[32,256]{1,0:T(8,128)(2,1)S(1)}, u32[]{:S(2)}, u32[]{:S(2)}) collective-permute-start(bf16[32,256]{1,0:T(8,128)(2,1)S(1)} %get-tuple-element.16), channel_id=1, source_target_pairs={{0,1},{1,16},{2,33},{3,48},{4,65},{5,80},{6,97},{7,112},{8,129},{9... | collective-permute-start | bytes 49160 | tf_op jit(solution)/shard_map/ppermute | solution.py:69
  131.6 18.0 %collective-permute-start.1 = (bf16[32,256]{1,0:T(8,128)(2,1)S(1)}, bf16[32,256]{1,0:T(8,128)(2,1)S(1)}, u32[]{:S(2)}, u32[]{:S(2)}) collective-permute-start(bf16[32,256]{1,0:T(8,128)(2,1)S(1)} %get-tuple-element.17), channel_id=1, source_target_pairs={{0,0},{1,17},{2,32},{3,49},{4,64},{5,81},{6,96},{7,113},{8,128},{9... | collective-permute-start | bytes 49160 | tf_op jit(solution)/shard_map/ppermute | solution.py:68
  145.4 4.9 %collective-permute-start.4 = (f32[3,128,128]{2,1,0:T(8,128)S(1)}, f32[3,128,128]{2,1,0:T(8,128)S(1)}, u32[]{:S(2)}, u32[]{:S(2)}) collective-permute-start(f32[3,128,128]{2,1,0:T(8,128)S(1)} %bitcast.37), channel_id=1, source_target_pairs={{0,1},{1,0},{2,3},{3,2},{4,5},{5,4},{6,7},{7,6},{8,9},{9,8},{10,11... | collective-permute-start | bytes 589832 | tf_op jit(solution)/shard_map/ppermute | solution.py:85

commit v3 on v2

v3 whole, which is shorter than its diff:
```python
import jax
import jax.numpy as jnp
from jax import lax
from jax.sharding import Mesh, PartitionSpec as P

AXES = ("x", "zh", "zl", "y", "core")
SIZES = (4, 4, 4, 4, 2)
SWAP = [(0, 1), (1, 0)]


def exchange(parts, axes):
    return lax.all_to_all(parts, axes, 0, 0)


def gather(block, axes, count):
    return exchange(jnp.broadcast_to(block[None], (count, *block.shape)), axes)


def device_id(x, zh, zl, y, core):
    return (((x * 4 + zh) * 4 + zl) * 4 + y) * 2 + core


TURN = [
    (device_id(a, b, c, d, k), device_id(d, c, a, b, k))
    for a in range(4)
    for b in range(4)
    for c in range(4)
    for d in range(4)
    for k in range(2)
]


def per_device(
    inverse_pool, factor_one, factor_two, diag_inv_one, diag_inv_two, struct_one, struct_two
):
    row_count, width = factor_one.shape
    half = width // 2
    chunk = 2 * row_count
    core = lax.axis_index("core")
    first = core == 0
    struct = jnp.where(first, struct_one, struct_two)
    mask = lax.dynamic_slice_in_dim(struct, lax.axis_index(("x", "zh")) * 4, 4)

    pool = inverse_pool.reshape(4, 4, chunk, -1).transpose(1, 0, 2, 3).reshape(inverse_pool.shape)
    sibling_pool = lax.ppermute(pool, "core", SWAP)

    both = jnp.broadcast_to(
        jnp.stack([factor_one, factor_two])[None], (4, 2, row_count, width)
    ).reshape(8, row_count, width)
    rows = exchange(both, ("zl", "core")).reshape(4, chunk, width)
    rows = rows * mask.astype(jnp.bfloat16)[:, None, None]
    strip = gather(lax.ppermute(rows, AXES, TURN), "x", 4)

    def part(which):
        piece = lax.dynamic_slice_in_dim(strip, 2 * which, 2, axis=1)
        return piece.transpose(1, 0, 2, 3).reshape(-1, width)

    partial = jnp.dot(pool, part(core), preferred_element_type=jnp.float32) + jnp.dot(
        sibling_pool, part(1 - core), preferred_element_type=jnp.float32
    )
    product = jnp.sum(exchange(partial.reshape(4, -1, width), "y"), axis=0)

    column = jnp.sum(exchange(product.reshape(4, chunk, width), "zl"), axis=0)
    own = lax.dynamic_index_in_dim(mask, lax.axis_index("zl"), keepdims=False)
    column = (-(column * own.astype(jnp.float32))).astype(jnp.bfloat16)
    column = exchange(column.reshape(2, row_count, width), "core")

    flat = rows.reshape(-1, width).astype(jnp.float32)

    def term(left, right):
        return lax.dot_general(
            flat[:, left],
            product[:, right],
            (((0,), (0,)), ((), ())),
            precision=lax.Precision.HIGHEST,
            preferred_element_type=jnp.float32,
        )

    low, high = slice(0, half), slice(half, width)
    packed = jnp.concatenate([term(low, low), term(low, high), term(high, high)], axis=0)
    shard = jnp.sum(exchange(packed.reshape(16, -1, half), ("x", "y")), axis=0)
    shard = jnp.sum(gather(shard, ("zh", "zl"), 16), axis=0)
    total = gather(shard, ("x", "y"), 16).reshape(3, half, half)
    sibling = lax.ppermute(total, "core", SWAP)

    def whole(t):
        return jnp.concatenate(
            [
                jnp.concatenate([t[0], t[1]], axis=1),
                jnp.concatenate([t[1].T, t[2]], axis=1),
            ],
            axis=0,
        )

    return (
        column[0],
        column[1],
        diag_inv_one + whole(jnp.where(first, total, sibling)),
        diag_inv_two + whole(jnp.where(first, sibling, total)),
    )


def solution(mesh):
    fine = Mesh(mesh.devices.reshape(SIZES), AXES)
    rows = P(AXES, None)
    in_specs = (P(("x", "zh"), ("zl", "y", "core")), rows, rows, P(), P(), P(), P())
    out_specs = (rows, rows, P(), P())
    return jax.shard_map(
        per_device, mesh=fine, in_specs=in_specs, out_specs=out_specs, check_vma=False
    )
```

time: 153 us -> 148 us (0.967)
  the two profiles are of different devices: /device:TPU:17 before, /device:TPU:1 now
where the time goes in v3:
time: 148 us; the launch traced here: 147 us
  starting transfers between devices  80.6 us (54%)
  waiting for transfers between devices  49.3 us (33%)
  local copies, waits for them, and re-layouts  9.47 us (6%)
  other arithmetic  3.96 us (3%)
  matrix products  1.74 us (1%)
  between operations  1.54 us (1%)
    all_to_all x8, starting transfers between devices, exchange(): return lax.all_to_all(parts, axes, 0, 0)  76 us
    all_to_all x8, waiting for transfers between devices, exchange(): return lax.all_to_all(parts, axes, 0, 0)  48.6 us
  transfers between devices with their start and end apart: 11, of which 8 were waited for; matrix products, arithmetic and copies ran while one was open for 4% of the time, Pallas kernels for 0%

profile of v3, /device:TPU:1, one launch (start us, length us, event | category | flops | bytes accessed | tf_op | source)
XLA Modules:
  0.0 146.6 jit_solution(3131222848586685753)
XLA Ops:
  0.6 0.7 pad_maximum_fusion.1
  1.4 0.7 broadcast_in_dim.8
  2.0 10.2 %all-to-all-start = ((bf16[8,32,256]{2,1,0:T(8,128)(2,1)}), bf16[8,32,256]{2,1,0:T(8,128)(2,1)S(1)}, u32[]{:S(2)}, u32[]{:S(2)}) async-start(bf16[8,32,256]{2,1,0:T(8,128)(2,1)} %bitcast.2), calls=%async_computation | async-start | bytes 262144 | tf_op jit(solution)/shard_map/all_to_all | solution.py:12
  12.2 1.3 copy.34
  13.5 2.0 %collective-permute-start.1 = (bf16[1024,512]{1,0:T(8,128)(2,1)S(1)}, bf16[1024,512]{1,0:T(8,128)(2,1)S(1)}, u32[]{:S(2)}, u32[]{:S(2)}) collective-permute-start(bf16[1024,512]{1,0:T(8,128)(2,1)S(1)} %bitcast.54), channel_id=1, source_target_pairs={{0,1},{1,0},{2,3},{3,2},{4,5},{5,4},{6,7},{7,6},{8,9},{9,8},{10,11... | collective-permute-start | bytes 3145736 | tf_op jit(solution)/shard_map/ppermute | solution.py:45
  15.5 0.0 copy-start.2
  15.6 0.0 copy-start.3
  15.6 0.6 copy-done.2
  16.2 0.0 copy-done.3
  16.2 0.1 dynamic-slice_convert_fusion
  16.3 1.7 %all-to-all-done = bf16[8,32,256]{2,1,0:T(8,128)(2,1)S(1)} async-done(((bf16[8,32,256]{2,1,0:T(8,128)(2,1)}), bf16[8,32,256]{2,1,0:T(8,128)(2,1)S(1)}, u32[]{:S(2)}, u32[]{:S(2)}) %all-to-all-start) | async-done | bytes 131104 | tf_op jit(solution)/shard_map/all_to_all | solution.py:12
  18.0 0.1 bitcast_multiply_fusion.1
  18.1 0.7 collective-permute-start
  18.8 0.0 collective-permute-done
  18.8 0.8 broadcast_in_dim.9
  19.6 10.2 %all-to-all-start.1 = ((bf16[4,4,64,256]{3,2,1,0:T(8,128)(2,1)}), bf16[4,4,64,256]{3,2,1,0:T(8,128)(2,1)S(1)}, u32[]{:S(2)}, u32[]{:S(2)}) async-start(bf16[4,4,64,256]{3,2,1,0:T(8,128)(2,1)} %broadcast_in_dim.9), calls=%async_computation.1 | async-start | bytes 1048576 | tf_op jit(solution)/shard_map/all_to_all | solution.py:12
  29.8 7.0 %all-to-all-done.1 = bf16[4,4,64,256]{3,2,1,0:T(8,128)(2,1)S(1)} async-done(((bf16[4,4,64,256]{3,2,1,0:T(8,128)(2,1)}), bf16[4,4,64,256]{3,2,1,0:T(8,128)(2,1)S(1)}, u32[]{:S(2)}, u32[]{:S(2)}) %all-to-all-start.1) | async-done | bytes 524320 | tf_op jit(solution)/shard_map/all_to_all | solution.py:12
  36.9 0.5 fusion.9
  37.4 0.0 collective-permute-done.1
  37.4 0.5 convolution_add_fusion
  37.9 1.1 copy.46
  38.9 12.8 %all-to-all-start.2 = ((f32[4,256,256]{1,2,0:T(8,128)}), f32[4,256,256]{1,2,0:T(8,128)S(1)}, u32[]{:S(2)}, u32[]{:S(2)}) async-start(f32[4,256,256]{1,2,0:T(8,128)} %bitcast.52), calls=%async_computation.2 | async-start | bytes 2097152 | tf_op jit(solution)/shard_map/all_to_all | solution.py:12
  51.7 0.1 mul.45
  51.8 0.1 mul.46
  51.9 0.1 bitcast_multiply_fusion
  52.0 10.8 %all-to-all-done.2 = f32[4,256,256]{1,2,0:T(8,128)S(1)} async-done(((f32[4,256,256]{1,2,0:T(8,128)}), f32[4,256,256]{1,2,0:T(8,128)S(1)}, u32[]{:S(2)}, u32[]{:S(2)}) %all-to-all-start.2) | async-done | bytes 1048608 | tf_op jit(solution)/shard_map/all_to_all | solution.py:12
  62.8 0.1 reduce_sum.36
  62.9 0.3 fusion.2
  63.1 0.3 fusion
  63.4 0.3 fusion.4
  63.6 0.7 pad_maximum_fusion
  64.3 3.5 %all-to-all-start.5 = ((f32[16,24,128]{2,1,0:T(8,128)}), f32[16,24,128]{2,1,0:T(8,128)S(1)}, u32[]{:S(2)}, u32[]{:S(2)}) async-start(f32[16,24,128]{2,1,0:T(8,128)} %bitcast.18), calls=%async_computation.5 | async-start | bytes 393216 | tf_op jit(solution)/shard_map/all_to_all | solution.py:12
  67.9 0.8 copy.38
  68.7 6.1 %all-to-all-done.5 = f32[16,24,128]{2,1,0:T(8,128)S(1)} async-done(((f32[16,24,128]{2,1,0:T(8,128)}), f32[16,24,128]{2,1,0:T(8,128)S(1)}, u32[]{:S(2)}, u32[]{:S(2)}) %all-to-all-start.5) | async-done | bytes 196640 | tf_op jit(solution)/shard_map/all_to_all | solution.py:12
  74.8 7.3 %all-to-all-start.3 = ((f32[4,64,256]{2,1,0:T(8,128)}), f32[4,64,256]{2,1,0:T(8,128)S(1)}, u32[]{:S(2)}, u32[]{:S(2)}) async-start(f32[4,64,256]{2,1,0:T(8,128)} %bitcast.12), calls=%async_computation.3 | async-start | bytes 524288 | tf_op jit(solution)/shard_map/all_to_all | solution.py:12
  82.1 5.6 %all-to-all-done.3 = f32[4,64,256]{2,1,0:T(8,128)S(1)} async-done(((f32[4,64,256]{2,1,0:T(8,128)}), f32[4,64,256]{2,1,0:T(8,128)S(1)}, u32[]{:S(2)}, u32[]{:S(2)}) %all-to-all-start.3) | async-done | bytes 262176 | tf_op jit(solution)/shard_map/all_to_all | solution.py:12
  87.7 0.7 broadcast_in_dim.10
  88.4 17.5 %all-to-all-start.6 = ((f32[16,24,128]{2,1,0:T(8,128)}), f32[16,24,128]{2,1,0:T(8,128)S(1)}, u32[]{:S(2)}, u32[]{:S(2)}) async-start(f32[16,24,128]{2,1,0:T(8,128)} %broadcast_in_dim.10), calls=%async_computation.6 | async-start | bytes 393216 | tf_op jit(solution)/shard_map/all_to_all | solution.py:12
  105.9 0.6 dynamic_slice.19
  107.2 11.2 %all-to-all-done.6 = f32[16,24,128]{2,1,0:T(8,128)S(1)} async-done(((f32[16,24,128]{2,1,0:T(8,128)}), f32[16,24,128]{2,1,0:T(8,128)S(1)}, u32[]{:S(2)}, u32[]{:S(2)}) %all-to-all-start.6) | async-done | bytes 196640 | tf_op jit(solution)/shard_map/all_to_all | solution.py:12
  118.3 0.7 broadcast_in_dim.11
  119.0 3.5 %all-to-all-start.7 = ((f32[16,24,128]{2,1,0:T(8,128)}), f32[16,24,128]{2,1,0:T(8,128)S(1)}, u32[]{:S(2)}, u32[]{:S(2)}) async-start(f32[16,24,128]{2,1,0:T(8,128)} %broadcast_in_dim.11), calls=%async_computation.7 | async-start | bytes 393216 | tf_op jit(solution)/shard_map/all_to_all | solution.py:12
  122.6 0.6 negate_convert_fusion
  123.2 6.3 %all-to-all-done.7 = f32[16,24,128]{2,1,0:T(8,128)S(1)} async-done(((f32[16,24,128]{2,1,0:T(8,128)}), f32[16,24,128]{2,1,0:T(8,128)S(1)}, u32[]{:S(2)}, u32[]{:S(2)}) %all-to-all-start.7) | async-done | bytes 196640 | tf_op jit(solution)/shard_map/all_to_all | solution.py:12
  129.5 11.1 %all-to-all-start.4 = ((bf16[2,32,256]{2,1,0:T(8,128)(2,1)}), bf16[2,32,256]{2,1,0:T(8,128)(2,1)S(1)}, u32[]{:S(2)}, u32[]{:S(2)}) async-start(bf16[2,32,256]{2,1,0:T(8,128)(2,1)} %bitcast.14), calls=%async_computation.4 | async-start | bytes 65536 | tf_op jit(solution)/shard_map/all_to_all | solution.py:12
  140.5 1.9 %collective-permute-start.2 = (f32[3,128,128]{2,1,0:T(8,128)S(1)}, f32[3,128,128]{2,1,0:T(8,128)S(1)}, u32[]{:S(2)}, u32[]{:S(2)}) collective-permute-start(f32[3,128,128]{2,1,0:T(8,128)S(1)} %bitcast.61), channel_id=1, source_target_pairs={{0,1},{1,0},{2,3},{3,2},{4,5},{5,4},{6,7},{7,6},{8,9},{9,8},{10,11... | collective-permute-start | bytes 589832 | tf_op jit(solution)/shard_map/ppermute | solution.py:84
  142.5 0.0 all-to-all-done.4
  142.5 0.6 slice_bitcast_fusion.8
  143.1 0.8 collective-permute-done.2
  143.9 0.0 copy-start
  143.9 0.1 copy.40
  144.0 0.1 copy.39
  144.1 0.7 copy-done
  144.9 0.0 copy-start.1
  144.9 0.7 maximum_add_fusion.1
  145.6 0.3 copy-done.1
  145.9 0.7 maximum_add_fusion
  (9 shorter events, 0.2 us)
Async XLA Ops:
  2.0 16.0 %all-to-all-start = ((bf16[8,32,256]{2,1,0:T(8,128)(2,1)}), bf16[8,32,256]{2,1,0:T(8,128)(2,1)S(1)}, u32[]{:S(2)}, u32[]{:S(2)}) async-start(bf16[8,32,256]{2,1,0:T(8,128)(2,1)} %bitcast.2), calls=%async_computation | async-start | bytes 262144 | tf_op jit(solution)/shard_map/all_to_all | solution.py:12
  13.5 23.8 %collective-permute-start.1 = (bf16[1024,512]{1,0:T(8,128)(2,1)S(1)}, bf16[1024,512]{1,0:T(8,128)(2,1)S(1)}, u32[]{:S(2)}, u32[]{:S(2)}) collective-permute-start(bf16[1024,512]{1,0:T(8,128)(2,1)S(1)} %bitcast.54), channel_id=1, source_target_pairs={{0,1},{1,0},{2,3},{3,2},{4,5},{5,4},{6,7},{7,6},{8,9},{9,8},{10,11... | collective-permute-start | bytes 3145736 | tf_op jit(solution)/shard_map/ppermute | solution.py:45
  15.5 0.7 copy-start.2
  15.6 0.7 copy-start.3
  18.1 0.7 collective-permute-start
  19.6 17.1 %all-to-all-start.1 = ((bf16[4,4,64,256]{3,2,1,0:T(8,128)(2,1)}), bf16[4,4,64,256]{3,2,1,0:T(8,128)(2,1)S(1)}, u32[]{:S(2)}, u32[]{:S(2)}) async-start(bf16[4,4,64,256]{3,2,1,0:T(8,128)(2,1)} %broadcast_in_dim.9), calls=%async_computation.1 | async-start | bytes 1048576 | tf_op jit(solution)/shard_map/all_to_all | solution.py:12
  38.9 23.8 %all-to-all-start.2 = ((f32[4,256,256]{1,2,0:T(8,128)}), f32[4,256,256]{1,2,0:T(8,128)S(1)}, u32[]{:S(2)}, u32[]{:S(2)}) async-start(f32[4,256,256]{1,2,0:T(8,128)} %bitcast.52), calls=%async_computation.2 | async-start | bytes 2097152 | tf_op jit(solution)/shard_map/all_to_all | solution.py:12
  64.3 10.4 %all-to-all-start.5 = ((f32[16,24,128]{2,1,0:T(8,128)}), f32[16,24,128]{2,1,0:T(8,128)S(1)}, u32[]{:S(2)}, u32[]{:S(2)}) async-start(f32[16,24,128]{2,1,0:T(8,128)} %bitcast.18), calls=%async_computation.5 | async-start | bytes 393216 | tf_op jit(solution)/shard_map/all_to_all | solution.py:12
  74.8 12.9 %all-to-all-start.3 = ((f32[4,64,256]{2,1,0:T(8,128)}), f32[4,64,256]{2,1,0:T(8,128)S(1)}, u32[]{:S(2)}, u32[]{:S(2)}) async-start(f32[4,64,256]{2,1,0:T(8,128)} %bitcast.12), calls=%async_computation.3 | async-start | bytes 524288 | tf_op jit(solution)/shard_map/all_to_all | solution.py:12
  88.4 30.0 %all-to-all-start.6 = ((f32[16,24,128]{2,1,0:T(8,128)}), f32[16,24,128]{2,1,0:T(8,128)S(1)}, u32[]{:S(2)}, u32[]{:S(2)}) async-start(f32[16,24,128]{2,1,0:T(8,128)} %broadcast_in_dim.10), calls=%async_computation.6 | async-start | bytes 393216 | tf_op jit(solution)/shard_map/all_to_all | solution.py:12
  119.0 10.4 %all-to-all-start.7 = ((f32[16,24,128]{2,1,0:T(8,128)}), f32[16,24,128]{2,1,0:T(8,128)S(1)}, u32[]{:S(2)}, u32[]{:S(2)}) async-start(f32[16,24,128]{2,1,0:T(8,128)} %broadcast_in_dim.11), calls=%async_computation.7 | async-start | bytes 393216 | tf_op jit(solution)/shard_map/all_to_all | solution.py:12
  129.5 13.0 %all-to-all-start.4 = ((bf16[2,32,256]{2,1,0:T(8,128)(2,1)}), bf16[2,32,256]{2,1,0:T(8,128)(2,1)S(1)}, u32[]{:S(2)}, u32[]{:S(2)}) async-start(bf16[2,32,256]{2,1,0:T(8,128)(2,1)} %bitcast.14), calls=%async_computation.4 | async-start | bytes 65536 | tf_op jit(solution)/shard_map/all_to_all | solution.py:12
  140.5 3.3 %collective-permute-start.2 = (f32[3,128,128]{2,1,0:T(8,128)S(1)}, f32[3,128,128]{2,1,0:T(8,128)S(1)}, u32[]{:S(2)}, u32[]{:S(2)}) collective-permute-start(f32[3,128,128]{2,1,0:T(8,128)S(1)} %bitcast.61), channel_id=1, source_target_pairs={{0,1},{1,0},{2,3},{3,2},{4,5},{5,4},{6,7},{7,6},{8,9},{9,8},{10,11... | collective-permute-start | bytes 589832 | tf_op jit(solution)/shard_map/ppermute | solution.py:84
  143.9 1.0 copy-start
  144.9 1.0 copy-start.1

commit v4 on v3

v4 whole, which is shorter than its diff:
```python
import jax
import jax.numpy as jnp
from jax import lax
from jax.experimental import pallas as pl
from jax.experimental.pallas import tpu as pltpu
from jax.sharding import Mesh, PartitionSpec as P

AXES = ("x", "zh", "zl", "y", "core")
SIZES = (4, 4, 4, 4, 2)
SWAP = [(0, 1), (1, 0)]
VMEM = pl.BlockSpec(memory_space=pltpu.VMEM)
SMEM = pl.BlockSpec(memory_space=pltpu.SMEM)
PARAMS = pltpu.CompilerParams(vmem_limit_bytes=32 * 1024 * 1024)


def exchange(parts, axes):
    return lax.all_to_all(parts, axes, 0, 0)


def gather(block, axes, count):
    return exchange(jnp.broadcast_to(block[None], (count, *block.shape)), axes)


def device_id(x, zh, zl, y, core):
    return (((x * 4 + zh) * 4 + zl) * 4 + y) * 2 + core


def turn_source(x, zh, zl, y):
    near = (1, 2, 3, 0) if zl < 2 else (2, 3, 0, 1)
    return zl, y, near[(zh - y) % 4], (y + 2 + x - zl) % 4


TURN = [
    (device_id(*turn_source(a, b, c, d), k), device_id(a, b, c, d, k))
    for a in range(4)
    for b in range(4)
    for c in range(4)
    for d in range(4)
    for k in range(2)
]


def multiply_kernel(pool, sibling, strip, out, rhs):
    core = lax.axis_index("core")
    shift = lax.axis_index("zl") - lax.axis_index("y") + 2
    depth = rhs.shape[0] // 2
    for side, which in ((0, core), (1, 1 - core)):
        for h in range(2):
            for j in range(4):
                start = side * depth + h * 256 + j * 64
                rhs[start : start + 64] = strip[(j + shift) & 3, 2 * which + h]
    for z in range(4):
        rows = slice(z * 256, (z + 1) * 256)
        block = jnp.dot(
            pool[rows], rhs[:depth], preferred_element_type=jnp.float32
        ) + jnp.dot(sibling[rows], rhs[depth:], preferred_element_type=jnp.float32)
        for y in range(4):
            out[y, z] = block[y * 64 : (y + 1) * 64]


def diagonal_kernel(parts, rows, packed, pieces):
    product = parts[0] + parts[1] + parts[2] + parts[3]
    left = rows[...]
    term = jnp.zeros((256, 256), jnp.float32)
    rest = product
    for _ in range(3):
        piece = rest.astype(jnp.bfloat16)
        rest = rest - piece.astype(jnp.float32)
        term = term + lax.dot_general(
            left, piece, (((0,), (0,)), ((), ())), preferred_element_type=jnp.float32
        )
    packed[0:128] = term[:128, :128]
    packed[128:256] = term[:128, 128:]
    packed[256:384] = term[128:, 128:]
    for z in range(4):
        pieces[z, 0:64] = product[z * 64 : (z + 1) * 64, :128]
        pieces[z, 64:128] = product[z * 64 : (z + 1) * 64, 128:]


def join_kernel(parts, pieces, out):
    shard = parts[0]
    for i in range(1, 16):
        shard = shard + parts[i]
    for z in range(4):
        out[z, 0:128] = pieces[z]
        out[z, 128:152] = shard


def split_kernel(mask, parts, shards, stay, leave):
    core = lax.axis_index("core")
    own = -mask[lax.axis_index("zl")].astype(jnp.float32)
    summed = parts[0] + parts[1] + parts[2] + parts[3]
    for i in range(4):
        shards[i] = summed[128:152]
    column = summed[0:128] * own
    low = jnp.concatenate([column[0:32], column[64:96]])
    high = jnp.concatenate([column[32:64], column[96:128]])
    stay[...] = jnp.where(core == 0, low, high)
    leave[...] = jnp.where(core == 0, high, low)


def finish_kernel(mine, swapped, inv_one, inv_two, column_one, column_two, diag_one, diag_two):
    first = lax.axis_index("core") == 0
    own, other = mine[...], swapped[...]
    one = jnp.where(first, own, other)
    two = jnp.where(first, other, own)
    for t, inv, diag, column in (
        (one, inv_one, diag_one, column_one),
        (two, inv_two, diag_two, column_two),
    ):
        diag[0:128, 0:128] = inv[0:128, 0:128] + t[0:128]
        diag[0:128, 128:256] = inv[0:128, 128:256] + t[128:256]
        diag[128:256, 0:128] = inv[128:256, 0:128] + t[128:256].T
        diag[128:256, 128:256] = inv[128:256, 128:256] + t[256:384]
        column[:, 0:128] = t[384:416].astype(jnp.bfloat16)
        column[:, 128:256] = t[416:448].astype(jnp.bfloat16)


def call(kernel, outs, args, scratch=(), scalars=0):
    many = isinstance(outs, list)
    return pl.pallas_call(
        kernel,
        out_shape=outs,
        in_specs=[SMEM] * scalars + [VMEM] * (len(args) - scalars),
        out_specs=[VMEM] * len(outs) if many else VMEM,
        scratch_shapes=list(scratch),
        compiler_params=PARAMS,
    )(*args)


def per_device(
    inverse_pool, factor_one, factor_two, diag_inv_one, diag_inv_two, struct_one, struct_two
):
    row_count, width = factor_one.shape
    f32 = jnp.float32
    core = lax.axis_index("core")
    first = core == 0
    struct = jnp.where(first, struct_one, struct_two)
    mask = lax.dynamic_slice_in_dim(struct, lax.axis_index(("x", "zh")) * 4, 4)
    sibling_pool = lax.ppermute(inverse_pool, "core", SWAP)

    both = jnp.broadcast_to(
        jnp.stack([factor_one, factor_two])[None], (4, 2, row_count, width)
    ).reshape(8, row_count, width)
    rows = exchange(both, ("zl", "core")).reshape(4, 2 * row_count, width)
    rows = rows * mask.astype(jnp.bfloat16)[:, None, None]
    rows = lax.optimization_barrier(rows)
    strip = gather(lax.ppermute(rows, AXES, TURN), "x", 4)

    partial = call(
        multiply_kernel,
        jax.ShapeDtypeStruct((4, 4, 64, 256), f32),
        (inverse_pool, sibling_pool, strip),
        [pltpu.VMEM((1024, 256), jnp.bfloat16)],
    )
    parts = exchange(partial.reshape(4, 256, width), "y")
    packed, pieces = call(
        diagonal_kernel,
        [jax.ShapeDtypeStruct((384, 128), f32), jax.ShapeDtypeStruct((4, 128, 128), f32)],
        (parts, rows.reshape(256, width)),
    )
    parts = exchange(packed.reshape(16, 24, 128), ("x", "y"))
    joined = call(join_kernel, jax.ShapeDtypeStruct((4, 152, 128), f32), (parts, pieces))
    quarter = jax.ShapeDtypeStruct((2 * row_count, 128), f32)
    shards, stay, leave = call(
        split_kernel,
        [jax.ShapeDtypeStruct((4, 24, 128), f32), quarter, quarter],
        (mask, exchange(joined, "zl")),
        scalars=1,
    )
    shard = jnp.sum(exchange(shards, "zh"), axis=0)
    total = gather(shard, ("x", "y"), 16).reshape(384, 128)
    swapped = lax.ppermute(jnp.concatenate([total, leave]), "core", SWAP)
    wide = jax.ShapeDtypeStruct((row_count, width), jnp.bfloat16)
    square = jax.ShapeDtypeStruct((width, width), f32)
    return tuple(
        call(
            finish_kernel,
            [wide, wide, square, square],
            (jnp.concatenate([total, stay]), swapped, diag_inv_one, diag_inv_two),
        )
    )


def solution(mesh):
    fine = Mesh(mesh.devices.reshape(SIZES), AXES)
    rows = P(AXES, None)
    in_specs = (P(("x", "zh"), ("zl", "y", "core")), rows, rows, P(), P(), P(), P())
    out_specs = (rows, rows, P(), P())
    return jax.shard_map(
        per_device, mesh=fine, in_specs=in_specs, out_specs=out_specs, check_vma=False
    )
```

time: 148 us -> 130 us (0.88)
  blocking collectives: 0 us -> 85.1 us
  starting transfers between devices: 80.6 us -> 33.1 us
  waiting for transfers between devices: 49.3 us -> 6.57 us
  local copies, waits for them, and re-layouts: 9.47 us -> 0.74 us
  other arithmetic: 3.96 us -> 0.95 us
  Pallas kernels: 0 us -> 2.5 us
  matrix products: 1.74 us -> 0 us
    all_to_all x0 -> x6, blocking collectives: none -> 85.1 us  [exchange(): return lax.all_to_all(parts, axes, 0, 0)]
    all_to_all x8 -> x1, starting transfers between devices: 76 us -> 10.3 us  [exchange(): return lax.all_to_all(parts, axes, 0, 0)]
    all_to_all x8 -> x1, waiting for transfers between devices: 48.6 us -> 3.55 us  [exchange(): return lax.all_to_all(parts, axes, 0, 0)]
    ppermute x2, starting transfers between devices: 3.94 us -> 13.2 us  [the longest x1 11.1 us: per_device(): swapped = lax.ppermute(jnp.concatenate([total, leave]), 'core', SWAP)]
    ppermute x1, starting transfers between devices: 0.67 us -> 9.54 us  [per_device(): strip = gather(lax.ppermute(rows, AXES, TURN), 'x', 4)]
    pallas_call x0 -> x5, Pallas kernels: none -> 2.5 us  [call(): pl.pallas_call(kernel, out_shape=outs, in_specs=[SMEM] * scalars + [VMEM]...]
    broadcast_in_dim x3 -> x2, local copies, waits for them, and re-layouts: 2.22 us -> 0.06 us  [gather(): return exchange(jnp.broadcast_to(block[None], (count, *block.shape)), axes)]
    ppermute x1, waiting for transfers between devices: 0.01 us -> 1.93 us  [per_device(): strip = gather(lax.ppermute(rows, AXES, TURN), 'x', 4)]
  transfers between devices with their start and end apart: 11 -> 4, of which waited for: 8 -> 3; matrix products, arithmetic and copies ran while one was open for 4% -> 0% of each run, Pallas kernels for 0% -> 0%
where the time goes in v4:
time: 130 us
  blocking collectives  85.1 us (65%)
  starting transfers between devices  33.1 us (25%)
  waiting for transfers between devices  6.57 us (5%)
  Pallas kernels  2.5 us (2%)
    all_to_all x6, blocking collectives, exchange(): return lax.all_to_all(parts, axes, 0, 0)  85.1 us
    ppermute x1, starting transfers between devices, per_device(): swapped = lax.ppermute(jnp.concatenate([total, leave]), 'core', SWAP)  11.1 us
    all_to_all x1, starting transfers between devices, exchange(): return lax.all_to_all(parts, axes, 0, 0)  10.3 us
    ppermute x1, starting transfers between devices, per_device(): strip = gather(lax.ppermute(rows, AXES, TURN), 'x', 4)  9.54 us
    all_to_all x1, waiting for transfers between devices, exchange(): return lax.all_to_all(parts, axes, 0, 0)  3.55 us
  transfers between devices with their start and end apart: 4, of which 3 were waited for; matrix products, arithmetic and copies ran while one was open for 0% of the time, Pallas kernels for 0%

profile of v4, /device:TPU:1, one launch (start us, length us, event | category | flops | bytes accessed | tf_op | source)
XLA Modules:
  0.0 129.6 jit_solution(7327520198079656169)
XLA Ops:
  0.6 0.7 pad_maximum_fusion.2
  1.4 0.7 broadcast_in_dim.6
  2.0 0.0 copy-start.3
  2.0 0.0 copy-start.4
  2.0 10.3 %all-to-all-start = ((bf16[8,32,256]{2,1,0:T(8,128)(2,1)}), bf16[8,32,256]{2,1,0:T(8,128)(2,1)S(1)}, u32[]{:S(2)}, u32[]{:S(2)}) async-start(bf16[8,32,256]{2,1,0:T(8,128)(2,1)} %bitcast.2), calls=%async_computation | async-start | bytes 262144 | tf_op jit(solution)/shard_map/all_to_all | solution.py:17
  12.3 0.0 copy-start
  12.3 2.2 %collective-permute-start = (bf16[1024,512]{1,0:T(8,128)(2,1)}, bf16[1024,512]{1,0:T(8,128)(2,1)S(1)}, u32[]{:S(2)}, u32[]{:S(2)}) collective-permute-start(bf16[1024,512]{1,0:T(8,128)(2,1)} %pool.1), channel_id=1, source_target_pairs={{0,1},{1,0},{2,3},{3,2},{4,5},{5,4},{6,7},{7,6},{8,9},{9,8},{10,11... | collective-permute-start | bytes 3145736 | tf_op jit(solution)/shard_map/ppermute | solution.py:140
  14.5 0.0 copy-done.3
  14.5 0.0 copy-done.4
  14.5 0.1 fusion
  14.6 3.5 %all-to-all-done = bf16[8,32,256]{2,1,0:T(8,128)(2,1)S(1)} async-done(((bf16[8,32,256]{2,1,0:T(8,128)(2,1)}), bf16[8,32,256]{2,1,0:T(8,128)(2,1)S(1)}, u32[]{:S(2)}, u32[]{:S(2)}) %all-to-all-start) | async-done | bytes 131104 | tf_op jit(solution)/shard_map/all_to_all | solution.py:17
  18.2 0.1 bitcast_multiply_fusion
  18.2 9.5 %collective-permute-start.1 = (bf16[4,64,256]{2,1,0:T(8,128)(2,1)S(1)}, bf16[4,64,256]{2,1,0:T(8,128)(2,1)S(1)}, u32[]{:S(2)}, u32[]{:S(2)}) collective-permute-start(bf16[4,64,256]{2,1,0:T(8,128)(2,1)S(1)} %bitcast_multiply_fusion), channel_id=1, source_target_pairs={{12,0},{13,1},{38,2},{39,3},{88,4},{89,5},{114,6},{115,7},{138,8},... | collective-permute-start | bytes 393224 | tf_op jit(solution)/shard_map/ppermute | solution.py:148
  27.8 1.9 %collective-permute-done.1 = bf16[4,64,256]{2,1,0:T(8,128)(2,1)S(1)} collective-permute-done((bf16[4,64,256]{2,1,0:T(8,128)(2,1)S(1)}, bf16[4,64,256]{2,1,0:T(8,128)(2,1)S(1)}, u32[]{:S(2)}, u32[]{:S(2)}) %collective-permute-start.1) | collective-permute-done | bytes 131104 | tf_op jit(solution)/shard_map/ppermute | solution.py:148
  29.8 12.4 %all_to_all.35.strip = bf16[4,4,64,256]{3,2,1,0:T(8,128)(2,1)S(1)} all-to-all(bf16[4,4,64,256]{3,2,1,0:T(8,128)(2,1)S(1)} %broadcast_in_dim.7), channel_id=1, replica_groups=mesh['x'=4,'zh'=4,'zl'=4,'y'=4,'core'=2] {'x'}, dimensions={0} | all-to-all | bytes 1048576 | tf_op jit(solution)/shard_map/all_to_all | solution.py:17
  42.2 0.0 collective-permute-done.sibling
  42.2 0.0 copy-done
  42.2 0.7 shard_map.102
  42.9 17.8 %all_to_all.36.parts = f32[4,256,256]{2,1,0:T(8,128)S(1)} all-to-all(f32[4,256,256]{2,1,0:T(8,128)S(1)} %bitcast.10), channel_id=1, replica_groups=mesh['x'=4,'zh'=4,'zl'=4,'y'=4,'core'=2] {'y'}, dimensions={0} | all-to-all | bytes 2097152 | tf_op jit(solution)/shard_map/all_to_all | solution.py:17
  60.7 0.3 shard_map.103
  61.0 9.6 %all_to_all.37.parts = f32[16,24,128]{2,1,0:T(8,128)S(1)} all-to-all(f32[16,24,128]{2,1,0:T(8,128)S(1)} %bitcast.12), channel_id=1, replica_groups=mesh['x'=4,'zh'=4,'zl'=4,'y'=4,'core'=2] {'x','y'}, dimensions={0} | all-to-all | bytes 393216 | tf_op jit(solution)/shard_map/all_to_all | solution.py:17
  70.7 12.6 %all_to_all.38.parts = f32[4,152,128]{2,1,0:T(8,128)S(1)} all-to-all(f32[4,152,128]{2,1,0:T(8,128)S(1)} %shard_map.104), channel_id=1, replica_groups=mesh['x'=4,'zh'=4,'zl'=4,'y'=4,'core'=2] {'zl'}, dimensions={0} | all-to-all | bytes 622592 | tf_op jit(solution)/shard_map/all_to_all | solution.py:17
  83.2 0.6 shard_map.105
  83.8 22.5 %all_to_all.39 = f32[4,24,128]{2,1,0:T(8,128)S(1)} all-to-all(f32[4,24,128]{2,1,0:T(8,128)S(1)} %get-tuple-element.11), channel_id=1, replica_groups=mesh['x'=4,'zh'=4,'zl'=4,'y'=4,'core'=2] {'zh'}, dimensions={0} | all-to-all | bytes 98304 | tf_op jit(solution)/shard_map/all_to_all | solution.py:17
  106.4 10.2 %all_to_all.40 = f32[16,24,128]{2,1,0:T(8,128)S(1)} all-to-all(f32[16,24,128]{2,1,0:T(8,128)S(1)} %broadcast_in_dim.8), channel_id=1, replica_groups=mesh['x'=4,'zh'=4,'zl'=4,'y'=4,'core'=2] {'x','y'}, dimensions={0} | all-to-all | bytes 393216 | tf_op jit(solution)/shard_map/all_to_all | solution.py:17
  116.5 0.0 copy-start.1
  116.5 0.0 copy-start.2
  116.6 11.1 %collective-permute-start.2 = (f32[448,128]{1,0:T(8,128)S(1)}, f32[448,128]{1,0:T(8,128)S(1)}, u32[]{:S(2)}, u32[]{:S(2)}) collective-permute-start(f32[448,128]{1,0:T(8,128)S(1)} %get-tuple-element.16), channel_id=1, source_target_pairs={{0,1},{1,0},{2,3},{3,2},{4,5},{5,4},{6,7},{7,6},{8,9},{9,8},{10,11... | collective-permute-start | bytes 688136 | tf_op jit(solution)/shard_map/ppermute | solution.py:173
  127.6 1.1 collective-permute-done.2.swapped
  128.7 0.0 copy-done.1
  128.7 0.0 copy-done.2
  128.7 0.9 shard_map.106
  (6 shorter events, 0.1 us)
Async XLA Ops:
  2.0 12.5 %copy-start.3 = (s32[64]{0:T(128)S(1)}, s32[64]{0:T(128)}, u32[]{:S(2)}) copy-start(s32[64]{0:T(128)} %param.12) | copy-start | bytes 772
  2.0 12.5 %copy-start.4 = (s32[64]{0:T(128)S(1)}, s32[64]{0:T(128)}, u32[]{:S(2)}) copy-start(s32[64]{0:T(128)} %param.13) | copy-start | bytes 772
  2.0 16.1 %all-to-all-start = ((bf16[8,32,256]{2,1,0:T(8,128)(2,1)}), bf16[8,32,256]{2,1,0:T(8,128)(2,1)S(1)}, u32[]{:S(2)}, u32[]{:S(2)}) async-start(bf16[8,32,256]{2,1,0:T(8,128)(2,1)} %bitcast.2), calls=%async_computation | async-start | bytes 262144 | tf_op jit(solution)/shard_map/all_to_all | solution.py:17
  12.3 29.8 %copy-start = (bf16[1024,512]{1,0:T(8,128)(2,1)S(1)}, bf16[1024,512]{1,0:T(8,128)(2,1)}, u32[]{:S(2)}) copy-start(bf16[1024,512]{1,0:T(8,128)(2,1)} %pool.1) | copy-start | bytes 3145732
  12.3 29.8 %collective-permute-start = (bf16[1024,512]{1,0:T(8,128)(2,1)}, bf16[1024,512]{1,0:T(8,128)(2,1)S(1)}, u32[]{:S(2)}, u32[]{:S(2)}) collective-permute-start(bf16[1024,512]{1,0:T(8,128)(2,1)} %pool.1), channel_id=1, source_target_pairs={{0,1},{1,0},{2,3},{3,2},{4,5},{5,4},{6,7},{7,6},{8,9},{9,8},{10,11... | collective-permute-start | bytes 3145736 | tf_op jit(solution)/shard_map/ppermute | solution.py:140
  18.2 11.5 %collective-permute-start.1 = (bf16[4,64,256]{2,1,0:T(8,128)(2,1)S(1)}, bf16[4,64,256]{2,1,0:T(8,128)(2,1)S(1)}, u32[]{:S(2)}, u32[]{:S(2)}) collective-permute-start(bf16[4,64,256]{2,1,0:T(8,128)(2,1)S(1)} %bitcast_multiply_fusion), channel_id=1, source_target_pairs={{12,0},{13,1},{38,2},{39,3},{88,4},{89,5},{114,6},{115,7},{138,8},... | collective-permute-start | bytes 393224 | tf_op jit(solution)/shard_map/ppermute | solution.py:148
  116.5 12.2 %copy-start.1 = (f32[256,256]{1,0:T(8,128)S(1)}, f32[256,256]{1,0:T(8,128)}, u32[]{:S(2)}) copy-start(f32[256,256]{1,0:T(8,128)} %inv_one.1) | copy-start | bytes 786436
  116.5 12.2 %copy-start.2 = (f32[256,256]{1,0:T(8,128)S(1)}, f32[256,256]{1,0:T(8,128)}, u32[]{:S(2)}) copy-start(f32[256,256]{1,0:T(8,128)} %inv_two.1) | copy-start | bytes 786436
  116.6 12.2 %collective-permute-start.2 = (f32[448,128]{1,0:T(8,128)S(1)}, f32[448,128]{1,0:T(8,128)S(1)}, u32[]{:S(2)}, u32[]{:S(2)}) collective-permute-start(f32[448,128]{1,0:T(8,128)S(1)} %get-tuple-element.16), channel_id=1, source_target_pairs={{0,1},{1,0},{2,3},{3,2},{4,5},{5,4},{6,7},{7,6},{8,9},{9,8},{10,11... | collective-permute-start | bytes 688136 | tf_op jit(solution)/shard_map/ppermute | solution.py:173

commit v5 on v4

v5 whole, which is shorter than its diff:
```python
import jax
import jax.numpy as jnp
from jax import lax
from jax.experimental import pallas as pl
from jax.experimental.pallas import tpu as pltpu
from jax.sharding import Mesh, PartitionSpec as P

AXES = ("x", "zh", "zl", "y", "core")
SIZES = (4, 4, 4, 4, 2)
SWAP = [(0, 1), (1, 0)]
VMEM = pl.BlockSpec(memory_space=pltpu.VMEM)
SMEM = pl.BlockSpec(memory_space=pltpu.SMEM)
PARAMS = pltpu.CompilerParams(vmem_limit_bytes=32 * 1024 * 1024)


def exchange(parts, axes):
    return lax.all_to_all(parts, axes, 0, 0)


def gather(block, axes, count):
    return exchange(jnp.broadcast_to(block[None], (count, *block.shape)), axes)


def rotate(parts, axis):
    return [parts[0]] + [
        lax.ppermute(parts[s], axis, [(i, (i + s) % 4) for i in range(4)]) for s in (1, 2, 3)
    ]


def device_id(x, zh, zl, y, core):
    return (((x * 4 + zh) * 4 + zl) * 4 + y) * 2 + core


def turn_source(x, zh, zl, y):
    near = (1, 2, 3, 0) if zl < 2 else (2, 3, 0, 1)
    return zl, y, near[(zh - y) % 4], (y + 2 + x - zl) % 4


TURN = [
    (device_id(*turn_source(a, b, c, d), k), device_id(a, b, c, d, k))
    for a in range(4)
    for b in range(4)
    for c in range(4)
    for d in range(4)
    for k in range(2)
]


def multiply_kernel(pool, sibling, strip, rows, diag, out0, out1, out2, out3, rhs, full):
    core, y = lax.axis_index("core"), lax.axis_index("y")
    shift = lax.axis_index("zl") - y + 2
    depth = rhs.shape[0] // 2
    for side, which in ((0, core), (1, 1 - core)):
        for h in range(2):
            for j in range(4):
                start = side * depth + h * 256 + j * 64
                rhs[start : start + 64] = strip[(j + shift) & 3, 2 * which + h]
    for z in range(4):
        take = slice(z * 256, (z + 1) * 256)
        block = jnp.dot(
            pool[take], rhs[:depth], preferred_element_type=jnp.float32
        ) + jnp.dot(sibling[take], rhs[depth:], preferred_element_type=jnp.float32)
        for j in range(4):
            full[j, z * 64 : (z + 1) * 64] = block[j * 64 : (j + 1) * 64]
    term = jnp.zeros((256, 256), jnp.float32)
    for j in range(4):
        left, rest = rows[j], full[j]
        for _ in range(3):
            piece = rest.astype(jnp.bfloat16)
            rest = rest - piece.astype(jnp.float32)
            term = term + lax.dot_general(
                left, piece, (((0,), (0,)), ((), ())), preferred_element_type=jnp.float32
            )
    diag[0:256] = term[:, :128]
    diag[256:512] = term[:, 128:]
    for hop, out in enumerate((out0, out1, out2, out3)):
        out[...] = full[(y + hop) & 3]


def turn_kernel(in0, in1, in2, in3, out0, out1, out2, out3, full):
    zl = lax.axis_index("zl")
    full[...] = in0[...] + in1[...] + in2[...] + in3[...]
    for hop, out in enumerate((out0, out1, out2, out3)):
        out[...] = full[pl.ds(pl.multiple_of(((zl + hop) & 3) * 64, 64), 64)]


def split_kernel(mask, in0, in1, in2, in3, stay, leave):
    core = lax.axis_index("core")
    own = -mask[lax.axis_index("zl")].astype(jnp.float32)
    column = (in0[...] + in1[...] + in2[...] + in3[...]) * own
    low = jnp.concatenate([column[0:32, 0:128], column[0:32, 128:256]])
    high = jnp.concatenate([column[32:64, 0:128], column[32:64, 128:256]])
    stay[...] = jnp.where(core == 0, low, high)
    leave[...] = jnp.where(core == 0, high, low)


def finish_kernel(total, stay, swapped, inv_one, inv_two, column_one, column_two, diag_one, diag_two):
    first = lax.axis_index("core") == 0
    own, other = total[...], swapped[0:512]
    own_column, other_column = stay[...], swapped[512:576]
    for swap, inv, diag, column in (
        (False, inv_one, diag_one, column_one),
        (True, inv_two, diag_two, column_two),
    ):
        pick = first != swap
        t = jnp.where(pick, own, other)
        c = jnp.where(pick, own_column, other_column).astype(jnp.bfloat16)
        diag[:, 0:128] = inv[:, 0:128] + t[0:256]
        diag[:, 128:256] = inv[:, 128:256] + t[256:512]
        column[:, 0:128] = c[0:32]
        column[:, 128:256] = c[32:64]


def call(kernel, outs, args, scratch=(), scalars=0):
    many = isinstance(outs, list)
    return pl.pallas_call(
        kernel,
        out_shape=outs,
        in_specs=[SMEM] * scalars + [VMEM] * (len(args) - scalars),
        out_specs=[VMEM] * len(outs) if many else VMEM,
        scratch_shapes=list(scratch),
        compiler_params=PARAMS,
    )(*args)


def per_device(
    inverse_pool, factor_one, factor_two, diag_inv_one, diag_inv_two, struct_one, struct_two
):
    row_count, width = factor_one.shape
    f32 = jnp.float32
    core = lax.axis_index("core")
    first = core == 0
    struct = jnp.where(first, struct_one, struct_two)
    mask = lax.dynamic_slice_in_dim(struct, lax.axis_index(("x", "zh")) * 4, 4)
    sibling_pool = lax.ppermute(inverse_pool, "core", SWAP)

    both = jnp.broadcast_to(
        jnp.stack([factor_one, factor_two])[None], (4, 2, row_count, width)
    ).reshape(8, row_count, width)
    rows = exchange(both, ("zl", "core")).reshape(4, 2 * row_count, width)
    rows = rows * mask.astype(jnp.bfloat16)[:, None, None]
    rows = lax.optimization_barrier(rows)
    strip = gather(lax.ppermute(rows, AXES, TURN), "x", 4)
    around = gather(rows, "y", 4).reshape(4, 256, width)

    quarter = jax.ShapeDtypeStruct((256, width), f32)
    diag, *parts = call(
        multiply_kernel,
        [jax.ShapeDtypeStruct((512, 128), f32)] + [quarter] * 4,
        (inverse_pool, sibling_pool, strip, around),
        [pltpu.VMEM((1024, width), jnp.bfloat16), pltpu.VMEM((4, 256, width), f32)],
    )
    shard = jnp.sum(exchange(diag.reshape(64, 8, 128), ("x", "y", "zl")), axis=0)
    parts = rotate(parts, "y")
    shard = jnp.sum(gather(shard, ("zh", "zl"), 16).reshape(4, 32, 128), axis=0)
    parts = call(
        turn_kernel,
        [jax.ShapeDtypeStruct((2 * row_count, width), f32)] * 4,
        parts,
        [pltpu.VMEM((256, width), f32)],
    )
    parts = rotate(parts, "zl")
    half = jax.ShapeDtypeStruct((2 * row_count, 128), f32)
    stay, leave = call(split_kernel, [half, half], (mask, *parts), scalars=1)
    total = gather(shard, ("x", "y"), 16).reshape(512, 128)
    swapped = lax.ppermute(jnp.concatenate([total, leave]), "core", SWAP)
    wide = jax.ShapeDtypeStruct((row_count, width), jnp.bfloat16)
    square = jax.ShapeDtypeStruct((width, width), f32)
    return tuple(
        call(
            finish_kernel,
            [wide, wide, square, square],
            (total, stay, swapped, diag_inv_one, diag_inv_two),
        )
    )


def solution(mesh):
    fine = Mesh(mesh.devices.reshape(SIZES), AXES)
    rows = P(AXES, None)
    in_specs = (P(("x", "zh"), ("zl", "y", "core")), rows, rows, P(), P(), P(), P())
    out_specs = (rows, rows, P(), P())
    return jax.shard_map(
        per_device, mesh=fine, in_specs=in_specs, out_specs=out_specs, check_vma=False
    )
```

time: 130 us -> 123 us (0.946)
  blocking collectives: 85.1 us -> 33.5 us
  starting transfers between devices: 33.1 us -> 68.2 us
  waiting for transfers between devices: 6.57 us -> 10.9 us
  local copies, waits for them, and re-layouts: 0.74 us -> 4.32 us
    all_to_all x6 -> x2, blocking collectives: 85.1 us -> 33.5 us  [exchange(): return lax.all_to_all(parts, axes, 0, 0)]
    ppermute x0 -> x6, starting transfers between devices: none -> 18.1 us  [rotate(): lax.ppermute(parts[s], axis, [(i, (i + s) % 4) for i in range(4)])]
    all_to_all x1 -> x4, starting transfers between devices: 10.3 us -> 27.5 us  [exchange(): return lax.all_to_all(parts, axes, 0, 0)]
    broadcast_in_dim x2 -> x4, local copies, waits for them, and re-layouts: 0.06 us -> 2.27 us  [gather(): return exchange(jnp.broadcast_to(block[None], (count, *block.shape)), axes)]
    ppermute x0 -> x6, waiting for transfers between devices: none -> 2.19 us  [rotate(): lax.ppermute(parts[s], axis, [(i, (i + s) % 4) for i in range(4)])]
    all_to_all x1 -> x4, waiting for transfers between devices: 3.55 us -> 5.55 us  [exchange(): return lax.all_to_all(parts, axes, 0, 0)]
    unnamed x10 -> x14, local copies, waits for them, and re-layouts: 0.02 us -> 1.38 us
    pallas_call x5 -> x4, Pallas kernels: 2.5 us -> 3.67 us  [call(): pl.pallas_call(kernel, out_shape=outs, in_specs=[SMEM] * scalars + [VMEM]...]
  transfers between devices with their start and end apart: 4 -> 13, of which waited for: 3 -> 6; matrix products, arithmetic and copies ran while one was open for 0% -> 1% of each run, Pallas kernels for 0% -> 1%
where the time goes in v5:
time: 123 us; the launch traced here: 122 us
  starting transfers between devices  68.2 us (55%)
  blocking collectives  33.5 us (27%)
  waiting for transfers between devices  10.9 us (9%)
  local copies, waits for them, and re-layouts  4.32 us (4%)
  Pallas kernels  3.67 us (3%)
    all_to_all x2, blocking collectives, exchange(): return lax.all_to_all(parts, axes, 0, 0)  33.5 us
    all_to_all x4, starting transfers between devices, exchange(): return lax.all_to_all(parts, axes, 0, 0)  27.5 us
    ppermute x6, starting transfers between devices, rotate(): lax.ppermute(parts[s], axis, [(i, (i + s) % 4) for i in range(4)])  18.1 us
    ppermute x1, starting transfers between devices, per_device(): strip = gather(lax.ppermute(rows, AXES, TURN), 'x', 4)  10.4 us
    ppermute x1, starting transfers between devices, per_device(): swapped = lax.ppermute(jnp.concatenate([total, leave]), 'core', SWAP)  10.3 us
    all_to_all x4, waiting for transfers between devices, exchange(): return lax.all_to_all(parts, axes, 0, 0)  5.55 us
    pallas_call x4, Pallas kernels, call(): pl.pallas_call(kernel, out_shape=outs, in_specs=[SMEM] * scalars + [VMEM]...  3.67 us
  transfers between devices with their start and end apart: 13, of which 6 were waited for; matrix products, arithmetic and copies ran while one was open for 1% of the time, Pallas kernels for 1%

profile of v5, /device:TPU:1, one launch (start us, length us, event | category | flops | bytes accessed | tf_op | source)
XLA Modules:
  0.0 122.5 jit_solution(14501679140342087659)
XLA Ops:
  0.6 0.7 pad_maximum_fusion.1
  1.4 0.7 broadcast_in_dim.10
  2.0 10.2 %all-to-all-start = ((bf16[8,32,256]{2,1,0:T(8,128)(2,1)}), bf16[8,32,256]{2,1,0:T(8,128)(2,1)S(1)}, u32[]{:S(2)}, u32[]{:S(2)}) async-start(bf16[8,32,256]{2,1,0:T(8,128)(2,1)} %bitcast.2), calls=%async_computation | async-start | bytes 262144 | tf_op jit(solution)/shard_map/all_to_all | solution.py:17
  12.2 2.0 %collective-permute-start = (bf16[1024,512]{1,0:T(8,128)(2,1)}, bf16[1024,512]{1,0:T(8,128)(2,1)S(1)}, u32[]{:S(2)}, u32[]{:S(2)}) collective-permute-start(bf16[1024,512]{1,0:T(8,128)(2,1)} %pool.1), channel_id=1, source_target_pairs={{0,1},{1,0},{2,3},{3,2},{4,5},{5,4},{6,7},{7,6},{8,9},{9,8},{10,11... | collective-permute-start | bytes 3145736 | tf_op jit(solution)/shard_map/ppermute | solution.py:135
  14.2 0.0 copy-start.5
  14.2 0.0 copy-start.6
  14.2 0.6 copy-done.5
  14.9 0.0 copy-done.6
  14.9 0.1 fusion
  15.0 3.0 %all-to-all-done = bf16[8,32,256]{2,1,0:T(8,128)(2,1)S(1)} async-done(((bf16[8,32,256]{2,1,0:T(8,128)(2,1)}), bf16[8,32,256]{2,1,0:T(8,128)(2,1)S(1)}, u32[]{:S(2)}, u32[]{:S(2)}) %all-to-all-start) | async-done | bytes 131104 | tf_op jit(solution)/shard_map/all_to_all | solution.py:17
  18.0 0.1 bitcast_multiply_fusion
  18.1 0.9 broadcast_in_dim.12
  19.0 3.5 %all-to-all-start.2 = ((bf16[4,4,64,256]{3,2,1,0:T(8,128)(2,1)}), bf16[4,4,64,256]{3,2,1,0:T(8,128)(2,1)S(1)}, u32[]{:S(2)}, u32[]{:S(2)}) async-start(bf16[4,4,64,256]{3,2,1,0:T(8,128)(2,1)} %broadcast_in_dim.12), calls=%async_computation.2 | async-start | bytes 1048576 | tf_op jit(solution)/shard_map/all_to_all | solution.py:17
  22.5 0.0 copy-start
  22.5 10.4 %collective-permute-start.1 = (bf16[4,64,256]{2,1,0:T(8,128)(2,1)S(1)}, bf16[4,64,256]{2,1,0:T(8,128)(2,1)S(1)}, u32[]{:S(2)}, u32[]{:S(2)}) collective-permute-start(bf16[4,64,256]{2,1,0:T(8,128)(2,1)S(1)} %bitcast_multiply_fusion), channel_id=1, source_target_pairs={{12,0},{13,1},{38,2},{39,3},{88,4},{89,5},{114,6},{115,7},{138,8},... | collective-permute-start | bytes 393224 | tf_op jit(solution)/shard_map/ppermute | solution.py:143
  32.8 1.9 %collective-permute-done.1 = bf16[4,64,256]{2,1,0:T(8,128)(2,1)S(1)} collective-permute-done((bf16[4,64,256]{2,1,0:T(8,128)(2,1)S(1)}, bf16[4,64,256]{2,1,0:T(8,128)(2,1)S(1)}, u32[]{:S(2)}, u32[]{:S(2)}) %collective-permute-start.1) | collective-permute-done | bytes 131104 | tf_op jit(solution)/shard_map/ppermute | solution.py:143
  34.8 0.0 all-to-all-done.2
  34.8 12.0 %all_to_all.30.strip = bf16[4,4,64,256]{3,2,1,0:T(8,128)(2,1)S(1)} all-to-all(bf16[4,4,64,256]{3,2,1,0:T(8,128)(2,1)S(1)} %broadcast_in_dim.11), channel_id=1, replica_groups=mesh['x'=4,'zh'=4,'zl'=4,'y'=4,'core'=2] {'x'}, dimensions={0} | all-to-all | bytes 1048576 | tf_op jit(solution)/shard_map/all_to_all | solution.py:17
  46.8 0.0 collective-permute-done.sibling
  46.8 0.0 copy-done
  46.8 2.2 %shard_map.102 = (f32[512,128]{1,0:T(8,128)S(1)}, f32[256,256]{1,0:T(8,128)S(1)}, f32[256,256]{1,0:T(8,128)S(1)}, f32[256,256]{1,0:T(8,128)S(1)}, f32[256,256]{1,0:T(8,128)S(1)}) custom-call(bf16[1024,512]{1,0:T(8,128)(2,1)S(1)} %copy-done, bf16[1024,512]{1,0:T(8,128)(2,1)S(1)} %collective-permute-done.sibling, ...), custom_call_target="tpu_custom_call" | custom-call | tf_op jit(solution)/shard_map/pallas_call | solution.py:116
  49.0 0.0 copy-start.3
  49.0 0.7 copy-done.3
  49.7 21.6 %all_to_all.31 = f32[64,8,128]{2,1,0:T(8,128)S(1)} all-to-all(f32[64,8,128]{2,1,0:T(8,128)S(1)} %bitcast.15), channel_id=1, replica_groups=mesh['x'=4,'zh'=4,'zl'=4,'y'=4,'core'=2] {'x','y','zl'}, dimensions={0} | all-to-all | bytes 524288 | tf_op jit(solution)/shard_map/all_to_all | solution.py:17
  71.2 0.0 copy-start.4
  71.2 0.1 reduce_sum.18
  71.3 0.6 broadcast_in_dim.13
  71.9 10.4 %all-to-all-start.4 = ((f32[16,8,128]{2,1,0:T(8,128)}), f32[16,8,128]{2,1,0:T(8,128)S(1)}, u32[]{:S(2)}, u32[]{:S(2)}) async-start(f32[16,8,128]{2,1,0:T(8,128)} %broadcast_in_dim.13), calls=%async_computation.4 | async-start | bytes 131072 | tf_op jit(solution)/shard_map/all_to_all | solution.py:17
  82.3 0.0 copy-done.4
  82.3 2.1 %collective-permute-start.2 = (f32[256,256]{1,0:T(8,128)S(1)}, f32[256,256]{1,0:T(8,128)S(1)}, u32[]{:S(2)}, u32[]{:S(2)}) collective-permute-start(f32[256,256]{1,0:T(8,128)S(1)} %copy-done.4), channel_id=1, source_target_pairs={{0,2},{2,4},{4,6},{6,0},{1,3},{3,5},{5,7},{7,1},{8,10},{10,12},{12... | collective-permute-start | bytes 786440 | tf_op jit(solution)/shard_map/ppermute | solution.py:26
  84.5 4.0 %collective-permute-start.3 = (f32[256,256]{1,0:T(8,128)S(1)}, f32[256,256]{1,0:T(8,128)S(1)}, u32[]{:S(2)}, u32[]{:S(2)}) collective-permute-start(f32[256,256]{1,0:T(8,128)S(1)} %get-tuple-element.18), channel_id=1, source_target_pairs={{0,4},{2,6},{4,0},{6,2},{1,5},{3,7},{5,1},{7,3},{8,12},{10,14},{12... | collective-permute-start | bytes 786440 | tf_op jit(solution)/shard_map/ppermute | solution.py:26
  88.5 2.9 %collective-permute-start.4 = (f32[256,256]{1,0:T(8,128)S(1)}, f32[256,256]{1,0:T(8,128)S(1)}, u32[]{:S(2)}, u32[]{:S(2)}) collective-permute-start(f32[256,256]{1,0:T(8,128)S(1)} %get-tuple-element.19), channel_id=1, source_target_pairs={{0,6},{2,0},{4,2},{6,4},{1,7},{3,1},{5,3},{7,5},{8,14},{10,8},{12,... | collective-permute-start | bytes 786440 | tf_op jit(solution)/shard_map/ppermute | solution.py:26
  91.4 2.5 %all-to-all-done.4 = f32[16,8,128]{2,1,0:T(8,128)S(1)} async-done(((f32[16,8,128]{2,1,0:T(8,128)}), f32[16,8,128]{2,1,0:T(8,128)S(1)}, u32[]{:S(2)}, u32[]{:S(2)}) %all-to-all-start.4) | async-done | bytes 65568 | tf_op jit(solution)/shard_map/all_to_all | solution.py:17
  93.9 0.7 broadcast_in_dim.14
  94.6 3.5 %all-to-all-start.5 = ((f32[16,32,128]{2,1,0:T(8,128)}), f32[16,32,128]{2,1,0:T(8,128)S(1)}, u32[]{:S(2)}, u32[]{:S(2)}) async-start(f32[16,32,128]{2,1,0:T(8,128)} %broadcast_in_dim.14), calls=%async_computation.5 | async-start | bytes 524288 | tf_op jit(solution)/shard_map/all_to_all | solution.py:17
  98.2 0.0 collective-permute-done.2.in1
  98.2 0.0 collective-permute-done.3.in2
  98.2 0.0 collective-permute-done.4.in3
  98.2 0.1 shard_map.103
  98.3 2.7 %collective-permute-start.5 = (f32[64,256]{1,0:T(8,128)S(1)}, f32[64,256]{1,0:T(8,128)S(1)}, u32[]{:S(2)}, u32[]{:S(2)}) collective-permute-start(f32[64,256]{1,0:T(8,128)S(1)} %get-tuple-element.21), channel_id=1, source_target_pairs={{0,8},{8,16},{16,24},{24,0},{1,9},{9,17},{17,25},{25,1},{2,10},{10... | collective-permute-start | bytes 196616 | tf_op jit(solution)/shard_map/ppermute | solution.py:26
  101.0 2.9 %collective-permute-start.6 = (f32[64,256]{1,0:T(8,128)S(1)}, f32[64,256]{1,0:T(8,128)S(1)}, u32[]{:S(2)}, u32[]{:S(2)}) collective-permute-start(f32[64,256]{1,0:T(8,128)S(1)} %get-tuple-element.22), channel_id=1, source_target_pairs={{0,16},{8,24},{16,0},{24,8},{1,17},{9,25},{17,1},{25,9},{2,18},{10... | collective-permute-start | bytes 196616 | tf_op jit(solution)/shard_map/ppermute | solution.py:26
  103.9 3.4 %collective-permute-start.7 = (f32[64,256]{1,0:T(8,128)S(1)}, f32[64,256]{1,0:T(8,128)S(1)}, u32[]{:S(2)}, u32[]{:S(2)}) collective-permute-start(f32[64,256]{1,0:T(8,128)S(1)} %get-tuple-element.23), channel_id=1, source_target_pairs={{0,24},{8,0},{16,8},{24,16},{1,25},{9,1},{17,9},{25,17},{2,26},{10... | collective-permute-start | bytes 196616 | tf_op jit(solution)/shard_map/ppermute | solution.py:26
  107.3 0.0 collective-permute-done.5.in1
  107.3 0.2 collective-permute-done.6.in2
  107.6 2.0 %collective-permute-done.7.in3 = f32[64,256]{1,0:T(8,128)S(1)} collective-permute-done((f32[64,256]{1,0:T(8,128)S(1)}, f32[64,256]{1,0:T(8,128)S(1)}, u32[]{:S(2)}, u32[]{:S(2)}) %collective-permute-start.7) | collective-permute-done | bytes 65568 | tf_op jit(solution)/shard_map/ppermute | solution.py:26
  109.5 0.6 shard_map.104
  110.1 0.0 all-to-all-done.5
  110.1 0.0 copy-start.1
  110.1 0.0 copy-start.2
  110.2 10.3 %collective-permute-start.8 = (f32[576,128]{1,0:T(8,128)S(1)}, f32[576,128]{1,0:T(8,128)S(1)}, u32[]{:S(2)}, u32[]{:S(2)}) collective-permute-start(f32[576,128]{1,0:T(8,128)S(1)} %pad_maximum_fusion), channel_id=1, source_target_pairs={{0,1},{1,0},{2,3},{3,2},{4,5},{5,4},{6,7},{7,6},{8,9},{9,8},{10,11... | collective-permute-start | bytes 884744 | tf_op jit(solution)/shard_map/ppermute | solution.py:166
  120.4 1.2 collective-permute-done.8.swapped
  121.6 0.0 copy-done.1
  121.6 0.0 copy-done.2
  121.6 0.9 shard_map.105
  (4 shorter events, 0.1 us)
Async XLA Ops:
  2.0 16.0 %all-to-all-start = ((bf16[8,32,256]{2,1,0:T(8,128)(2,1)}), bf16[8,32,256]{2,1,0:T(8,128)(2,1)S(1)}, u32[]{:S(2)}, u32[]{:S(2)}) async-start(bf16[8,32,256]{2,1,0:T(8,128)(2,1)} %bitcast.2), calls=%async_computation | async-start | bytes 262144 | tf_op jit(solution)/shard_map/all_to_all | solution.py:17
  12.2 34.6 %collective-permute-start = (bf16[1024,512]{1,0:T(8,128)(2,1)}, bf16[1024,512]{1,0:T(8,128)(2,1)S(1)}, u32[]{:S(2)}, u32[]{:S(2)}) collective-permute-start(bf16[1024,512]{1,0:T(8,128)(2,1)} %pool.1), channel_id=1, source_target_pairs={{0,1},{1,0},{2,3},{3,2},{4,5},{5,4},{6,7},{7,6},{8,9},{9,8},{10,11... | collective-permute-start | bytes 3145736 | tf_op jit(solution)/shard_map/ppermute | solution.py:135
  14.2 0.7 copy-start.5
  14.2 0.7 copy-start.6
  19.0 15.8 %all-to-all-start.2 = ((bf16[4,4,64,256]{3,2,1,0:T(8,128)(2,1)}), bf16[4,4,64,256]{3,2,1,0:T(8,128)(2,1)S(1)}, u32[]{:S(2)}, u32[]{:S(2)}) async-start(bf16[4,4,64,256]{3,2,1,0:T(8,128)(2,1)} %broadcast_in_dim.12), calls=%async_computation.2 | async-start | bytes 1048576 | tf_op jit(solution)/shard_map/all_to_all | solution.py:17
  22.5 24.3 %copy-start = (bf16[1024,512]{1,0:T(8,128)(2,1)S(1)}, bf16[1024,512]{1,0:T(8,128)(2,1)}, u32[]{:S(2)}) copy-start(bf16[1024,512]{1,0:T(8,128)(2,1)} %pool.1) | copy-start | bytes 3145732
  22.5 12.3 %collective-permute-start.1 = (bf16[4,64,256]{2,1,0:T(8,128)(2,1)S(1)}, bf16[4,64,256]{2,1,0:T(8,128)(2,1)S(1)}, u32[]{:S(2)}, u32[]{:S(2)}) collective-permute-start(bf16[4,64,256]{2,1,0:T(8,128)(2,1)S(1)} %bitcast_multiply_fusion), channel_id=1, source_target_pairs={{12,0},{13,1},{38,2},{39,3},{88,4},{89,5},{114,6},{115,7},{138,8},... | collective-permute-start | bytes 393224 | tf_op jit(solution)/shard_map/ppermute | solution.py:143
  49.0 0.7 copy-start.3
  71.2 11.1 %copy-start.4 = (f32[256,256]{1,0:T(8,128)S(1)}, f32[256,256]{1,0:T(8,128)}, u32[]{:S(2)}) copy-start(f32[256,256]{1,0:T(8,128)} %copy-done.3) | copy-start | bytes 786436
  71.9 22.0 %all-to-all-start.4 = ((f32[16,8,128]{2,1,0:T(8,128)}), f32[16,8,128]{2,1,0:T(8,128)S(1)}, u32[]{:S(2)}, u32[]{:S(2)}) async-start(f32[16,8,128]{2,1,0:T(8,128)} %broadcast_in_dim.13), calls=%async_computation.4 | async-start | bytes 131072 | tf_op jit(solution)/shard_map/all_to_all | solution.py:17
  82.3 15.8 %collective-permute-start.2 = (f32[256,256]{1,0:T(8,128)S(1)}, f32[256,256]{1,0:T(8,128)S(1)}, u32[]{:S(2)}, u32[]{:S(2)}) collective-permute-start(f32[256,256]{1,0:T(8,128)S(1)} %copy-done.4), channel_id=1, source_target_pairs={{0,2},{2,4},{4,6},{6,0},{1,3},{3,5},{5,7},{7,1},{8,10},{10,12},{12... | collective-permute-start | bytes 786440 | tf_op jit(solution)/shard_map/ppermute | solution.py:26
  84.5 13.7 %collective-permute-start.3 = (f32[256,256]{1,0:T(8,128)S(1)}, f32[256,256]{1,0:T(8,128)S(1)}, u32[]{:S(2)}, u32[]{:S(2)}) collective-permute-start(f32[256,256]{1,0:T(8,128)S(1)} %get-tuple-element.18), channel_id=1, source_target_pairs={{0,4},{2,6},{4,0},{6,2},{1,5},{3,7},{5,1},{7,3},{8,12},{10,14},{12... | collective-permute-start | bytes 786440 | tf_op jit(solution)/shard_map/ppermute | solution.py:26
  88.5 9.7 %collective-permute-start.4 = (f32[256,256]{1,0:T(8,128)S(1)}, f32[256,256]{1,0:T(8,128)S(1)}, u32[]{:S(2)}, u32[]{:S(2)}) collective-permute-start(f32[256,256]{1,0:T(8,128)S(1)} %get-tuple-element.19), channel_id=1, source_target_pairs={{0,6},{2,0},{4,2},{6,4},{1,7},{3,1},{5,3},{7,5},{8,14},{10,8},{12,... | collective-permute-start | bytes 786440 | tf_op jit(solution)/shard_map/ppermute | solution.py:26
  94.6 15.5 %all-to-all-start.5 = ((f32[16,32,128]{2,1,0:T(8,128)}), f32[16,32,128]{2,1,0:T(8,128)S(1)}, u32[]{:S(2)}, u32[]{:S(2)}) async-start(f32[16,32,128]{2,1,0:T(8,128)} %broadcast_in_dim.14), calls=%async_computation.5 | async-start | bytes 524288 | tf_op jit(solution)/shard_map/all_to_all | solution.py:17
  98.3 9.0 %collective-permute-start.5 = (f32[64,256]{1,0:T(8,128)S(1)}, f32[64,256]{1,0:T(8,128)S(1)}, u32[]{:S(2)}, u32[]{:S(2)}) collective-permute-start(f32[64,256]{1,0:T(8,128)S(1)} %get-tuple-element.21), channel_id=1, source_target_pairs={{0,8},{8,16},{16,24},{24,0},{1,9},{9,17},{17,25},{25,1},{2,10},{10... | collective-permute-start | bytes 196616 | tf_op jit(solution)/shard_map/ppermute | solution.py:26
  101.0 6.6 %collective-permute-start.6 = (f32[64,256]{1,0:T(8,128)S(1)}, f32[64,256]{1,0:T(8,128)S(1)}, u32[]{:S(2)}, u32[]{:S(2)}) collective-permute-start(f32[64,256]{1,0:T(8,128)S(1)} %get-tuple-element.22), channel_id=1, source_target_pairs={{0,16},{8,24},{16,0},{24,8},{1,17},{9,25},{17,1},{25,9},{2,18},{10... | collective-permute-start | bytes 196616 | tf_op jit(solution)/shard_map/ppermute | solution.py:26
  103.9 5.6 %collective-permute-start.7 = (f32[64,256]{1,0:T(8,128)S(1)}, f32[64,256]{1,0:T(8,128)S(1)}, u32[]{:S(2)}, u32[]{:S(2)}) collective-permute-start(f32[64,256]{1,0:T(8,128)S(1)} %get-tuple-element.23), channel_id=1, source_target_pairs={{0,24},{8,0},{16,8},{24,16},{1,25},{9,1},{17,9},{25,17},{2,26},{10... | collective-permute-start | bytes 196616 | tf_op jit(solution)/shard_map/ppermute | solution.py:26
  110.1 11.5 %copy-start.1 = (f32[256,256]{1,0:T(8,128)S(1)}, f32[256,256]{1,0:T(8,128)}, u32[]{:S(2)}) copy-start(f32[256,256]{1,0:T(8,128)} %inv_one.1) | copy-start | bytes 786436
  110.1 11.5 %copy-start.2 = (f32[256,256]{1,0:T(8,128)S(1)}, f32[256,256]{1,0:T(8,128)}, u32[]{:S(2)}) copy-start(f32[256,256]{1,0:T(8,128)} %inv_two.1) | copy-start | bytes 786436
  110.2 11.5 %collective-permute-start.8 = (f32[576,128]{1,0:T(8,128)S(1)}, f32[576,128]{1,0:T(8,128)S(1)}, u32[]{:S(2)}, u32[]{:S(2)}) collective-permute-start(f32[576,128]{1,0:T(8,128)S(1)} %pad_maximum_fusion), channel_id=1, source_target_pairs={{0,1},{1,0},{2,3},{3,2},{4,5},{5,4},{6,7},{7,6},{8,9},{9,8},{10,11... | collective-permute-start | bytes 884744 | tf_op jit(solution)/shard_map/ppermute | solution.py:166

commit v6 on v5

--- a/solution.py
+++ b/solution.py
@@ -64,13 +64,11 @@
             full[j, z * 64 : (z + 1) * 64] = block[j * 64 : (j + 1) * 64]
     term = jnp.zeros((256, 256), jnp.float32)
     for j in range(4):
-        left, rest = rows[j], full[j]
+        left, rest = rows[j].T, full[j]
         for _ in range(3):
             piece = rest.astype(jnp.bfloat16)
             rest = rest - piece.astype(jnp.float32)
-            term = term + lax.dot_general(
-                left, piece, (((0,), (0,)), ((), ())), preferred_element_type=jnp.float32
-            )
+            term = term + jnp.dot(left, piece, preferred_element_type=jnp.float32)
     diag[0:256] = term[:, :128]
     diag[256:512] = term[:, 128:]
     for hop, out in enumerate((out0, out1, out2, out3)):
@@ -152,6 +150,7 @@
     )
     shard = jnp.sum(exchange(diag.reshape(64, 8, 128), ("x", "y", "zl")), axis=0)
     parts = rotate(parts, "y")
+    shard, parts = lax.optimization_barrier((shard, parts))
     shard = jnp.sum(gather(shard, ("zh", "zl"), 16).reshape(4, 32, 128), axis=0)
     parts = call(
         turn_kernel,
@@ -160,6 +159,7 @@
         [pltpu.VMEM((256, width), f32)],
     )
     parts = rotate(parts, "zl")
+    shard, parts = lax.optimization_barrier((shard, parts))
     half = jax.ShapeDtypeStruct((2 * row_count, 128), f32)
     stay, leave = call(split_kernel, [half, half], (mask, *parts), scalars=1)
     total = gather(shard, ("x", "y"), 16).reshape(512, 128)

time: 123 us -> 131 us (1.065)
  blocking collectives: 33.5 us -> 12 us
  starting transfers between devices: 68.2 us -> 85.4 us
  waiting for transfers between devices: 10.9 us -> 22.5 us
    all_to_all x2 -> x1, blocking collectives: 33.5 us -> 12 us  [exchange(): return lax.all_to_all(parts, axes, 0, 0)]
    all_to_all x4 -> x5, starting transfers between devices: 27.5 us -> 44.5 us  [exchange(): return lax.all_to_all(parts, axes, 0, 0)]
    ppermute x6, waiting for transfers between devices: 2.19 us -> 8.43 us  [rotate(): lax.ppermute(parts[s], axis, [(i, (i + s) % 4) for i in range(4)])]
    all_to_all x4 -> x5, waiting for transfers between devices: 5.55 us -> 10.9 us  [exchange(): return lax.all_to_all(parts, axes, 0, 0)]
    ppermute x6, starting transfers between devices: 18.1 us -> 20.7 us  [rotate(): lax.ppermute(parts[s], axis, [(i, (i + s) % 4) for i in range(4)])]
    ppermute x1, starting transfers between devices: 10.3 us -> 7.92 us  [per_device(): swapped = lax.ppermute(jnp.concatenate([total, leave]), 'core', SWAP)]
  transfers between devices with their start and end apart: 13 -> 14, of which waited for: 6 -> 8; matrix products, arithmetic and copies ran while one was open for 1% -> 1% of each run, Pallas kernels for 1% -> 0%
where the time goes in v6:
time: 131 us; the launch traced here: 130 us
  starting transfers between devices  85.4 us (65%)
  waiting for transfers between devices  22.5 us (17%)
  blocking collectives  12 us (9%)
  Pallas kernels  4.39 us (3%)
  local copies, waits for them, and re-layouts  4.31 us (3%)
    all_to_all x5, starting transfers between devices, exchange(): return lax.all_to_all(parts, axes, 0, 0)  44.5 us
    ppermute x6, starting transfers between devices, rotate(): lax.ppermute(parts[s], axis, [(i, (i + s) % 4) for i in range(4)])  20.7 us
    all_to_all x1, blocking collectives, exchange(): return lax.all_to_all(parts, axes, 0, 0)  12 us
    all_to_all x5, waiting for transfers between devices, exchange(): return lax.all_to_all(parts, axes, 0, 0)  10.9 us
    ppermute x1, starting transfers between devices, per_device(): strip = gather(lax.ppermute(rows, AXES, TURN), 'x', 4)  10.4 us
    ppermute x6, waiting for transfers between devices, rotate(): lax.ppermute(parts[s], axis, [(i, (i + s) % 4) for i in range(4)])  8.43 us
    ppermute x1, starting transfers between devices, per_device(): swapped = lax.ppermute(jnp.concatenate([total, leave]), 'core', SWAP)  7.92 us
    pallas_call x4, Pallas kernels, call(): pl.pallas_call(kernel, out_shape=outs, in_specs=[SMEM] * scalars + [VMEM]...  4.39 us
  transfers between devices with their start and end apart: 14, of which 8 were waited for; matrix products, arithmetic and copies ran while one was open for 1% of the time, Pallas kernels for 0%

profile of v6, /device:TPU:1, one launch (start us, length us, event | category | flops | bytes accessed | tf_op | source)
XLA Modules:
  0.0 130.4 jit_solution(5074675146742347406)
XLA Ops:
  0.6 0.7 pad_maximum_fusion.1
  1.4 0.7 broadcast_in_dim.10
  2.0 10.2 %all-to-all-start = ((bf16[8,32,256]{2,1,0:T(8,128)(2,1)}), bf16[8,32,256]{2,1,0:T(8,128)(2,1)S(1)}, u32[]{:S(2)}, u32[]{:S(2)}) async-start(bf16[8,32,256]{2,1,0:T(8,128)(2,1)} %bitcast.2), calls=%async_computation | async-start | bytes 262144 | tf_op jit(solution)/shard_map/all_to_all | solution.py:17
  12.2 2.0 %collective-permute-start = (bf16[1024,512]{1,0:T(8,128)(2,1)}, bf16[1024,512]{1,0:T(8,128)(2,1)S(1)}, u32[]{:S(2)}, u32[]{:S(2)}) collective-permute-start(bf16[1024,512]{1,0:T(8,128)(2,1)} %pool.1), channel_id=1, source_target_pairs={{0,1},{1,0},{2,3},{3,2},{4,5},{5,4},{6,7},{7,6},{8,9},{9,8},{10,11... | collective-permute-start | bytes 3145736 | tf_op jit(solution)/shard_map/ppermute | solution.py:133
  14.2 0.0 copy-start.5
  14.2 0.0 copy-start.6
  14.2 0.6 copy-done.5
  14.9 0.0 copy-done.6
  14.9 0.1 fusion
  15.0 3.0 %all-to-all-done = bf16[8,32,256]{2,1,0:T(8,128)(2,1)S(1)} async-done(((bf16[8,32,256]{2,1,0:T(8,128)(2,1)}), bf16[8,32,256]{2,1,0:T(8,128)(2,1)S(1)}, u32[]{:S(2)}, u32[]{:S(2)}) %all-to-all-start) | async-done | bytes 131104 | tf_op jit(solution)/shard_map/all_to_all | solution.py:17
  18.0 0.1 bitcast_multiply_fusion
  18.1 0.9 broadcast_in_dim.12
  19.0 3.5 %all-to-all-start.2 = ((bf16[4,4,64,256]{3,2,1,0:T(8,128)(2,1)}), bf16[4,4,64,256]{3,2,1,0:T(8,128)(2,1)S(1)}, u32[]{:S(2)}, u32[]{:S(2)}) async-start(bf16[4,4,64,256]{3,2,1,0:T(8,128)(2,1)} %broadcast_in_dim.12), calls=%async_computation.2 | async-start | bytes 1048576 | tf_op jit(solution)/shard_map/all_to_all | solution.py:17
  22.5 0.0 copy-start
  22.5 10.4 %collective-permute-start.1 = (bf16[4,64,256]{2,1,0:T(8,128)(2,1)S(1)}, bf16[4,64,256]{2,1,0:T(8,128)(2,1)S(1)}, u32[]{:S(2)}, u32[]{:S(2)}) collective-permute-start(bf16[4,64,256]{2,1,0:T(8,128)(2,1)S(1)} %bitcast_multiply_fusion), channel_id=1, source_target_pairs={{12,0},{13,1},{38,2},{39,3},{88,4},{89,5},{114,6},{115,7},{138,8},... | collective-permute-start | bytes 393224 | tf_op jit(solution)/shard_map/ppermute | solution.py:141
  32.8 1.9 %collective-permute-done.1 = bf16[4,64,256]{2,1,0:T(8,128)(2,1)S(1)} collective-permute-done((bf16[4,64,256]{2,1,0:T(8,128)(2,1)S(1)}, bf16[4,64,256]{2,1,0:T(8,128)(2,1)S(1)}, u32[]{:S(2)}, u32[]{:S(2)}) %collective-permute-start.1) | collective-permute-done | bytes 131104 | tf_op jit(solution)/shard_map/ppermute | solution.py:141
  34.8 0.0 all-to-all-done.2
  34.8 12.0 %all_to_all.30.strip = bf16[4,4,64,256]{3,2,1,0:T(8,128)(2,1)S(1)} all-to-all(bf16[4,4,64,256]{3,2,1,0:T(8,128)(2,1)S(1)} %broadcast_in_dim.11), channel_id=1, replica_groups=mesh['x'=4,'zh'=4,'zl'=4,'y'=4,'core'=2] {'x'}, dimensions={0} | all-to-all | bytes 1048576 | tf_op jit(solution)/shard_map/all_to_all | solution.py:17
  46.8 0.0 collective-permute-done.sibling
  46.8 0.0 copy-done
  46.8 2.9 %shard_map.102 = (f32[512,128]{1,0:T(8,128)}, f32[256,256]{1,0:T(8,128)S(1)}, f32[256,256]{1,0:T(8,128)S(1)}, f32[256,256]{1,0:T(8,128)S(1)}, f32[256,256]{1,0:T(8,128)S(1)}) custom-call(bf16[1024,512]{1,0:T(8,128)(2,1)S(1)} %copy-done, bf16[1024,512]{1,0:T(8,128)(2,1)S(1)} %collective-permute-done.sibling, bf16[4,4,64,256]{3,2,1,0:T(8,128)(2,1)S(1)} %all_to_all.30.strip, ...), custom_call_target="tpu_custom_call" | custom-call | tf_op jit(solution)/shard_map/pallas_call | solution.py:114
  49.7 0.0 copy-start.3
  49.7 0.7 copy-done.3
  50.4 0.0 copy-start.4
  50.4 11.6 %all-to-all-start.3 = ((f32[64,8,128]{2,1,0:T(8,128)}), f32[64,8,128]{2,1,0:T(8,128)S(1)}, u32[]{:S(2)}, u32[]{:S(2)}) async-start(f32[64,8,128]{2,1,0:T(8,128)} %bitcast.5), calls=%async_computation.3 | async-start | bytes 524288 | tf_op jit(solution)/shard_map/all_to_all | solution.py:17
  62.0 0.0 copy-done.4
  62.0 2.9 %collective-permute-start.2 = (f32[256,256]{1,0:T(8,128)S(1)}, f32[256,256]{1,0:T(8,128)S(1)}, u32[]{:S(2)}, u32[]{:S(2)}) collective-permute-start(f32[256,256]{1,0:T(8,128)S(1)} %copy-done.4), channel_id=1, source_target_pairs={{0,2},{2,4},{4,6},{6,0},{1,3},{3,5},{5,7},{7,1},{8,10},{10,12},{12... | collective-permute-start | bytes 786440 | tf_op jit(solution)/shard_map/ppermute | solution.py:26
  64.9 4.3 %collective-permute-start.3 = (f32[256,256]{1,0:T(8,128)S(1)}, f32[256,256]{1,0:T(8,128)S(1)}, u32[]{:S(2)}, u32[]{:S(2)}) collective-permute-start(f32[256,256]{1,0:T(8,128)S(1)} %get-tuple-element.28), channel_id=1, source_target_pairs={{0,4},{2,6},{4,0},{6,2},{1,5},{3,7},{5,1},{7,3},{8,12},{10,14},{12... | collective-permute-start | bytes 786440 | tf_op jit(solution)/shard_map/ppermute | solution.py:26
  69.2 3.1 %collective-permute-start.4 = (f32[256,256]{1,0:T(8,128)S(1)}, f32[256,256]{1,0:T(8,128)S(1)}, u32[]{:S(2)}, u32[]{:S(2)}) collective-permute-start(f32[256,256]{1,0:T(8,128)S(1)} %get-tuple-element.29), channel_id=1, source_target_pairs={{0,6},{2,0},{4,2},{6,4},{1,7},{3,1},{5,3},{7,5},{8,14},{10,8},{12,... | collective-permute-start | bytes 786440 | tf_op jit(solution)/shard_map/ppermute | solution.py:26
  72.3 0.0 all-to-all-done.3
  72.3 0.1 reduce_sum.18
  72.4 0.8 collective-permute-done.2.in1
  73.2 6.4 %collective-permute-done.3.in2 = f32[256,256]{1,0:T(8,128)S(1)} collective-permute-done((f32[256,256]{1,0:T(8,128)S(1)}, f32[256,256]{1,0:T(8,128)S(1)}, u32[]{:S(2)}, u32[]{:S(2)}) %collective-permute-start.3) | collective-permute-done | bytes 262176 | tf_op jit(solution)/shard_map/ppermute | solution.py:26
  79.7 0.0 collective-permute-done.4.in3
  79.7 0.6 broadcast_in_dim.13
  80.3 12.5 %all-to-all-start.4 = ((f32[16,8,128]{2,1,0:T(8,128)}), f32[16,8,128]{2,1,0:T(8,128)S(1)}, u32[]{:S(2)}, u32[]{:S(2)}) async-start(f32[16,8,128]{2,1,0:T(8,128)} %broadcast_in_dim.13), calls=%async_computation.4 | async-start | bytes 131072 | tf_op jit(solution)/shard_map/all_to_all | solution.py:17
  92.8 0.1 shard_map.103
  92.9 3.3 %collective-permute-start.5 = (f32[64,256]{1,0:T(8,128)S(1)}, f32[64,256]{1,0:T(8,128)S(1)}, u32[]{:S(2)}, u32[]{:S(2)}) collective-permute-start(f32[64,256]{1,0:T(8,128)S(1)} %get-tuple-element.36), channel_id=1, source_target_pairs={{0,8},{8,16},{16,24},{24,0},{1,9},{9,17},{17,25},{25,1},{2,10},{10... | collective-permute-start | bytes 196616 | tf_op jit(solution)/shard_map/ppermute | solution.py:26
  96.1 4.0 %collective-permute-start.6 = (f32[64,256]{1,0:T(8,128)S(1)}, f32[64,256]{1,0:T(8,128)S(1)}, u32[]{:S(2)}, u32[]{:S(2)}) collective-permute-start(f32[64,256]{1,0:T(8,128)S(1)} %get-tuple-element.37), channel_id=1, source_target_pairs={{0,16},{8,24},{16,0},{24,8},{1,17},{9,25},{17,1},{25,9},{2,18},{10... | collective-permute-start | bytes 196616 | tf_op jit(solution)/shard_map/ppermute | solution.py:26
  100.1 3.1 %collective-permute-start.7 = (f32[64,256]{1,0:T(8,128)S(1)}, f32[64,256]{1,0:T(8,128)S(1)}, u32[]{:S(2)}, u32[]{:S(2)}) collective-permute-start(f32[64,256]{1,0:T(8,128)S(1)} %get-tuple-element.38), channel_id=1, source_target_pairs={{0,24},{8,0},{16,8},{24,16},{1,25},{9,1},{17,9},{25,17},{2,26},{10... | collective-permute-start | bytes 196616 | tf_op jit(solution)/shard_map/ppermute | solution.py:26
  103.2 1.1 all-to-all-done.4
  104.4 0.0 collective-permute-done.5.in1
  104.4 0.0 collective-permute-done.6.in2
  104.4 1.2 collective-permute-done.7.in3
  105.5 0.7 broadcast_in_dim.14
  106.3 6.8 %all-to-all-start.5 = ((f32[16,32,128]{2,1,0:T(8,128)}), f32[16,32,128]{2,1,0:T(8,128)S(1)}, u32[]{:S(2)}, u32[]{:S(2)}) async-start(f32[16,32,128]{2,1,0:T(8,128)} %broadcast_in_dim.14), calls=%async_computation.5 | async-start | bytes 524288 | tf_op jit(solution)/shard_map/all_to_all | solution.py:17
  113.1 0.6 shard_map.104
  113.7 6.7 %all-to-all-done.5 = f32[16,32,128]{2,1,0:T(8,128)S(1)} async-done(((f32[16,32,128]{2,1,0:T(8,128)}), f32[16,32,128]{2,1,0:T(8,128)S(1)}, u32[]{:S(2)}, u32[]{:S(2)}) %all-to-all-start.5) | async-done | bytes 262176 | tf_op jit(solution)/shard_map/all_to_all | solution.py:17
  120.4 0.0 copy-start.1
  120.4 0.0 copy-start.2
  120.4 7.9 %collective-permute-start.8 = (f32[576,128]{1,0:T(8,128)S(1)}, f32[576,128]{1,0:T(8,128)S(1)}, u32[]{:S(2)}, u32[]{:S(2)}) collective-permute-start(f32[576,128]{1,0:T(8,128)S(1)} %pad_maximum_fusion), channel_id=1, source_target_pairs={{0,1},{1,0},{2,3},{3,2},{4,5},{5,4},{6,7},{7,6},{8,9},{9,8},{10,11... | collective-permute-start | bytes 884744 | tf_op jit(solution)/shard_map/ppermute | solution.py:166
  128.4 1.2 collective-permute-done.8.swapped
  129.5 0.0 copy-done.1
  129.5 0.0 copy-done.2
  129.5 0.9 shard_map.105
  (4 shorter events, 0.1 us)
Async XLA Ops:
  2.0 16.0 %all-to-all-start = ((bf16[8,32,256]{2,1,0:T(8,128)(2,1)}), bf16[8,32,256]{2,1,0:T(8,128)(2,1)S(1)}, u32[]{:S(2)}, u32[]{:S(2)}) async-start(bf16[8,32,256]{2,1,0:T(8,128)(2,1)} %bitcast.2), calls=%async_computation | async-start | bytes 262144 | tf_op jit(solution)/shard_map/all_to_all | solution.py:17
  12.2 34.6 %collective-permute-start = (bf16[1024,512]{1,0:T(8,128)(2,1)}, bf16[1024,512]{1,0:T(8,128)(2,1)S(1)}, u32[]{:S(2)}, u32[]{:S(2)}) collective-permute-start(bf16[1024,512]{1,0:T(8,128)(2,1)} %pool.1), channel_id=1, source_target_pairs={{0,1},{1,0},{2,3},{3,2},{4,5},{5,4},{6,7},{7,6},{8,9},{9,8},{10,11... | collective-permute-start | bytes 3145736 | tf_op jit(solution)/shard_map/ppermute | solution.py:133
  14.2 0.7 copy-start.5
  14.2 0.7 copy-start.6
  19.0 15.8 %all-to-all-start.2 = ((bf16[4,4,64,256]{3,2,1,0:T(8,128)(2,1)}), bf16[4,4,64,256]{3,2,1,0:T(8,128)(2,1)S(1)}, u32[]{:S(2)}, u32[]{:S(2)}) async-start(bf16[4,4,64,256]{3,2,1,0:T(8,128)(2,1)} %broadcast_in_dim.12), calls=%async_computation.2 | async-start | bytes 1048576 | tf_op jit(solution)/shard_map/all_to_all | solution.py:17
  22.5 24.3 %copy-start = (bf16[1024,512]{1,0:T(8,128)(2,1)S(1)}, bf16[1024,512]{1,0:T(8,128)(2,1)}, u32[]{:S(2)}) copy-start(bf16[1024,512]{1,0:T(8,128)(2,1)} %pool.1) | copy-start | bytes 3145732
  22.5 12.3 %collective-permute-start.1 = (bf16[4,64,256]{2,1,0:T(8,128)(2,1)S(1)}, bf16[4,64,256]{2,1,0:T(8,128)(2,1)S(1)}, u32[]{:S(2)}, u32[]{:S(2)}) collective-permute-start(bf16[4,64,256]{2,1,0:T(8,128)(2,1)S(1)} %bitcast_multiply_fusion), channel_id=1, source_target_pairs={{12,0},{13,1},{38,2},{39,3},{88,4},{89,5},{114,6},{115,7},{138,8},... | collective-permute-start | bytes 393224 | tf_op jit(solution)/shard_map/ppermute | solution.py:141
  49.7 0.7 copy-start.3
  50.4 11.6 %copy-start.4 = (f32[256,256]{1,0:T(8,128)S(1)}, f32[256,256]{1,0:T(8,128)}, u32[]{:S(2)}) copy-start(f32[256,256]{1,0:T(8,128)} %copy-done.3) | copy-start | bytes 786436
  50.4 22.0 %all-to-all-start.3 = ((f32[64,8,128]{2,1,0:T(8,128)}), f32[64,8,128]{2,1,0:T(8,128)S(1)}, u32[]{:S(2)}, u32[]{:S(2)}) async-start(f32[64,8,128]{2,1,0:T(8,128)} %bitcast.5), calls=%async_computation.3 | async-start | bytes 524288 | tf_op jit(solution)/shard_map/all_to_all | solution.py:17
  62.0 11.2 %collective-permute-start.2 = (f32[256,256]{1,0:T(8,128)S(1)}, f32[256,256]{1,0:T(8,128)S(1)}, u32[]{:S(2)}, u32[]{:S(2)}) collective-permute-start(f32[256,256]{1,0:T(8,128)S(1)} %copy-done.4), channel_id=1, source_target_pairs={{0,2},{2,4},{4,6},{6,0},{1,3},{3,5},{5,7},{7,1},{8,10},{10,12},{12... | collective-permute-start | bytes 786440 | tf_op jit(solution)/shard_map/ppermute | solution.py:26
  64.9 14.7 %collective-permute-start.3 = (f32[256,256]{1,0:T(8,128)S(1)}, f32[256,256]{1,0:T(8,128)S(1)}, u32[]{:S(2)}, u32[]{:S(2)}) collective-permute-start(f32[256,256]{1,0:T(8,128)S(1)} %get-tuple-element.28), channel_id=1, source_target_pairs={{0,4},{2,6},{4,0},{6,2},{1,5},{3,7},{5,1},{7,3},{8,12},{10,14},{12... | collective-permute-start | bytes 786440 | tf_op jit(solution)/shard_map/ppermute | solution.py:26
  69.2 10.4 %collective-permute-start.4 = (f32[256,256]{1,0:T(8,128)S(1)}, f32[256,256]{1,0:T(8,128)S(1)}, u32[]{:S(2)}, u32[]{:S(2)}) collective-permute-start(f32[256,256]{1,0:T(8,128)S(1)} %get-tuple-element.29), channel_id=1, source_target_pairs={{0,6},{2,0},{4,2},{6,4},{1,7},{3,1},{5,3},{7,5},{8,14},{10,8},{12,... | collective-permute-start | bytes 786440 | tf_op jit(solution)/shard_map/ppermute | solution.py:26
  80.3 24.0 %all-to-all-start.4 = ((f32[16,8,128]{2,1,0:T(8,128)}), f32[16,8,128]{2,1,0:T(8,128)S(1)}, u32[]{:S(2)}, u32[]{:S(2)}) async-start(f32[16,8,128]{2,1,0:T(8,128)} %broadcast_in_dim.13), calls=%async_computation.4 | async-start | bytes 131072 | tf_op jit(solution)/shard_map/all_to_all | solution.py:17
  92.9 11.5 %collective-permute-start.5 = (f32[64,256]{1,0:T(8,128)S(1)}, f32[64,256]{1,0:T(8,128)S(1)}, u32[]{:S(2)}, u32[]{:S(2)}) collective-permute-start(f32[64,256]{1,0:T(8,128)S(1)} %get-tuple-element.36), channel_id=1, source_target_pairs={{0,8},{8,16},{16,24},{24,0},{1,9},{9,17},{17,25},{25,1},{2,10},{10... | collective-permute-start | bytes 196616 | tf_op jit(solution)/shard_map/ppermute | solution.py:26
  96.1 8.2 %collective-permute-start.6 = (f32[64,256]{1,0:T(8,128)S(1)}, f32[64,256]{1,0:T(8,128)S(1)}, u32[]{:S(2)}, u32[]{:S(2)}) collective-permute-start(f32[64,256]{1,0:T(8,128)S(1)} %get-tuple-element.37), channel_id=1, source_target_pairs={{0,16},{8,24},{16,0},{24,8},{1,17},{9,25},{17,1},{25,9},{2,18},{10... | collective-permute-start | bytes 196616 | tf_op jit(solution)/shard_map/ppermute | solution.py:26
  100.1 5.4 %collective-permute-start.7 = (f32[64,256]{1,0:T(8,128)S(1)}, f32[64,256]{1,0:T(8,128)S(1)}, u32[]{:S(2)}, u32[]{:S(2)}) collective-permute-start(f32[64,256]{1,0:T(8,128)S(1)} %get-tuple-element.38), channel_id=1, source_target_pairs={{0,24},{8,0},{16,8},{24,16},{1,25},{9,1},{17,9},{25,17},{2,26},{10... | collective-permute-start | bytes 196616 | tf_op jit(solution)/shard_map/ppermute | solution.py:26
  106.3 14.1 %all-to-all-start.5 = ((f32[16,32,128]{2,1,0:T(8,128)}), f32[16,32,128]{2,1,0:T(8,128)S(1)}, u32[]{:S(2)}, u32[]{:S(2)}) async-start(f32[16,32,128]{2,1,0:T(8,128)} %broadcast_in_dim.14), calls=%async_computation.5 | async-start | bytes 524288 | tf_op jit(solution)/shard_map/all_to_all | solution.py:17
  120.4 9.1 %copy-start.1 = (f32[256,256]{1,0:T(8,128)S(1)}, f32[256,256]{1,0:T(8,128)}, u32[]{:S(2)}) copy-start(f32[256,256]{1,0:T(8,128)} %inv_one.1) | copy-start | bytes 786436
  120.4 9.1 %copy-start.2 = (f32[256,256]{1,0:T(8,128)S(1)}, f32[256,256]{1,0:T(8,128)}, u32[]{:S(2)}) copy-start(f32[256,256]{1,0:T(8,128)} %inv_two.1) | copy-start | bytes 786436
  120.4 9.1 %collective-permute-start.8 = (f32[576,128]{1,0:T(8,128)S(1)}, f32[576,128]{1,0:T(8,128)S(1)}, u32[]{:S(2)}, u32[]{:S(2)}) collective-permute-start(f32[576,128]{1,0:T(8,128)S(1)} %pad_maximum_fusion), channel_id=1, source_target_pairs={{0,1},{1,0},{2,3},{3,2},{4,5},{5,4},{6,7},{7,6},{8,9},{9,8},{10,11... | collective-permute-start | bytes 884744 | tf_op jit(solution)/shard_map/ppermute | solution.py:166

commit v7 on v5

--- a/solution.py
+++ b/solution.py
@@ -21,12 +21,6 @@
     return exchange(jnp.broadcast_to(block[None], (count, *block.shape)), axes)
 
 
-def rotate(parts, axis):
-    return [parts[0]] + [
-        lax.ppermute(parts[s], axis, [(i, (i + s) % 4) for i in range(4)]) for s in (1, 2, 3)
-    ]
-
-
 def device_id(x, zh, zl, y, core):
     return (((x * 4 + zh) * 4 + zl) * 4 + y) * 2 + core
 
@@ -46,9 +40,9 @@
 ]
 
 
-def multiply_kernel(pool, sibling, strip, rows, diag, out0, out1, out2, out3, rhs, full):
-    core, y = lax.axis_index("core"), lax.axis_index("y")
-    shift = lax.axis_index("zl") - y + 2
+def multiply_kernel(pool, sibling, strip, rows, diag, out, rhs, full):
+    core = lax.axis_index("core")
+    shift = lax.axis_index("zl") - lax.axis_index("y") + 2
     depth = rhs.shape[0] // 2
     for side, which in ((0, core), (1, 1 - core)):
         for h in range(2):
@@ -60,6 +54,7 @@
         block = jnp.dot(
             pool[take], rhs[:depth], preferred_element_type=jnp.float32
         ) + jnp.dot(sibling[take], rhs[depth:], preferred_element_type=jnp.float32)
+        out[take] = block
         for j in range(4):
             full[j, z * 64 : (z + 1) * 64] = block[j * 64 : (j + 1) * 64]
     term = jnp.zeros((256, 256), jnp.float32)
@@ -73,21 +68,12 @@
             )
     diag[0:256] = term[:, :128]
     diag[256:512] = term[:, 128:]
-    for hop, out in enumerate((out0, out1, out2, out3)):
-        out[...] = full[(y + hop) & 3]
 
 
-def turn_kernel(in0, in1, in2, in3, out0, out1, out2, out3, full):
-    zl = lax.axis_index("zl")
-    full[...] = in0[...] + in1[...] + in2[...] + in3[...]
-    for hop, out in enumerate((out0, out1, out2, out3)):
-        out[...] = full[pl.ds(pl.multiple_of(((zl + hop) & 3) * 64, 64), 64)]
-
-
-def split_kernel(mask, in0, in1, in2, in3, stay, leave):
+def split_kernel(mask, parts, stay, leave):
     core = lax.axis_index("core")
     own = -mask[lax.axis_index("zl")].astype(jnp.float32)
-    column = (in0[...] + in1[...] + in2[...] + in3[...]) * own
+    column = (parts[0] + parts[1] + parts[2] + parts[3]) * own
     low = jnp.concatenate([column[0:32, 0:128], column[0:32, 128:256]])
     high = jnp.concatenate([column[32:64, 0:128], column[32:64, 128:256]])
     stay[...] = jnp.where(core == 0, low, high)
@@ -143,26 +129,20 @@
     strip = gather(lax.ppermute(rows, AXES, TURN), "x", 4)
     around = gather(rows, "y", 4).reshape(4, 256, width)
 
-    quarter = jax.ShapeDtypeStruct((256, width), f32)
-    diag, *parts = call(
+    diag, partial = call(
         multiply_kernel,
-        [jax.ShapeDtypeStruct((512, 128), f32)] + [quarter] * 4,
+        [jax.ShapeDtypeStruct((512, 128), f32), jax.ShapeDtypeStruct((1024, width), f32)],
         (inverse_pool, sibling_pool, strip, around),
         [pltpu.VMEM((1024, width), jnp.bfloat16), pltpu.VMEM((4, 256, width), f32)],
     )
+    product = lax.psum_scatter(partial, "zl", scatter_dimension=0, tiled=True)
     shard = jnp.sum(exchange(diag.reshape(64, 8, 128), ("x", "y", "zl")), axis=0)
-    parts = rotate(parts, "y")
     shard = jnp.sum(gather(shard, ("zh", "zl"), 16).reshape(4, 32, 128), axis=0)
-    parts = call(
-        turn_kernel,
-        [jax.ShapeDtypeStruct((2 * row_count, width), f32)] * 4,
-        parts,
-        [pltpu.VMEM((256, width), f32)],
-    )
-    parts = rotate(parts, "zl")
+    total = gather(shard, ("x", "y"), 16).reshape(512, 128)
+    total, product = lax.optimization_barrier((total, product))
     half = jax.ShapeDtypeStruct((2 * row_count, 128), f32)
-    stay, leave = call(split_kernel, [half, half], (mask, *parts), scalars=1)
-    total = gather(shard, ("x", "y"), 16).reshape(512, 128)
+    parts = exchange(product.reshape(4, 2 * row_count, width), "y")
+    stay, leave = call(split_kernel, [half, half], (mask, parts), scalars=1)
     swapped = lax.ppermute(jnp.concatenate([total, leave]), "core", SWAP)
     wide = jax.ShapeDtypeStruct((row_count, width), jnp.bfloat16)
     square = jax.ShapeDtypeStruct((width, width), f32)

time: 123 us -> 140 us (1.14)
  blocking collectives: 33.5 us -> 75.6 us
  starting transfers between devices: 68.2 us -> 36.1 us
  between operations: 0.89 us -> 14.2 us
  waiting for transfers between devices: 10.9 us -> 6.19 us
    all_to_all x2 -> x5, blocking collectives: 33.5 us -> 75.6 us  [exchange(): return lax.all_to_all(parts, axes, 0, 0)]
    ppermute x6 -> x0, starting transfers between devices: 18.1 us -> none  [rotate(): lax.ppermute(parts[s], axis, [(i, (i + s) % 4) for i in range(4)])]
    all_to_all x4 -> x2, starting transfers between devices: 27.5 us -> 13.6 us  [exchange(): return lax.all_to_all(parts, axes, 0, 0)]
    all_to_all x4 -> x2, waiting for transfers between devices: 5.55 us -> 3.05 us  [exchange(): return lax.all_to_all(parts, axes, 0, 0)]
    ppermute x6 -> x0, waiting for transfers between devices: 2.19 us -> none  [rotate(): lax.ppermute(parts[s], axis, [(i, (i + s) % 4) for i in range(4)])]
    pallas_call x4 -> x3, Pallas kernels: 3.67 us -> 3.39 us  [call(): pl.pallas_call(kernel, out_shape=outs, in_specs=[SMEM] * scalars + [VMEM]...]
  transfers between devices with their start and end apart: 13 -> 6, of which waited for: 6 -> 3; matrix products, arithmetic and copies ran while one was open for 1% -> 1% of each run, Pallas kernels for 1% -> 0%
where the time goes in v7:
time: 140 us
  blocking collectives  75.6 us (54%)
  starting transfers between devices  36.1 us (26%)
  between operations  14.2 us (10%)
  waiting for transfers between devices  6.19 us (4%)
  Pallas kernels  3.39 us (2%)
  local copies, waits for them, and re-layouts  3.23 us (2%)
    all_to_all x5, blocking collectives, exchange(): return lax.all_to_all(parts, axes, 0, 0)  75.6 us
    all_to_all x2, starting transfers between devices, exchange(): return lax.all_to_all(parts, axes, 0, 0)  13.6 us
    ppermute x1, starting transfers between devices, per_device(): strip = gather(lax.ppermute(rows, AXES, TURN), 'x', 4)  10.3 us
    ppermute x1, starting transfers between devices, per_device(): swapped = lax.ppermute(jnp.concatenate([total, leave]), 'core', SWAP)  10.1 us
    pallas_call x3, Pallas kernels, call(): pl.pallas_call(kernel, out_shape=outs, in_specs=[SMEM] * scalars + [VMEM]...  3.39 us
    all_to_all x2, waiting for transfers between devices, exchange(): return lax.all_to_all(parts, axes, 0, 0)  3.05 us
  transfers between devices with their start and end apart: 6, of which 3 were waited for; matrix products, arithmetic and copies ran while one was open for 1% of the time, Pallas kernels for 0%

profile of v7, /device:TPU:1, one launch (start us, length us, event | category | flops | bytes accessed | tf_op | source)
XLA Modules:
  0.0 139.7 jit_solution(9480155421285957374)
XLA Ops:
  7.2 0.7 pad_maximum_fusion.1
  7.9 0.7 broadcast_in_dim.10
  8.6 10.2 %all-to-all-start = ((bf16[8,32,256]{2,1,0:T(8,128)(2,1)}), bf16[8,32,256]{2,1,0:T(8,128)(2,1)S(1)}, u32[]{:S(2)}, u32[]{:S(2)}) async-start(bf16[8,32,256]{2,1,0:T(8,128)(2,1)} %bitcast.2), calls=%async_computation | async-start | bytes 262144 | tf_op jit(solution)/shard_map/all_to_all | solution.py:17
  18.7 2.0 %collective-permute-start = (bf16[1024,512]{1,0:T(8,128)(2,1)}, bf16[1024,512]{1,0:T(8,128)(2,1)S(1)}, u32[]{:S(2)}, u32[]{:S(2)}) collective-permute-start(bf16[1024,512]{1,0:T(8,128)(2,1)} %pool.1), channel_id=1, source_target_pairs={{0,1},{1,0},{2,3},{3,2},{4,5},{5,4},{6,7},{7,6},{8,9},{9,8},{10,11... | collective-permute-start | bytes 3145736 | tf_op jit(solution)/shard_map/ppermute | solution.py:121
  20.8 0.0 copy-start.4
  20.8 0.0 copy-start.5
  20.8 0.6 copy-done.4
  21.4 0.0 copy-done.5
  21.4 0.1 fusion
  21.5 3.0 %all-to-all-done = bf16[8,32,256]{2,1,0:T(8,128)(2,1)S(1)} async-done(((bf16[8,32,256]{2,1,0:T(8,128)(2,1)}), bf16[8,32,256]{2,1,0:T(8,128)(2,1)S(1)}, u32[]{:S(2)}, u32[]{:S(2)}) %all-to-all-start) | async-done | bytes 131104 | tf_op jit(solution)/shard_map/all_to_all | solution.py:17
  24.6 0.1 bitcast_multiply_fusion
  24.6 0.8 broadcast_in_dim.12
  25.5 3.5 %all-to-all-start.2 = ((bf16[4,4,64,256]{3,2,1,0:T(8,128)(2,1)}), bf16[4,4,64,256]{3,2,1,0:T(8,128)(2,1)S(1)}, u32[]{:S(2)}, u32[]{:S(2)}) async-start(bf16[4,4,64,256]{3,2,1,0:T(8,128)(2,1)} %broadcast_in_dim.12), calls=%async_computation.2 | async-start | bytes 1048576 | tf_op jit(solution)/shard_map/all_to_all | solution.py:17
  29.0 0.0 copy-start
  29.0 0.0 reduce-scatter.2.cloned.1.call-start
  29.0 10.3 %collective-permute-start.1 = (bf16[4,64,256]{2,1,0:T(8,128)(2,1)S(1)}, bf16[4,64,256]{2,1,0:T(8,128)(2,1)S(1)}, u32[]{:S(2)}, u32[]{:S(2)}) collective-permute-start(bf16[4,64,256]{2,1,0:T(8,128)(2,1)S(1)} %bitcast_multiply_fusion), channel_id=1, source_target_pairs={{12,0},{13,1},{38,2},{39,3},{88,4},{89,5},{114,6},{115,7},{138,8},... | collective-permute-start | bytes 393224 | tf_op jit(solution)/shard_map/ppermute | solution.py:129
  39.4 1.9 %collective-permute-done.1 = bf16[4,64,256]{2,1,0:T(8,128)(2,1)S(1)} collective-permute-done((bf16[4,64,256]{2,1,0:T(8,128)(2,1)S(1)}, bf16[4,64,256]{2,1,0:T(8,128)(2,1)S(1)}, u32[]{:S(2)}, u32[]{:S(2)}) %collective-permute-start.1) | collective-permute-done | bytes 131104 | tf_op jit(solution)/shard_map/ppermute | solution.py:129
  41.3 0.0 all-to-all-done.2
  41.3 12.0 %all_to_all.35.strip = bf16[4,4,64,256]{3,2,1,0:T(8,128)(2,1)S(1)} all-to-all(bf16[4,4,64,256]{3,2,1,0:T(8,128)(2,1)S(1)} %broadcast_in_dim.11), channel_id=1, replica_groups=mesh['x'=4,'zh'=4,'zl'=4,'y'=4,'core'=2] {'x'}, dimensions={0} | all-to-all | bytes 1048576 | tf_op jit(solution)/shard_map/all_to_all | solution.py:17
  53.3 0.0 collective-permute-done.sibling
  53.3 0.0 copy-done
  53.3 2.0 %shard_map.102 = (f32[512,128]{1,0:T(8,128)S(1)}, f32[1024,256]{1,0:T(8,128)S(1)}) custom-call(bf16[1024,512]{1,0:T(8,128)(2,1)S(1)} %copy-done, bf16[1024,512]{1,0:T(8,128)(2,1)S(1)} %collective-permute-done.sibling, bf16[4,4,64,256]{3,2,1,0:T(8,128)(2,1)S(1)} %all_to_all.35.strip, bf16[4,256,256]{2,1,0:T(8,128)(2,1)S(1)} %bitcast.15), custom_call_target="tpu_custom_call" | custom-call | tf_op jit(solution)/shard_map/pallas_call | solution.py:102
  55.3 0.0 copy-start.1
  55.3 1.0 copy-done.1
  56.3 0.0 reduce-scatter.2.cloned.1.call-update
  56.3 21.6 %all_to_all.36 = f32[64,8,128]{2,1,0:T(8,128)S(1)} all-to-all(f32[64,8,128]{2,1,0:T(8,128)S(1)} %bitcast.16), channel_id=1, replica_groups=mesh['x'=4,'zh'=4,'zl'=4,'y'=4,'core'=2] {'x','y','zl'}, dimensions={0} | all-to-all | bytes 524288 | tf_op jit(solution)/shard_map/all_to_all | solution.py:17
  77.9 0.1 reduce_sum.18
  77.9 23.2 %all_to_all.37 = f32[16,8,128]{2,1,0:T(8,128)S(1)} all-to-all(f32[16,8,128]{2,1,0:T(8,128)S(1)} %broadcast_in_dim.13), channel_id=1, replica_groups=mesh['x'=4,'zh'=4,'zl'=4,'y'=4,'core'=2] {'zh','zl'}, dimensions={0} | all-to-all | bytes 131072 | tf_op jit(solution)/shard_map/all_to_all | solution.py:17
  101.1 10.0 %all_to_all.38 = f32[16,32,128]{2,1,0:T(8,128)S(1)} all-to-all(f32[16,32,128]{2,1,0:T(8,128)S(1)} %broadcast_in_dim.14), channel_id=1, replica_groups=mesh['x'=4,'zh'=4,'zl'=4,'y'=4,'core'=2] {'x','y'}, dimensions={0} | all-to-all | bytes 524288 | tf_op jit(solution)/shard_map/all_to_all | solution.py:17
  111.2 0.0 reduce-scatter.2.cloned.1.call-done
  111.2 8.9 %all_to_all.39.parts = f32[4,64,256]{2,1,0:T(8,128)S(1)} all-to-all(f32[4,64,256]{2,1,0:T(8,128)} %bitcast.19), channel_id=1, replica_groups=mesh['x'=4,'zh'=4,'zl'=4,'y'=4,'core'=2] {'y'}, dimensions={0} | all-to-all | bytes 524288 | tf_op jit(solution)/shard_map/all_to_all | solution.py:17
  120.1 0.6 shard_map.103
  120.6 0.0 copy-start.2
  120.6 0.0 copy-start.3
  120.7 10.1 %collective-permute-start.2 = (f32[576,128]{1,0:T(8,128)S(1)}, f32[576,128]{1,0:T(8,128)S(1)}, u32[]{:S(2)}, u32[]{:S(2)}) collective-permute-start(f32[576,128]{1,0:T(8,128)S(1)} %pad_maximum_fusion), channel_id=1, source_target_pairs={{0,1},{1,0},{2,3},{3,2},{4,5},{5,4},{6,7},{7,6},{8,9},{9,8},{10,11... | collective-permute-start | bytes 884744 | tf_op jit(solution)/shard_map/ppermute | solution.py:146
  130.8 1.2 collective-permute-done.2.swapped
  132.0 0.0 copy-done.2
  132.0 0.0 copy-done.3
  132.0 0.9 shard_map.104
  (6 shorter events, 0.1 us)
Async XLA Ops:
  8.6 16.0 %all-to-all-start = ((bf16[8,32,256]{2,1,0:T(8,128)(2,1)}), bf16[8,32,256]{2,1,0:T(8,128)(2,1)S(1)}, u32[]{:S(2)}, u32[]{:S(2)}) async-start(bf16[8,32,256]{2,1,0:T(8,128)(2,1)} %bitcast.2), calls=%async_computation | async-start | bytes 262144 | tf_op jit(solution)/shard_map/all_to_all | solution.py:17
  18.7 34.6 %collective-permute-start = (bf16[1024,512]{1,0:T(8,128)(2,1)}, bf16[1024,512]{1,0:T(8,128)(2,1)S(1)}, u32[]{:S(2)}, u32[]{:S(2)}) collective-permute-start(bf16[1024,512]{1,0:T(8,128)(2,1)} %pool.1), channel_id=1, source_target_pairs={{0,1},{1,0},{2,3},{3,2},{4,5},{5,4},{6,7},{7,6},{8,9},{9,8},{10,11... | collective-permute-start | bytes 3145736 | tf_op jit(solution)/shard_map/ppermute | solution.py:121
  20.8 0.7 copy-start.4
  20.8 0.7 copy-start.5
  25.5 15.8 %all-to-all-start.2 = ((bf16[4,4,64,256]{3,2,1,0:T(8,128)(2,1)}), bf16[4,4,64,256]{3,2,1,0:T(8,128)(2,1)S(1)}, u32[]{:S(2)}, u32[]{:S(2)}) async-start(bf16[4,4,64,256]{3,2,1,0:T(8,128)(2,1)} %broadcast_in_dim.12), calls=%async_computation.2 | async-start | bytes 1048576 | tf_op jit(solution)/shard_map/all_to_all | solution.py:17
  29.0 24.3 %copy-start = (bf16[1024,512]{1,0:T(8,128)(2,1)S(1)}, bf16[1024,512]{1,0:T(8,128)(2,1)}, u32[]{:S(2)}) copy-start(bf16[1024,512]{1,0:T(8,128)(2,1)} %pool.1) | copy-start | bytes 3145732
  29.0 82.2 %reduce-scatter.2.cloned.1.call-start = ((), (), s32[]{:S(2)}) async-start(), calls=%async_computation.8 | async-start | bytes 1310720 | tf_op jit(solution)/shard_map/reduce_scatter | solution.py:138
  29.0 12.2 %collective-permute-start.1 = (bf16[4,64,256]{2,1,0:T(8,128)(2,1)S(1)}, bf16[4,64,256]{2,1,0:T(8,128)(2,1)S(1)}, u32[]{:S(2)}, u32[]{:S(2)}) collective-permute-start(bf16[4,64,256]{2,1,0:T(8,128)(2,1)S(1)} %bitcast_multiply_fusion), channel_id=1, source_target_pairs={{12,0},{13,1},{38,2},{39,3},{88,4},{89,5},{114,6},{115,7},{138,8},... | collective-permute-start | bytes 393224 | tf_op jit(solution)/shard_map/ppermute | solution.py:129
  55.3 1.0 copy-start.1
  120.6 11.4 %copy-start.2 = (f32[256,256]{1,0:T(8,128)S(1)}, f32[256,256]{1,0:T(8,128)}, u32[]{:S(2)}) copy-start(f32[256,256]{1,0:T(8,128)} %inv_one.1) | copy-start | bytes 786436
  120.6 11.4 %copy-start.3 = (f32[256,256]{1,0:T(8,128)S(1)}, f32[256,256]{1,0:T(8,128)}, u32[]{:S(2)}) copy-start(f32[256,256]{1,0:T(8,128)} %inv_two.1) | copy-start | bytes 786436
  120.7 11.3 %collective-permute-start.2 = (f32[576,128]{1,0:T(8,128)S(1)}, f32[576,128]{1,0:T(8,128)S(1)}, u32[]{:S(2)}, u32[]{:S(2)}) collective-permute-start(f32[576,128]{1,0:T(8,128)S(1)} %pad_maximum_fusion), channel_id=1, source_target_pairs={{0,1},{1,0},{2,3},{3,2},{4,5},{5,4},{6,7},{7,6},{8,9},{9,8},{10,11... | collective-permute-start | bytes 884744 | tf_op jit(solution)/shard_map/ppermute | solution.py:146
Sparse Core Ops, SparseCore 0:
  56.4 43.9 reduce-scatter.1

commit v8 on v7

--- a/solution.py
+++ b/solution.py
@@ -21,6 +21,10 @@
     return exchange(jnp.broadcast_to(block[None], (count, *block.shape)), axes)
 
 
+def pair(block, axis, flip):
+    return lax.ppermute(block, axis, [(i, i ^ flip) for i in range(4)])
+
+
 def device_id(x, zh, zl, y, core):
     return (((x * 4 + zh) * 4 + zl) * 4 + y) * 2 + core
 
@@ -40,9 +44,9 @@
 ]
 
 
-def multiply_kernel(pool, sibling, strip, rows, diag, out, rhs, full):
-    core = lax.axis_index("core")
-    shift = lax.axis_index("zl") - lax.axis_index("y") + 2
+def multiply_kernel(pool, sibling, strip, rows, diag, keep, send, rhs, full):
+    core, y = lax.axis_index("core"), lax.axis_index("y")
+    shift = lax.axis_index("zl") - y + 2
     depth = rhs.shape[0] // 2
     for side, which in ((0, core), (1, 1 - core)):
         for h in range(2):
@@ -54,7 +58,6 @@
         block = jnp.dot(
             pool[take], rhs[:depth], preferred_element_type=jnp.float32
         ) + jnp.dot(sibling[take], rhs[depth:], preferred_element_type=jnp.float32)
-        out[take] = block
         for j in range(4):
             full[j, z * 64 : (z + 1) * 64] = block[j * 64 : (j + 1) * 64]
     term = jnp.zeros((256, 256), jnp.float32)
@@ -68,12 +71,27 @@
             )
     diag[0:256] = term[:, :128]
     diag[256:512] = term[:, 128:]
+    keep[0], keep[1] = full[y], full[y ^ 3]
+    send[0], send[1] = full[y ^ 1], full[y ^ 2]
 
 
-def split_kernel(mask, parts, stay, leave):
+def half_kernel(kept, came, keep, send):
+    keep[...] = kept[0] + came[0]
+    send[...] = kept[1] + came[1]
+
+
+def chunk_kernel(kept, came, keep, send, full):
+    zl = lax.axis_index("zl")
+    for z in range(4):
+        full[z] = kept[z * 64 : (z + 1) * 64] + came[z * 64 : (z + 1) * 64]
+    keep[0], keep[1] = full[zl], full[zl ^ 2]
+    send[0], send[1] = full[zl ^ 1], full[zl ^ 3]
+
+
+def split_kernel(mask, kept, came, stay, leave):
     core = lax.axis_index("core")
     own = -mask[lax.axis_index("zl")].astype(jnp.float32)
-    column = (parts[0] + parts[1] + parts[2] + parts[3]) * own
+    column = (kept[...] + came[...]) * own
     low = jnp.concatenate([column[0:32, 0:128], column[0:32, 128:256]])
     high = jnp.concatenate([column[32:64, 0:128], column[32:64, 128:256]])
     stay[...] = jnp.where(core == 0, low, high)
@@ -129,20 +147,36 @@
     strip = gather(lax.ppermute(rows, AXES, TURN), "x", 4)
     around = gather(rows, "y", 4).reshape(4, 256, width)
 
-    diag, partial = call(
+    def buffers(*shapes):
+        return [jax.ShapeDtypeStruct(shape, f32) for shape in shapes]
+
+    chunk = 2 * row_count
+    diag, keep, send = call(
         multiply_kernel,
-        [jax.ShapeDtypeStruct((512, 128), f32), jax.ShapeDtypeStruct((1024, width), f32)],
+        buffers((512, 128), (2, 256, width), (2, 256, width)),
         (inverse_pool, sibling_pool, strip, around),
         [pltpu.VMEM((1024, width), jnp.bfloat16), pltpu.VMEM((4, 256, width), f32)],
     )
-    product = lax.psum_scatter(partial, "zl", scatter_dimension=0, tiled=True)
     shard = jnp.sum(exchange(diag.reshape(64, 8, 128), ("x", "y", "zl")), axis=0)
+    came = pair(send, "y", 1)
+    keep, send = call(half_kernel, buffers((256, width), (256, width)), (keep, came))
+    shard, keep, send = lax.optimization_barrier((shard, keep, send))
     shard = jnp.sum(gather(shard, ("zh", "zl"), 16).reshape(4, 32, 128), axis=0)
+    came = pair(send, "y", 3)
+    keep, send = call(
+        chunk_kernel,
+        buffers((2, chunk, width), (2, chunk, width)),
+        (keep, came),
+        [pltpu.VMEM((4, chunk, width), f32)],
+    )
+    came = pair(send, "zl", 1)
+    shard, keep, came = lax.optimization_barrier((shard, keep, came))
+    keep, send = call(half_kernel, buffers((chunk, width), (chunk, width)), (keep, came))
+    came = pair(send, "zl", 2)
+    stay, leave = call(
+        split_kernel, buffers((chunk, 128), (chunk, 128)), (mask, keep, came), scalars=1
+    )
     total = gather(shard, ("x", "y"), 16).reshape(512, 128)
-    total, product = lax.optimization_barrier((total, product))
-    half = jax.ShapeDtypeStruct((2 * row_count, 128), f32)
-    parts = exchange(product.reshape(4, 2 * row_count, width), "y")
-    stay, leave = call(split_kernel, [half, half], (mask, parts), scalars=1)
     swapped = lax.ppermute(jnp.concatenate([total, leave]), "core", SWAP)
     wide = jax.ShapeDtypeStruct((row_count, width), jnp.bfloat16)
     square = jax.ShapeDtypeStruct((width, width), f32)

time: 140 us -> 130 us (0.929)
  blocking collectives: 75.6 us -> 12 us
  starting transfers between devices: 36.1 us -> 74.4 us
  waiting for transfers between devices: 6.19 us -> 31.6 us
  between operations: 14.2 us -> 0.84 us
    all_to_all x5 -> x1, blocking collectives: 75.6 us -> 12 us  [exchange(): return lax.all_to_all(parts, axes, 0, 0)]
    all_to_all x2 -> x5, starting transfers between devices: 13.6 us -> 41.4 us  [exchange(): return lax.all_to_all(parts, axes, 0, 0)]
    ppermute x0 -> x4, waiting for transfers between devices: none -> 17 us  [pair(): return lax.ppermute(block, axis, [(i, i ^ flip) for i in range(4)])]
    ppermute x0 -> x4, starting transfers between devices: none -> 12.8 us  [pair(): return lax.ppermute(block, axis, [(i, i ^ flip) for i in range(4)])]
    all_to_all x2 -> x5, waiting for transfers between devices: 3.05 us -> 11.5 us  [exchange(): return lax.all_to_all(parts, axes, 0, 0)]
    ppermute x1, starting transfers between devices: 10.1 us -> 7.85 us  [per_device(): swapped = lax.ppermute(jnp.concatenate([total, leave]), 'core', SWAP)]
    pallas_call x3 -> x6, Pallas kernels: 3.39 us -> 4.41 us  [call(): pl.pallas_call(kernel, out_shape=outs, in_specs=[SMEM] * scalars + [VMEM]...]
  transfers between devices with their start and end apart: 6 -> 12, of which waited for: 3 -> 7; matrix products, arithmetic and copies ran while one was open for 1% -> 1% of each run, Pallas kernels for 0% -> 1%
where the time goes in v8:
time: 130 us; the launch traced here: 129 us
  starting transfers between devices  74.4 us (57%)
  waiting for transfers between devices  31.6 us (24%)
  blocking collectives  12 us (9%)
  local copies, waits for them, and re-layouts  4.42 us (3%)
  Pallas kernels  4.41 us (3%)
    all_to_all x5, starting transfers between devices, exchange(): return lax.all_to_all(parts, axes, 0, 0)  41.4 us
    ppermute x4, waiting for transfers between devices, pair(): return lax.ppermute(block, axis, [(i, i ^ flip) for i in range(4)])  17 us
    ppermute x4, starting transfers between devices, pair(): return lax.ppermute(block, axis, [(i, i ^ flip) for i in range(4)])  12.8 us
    all_to_all x1, blocking collectives, exchange(): return lax.all_to_all(parts, axes, 0, 0)  12 us
    all_to_all x5, waiting for transfers between devices, exchange(): return lax.all_to_all(parts, axes, 0, 0)  11.5 us
    ppermute x1, starting transfers between devices, per_device(): strip = gather(lax.ppermute(rows, AXES, TURN), 'x', 4)  10.4 us
    ppermute x1, starting transfers between devices, per_device(): swapped = lax.ppermute(jnp.concatenate([total, leave]), 'core', SWAP)  7.85 us
    pallas_call x6, Pallas kernels, call(): pl.pallas_call(kernel, out_shape=outs, in_specs=[SMEM] * scalars + [VMEM]...  4.41 us
  transfers between devices with their start and end apart: 12, of which 7 were waited for; matrix products, arithmetic and copies ran while one was open for 1% of the time, Pallas kernels for 1%

profile of v8, /device:TPU:1, one launch (start us, length us, event | category | flops | bytes accessed | tf_op | source)
XLA Modules:
  0.0 128.6 jit_solution(3964117389621386955)
XLA Ops:
  0.6 0.7 pad_maximum_fusion.1
  1.4 0.7 broadcast_in_dim.10
  2.0 10.2 %all-to-all-start = ((bf16[8,32,256]{2,1,0:T(8,128)(2,1)}), bf16[8,32,256]{2,1,0:T(8,128)(2,1)S(1)}, u32[]{:S(2)}, u32[]{:S(2)}) async-start(bf16[8,32,256]{2,1,0:T(8,128)(2,1)} %bitcast.2), calls=%async_computation | async-start | bytes 262144 | tf_op jit(solution)/shard_map/all_to_all | solution.py:17
  12.2 2.0 %collective-permute-start = (bf16[1024,512]{1,0:T(8,128)(2,1)}, bf16[1024,512]{1,0:T(8,128)(2,1)S(1)}, u32[]{:S(2)}, u32[]{:S(2)}) collective-permute-start(bf16[1024,512]{1,0:T(8,128)(2,1)} %pool.1), channel_id=1, source_target_pairs={{0,1},{1,0},{2,3},{3,2},{4,5},{5,4},{6,7},{7,6},{8,9},{9,8},{10,11... | collective-permute-start | bytes 3145736 | tf_op jit(solution)/shard_map/ppermute | solution.py:139
  14.2 0.0 copy-start.5
  14.2 0.0 copy-start.6
  14.2 0.6 copy-done.5
  14.9 0.0 copy-done.6
  14.9 0.1 fusion
  15.0 3.0 %all-to-all-done = bf16[8,32,256]{2,1,0:T(8,128)(2,1)S(1)} async-done(((bf16[8,32,256]{2,1,0:T(8,128)(2,1)}), bf16[8,32,256]{2,1,0:T(8,128)(2,1)S(1)}, u32[]{:S(2)}, u32[]{:S(2)}) %all-to-all-start) | async-done | bytes 131104 | tf_op jit(solution)/shard_map/all_to_all | solution.py:17
  18.0 0.1 bitcast_multiply_fusion
  18.1 0.9 broadcast_in_dim.12
  19.0 3.5 %all-to-all-start.2 = ((bf16[4,4,64,256]{3,2,1,0:T(8,128)(2,1)}), bf16[4,4,64,256]{3,2,1,0:T(8,128)(2,1)S(1)}, u32[]{:S(2)}, u32[]{:S(2)}) async-start(bf16[4,4,64,256]{3,2,1,0:T(8,128)(2,1)} %broadcast_in_dim.12), calls=%async_computation.2 | async-start | bytes 1048576 | tf_op jit(solution)/shard_map/all_to_all | solution.py:17
  22.5 0.0 copy-start
  22.5 10.4 %collective-permute-start.1 = (bf16[4,64,256]{2,1,0:T(8,128)(2,1)S(1)}, bf16[4,64,256]{2,1,0:T(8,128)(2,1)S(1)}, u32[]{:S(2)}, u32[]{:S(2)}) collective-permute-start(bf16[4,64,256]{2,1,0:T(8,128)(2,1)S(1)} %bitcast_multiply_fusion), channel_id=1, source_target_pairs={{12,0},{13,1},{38,2},{39,3},{88,4},{89,5},{114,6},{115,7},{138,8},... | collective-permute-start | bytes 393224 | tf_op jit(solution)/shard_map/ppermute | solution.py:147
  32.8 1.9 %collective-permute-done.1 = bf16[4,64,256]{2,1,0:T(8,128)(2,1)S(1)} collective-permute-done((bf16[4,64,256]{2,1,0:T(8,128)(2,1)S(1)}, bf16[4,64,256]{2,1,0:T(8,128)(2,1)S(1)}, u32[]{:S(2)}, u32[]{:S(2)}) %collective-permute-start.1) | collective-permute-done | bytes 131104 | tf_op jit(solution)/shard_map/ppermute | solution.py:147
  34.8 0.0 all-to-all-done.2
  34.8 12.0 %all_to_all.30.strip = bf16[4,4,64,256]{3,2,1,0:T(8,128)(2,1)S(1)} all-to-all(bf16[4,4,64,256]{3,2,1,0:T(8,128)(2,1)S(1)} %broadcast_in_dim.11), channel_id=1, replica_groups=mesh['x'=4,'zh'=4,'zl'=4,'y'=4,'core'=2] {'x'}, dimensions={0} | all-to-all | bytes 1048576 | tf_op jit(solution)/shard_map/all_to_all | solution.py:17
  46.8 0.0 collective-permute-done.sibling
  46.8 0.0 copy-done
  46.8 2.9 %shard_map.102 = (f32[512,128]{1,0:T(8,128)}, f32[2,256,256]{2,1,0:T(8,128)S(1)}, f32[2,256,256]{2,1,0:T(8,128)S(1)}) custom-call(bf16[1024,512]{1,0:T(8,128)(2,1)S(1)} %copy-done, bf16[1024,512]{1,0:T(8,128)(2,1)S(1)} %collective-permute-done.sibling, bf16[4,4,64,256]{3,2,1,0:T(8,128)(2,1)S(1)} %all_to_all.30.strip, bf16[4,256,256]{2,1,0:T(8,128)(2,1)S(1)} %bitcast.14), custom_call_target="tpu_custom_call" | custom-call | tf_op jit(solution)/shard_map/pallas_call | solution.py:120
  49.7 0.0 copy-start.3
  49.7 0.8 copy-done.3
  50.5 0.0 copy-start.4
  50.5 11.6 %all-to-all-start.3 = ((f32[64,8,128]{2,1,0:T(8,128)}), f32[64,8,128]{2,1,0:T(8,128)S(1)}, u32[]{:S(2)}, u32[]{:S(2)}) async-start(f32[64,8,128]{2,1,0:T(8,128)} %bitcast.5), calls=%async_computation.3 | async-start | bytes 524288 | tf_op jit(solution)/shard_map/all_to_all | solution.py:17
  62.1 0.0 copy-done.4
  62.1 2.9 %collective-permute-start.2 = (f32[2,256,256]{2,1,0:T(8,128)S(1)}, f32[2,256,256]{2,1,0:T(8,128)S(1)}, u32[]{:S(2)}, u32[]{:S(2)}) collective-permute-start(f32[2,256,256]{2,1,0:T(8,128)S(1)} %copy-done.4), channel_id=1, source_target_pairs={{0,2},{2,0},{4,6},{6,4},{1,3},{3,1},{5,7},{7,5},{8,10},{10,8},{12,... | collective-permute-start | bytes 1572872 | tf_op jit(solution)/shard_map/ppermute | solution.py:25
  65.0 13.1 %collective-permute-done.2.came = f32[2,256,256]{2,1,0:T(8,128)S(1)} collective-permute-done((f32[2,256,256]{2,1,0:T(8,128)S(1)}, f32[2,256,256]{2,1,0:T(8,128)S(1)}, u32[]{:S(2)}, u32[]{:S(2)}) %collective-permute-start.2) | collective-permute-done | bytes 524320 | tf_op jit(solution)/shard_map/ppermute | solution.py:25
  78.1 0.1 shard_map.103
  78.2 0.0 all-to-all-done.3
  78.2 0.1 reduce_sum.18
  78.3 3.8 %collective-permute-start.3 = (f32[256,256]{1,0:T(8,128)S(1)}, f32[256,256]{1,0:T(8,128)S(1)}, u32[]{:S(2)}, u32[]{:S(2)}) collective-permute-start(f32[256,256]{1,0:T(8,128)S(1)} %get-tuple-element.28), channel_id=1, source_target_pairs={{0,6},{2,4},{4,2},{6,0},{1,7},{3,5},{5,3},{7,1},{8,14},{10,12},{12... | collective-permute-start | bytes 786440 | tf_op jit(solution)/shard_map/ppermute | solution.py:25
  82.1 0.6 broadcast_in_dim.13
  82.7 12.5 %all-to-all-start.4 = ((f32[16,8,128]{2,1,0:T(8,128)}), f32[16,8,128]{2,1,0:T(8,128)S(1)}, u32[]{:S(2)}, u32[]{:S(2)}) async-start(f32[16,8,128]{2,1,0:T(8,128)} %broadcast_in_dim.13), calls=%async_computation.4 | async-start | bytes 131072 | tf_op jit(solution)/shard_map/all_to_all | solution.py:17
  95.2 0.0 collective-permute-done.3.came
  95.3 3.3 %collective-permute-start.4 = (f32[2,64,256]{2,1,0:T(8,128)S(1)}, f32[2,64,256]{2,1,0:T(8,128)S(1)}, u32[]{:S(2)}, u32[]{:S(2)}) collective-permute-start(f32[2,64,256]{2,1,0:T(8,128)S(1)} %get-tuple-element.30), channel_id=1, source_target_pairs={{0,8},{8,0},{16,24},{24,16},{1,9},{9,1},{17,25},{25,17},{2,10},{10... | collective-permute-start | bytes 393224 | tf_op jit(solution)/shard_map/ppermute | solution.py:25
  98.5 8.3 %all-to-all-done.4 = f32[16,8,128]{2,1,0:T(8,128)S(1)} async-done(((f32[16,8,128]{2,1,0:T(8,128)}), f32[16,8,128]{2,1,0:T(8,128)S(1)}, u32[]{:S(2)}, u32[]{:S(2)}) %all-to-all-start.4) | async-done | bytes 65568 | tf_op jit(solution)/shard_map/all_to_all | solution.py:17
  106.9 0.0 collective-permute-done.4.came
  106.9 0.7 broadcast_in_dim.14
  107.6 3.8 %all-to-all-start.5 = ((f32[16,32,128]{2,1,0:T(8,128)}), f32[16,32,128]{2,1,0:T(8,128)S(1)}, u32[]{:S(2)}, u32[]{:S(2)}) async-start(f32[16,32,128]{2,1,0:T(8,128)} %broadcast_in_dim.14), calls=%async_computation.5 | async-start | bytes 524288 | tf_op jit(solution)/shard_map/all_to_all | solution.py:17
  111.4 2.8 %collective-permute-start.5 = (f32[64,256]{1,0:T(8,128)S(1)}, f32[64,256]{1,0:T(8,128)S(1)}, u32[]{:S(2)}, u32[]{:S(2)}) collective-permute-start(f32[64,256]{1,0:T(8,128)S(1)} %get-tuple-element.35), channel_id=1, source_target_pairs={{0,16},{8,24},{16,0},{24,8},{1,17},{9,25},{17,1},{25,9},{2,18},{10... | collective-permute-start | bytes 196616 | tf_op jit(solution)/shard_map/ppermute | solution.py:25
  114.2 3.8 %collective-permute-done.5.came = f32[64,256]{1,0:T(8,128)S(1)} collective-permute-done((f32[64,256]{1,0:T(8,128)S(1)}, f32[64,256]{1,0:T(8,128)S(1)}, u32[]{:S(2)}, u32[]{:S(2)}) %collective-permute-start.5) | collective-permute-done | bytes 65568 | tf_op jit(solution)/shard_map/ppermute | solution.py:25
  118.0 0.6 shard_map.106
  118.6 0.1 all-to-all-done.5
  118.7 0.0 copy-start.1
  118.7 0.0 copy-start.2
  118.7 7.8 %collective-permute-start.6 = (f32[576,128]{1,0:T(8,128)S(1)}, f32[576,128]{1,0:T(8,128)S(1)}, u32[]{:S(2)}, u32[]{:S(2)}) collective-permute-start(f32[576,128]{1,0:T(8,128)S(1)} %pad_maximum_fusion), channel_id=1, source_target_pairs={{0,1},{1,0},{2,3},{3,2},{4,5},{5,4},{6,7},{7,6},{8,9},{9,8},{10,11... | collective-permute-start | bytes 884744 | tf_op jit(solution)/shard_map/ppermute | solution.py:180
  126.6 1.2 collective-permute-done.6.swapped
  127.8 0.0 copy-done.1
  127.8 0.0 copy-done.2
  127.8 0.9 shard_map.107
  (6 shorter events, 0.1 us)
Async XLA Ops:
  2.0 16.0 %all-to-all-start = ((bf16[8,32,256]{2,1,0:T(8,128)(2,1)}), bf16[8,32,256]{2,1,0:T(8,128)(2,1)S(1)}, u32[]{:S(2)}, u32[]{:S(2)}) async-start(bf16[8,32,256]{2,1,0:T(8,128)(2,1)} %bitcast.2), calls=%async_computation | async-start | bytes 262144 | tf_op jit(solution)/shard_map/all_to_all | solution.py:17
  12.2 34.6 %collective-permute-start = (bf16[1024,512]{1,0:T(8,128)(2,1)}, bf16[1024,512]{1,0:T(8,128)(2,1)S(1)}, u32[]{:S(2)}, u32[]{:S(2)}) collective-permute-start(bf16[1024,512]{1,0:T(8,128)(2,1)} %pool.1), channel_id=1, source_target_pairs={{0,1},{1,0},{2,3},{3,2},{4,5},{5,4},{6,7},{7,6},{8,9},{9,8},{10,11... | collective-permute-start | bytes 3145736 | tf_op jit(solution)/shard_map/ppermute | solution.py:139
  14.2 0.7 copy-start.5
  14.2 0.7 copy-start.6
  19.0 15.8 %all-to-all-start.2 = ((bf16[4,4,64,256]{3,2,1,0:T(8,128)(2,1)}), bf16[4,4,64,256]{3,2,1,0:T(8,128)(2,1)S(1)}, u32[]{:S(2)}, u32[]{:S(2)}) async-start(bf16[4,4,64,256]{3,2,1,0:T(8,128)(2,1)} %broadcast_in_dim.12), calls=%async_computation.2 | async-start | bytes 1048576 | tf_op jit(solution)/shard_map/all_to_all | solution.py:17
  22.5 24.3 %copy-start = (bf16[1024,512]{1,0:T(8,128)(2,1)S(1)}, bf16[1024,512]{1,0:T(8,128)(2,1)}, u32[]{:S(2)}) copy-start(bf16[1024,512]{1,0:T(8,128)(2,1)} %pool.1) | copy-start | bytes 3145732
  22.5 12.3 %collective-permute-start.1 = (bf16[4,64,256]{2,1,0:T(8,128)(2,1)S(1)}, bf16[4,64,256]{2,1,0:T(8,128)(2,1)S(1)}, u32[]{:S(2)}, u32[]{:S(2)}) collective-permute-start(bf16[4,64,256]{2,1,0:T(8,128)(2,1)S(1)} %bitcast_multiply_fusion), channel_id=1, source_target_pairs={{12,0},{13,1},{38,2},{39,3},{88,4},{89,5},{114,6},{115,7},{138,8},... | collective-permute-start | bytes 393224 | tf_op jit(solution)/shard_map/ppermute | solution.py:147
  49.7 0.8 copy-start.3
  50.5 11.6 %copy-start.4 = (f32[2,256,256]{2,1,0:T(8,128)S(1)}, f32[2,256,256]{2,1,0:T(8,128)}, u32[]{:S(2)}) copy-start(f32[2,256,256]{2,1,0:T(8,128)} %copy-done.3) | copy-start | bytes 1572868
  50.5 27.7 %all-to-all-start.3 = ((f32[64,8,128]{2,1,0:T(8,128)}), f32[64,8,128]{2,1,0:T(8,128)S(1)}, u32[]{:S(2)}, u32[]{:S(2)}) async-start(f32[64,8,128]{2,1,0:T(8,128)} %bitcast.5), calls=%async_computation.3 | async-start | bytes 524288 | tf_op jit(solution)/shard_map/all_to_all | solution.py:17
  62.1 16.1 %collective-permute-start.2 = (f32[2,256,256]{2,1,0:T(8,128)S(1)}, f32[2,256,256]{2,1,0:T(8,128)S(1)}, u32[]{:S(2)}, u32[]{:S(2)}) collective-permute-start(f32[2,256,256]{2,1,0:T(8,128)S(1)} %copy-done.4), channel_id=1, source_target_pairs={{0,2},{2,0},{4,6},{6,4},{1,3},{3,1},{5,7},{7,5},{8,10},{10,8},{12,... | collective-permute-start | bytes 1572872 | tf_op jit(solution)/shard_map/ppermute | solution.py:25
  78.3 16.9 %collective-permute-start.3 = (f32[256,256]{1,0:T(8,128)S(1)}, f32[256,256]{1,0:T(8,128)S(1)}, u32[]{:S(2)}, u32[]{:S(2)}) collective-permute-start(f32[256,256]{1,0:T(8,128)S(1)} %get-tuple-element.28), channel_id=1, source_target_pairs={{0,6},{2,4},{4,2},{6,0},{1,7},{3,5},{5,3},{7,1},{8,14},{10,12},{12... | collective-permute-start | bytes 786440 | tf_op jit(solution)/shard_map/ppermute | solution.py:25
  82.7 24.1 %all-to-all-start.4 = ((f32[16,8,128]{2,1,0:T(8,128)}), f32[16,8,128]{2,1,0:T(8,128)S(1)}, u32[]{:S(2)}, u32[]{:S(2)}) async-start(f32[16,8,128]{2,1,0:T(8,128)} %broadcast_in_dim.13), calls=%async_computation.4 | async-start | bytes 131072 | tf_op jit(solution)/shard_map/all_to_all | solution.py:17
  95.3 11.6 %collective-permute-start.4 = (f32[2,64,256]{2,1,0:T(8,128)S(1)}, f32[2,64,256]{2,1,0:T(8,128)S(1)}, u32[]{:S(2)}, u32[]{:S(2)}) collective-permute-start(f32[2,64,256]{2,1,0:T(8,128)S(1)} %get-tuple-element.30), channel_id=1, source_target_pairs={{0,8},{8,0},{16,24},{24,16},{1,9},{9,1},{17,25},{25,17},{2,10},{10... | collective-permute-start | bytes 393224 | tf_op jit(solution)/shard_map/ppermute | solution.py:25
  107.6 11.1 %all-to-all-start.5 = ((f32[16,32,128]{2,1,0:T(8,128)}), f32[16,32,128]{2,1,0:T(8,128)S(1)}, u32[]{:S(2)}, u32[]{:S(2)}) async-start(f32[16,32,128]{2,1,0:T(8,128)} %broadcast_in_dim.14), calls=%async_computation.5 | async-start | bytes 524288 | tf_op jit(solution)/shard_map/all_to_all | solution.py:17
  111.4 6.6 %collective-permute-start.5 = (f32[64,256]{1,0:T(8,128)S(1)}, f32[64,256]{1,0:T(8,128)S(1)}, u32[]{:S(2)}, u32[]{:S(2)}) collective-permute-start(f32[64,256]{1,0:T(8,128)S(1)} %get-tuple-element.35), channel_id=1, source_target_pairs={{0,16},{8,24},{16,0},{24,8},{1,17},{9,25},{17,1},{25,9},{2,18},{10... | collective-permute-start | bytes 196616 | tf_op jit(solution)/shard_map/ppermute | solution.py:25
  118.7 9.1 %copy-start.1 = (f32[256,256]{1,0:T(8,128)S(1)}, f32[256,256]{1,0:T(8,128)}, u32[]{:S(2)}) copy-start(f32[256,256]{1,0:T(8,128)} %inv_one.1) | copy-start | bytes 786436
  118.7 9.1 %copy-start.2 = (f32[256,256]{1,0:T(8,128)S(1)}, f32[256,256]{1,0:T(8,128)}, u32[]{:S(2)}) copy-start(f32[256,256]{1,0:T(8,128)} %inv_two.1) | copy-start | bytes 786436
  118.7 9.0 %collective-permute-start.6 = (f32[576,128]{1,0:T(8,128)S(1)}, f32[576,128]{1,0:T(8,128)S(1)}, u32[]{:S(2)}, u32[]{:S(2)}) collective-permute-start(f32[576,128]{1,0:T(8,128)S(1)} %pad_maximum_fusion), channel_id=1, source_target_pairs={{0,1},{1,0},{2,3},{3,2},{4,5},{5,4},{6,7},{7,6},{8,9},{9,8},{10,11... | collective-permute-start | bytes 884744 | tf_op jit(solution)/shard_map/ppermute | solution.py:180

commit v9 on v5

--- a/solution.py
+++ b/solution.py
@@ -71,8 +71,9 @@
             term = term + lax.dot_general(
                 left, piece, (((0,), (0,)), ((), ())), preferred_element_type=jnp.float32
             )
-    diag[0:256] = term[:, :128]
-    diag[256:512] = term[:, 128:]
+    diag[0:128] = term[:128, :128]
+    diag[128:256] = term[:128, 128:]
+    diag[256:384] = term[128:, 128:]
     for hop, out in enumerate((out0, out1, out2, out3)):
         out[...] = full[(y + hop) & 3]
 
@@ -96,8 +97,8 @@
 
 def finish_kernel(total, stay, swapped, inv_one, inv_two, column_one, column_two, diag_one, diag_two):
     first = lax.axis_index("core") == 0
-    own, other = total[...], swapped[0:512]
-    own_column, other_column = stay[...], swapped[512:576]
+    own, other = total[...], swapped[0:384]
+    own_column, other_column = stay[...], swapped[384:448]
     for swap, inv, diag, column in (
         (False, inv_one, diag_one, column_one),
         (True, inv_two, diag_two, column_two),
@@ -105,8 +106,10 @@
         pick = first != swap
         t = jnp.where(pick, own, other)
         c = jnp.where(pick, own_column, other_column).astype(jnp.bfloat16)
-        diag[:, 0:128] = inv[:, 0:128] + t[0:256]
-        diag[:, 128:256] = inv[:, 128:256] + t[256:512]
+        diag[0:128, 0:128] = inv[0:128, 0:128] + t[0:128]
+        diag[0:128, 128:256] = inv[0:128, 128:256] + t[128:256]
+        diag[128:256, 0:128] = inv[128:256, 0:128] + t[128:256].T
+        diag[128:256, 128:256] = inv[128:256, 128:256] + t[256:384]
         column[:, 0:128] = c[0:32]
         column[:, 128:256] = c[32:64]
 
@@ -146,13 +149,13 @@
     quarter = jax.ShapeDtypeStruct((256, width), f32)
     diag, *parts = call(
         multiply_kernel,
-        [jax.ShapeDtypeStruct((512, 128), f32)] + [quarter] * 4,
+        [jax.ShapeDtypeStruct((384, 128), f32)] + [quarter] * 4,
         (inverse_pool, sibling_pool, strip, around),
         [pltpu.VMEM((1024, width), jnp.bfloat16), pltpu.VMEM((4, 256, width), f32)],
     )
-    shard = jnp.sum(exchange(diag.reshape(64, 8, 128), ("x", "y", "zl")), axis=0)
+    shard = jnp.sum(exchange(diag.reshape(16, 24, 128), ("x", "y")), axis=0)
     parts = rotate(parts, "y")
-    shard = jnp.sum(gather(shard, ("zh", "zl"), 16).reshape(4, 32, 128), axis=0)
+    shard = jnp.sum(gather(shard, ("zh", "zl"), 16), axis=0)
     parts = call(
         turn_kernel,
         [jax.ShapeDtypeStruct((2 * row_count, width), f32)] * 4,
@@ -162,7 +165,7 @@
     parts = rotate(parts, "zl")
     half = jax.ShapeDtypeStruct((2 * row_count, 128), f32)
     stay, leave = call(split_kernel, [half, half], (mask, *parts), scalars=1)
-    total = gather(shard, ("x", "y"), 16).reshape(512, 128)
+    total = gather(shard, ("x", "y"), 16).reshape(384, 128)
     swapped = lax.ppermute(jnp.concatenate([total, leave]), "core", SWAP)
     wide = jax.ShapeDtypeStruct((row_count, width), jnp.bfloat16)
     square = jax.ShapeDtypeStruct((width, width), f32)

time: 123 us -> 119 us (0.967)
  blocking collectives: 33.5 us -> 25 us
  starting transfers between devices: 68.2 us -> 71.1 us
    all_to_all x2, blocking collectives: 33.5 us -> 25 us  [exchange(): return lax.all_to_all(parts, axes, 0, 0)]
    all_to_all x4, starting transfers between devices: 27.5 us -> 31.2 us  [exchange(): return lax.all_to_all(parts, axes, 0, 0)]
    ppermute x1, starting transfers between devices: 10.3 us -> 8.63 us  [per_device(): swapped = lax.ppermute(jnp.concatenate([total, leave]), 'core', SWAP)]
  transfers between devices with their start and end apart: 13 -> 13, of which waited for: 6 -> 6; matrix products, arithmetic and copies ran while one was open for 1% -> 2% of each run, Pallas kernels for 1% -> 1%
where the time goes in v9:
time: 119 us; the launch traced here: 118 us
  starting transfers between devices  71.1 us (60%)
  blocking collectives  25 us (21%)
  waiting for transfers between devices  11.7 us (10%)
  local copies, waits for them, and re-layouts  4.33 us (4%)
  Pallas kernels  3.72 us (3%)
    all_to_all x4, starting transfers between devices, exchange(): return lax.all_to_all(parts, axes, 0, 0)  31.2 us
    all_to_all x2, blocking collectives, exchange(): return lax.all_to_all(parts, axes, 0, 0)  25 us
    ppermute x6, starting transfers between devices, rotate(): lax.ppermute(parts[s], axis, [(i, (i + s) % 4) for i in range(4)])  18.9 us
    ppermute x1, starting transfers between devices, per_device(): strip = gather(lax.ppermute(rows, AXES, TURN), 'x', 4)  10.4 us
    ppermute x1, starting transfers between devices, per_device(): swapped = lax.ppermute(jnp.concatenate([total, leave]), 'core', SWAP)  8.63 us
    all_to_all x4, waiting for transfers between devices, exchange(): return lax.all_to_all(parts, axes, 0, 0)  6.25 us
    pallas_call x4, Pallas kernels, call(): pl.pallas_call(kernel, out_shape=outs, in_specs=[SMEM] * scalars + [VMEM]...  3.72 us
    ppermute x6, waiting for transfers between devices, rotate(): lax.ppermute(parts[s], axis, [(i, (i + s) % 4) for i in range(4)])  2.4 us
  transfers between devices with their start and end apart: 13, of which 6 were waited for; matrix products, arithmetic and copies ran while one was open for 2% of the time, Pallas kernels for 1%

profile of v9, /device:TPU:1, one launch (start us, length us, event | category | flops | bytes accessed | tf_op | source)
XLA Modules:
  0.0 117.6 jit_solution(11102605355938598721)
XLA Ops:
  0.6 0.7 pad_maximum_fusion.1
  1.4 0.7 broadcast_in_dim.10
  2.0 10.2 %all-to-all-start = ((bf16[8,32,256]{2,1,0:T(8,128)(2,1)}), bf16[8,32,256]{2,1,0:T(8,128)(2,1)S(1)}, u32[]{:S(2)}, u32[]{:S(2)}) async-start(bf16[8,32,256]{2,1,0:T(8,128)(2,1)} %bitcast.2), calls=%async_computation | async-start | bytes 262144 | tf_op jit(solution)/shard_map/all_to_all | solution.py:17
  12.2 2.0 %collective-permute-start = (bf16[1024,512]{1,0:T(8,128)(2,1)}, bf16[1024,512]{1,0:T(8,128)(2,1)S(1)}, u32[]{:S(2)}, u32[]{:S(2)}) collective-permute-start(bf16[1024,512]{1,0:T(8,128)(2,1)} %pool.1), channel_id=1, source_target_pairs={{0,1},{1,0},{2,3},{3,2},{4,5},{5,4},{6,7},{7,6},{8,9},{9,8},{10,11... | collective-permute-start | bytes 3145736 | tf_op jit(solution)/shard_map/ppermute | solution.py:138
  14.2 0.0 copy-start.5
  14.2 0.0 copy-start.6
  14.2 0.6 copy-done.5
  14.9 0.0 copy-done.6
  14.9 0.1 fusion
  15.0 3.0 %all-to-all-done = bf16[8,32,256]{2,1,0:T(8,128)(2,1)S(1)} async-done(((bf16[8,32,256]{2,1,0:T(8,128)(2,1)}), bf16[8,32,256]{2,1,0:T(8,128)(2,1)S(1)}, u32[]{:S(2)}, u32[]{:S(2)}) %all-to-all-start) | async-done | bytes 131104 | tf_op jit(solution)/shard_map/all_to_all | solution.py:17
  18.0 0.1 bitcast_multiply_fusion
  18.1 0.9 broadcast_in_dim.12
  19.0 3.5 %all-to-all-start.2 = ((bf16[4,4,64,256]{3,2,1,0:T(8,128)(2,1)}), bf16[4,4,64,256]{3,2,1,0:T(8,128)(2,1)S(1)}, u32[]{:S(2)}, u32[]{:S(2)}) async-start(bf16[4,4,64,256]{3,2,1,0:T(8,128)(2,1)} %broadcast_in_dim.12), calls=%async_computation.2 | async-start | bytes 1048576 | tf_op jit(solution)/shard_map/all_to_all | solution.py:17
  22.5 0.0 copy-start
  22.5 10.4 %collective-permute-start.1 = (bf16[4,64,256]{2,1,0:T(8,128)(2,1)S(1)}, bf16[4,64,256]{2,1,0:T(8,128)(2,1)S(1)}, u32[]{:S(2)}, u32[]{:S(2)}) collective-permute-start(bf16[4,64,256]{2,1,0:T(8,128)(2,1)S(1)} %bitcast_multiply_fusion), channel_id=1, source_target_pairs={{12,0},{13,1},{38,2},{39,3},{88,4},{89,5},{114,6},{115,7},{138,8},... | collective-permute-start | bytes 393224 | tf_op jit(solution)/shard_map/ppermute | solution.py:146
  32.8 1.9 %collective-permute-done.1 = bf16[4,64,256]{2,1,0:T(8,128)(2,1)S(1)} collective-permute-done((bf16[4,64,256]{2,1,0:T(8,128)(2,1)S(1)}, bf16[4,64,256]{2,1,0:T(8,128)(2,1)S(1)}, u32[]{:S(2)}, u32[]{:S(2)}) %collective-permute-start.1) | collective-permute-done | bytes 131104 | tf_op jit(solution)/shard_map/ppermute | solution.py:146
  34.8 0.0 all-to-all-done.2
  34.8 12.0 %all_to_all.30.strip = bf16[4,4,64,256]{3,2,1,0:T(8,128)(2,1)S(1)} all-to-all(bf16[4,4,64,256]{3,2,1,0:T(8,128)(2,1)S(1)} %broadcast_in_dim.11), channel_id=1, replica_groups=mesh['x'=4,'zh'=4,'zl'=4,'y'=4,'core'=2] {'x'}, dimensions={0} | all-to-all | bytes 1048576 | tf_op jit(solution)/shard_map/all_to_all | solution.py:17
  46.8 0.0 collective-permute-done.sibling
  46.8 0.0 copy-done
  46.8 2.2 %shard_map.102 = (f32[384,128]{1,0:T(8,128)S(1)}, f32[256,256]{1,0:T(8,128)S(1)}, f32[256,256]{1,0:T(8,128)S(1)}, f32[256,256]{1,0:T(8,128)S(1)}, f32[256,256]{1,0:T(8,128)S(1)}) custom-call(bf16[1024,512]{1,0:T(8,128)(2,1)S(1)} %copy-done, bf16[1024,512]{1,0:T(8,128)(2,1)S(1)} %collective-permute-done.sibling, ...), custom_call_target="tpu_custom_call" | custom-call | tf_op jit(solution)/shard_map/pallas_call | solution.py:119
  49.0 0.0 copy-start.3
  49.0 0.7 copy-done.3
  49.7 13.0 %all_to_all.31 = f32[16,24,128]{2,1,0:T(8,128)S(1)} all-to-all(f32[16,24,128]{2,1,0:T(8,128)S(1)} %bitcast.12), channel_id=1, replica_groups=mesh['x'=4,'zh'=4,'zl'=4,'y'=4,'core'=2] {'x','y'}, dimensions={0} | all-to-all | bytes 393216 | tf_op jit(solution)/shard_map/all_to_all | solution.py:17
  62.7 0.0 copy-start.4
  62.7 0.7 broadcast_in_dim.13
  63.4 14.1 %all-to-all-start.4 = ((f32[16,24,128]{2,1,0:T(8,128)}), f32[16,24,128]{2,1,0:T(8,128)S(1)}, u32[]{:S(2)}, u32[]{:S(2)}) async-start(f32[16,24,128]{2,1,0:T(8,128)} %broadcast_in_dim.13), calls=%async_computation.4 | async-start | bytes 393216 | tf_op jit(solution)/shard_map/all_to_all | solution.py:17
  77.5 0.0 copy-done.4
  77.5 2.2 %collective-permute-start.2 = (f32[256,256]{1,0:T(8,128)S(1)}, f32[256,256]{1,0:T(8,128)S(1)}, u32[]{:S(2)}, u32[]{:S(2)}) collective-permute-start(f32[256,256]{1,0:T(8,128)S(1)} %copy-done.4), channel_id=1, source_target_pairs={{0,2},{2,4},{4,6},{6,0},{1,3},{3,5},{5,7},{7,1},{8,10},{10,12},{12... | collective-permute-start | bytes 786440 | tf_op jit(solution)/shard_map/ppermute | solution.py:26
  79.7 3.8 %collective-permute-start.3 = (f32[256,256]{1,0:T(8,128)S(1)}, f32[256,256]{1,0:T(8,128)S(1)}, u32[]{:S(2)}, u32[]{:S(2)}) collective-permute-start(f32[256,256]{1,0:T(8,128)S(1)} %get-tuple-element.18), channel_id=1, source_target_pairs={{0,4},{2,6},{4,0},{6,2},{1,5},{3,7},{5,1},{7,3},{8,12},{10,14},{12... | collective-permute-start | bytes 786440 | tf_op jit(solution)/shard_map/ppermute | solution.py:26
  83.4 3.2 %collective-permute-start.4 = (f32[256,256]{1,0:T(8,128)S(1)}, f32[256,256]{1,0:T(8,128)S(1)}, u32[]{:S(2)}, u32[]{:S(2)}) collective-permute-start(f32[256,256]{1,0:T(8,128)S(1)} %get-tuple-element.19), channel_id=1, source_target_pairs={{0,6},{2,0},{4,2},{6,4},{1,7},{3,1},{5,3},{7,5},{8,14},{10,8},{12,... | collective-permute-start | bytes 786440 | tf_op jit(solution)/shard_map/ppermute | solution.py:26
  86.6 3.2 %all-to-all-done.4 = f32[16,24,128]{2,1,0:T(8,128)S(1)} async-done(((f32[16,24,128]{2,1,0:T(8,128)}), f32[16,24,128]{2,1,0:T(8,128)S(1)}, u32[]{:S(2)}, u32[]{:S(2)}) %all-to-all-start.4) | async-done | bytes 196640 | tf_op jit(solution)/shard_map/all_to_all | solution.py:17
  89.9 0.7 broadcast_in_dim.14
  90.5 3.5 %all-to-all-start.5 = ((f32[16,24,128]{2,1,0:T(8,128)}), f32[16,24,128]{2,1,0:T(8,128)S(1)}, u32[]{:S(2)}, u32[]{:S(2)}) async-start(f32[16,24,128]{2,1,0:T(8,128)} %broadcast_in_dim.14), calls=%async_computation.5 | async-start | bytes 393216 | tf_op jit(solution)/shard_map/all_to_all | solution.py:17
  94.1 0.0 collective-permute-done.2.in1
  94.1 0.0 collective-permute-done.3.in2
  94.1 0.0 collective-permute-done.4.in3
  94.1 0.1 shard_map.103
  94.2 3.4 %collective-permute-start.5 = (f32[64,256]{1,0:T(8,128)S(1)}, f32[64,256]{1,0:T(8,128)S(1)}, u32[]{:S(2)}, u32[]{:S(2)}) collective-permute-start(f32[64,256]{1,0:T(8,128)S(1)} %get-tuple-element.21), channel_id=1, source_target_pairs={{0,8},{8,16},{16,24},{24,0},{1,9},{9,17},{17,25},{25,1},{2,10},{10... | collective-permute-start | bytes 196616 | tf_op jit(solution)/shard_map/ppermute | solution.py:26
  97.6 3.4 %collective-permute-start.6 = (f32[64,256]{1,0:T(8,128)S(1)}, f32[64,256]{1,0:T(8,128)S(1)}, u32[]{:S(2)}, u32[]{:S(2)}) collective-permute-start(f32[64,256]{1,0:T(8,128)S(1)} %get-tuple-element.22), channel_id=1, source_target_pairs={{0,16},{8,24},{16,0},{24,8},{1,17},{9,25},{17,1},{25,9},{2,18},{10... | collective-permute-start | bytes 196616 | tf_op jit(solution)/shard_map/ppermute | solution.py:26
  101.1 2.9 %collective-permute-start.7 = (f32[64,256]{1,0:T(8,128)S(1)}, f32[64,256]{1,0:T(8,128)S(1)}, u32[]{:S(2)}, u32[]{:S(2)}) collective-permute-start(f32[64,256]{1,0:T(8,128)S(1)} %get-tuple-element.23), channel_id=1, source_target_pairs={{0,24},{8,0},{16,8},{24,16},{1,25},{9,1},{17,9},{25,17},{2,26},{10... | collective-permute-start | bytes 196616 | tf_op jit(solution)/shard_map/ppermute | solution.py:26
  104.0 0.0 collective-permute-done.5.in1
  104.0 0.5 collective-permute-done.6.in2
  104.5 1.8 %collective-permute-done.7.in3 = f32[64,256]{1,0:T(8,128)S(1)} collective-permute-done((f32[64,256]{1,0:T(8,128)S(1)}, f32[64,256]{1,0:T(8,128)S(1)}, u32[]{:S(2)}, u32[]{:S(2)}) %collective-permute-start.7) | collective-permute-done | bytes 65568 | tf_op jit(solution)/shard_map/ppermute | solution.py:26
  106.4 0.0 copy-start.2
  106.4 0.6 shard_map.104
  106.9 0.0 copy-start.1
  107.0 0.0 all-to-all-done.5
  107.0 8.6 %collective-permute-start.8 = (f32[448,128]{1,0:T(8,128)S(1)}, f32[448,128]{1,0:T(8,128)S(1)}, u32[]{:S(2)}, u32[]{:S(2)}) collective-permute-start(f32[448,128]{1,0:T(8,128)S(1)} %pad_maximum_fusion), channel_id=1, source_target_pairs={{0,1},{1,0},{2,3},{3,2},{4,5},{5,4},{6,7},{7,6},{8,9},{9,8},{10,11... | collective-permute-start | bytes 688136 | tf_op jit(solution)/shard_map/ppermute | solution.py:169
  115.6 1.1 collective-permute-done.8.swapped
  116.7 0.0 copy-done.2
  116.7 0.0 copy-done.1
  116.7 0.9 shard_map.105
  (5 shorter events, 0.1 us)
Async XLA Ops:
  2.0 16.0 %all-to-all-start = ((bf16[8,32,256]{2,1,0:T(8,128)(2,1)}), bf16[8,32,256]{2,1,0:T(8,128)(2,1)S(1)}, u32[]{:S(2)}, u32[]{:S(2)}) async-start(bf16[8,32,256]{2,1,0:T(8,128)(2,1)} %bitcast.2), calls=%async_computation | async-start | bytes 262144 | tf_op jit(solution)/shard_map/all_to_all | solution.py:17
  12.2 34.6 %collective-permute-start = (bf16[1024,512]{1,0:T(8,128)(2,1)}, bf16[1024,512]{1,0:T(8,128)(2,1)S(1)}, u32[]{:S(2)}, u32[]{:S(2)}) collective-permute-start(bf16[1024,512]{1,0:T(8,128)(2,1)} %pool.1), channel_id=1, source_target_pairs={{0,1},{1,0},{2,3},{3,2},{4,5},{5,4},{6,7},{7,6},{8,9},{9,8},{10,11... | collective-permute-start | bytes 3145736 | tf_op jit(solution)/shard_map/ppermute | solution.py:138
  14.2 0.7 copy-start.5
  14.2 0.7 copy-start.6
  19.0 15.8 %all-to-all-start.2 = ((bf16[4,4,64,256]{3,2,1,0:T(8,128)(2,1)}), bf16[4,4,64,256]{3,2,1,0:T(8,128)(2,1)S(1)}, u32[]{:S(2)}, u32[]{:S(2)}) async-start(bf16[4,4,64,256]{3,2,1,0:T(8,128)(2,1)} %broadcast_in_dim.12), calls=%async_computation.2 | async-start | bytes 1048576 | tf_op jit(solution)/shard_map/all_to_all | solution.py:17
  22.5 24.3 %copy-start = (bf16[1024,512]{1,0:T(8,128)(2,1)S(1)}, bf16[1024,512]{1,0:T(8,128)(2,1)}, u32[]{:S(2)}) copy-start(bf16[1024,512]{1,0:T(8,128)(2,1)} %pool.1) | copy-start | bytes 3145732
  22.5 12.3 %collective-permute-start.1 = (bf16[4,64,256]{2,1,0:T(8,128)(2,1)S(1)}, bf16[4,64,256]{2,1,0:T(8,128)(2,1)S(1)}, u32[]{:S(2)}, u32[]{:S(2)}) collective-permute-start(bf16[4,64,256]{2,1,0:T(8,128)(2,1)S(1)} %bitcast_multiply_fusion), channel_id=1, source_target_pairs={{12,0},{13,1},{38,2},{39,3},{88,4},{89,5},{114,6},{115,7},{138,8},... | collective-permute-start | bytes 393224 | tf_op jit(solution)/shard_map/ppermute | solution.py:146
  49.0 0.7 copy-start.3
  62.7 14.8 %copy-start.4 = (f32[256,256]{1,0:T(8,128)S(1)}, f32[256,256]{1,0:T(8,128)}, u32[]{:S(2)}) copy-start(f32[256,256]{1,0:T(8,128)} %copy-done.3) | copy-start | bytes 786436
  63.4 26.4 %all-to-all-start.4 = ((f32[16,24,128]{2,1,0:T(8,128)}), f32[16,24,128]{2,1,0:T(8,128)S(1)}, u32[]{:S(2)}, u32[]{:S(2)}) async-start(f32[16,24,128]{2,1,0:T(8,128)} %broadcast_in_dim.13), calls=%async_computation.4 | async-start | bytes 393216 | tf_op jit(solution)/shard_map/all_to_all | solution.py:17
  77.5 16.6 %collective-permute-start.2 = (f32[256,256]{1,0:T(8,128)S(1)}, f32[256,256]{1,0:T(8,128)S(1)}, u32[]{:S(2)}, u32[]{:S(2)}) collective-permute-start(f32[256,256]{1,0:T(8,128)S(1)} %copy-done.4), channel_id=1, source_target_pairs={{0,2},{2,4},{4,6},{6,0},{1,3},{3,5},{5,7},{7,1},{8,10},{10,12},{12... | collective-permute-start | bytes 786440 | tf_op jit(solution)/shard_map/ppermute | solution.py:26
  79.7 14.4 %collective-permute-start.3 = (f32[256,256]{1,0:T(8,128)S(1)}, f32[256,256]{1,0:T(8,128)S(1)}, u32[]{:S(2)}, u32[]{:S(2)}) collective-permute-start(f32[256,256]{1,0:T(8,128)S(1)} %get-tuple-element.18), channel_id=1, source_target_pairs={{0,4},{2,6},{4,0},{6,2},{1,5},{3,7},{5,1},{7,3},{8,12},{10,14},{12... | collective-permute-start | bytes 786440 | tf_op jit(solution)/shard_map/ppermute | solution.py:26
  83.4 10.7 %collective-permute-start.4 = (f32[256,256]{1,0:T(8,128)S(1)}, f32[256,256]{1,0:T(8,128)S(1)}, u32[]{:S(2)}, u32[]{:S(2)}) collective-permute-start(f32[256,256]{1,0:T(8,128)S(1)} %get-tuple-element.19), channel_id=1, source_target_pairs={{0,6},{2,0},{4,2},{6,4},{1,7},{3,1},{5,3},{7,5},{8,14},{10,8},{12,... | collective-permute-start | bytes 786440 | tf_op jit(solution)/shard_map/ppermute | solution.py:26
  90.5 16.4 %all-to-all-start.5 = ((f32[16,24,128]{2,1,0:T(8,128)}), f32[16,24,128]{2,1,0:T(8,128)S(1)}, u32[]{:S(2)}, u32[]{:S(2)}) async-start(f32[16,24,128]{2,1,0:T(8,128)} %broadcast_in_dim.14), calls=%async_computation.5 | async-start | bytes 393216 | tf_op jit(solution)/shard_map/all_to_all | solution.py:17
  94.2 9.8 %collective-permute-start.5 = (f32[64,256]{1,0:T(8,128)S(1)}, f32[64,256]{1,0:T(8,128)S(1)}, u32[]{:S(2)}, u32[]{:S(2)}) collective-permute-start(f32[64,256]{1,0:T(8,128)S(1)} %get-tuple-element.21), channel_id=1, source_target_pairs={{0,8},{8,16},{16,24},{24,0},{1,9},{9,17},{17,25},{25,1},{2,10},{10... | collective-permute-start | bytes 196616 | tf_op jit(solution)/shard_map/ppermute | solution.py:26
  97.6 6.9 %collective-permute-start.6 = (f32[64,256]{1,0:T(8,128)S(1)}, f32[64,256]{1,0:T(8,128)S(1)}, u32[]{:S(2)}, u32[]{:S(2)}) collective-permute-start(f32[64,256]{1,0:T(8,128)S(1)} %get-tuple-element.22), channel_id=1, source_target_pairs={{0,16},{8,24},{16,0},{24,8},{1,17},{9,25},{17,1},{25,9},{2,18},{10... | collective-permute-start | bytes 196616 | tf_op jit(solution)/shard_map/ppermute | solution.py:26
  101.1 5.3 %collective-permute-start.7 = (f32[64,256]{1,0:T(8,128)S(1)}, f32[64,256]{1,0:T(8,128)S(1)}, u32[]{:S(2)}, u32[]{:S(2)}) collective-permute-start(f32[64,256]{1,0:T(8,128)S(1)} %get-tuple-element.23), channel_id=1, source_target_pairs={{0,24},{8,0},{16,8},{24,16},{1,25},{9,1},{17,9},{25,17},{2,26},{10... | collective-permute-start | bytes 196616 | tf_op jit(solution)/shard_map/ppermute | solution.py:26
  106.4 10.4 %copy-start.2 = (f32[256,256]{1,0:T(8,128)S(1)}, f32[256,256]{1,0:T(8,128)}, u32[]{:S(2)}) copy-start(f32[256,256]{1,0:T(8,128)} %inv_two.1) | copy-start | bytes 786436
  106.9 9.8 %copy-start.1 = (f32[256,256]{1,0:T(8,128)S(1)}, f32[256,256]{1,0:T(8,128)}, u32[]{:S(2)}) copy-start(f32[256,256]{1,0:T(8,128)} %inv_one.1) | copy-start | bytes 786436
  107.0 9.7 %collective-permute-start.8 = (f32[448,128]{1,0:T(8,128)S(1)}, f32[448,128]{1,0:T(8,128)S(1)}, u32[]{:S(2)}, u32[]{:S(2)}) collective-permute-start(f32[448,128]{1,0:T(8,128)S(1)} %pad_maximum_fusion), channel_id=1, source_target_pairs={{0,1},{1,0},{2,3},{3,2},{4,5},{5,4},{6,7},{7,6},{8,9},{9,8},{10,11... | collective-permute-start | bytes 688136 | tf_op jit(solution)/shard_map/ppermute | solution.py:169

commit v10 on v5

--- a/solution.py
+++ b/solution.py
@@ -77,19 +77,23 @@
         out[...] = full[(y + hop) & 3]
 
 
-def turn_kernel(in0, in1, in2, in3, out0, out1, out2, out3, full):
-    zl = lax.axis_index("zl")
-    full[...] = in0[...] + in1[...] + in2[...] + in3[...]
-    for hop, out in enumerate((out0, out1, out2, out3)):
-        out[...] = full[pl.ds(pl.multiple_of(((zl + hop) & 3) * 64, 64), 64)]
+def join_kernel(in0, in1, in2, in3, quarter, joined):
+    total = in0[...] + in1[...] + in2[...] + in3[...]
+    for z in range(4):
+        joined[z, 0:64] = total[z * 64 : (z + 1) * 64, :128]
+        joined[z, 64:128] = total[z * 64 : (z + 1) * 64, 128:]
+        joined[z, 128:136] = quarter[...]
 
 
-def split_kernel(mask, in0, in1, in2, in3, stay, leave):
+def split_kernel(mask, parts, shards, stay, leave):
     core = lax.axis_index("core")
     own = -mask[lax.axis_index("zl")].astype(jnp.float32)
-    column = (in0[...] + in1[...] + in2[...] + in3[...]) * own
-    low = jnp.concatenate([column[0:32, 0:128], column[0:32, 128:256]])
-    high = jnp.concatenate([column[32:64, 0:128], column[32:64, 128:256]])
+    for i in range(16):
+        for z in range(4):
+            shards[i, z * 8 : (z + 1) * 8] = parts[z, 128:136]
+    column = (parts[0, 0:128] + parts[1, 0:128] + parts[2, 0:128] + parts[3, 0:128]) * own
+    low = jnp.concatenate([column[0:32], column[64:96]])
+    high = jnp.concatenate([column[32:64], column[96:128]])
     stay[...] = jnp.where(core == 0, low, high)
     leave[...] = jnp.where(core == 0, high, low)
 
@@ -150,19 +154,19 @@
         (inverse_pool, sibling_pool, strip, around),
         [pltpu.VMEM((1024, width), jnp.bfloat16), pltpu.VMEM((4, 256, width), f32)],
     )
-    shard = jnp.sum(exchange(diag.reshape(64, 8, 128), ("x", "y", "zl")), axis=0)
+    def buffers(*shapes):
+        return [jax.ShapeDtypeStruct(shape, f32) for shape in shapes]
+
+    shard = jnp.sum(exchange(diag.reshape(16, 32, 128), ("x", "y")), axis=0)
     parts = rotate(parts, "y")
-    shard = jnp.sum(gather(shard, ("zh", "zl"), 16).reshape(4, 32, 128), axis=0)
-    parts = call(
-        turn_kernel,
-        [jax.ShapeDtypeStruct((2 * row_count, width), f32)] * 4,
-        parts,
-        [pltpu.VMEM((256, width), f32)],
+    quarters = jnp.broadcast_to(shard.reshape(1, 4, 8, 128), (4, 4, 8, 128)).reshape(16, 8, 128)
+    quarter = jnp.sum(exchange(quarters, ("zh", "zl")), axis=0)
+    (joined,) = call(join_kernel, buffers((4, 136, 128)), (*parts, quarter))
+    half = (2 * row_count, 128)
+    shards, stay, leave = call(
+        split_kernel, buffers((16, 32, 128), half, half), (mask, exchange(joined, "zl")), scalars=1
     )
-    parts = rotate(parts, "zl")
-    half = jax.ShapeDtypeStruct((2 * row_count, 128), f32)
-    stay, leave = call(split_kernel, [half, half], (mask, *parts), scalars=1)
-    total = gather(shard, ("x", "y"), 16).reshape(512, 128)
+    total = exchange(shards, ("x", "y")).reshape(512, 128)
     swapped = lax.ppermute(jnp.concatenate([total, leave]), "core", SWAP)
     wide = jax.ShapeDtypeStruct((row_count, width), jnp.bfloat16)
     square = jax.ShapeDtypeStruct((width, width), f32)

time: 123 us -> 127 us (1.033)
  blocking collectives: 33.5 us -> 57.5 us
  starting transfers between devices: 68.2 us -> 53.1 us
  waiting for transfers between devices: 10.9 us -> 6.18 us
  local copies, waits for them, and re-layouts: 4.32 us -> 2.94 us
    all_to_all x2 -> x4, blocking collectives: 33.5 us -> 57.5 us  [exchange(): return lax.all_to_all(parts, axes, 0, 0)]
    all_to_all x4 -> x3, starting transfers between devices: 27.5 us -> 20 us  [exchange(): return lax.all_to_all(parts, axes, 0, 0)]
    ppermute x6 -> x3, starting transfers between devices: 18.1 us -> 10.7 us  [rotate(): lax.ppermute(parts[s], axis, [(i, (i + s) % 4) for i in range(4)])]
    all_to_all x4 -> x3, waiting for transfers between devices: 5.55 us -> 3.05 us  [exchange(): return lax.all_to_all(parts, axes, 0, 0)]
    ppermute x6 -> x3, waiting for transfers between devices: 2.19 us -> 0.01 us  [rotate(): lax.ppermute(parts[s], axis, [(i, (i + s) % 4) for i in range(4)])]
    broadcast_in_dim x4 -> x2, local copies, waits for them, and re-layouts: 2.27 us -> 0.89 us  [gather(): return exchange(jnp.broadcast_to(block[None], (count, *block.shape)), axes)]
  transfers between devices with their start and end apart: 13 -> 9, of which waited for: 6 -> 3; matrix products, arithmetic and copies ran while one was open for 1% -> 1% of each run, Pallas kernels for 1% -> 0%
where the time goes in v10:
time: 127 us; the launch traced here: 126 us
  blocking collectives  57.5 us (45%)
  starting transfers between devices  53.1 us (42%)
  waiting for transfers between devices  6.18 us (5%)
  Pallas kernels  4.36 us (3%)
  local copies, waits for them, and re-layouts  2.94 us (2%)
    all_to_all x4, blocking collectives, exchange(): return lax.all_to_all(parts, axes, 0, 0)  57.5 us
    all_to_all x3, starting transfers between devices, exchange(): return lax.all_to_all(parts, axes, 0, 0)  20 us
    ppermute x3, starting transfers between devices, rotate(): lax.ppermute(parts[s], axis, [(i, (i + s) % 4) for i in range(4)])  10.7 us
    ppermute x1, starting transfers between devices, per_device(): strip = gather(lax.ppermute(rows, AXES, TURN), 'x', 4)  10.4 us
    ppermute x1, starting transfers between devices, per_device(): swapped = lax.ppermute(jnp.concatenate([total, leave]), 'core', SWAP)  10.1 us
    pallas_call x4, Pallas kernels, call(): pl.pallas_call(kernel, out_shape=outs, in_specs=[SMEM] * scalars + [VMEM]...  4.36 us
    all_to_all x3, waiting for transfers between devices, exchange(): return lax.all_to_all(parts, axes, 0, 0)  3.05 us
  transfers between devices with their start and end apart: 9, of which 3 were waited for; matrix products, arithmetic and copies ran while one was open for 1% of the time, Pallas kernels for 0%

profile of v10, /device:TPU:1, one launch (start us, length us, event | category | flops | bytes accessed | tf_op | source)
XLA Modules:
  0.0 125.9 jit_solution(9288093960744283700)
XLA Ops:
  0.6 0.7 pad_maximum_fusion.1
  1.4 0.7 broadcast_in_dim.10
  2.0 10.2 %all-to-all-start = ((bf16[8,32,256]{2,1,0:T(8,128)(2,1)}), bf16[8,32,256]{2,1,0:T(8,128)(2,1)S(1)}, u32[]{:S(2)}, u32[]{:S(2)}) async-start(bf16[8,32,256]{2,1,0:T(8,128)(2,1)} %bitcast.2), calls=%async_computation | async-start | bytes 262144 | tf_op jit(solution)/shard_map/all_to_all | solution.py:17
  12.2 2.0 %collective-permute-start = (bf16[1024,512]{1,0:T(8,128)(2,1)}, bf16[1024,512]{1,0:T(8,128)(2,1)S(1)}, u32[]{:S(2)}, u32[]{:S(2)}) collective-permute-start(bf16[1024,512]{1,0:T(8,128)(2,1)} %pool.1), channel_id=1, source_target_pairs={{0,1},{1,0},{2,3},{3,2},{4,5},{5,4},{6,7},{7,6},{8,9},{9,8},{10,11... | collective-permute-start | bytes 3145736 | tf_op jit(solution)/shard_map/ppermute | solution.py:139
  14.2 0.0 copy-start.5
  14.2 0.0 copy-start.6
  14.2 0.6 copy-done.5
  14.9 0.0 copy-done.6
  14.9 0.1 fusion
  15.0 3.0 %all-to-all-done = bf16[8,32,256]{2,1,0:T(8,128)(2,1)S(1)} async-done(((bf16[8,32,256]{2,1,0:T(8,128)(2,1)}), bf16[8,32,256]{2,1,0:T(8,128)(2,1)S(1)}, u32[]{:S(2)}, u32[]{:S(2)}) %all-to-all-start) | async-done | bytes 131104 | tf_op jit(solution)/shard_map/all_to_all | solution.py:17
  18.0 0.1 bitcast_multiply_fusion
  18.1 0.8 broadcast_in_dim.12
  19.0 3.5 %all-to-all-start.2 = ((bf16[4,4,64,256]{3,2,1,0:T(8,128)(2,1)}), bf16[4,4,64,256]{3,2,1,0:T(8,128)(2,1)S(1)}, u32[]{:S(2)}, u32[]{:S(2)}) async-start(bf16[4,4,64,256]{3,2,1,0:T(8,128)(2,1)} %broadcast_in_dim.12), calls=%async_computation.2 | async-start | bytes 1048576 | tf_op jit(solution)/shard_map/all_to_all | solution.py:17
  22.4 0.0 copy-start
  22.5 10.4 %collective-permute-start.1 = (bf16[4,64,256]{2,1,0:T(8,128)(2,1)S(1)}, bf16[4,64,256]{2,1,0:T(8,128)(2,1)S(1)}, u32[]{:S(2)}, u32[]{:S(2)}) collective-permute-start(bf16[4,64,256]{2,1,0:T(8,128)(2,1)S(1)} %bitcast_multiply_fusion), channel_id=1, source_target_pairs={{12,0},{13,1},{38,2},{39,3},{88,4},{89,5},{114,6},{115,7},{138,8},... | collective-permute-start | bytes 393224 | tf_op jit(solution)/shard_map/ppermute | solution.py:147
  32.8 1.9 %collective-permute-done.1 = bf16[4,64,256]{2,1,0:T(8,128)(2,1)S(1)} collective-permute-done((bf16[4,64,256]{2,1,0:T(8,128)(2,1)S(1)}, bf16[4,64,256]{2,1,0:T(8,128)(2,1)S(1)}, u32[]{:S(2)}, u32[]{:S(2)}) %collective-permute-start.1) | collective-permute-done | bytes 131104 | tf_op jit(solution)/shard_map/ppermute | solution.py:147
  34.7 0.0 all-to-all-done.2
  34.8 12.0 %all_to_all.35.strip = bf16[4,4,64,256]{3,2,1,0:T(8,128)(2,1)S(1)} all-to-all(bf16[4,4,64,256]{3,2,1,0:T(8,128)(2,1)S(1)} %broadcast_in_dim.11), channel_id=1, replica_groups=mesh['x'=4,'zh'=4,'zl'=4,'y'=4,'core'=2] {'x'}, dimensions={0} | all-to-all | bytes 1048576 | tf_op jit(solution)/shard_map/all_to_all | solution.py:17
  46.8 0.0 collective-permute-done.sibling
  46.8 0.0 copy-done
  46.8 2.9 %shard_map.102 = (f32[512,128]{1,0:T(8,128)}, f32[256,256]{1,0:T(8,128)S(1)}, f32[256,256]{1,0:T(8,128)S(1)}, f32[256,256]{1,0:T(8,128)S(1)}, f32[256,256]{1,0:T(8,128)S(1)}) custom-call(bf16[1024,512]{1,0:T(8,128)(2,1)S(1)} %copy-done, bf16[1024,512]{1,0:T(8,128)(2,1)S(1)} %collective-permute-done.sibling, bf16[4,4,64,256]{3,2,1,0:T(8,128)(2,1)S(1)} %all_to_all.35.strip, ...), custom_call_target="tpu_custom_call" | custom-call | tf_op jit(solution)/shard_map/pallas_call | solution.py:120
  49.7 0.0 copy-start.3
  49.7 0.7 copy-done.3
  50.4 0.0 copy-start.4
  50.4 6.4 %all-to-all-start.3 = ((f32[16,32,128]{2,1,0:T(8,128)}), f32[16,32,128]{2,1,0:T(8,128)S(1)}, u32[]{:S(2)}, u32[]{:S(2)}) async-start(f32[16,32,128]{2,1,0:T(8,128)} %bitcast.5), calls=%async_computation.3 | async-start | bytes 524288 | tf_op jit(solution)/shard_map/all_to_all | solution.py:17
  56.8 0.0 copy-done.4
  56.8 3.3 %collective-permute-start.2 = (f32[256,256]{1,0:T(8,128)S(1)}, f32[256,256]{1,0:T(8,128)S(1)}, u32[]{:S(2)}, u32[]{:S(2)}) collective-permute-start(f32[256,256]{1,0:T(8,128)S(1)} %copy-done.4), channel_id=1, source_target_pairs={{0,2},{2,4},{4,6},{6,0},{1,3},{3,5},{5,7},{7,1},{8,10},{10,12},{12... | collective-permute-start | bytes 786440 | tf_op jit(solution)/shard_map/ppermute | solution.py:26
  60.1 4.3 %collective-permute-start.3 = (f32[256,256]{1,0:T(8,128)S(1)}, f32[256,256]{1,0:T(8,128)S(1)}, u32[]{:S(2)}, u32[]{:S(2)}) collective-permute-start(f32[256,256]{1,0:T(8,128)S(1)} %get-tuple-element.14), channel_id=1, source_target_pairs={{0,4},{2,6},{4,0},{6,2},{1,5},{3,7},{5,1},{7,3},{8,12},{10,14},{12... | collective-permute-start | bytes 786440 | tf_op jit(solution)/shard_map/ppermute | solution.py:26
  64.4 3.1 %collective-permute-start.4 = (f32[256,256]{1,0:T(8,128)S(1)}, f32[256,256]{1,0:T(8,128)S(1)}, u32[]{:S(2)}, u32[]{:S(2)}) collective-permute-start(f32[256,256]{1,0:T(8,128)S(1)} %get-tuple-element.15), channel_id=1, source_target_pairs={{0,6},{2,0},{4,2},{6,4},{1,7},{3,1},{5,3},{7,5},{8,14},{10,8},{12,... | collective-permute-start | bytes 786440 | tf_op jit(solution)/shard_map/ppermute | solution.py:26
  67.5 0.0 all-to-all-done.3
  67.5 25.5 %all_to_all.36 = f32[16,8,128]{2,1,0:T(8,128)S(1)} all-to-all(f32[16,8,128]{2,1,0:T(8,128)S(1)} %bitcast.15), channel_id=1, replica_groups=mesh['x'=4,'zh'=4,'zl'=4,'y'=4,'core'=2] {'zh','zl'}, dimensions={0} | all-to-all | bytes 131072 | tf_op jit(solution)/shard_map/all_to_all | solution.py:17
  93.0 0.0 collective-permute-done.2.in1
  93.0 0.0 collective-permute-done.3.in2
  93.0 0.0 collective-permute-done.4.in3
  93.0 0.1 shard_map.103
  93.1 8.9 %all_to_all.37.parts = f32[4,136,128]{2,1,0:T(8,128)S(1)} all-to-all(f32[4,136,128]{2,1,0:T(8,128)S(1)} %shard_map.103), channel_id=1, replica_groups=mesh['x'=4,'zh'=4,'zl'=4,'y'=4,'core'=2] {'zl'}, dimensions={0} | all-to-all | bytes 557056 | tf_op jit(solution)/shard_map/all_to_all | solution.py:17
  102.0 0.6 shard_map.104
  102.6 11.2 %all_to_all.38 = f32[16,32,128]{2,1,0:T(8,128)S(1)} all-to-all(f32[16,32,128]{2,1,0:T(8,128)S(1)} %get-tuple-element.17), channel_id=1, replica_groups=mesh['x'=4,'zh'=4,'zl'=4,'y'=4,'core'=2] {'x','y'}, dimensions={0} | all-to-all | bytes 524288 | tf_op jit(solution)/shard_map/all_to_all | solution.py:17
  113.8 0.0 copy-start.1
  113.8 0.0 copy-start.2
  113.8 10.1 %collective-permute-start.5 = (f32[576,128]{1,0:T(8,128)S(1)}, f32[576,128]{1,0:T(8,128)S(1)}, u32[]{:S(2)}, u32[]{:S(2)}) collective-permute-start(f32[576,128]{1,0:T(8,128)S(1)} %pad_maximum_fusion), channel_id=1, source_target_pairs={{0,1},{1,0},{2,3},{3,2},{4,5},{5,4},{6,7},{7,6},{8,9},{9,8},{10,11... | collective-permute-start | bytes 884744 | tf_op jit(solution)/shard_map/ppermute | solution.py:170
  123.9 1.2 collective-permute-done.5.swapped
  125.1 0.0 copy-done.1
  125.1 0.0 copy-done.2
  125.1 0.9 shard_map.105
  (6 shorter events, 0.1 us)
Async XLA Ops:
  2.0 16.0 %all-to-all-start = ((bf16[8,32,256]{2,1,0:T(8,128)(2,1)}), bf16[8,32,256]{2,1,0:T(8,128)(2,1)S(1)}, u32[]{:S(2)}, u32[]{:S(2)}) async-start(bf16[8,32,256]{2,1,0:T(8,128)(2,1)} %bitcast.2), calls=%async_computation | async-start | bytes 262144 | tf_op jit(solution)/shard_map/all_to_all | solution.py:17
  12.2 34.6 %collective-permute-start = (bf16[1024,512]{1,0:T(8,128)(2,1)}, bf16[1024,512]{1,0:T(8,128)(2,1)S(1)}, u32[]{:S(2)}, u32[]{:S(2)}) collective-permute-start(bf16[1024,512]{1,0:T(8,128)(2,1)} %pool.1), channel_id=1, source_target_pairs={{0,1},{1,0},{2,3},{3,2},{4,5},{5,4},{6,7},{7,6},{8,9},{9,8},{10,11... | collective-permute-start | bytes 3145736 | tf_op jit(solution)/shard_map/ppermute | solution.py:139
  14.2 0.7 copy-start.5
  14.2 0.7 copy-start.6
  19.0 15.8 %all-to-all-start.2 = ((bf16[4,4,64,256]{3,2,1,0:T(8,128)(2,1)}), bf16[4,4,64,256]{3,2,1,0:T(8,128)(2,1)S(1)}, u32[]{:S(2)}, u32[]{:S(2)}) async-start(bf16[4,4,64,256]{3,2,1,0:T(8,128)(2,1)} %broadcast_in_dim.12), calls=%async_computation.2 | async-start | bytes 1048576 | tf_op jit(solution)/shard_map/all_to_all | solution.py:17
  22.4 24.3 %copy-start = (bf16[1024,512]{1,0:T(8,128)(2,1)S(1)}, bf16[1024,512]{1,0:T(8,128)(2,1)}, u32[]{:S(2)}) copy-start(bf16[1024,512]{1,0:T(8,128)(2,1)} %pool.1) | copy-start | bytes 3145732
  22.5 12.3 %collective-permute-start.1 = (bf16[4,64,256]{2,1,0:T(8,128)(2,1)S(1)}, bf16[4,64,256]{2,1,0:T(8,128)(2,1)S(1)}, u32[]{:S(2)}, u32[]{:S(2)}) collective-permute-start(bf16[4,64,256]{2,1,0:T(8,128)(2,1)S(1)} %bitcast_multiply_fusion), channel_id=1, source_target_pairs={{12,0},{13,1},{38,2},{39,3},{88,4},{89,5},{114,6},{115,7},{138,8},... | collective-permute-start | bytes 393224 | tf_op jit(solution)/shard_map/ppermute | solution.py:147
  49.7 0.7 copy-start.3
  50.4 6.4 %copy-start.4 = (f32[256,256]{1,0:T(8,128)S(1)}, f32[256,256]{1,0:T(8,128)}, u32[]{:S(2)}) copy-start(f32[256,256]{1,0:T(8,128)} %copy-done.3) | copy-start | bytes 786436
  50.4 17.1 %all-to-all-start.3 = ((f32[16,32,128]{2,1,0:T(8,128)}), f32[16,32,128]{2,1,0:T(8,128)S(1)}, u32[]{:S(2)}, u32[]{:S(2)}) async-start(f32[16,32,128]{2,1,0:T(8,128)} %bitcast.5), calls=%async_computation.3 | async-start | bytes 524288 | tf_op jit(solution)/shard_map/all_to_all | solution.py:17
  56.8 36.2 %collective-permute-start.2 = (f32[256,256]{1,0:T(8,128)S(1)}, f32[256,256]{1,0:T(8,128)S(1)}, u32[]{:S(2)}, u32[]{:S(2)}) collective-permute-start(f32[256,256]{1,0:T(8,128)S(1)} %copy-done.4), channel_id=1, source_target_pairs={{0,2},{2,4},{4,6},{6,0},{1,3},{3,5},{5,7},{7,1},{8,10},{10,12},{12... | collective-permute-start | bytes 786440 | tf_op jit(solution)/shard_map/ppermute | solution.py:26
  60.1 33.0 %collective-permute-start.3 = (f32[256,256]{1,0:T(8,128)S(1)}, f32[256,256]{1,0:T(8,128)S(1)}, u32[]{:S(2)}, u32[]{:S(2)}) collective-permute-start(f32[256,256]{1,0:T(8,128)S(1)} %get-tuple-element.14), channel_id=1, source_target_pairs={{0,4},{2,6},{4,0},{6,2},{1,5},{3,7},{5,1},{7,3},{8,12},{10,14},{12... | collective-permute-start | bytes 786440 | tf_op jit(solution)/shard_map/ppermute | solution.py:26
  64.4 28.7 %collective-permute-start.4 = (f32[256,256]{1,0:T(8,128)S(1)}, f32[256,256]{1,0:T(8,128)S(1)}, u32[]{:S(2)}, u32[]{:S(2)}) collective-permute-start(f32[256,256]{1,0:T(8,128)S(1)} %get-tuple-element.15), channel_id=1, source_target_pairs={{0,6},{2,0},{4,2},{6,4},{1,7},{3,1},{5,3},{7,5},{8,14},{10,8},{12,... | collective-permute-start | bytes 786440 | tf_op jit(solution)/shard_map/ppermute | solution.py:26
  113.8 11.3 %copy-start.1 = (f32[256,256]{1,0:T(8,128)S(1)}, f32[256,256]{1,0:T(8,128)}, u32[]{:S(2)}) copy-start(f32[256,256]{1,0:T(8,128)} %inv_one.1) | copy-start | bytes 786436
  113.8 11.3 %copy-start.2 = (f32[256,256]{1,0:T(8,128)S(1)}, f32[256,256]{1,0:T(8,128)}, u32[]{:S(2)}) copy-start(f32[256,256]{1,0:T(8,128)} %inv_two.1) | copy-start | bytes 786436
  113.8 11.3 %collective-permute-start.5 = (f32[576,128]{1,0:T(8,128)S(1)}, f32[576,128]{1,0:T(8,128)S(1)}, u32[]{:S(2)}, u32[]{:S(2)}) collective-permute-start(f32[576,128]{1,0:T(8,128)S(1)} %pad_maximum_fusion), channel_id=1, source_target_pairs={{0,1},{1,0},{2,3},{3,2},{4,5},{5,4},{6,7},{7,6},{8,9},{9,8},{10,11... | collective-permute-start | bytes 884744 | tf_op jit(solution)/shard_map/ppermute | solution.py:170

commit v11 on v10

--- a/solution.py
+++ b/solution.py
@@ -159,8 +159,9 @@
 
     shard = jnp.sum(exchange(diag.reshape(16, 32, 128), ("x", "y")), axis=0)
     parts = rotate(parts, "y")
-    quarters = jnp.broadcast_to(shard.reshape(1, 4, 8, 128), (4, 4, 8, 128)).reshape(16, 8, 128)
-    quarter = jnp.sum(exchange(quarters, ("zh", "zl")), axis=0)
+    quarters = jnp.broadcast_to(shard.reshape(1, 4, 1, 8, 128), (4, 4, 2, 8, 128))
+    quarters = exchange(quarters.reshape(16, 16, 128), ("zh", "zl"))
+    quarter = jnp.sum(quarters[:, :8], axis=0)
     (joined,) = call(join_kernel, buffers((4, 136, 128)), (*parts, quarter))
     half = (2 * row_count, 128)
     shards, stay, leave = call(

time: 127 us -> 129 us (1.016)
  blocking collectives: 57.5 us -> 47.3 us
  starting transfers between devices: 53.1 us -> 59.8 us
  waiting for transfers between devices: 6.18 us -> 11.7 us
    all_to_all x4, blocking collectives: 57.5 us -> 47.3 us  [exchange(): return lax.all_to_all(parts, axes, 0, 0)]
    all_to_all x3, starting transfers between devices: 20 us -> 27.8 us  [exchange(): return lax.all_to_all(parts, axes, 0, 0)]
    all_to_all x3, waiting for transfers between devices: 3.05 us -> 5.97 us  [exchange(): return lax.all_to_all(parts, axes, 0, 0)]
    ppermute x3, waiting for transfers between devices: 0.01 us -> 2.6 us  [rotate(): lax.ppermute(parts[s], axis, [(i, (i + s) % 4) for i in range(4)])]
    ppermute x3, starting transfers between devices: 10.7 us -> 9.03 us  [rotate(): lax.ppermute(parts[s], axis, [(i, (i + s) % 4) for i in range(4)])]
  transfers between devices with their start and end apart: 9 -> 9, of which waited for: 3 -> 6; matrix products, arithmetic and copies ran while one was open for 1% -> 1% of each run, Pallas kernels for 0% -> 0%
where the time goes in v11:
time: 129 us; the launch traced here: 128 us
  starting transfers between devices  59.8 us (46%)
  blocking collectives  47.3 us (37%)
  waiting for transfers between devices  11.7 us (9%)
  Pallas kernels  3.64 us (3%)
  local copies, waits for them, and re-layouts  3.6 us (3%)
    all_to_all x4, blocking collectives, exchange(): return lax.all_to_all(parts, axes, 0, 0)  47.3 us
    all_to_all x3, starting transfers between devices, exchange(): return lax.all_to_all(parts, axes, 0, 0)  27.8 us
    ppermute x1, starting transfers between devices, per_device(): swapped = lax.ppermute(jnp.concatenate([total, leave]), 'core', SWAP)  10.6 us
    ppermute x1, starting transfers between devices, per_device(): strip = gather(lax.ppermute(rows, AXES, TURN), 'x', 4)  10.4 us
    ppermute x3, starting transfers between devices, rotate(): lax.ppermute(parts[s], axis, [(i, (i + s) % 4) for i in range(4)])  9.03 us
    all_to_all x3, waiting for transfers between devices, exchange(): return lax.all_to_all(parts, axes, 0, 0)  5.97 us
    pallas_call x4, Pallas kernels, call(): pl.pallas_call(kernel, out_shape=outs, in_specs=[SMEM] * scalars + [VMEM]...  3.64 us
    ppermute x3, waiting for transfers between devices, rotate(): lax.ppermute(parts[s], axis, [(i, (i + s) % 4) for i in range(4)])  2.6 us
  transfers between devices with their start and end apart: 9, of which 6 were waited for; matrix products, arithmetic and copies ran while one was open for 1% of the time, Pallas kernels for 0%

profile of v11, /device:TPU:1, one launch (start us, length us, event | category | flops | bytes accessed | tf_op | source)
XLA Modules:
  0.0 127.9 jit_solution(11728923709913224890)
XLA Ops:
  0.6 0.7 pad_maximum_fusion.1
  1.4 0.7 broadcast_in_dim.10
  2.0 10.2 %all-to-all-start = ((bf16[8,32,256]{2,1,0:T(8,128)(2,1)}), bf16[8,32,256]{2,1,0:T(8,128)(2,1)S(1)}, u32[]{:S(2)}, u32[]{:S(2)}) async-start(bf16[8,32,256]{2,1,0:T(8,128)(2,1)} %bitcast.2), calls=%async_computation | async-start | bytes 262144 | tf_op jit(solution)/shard_map/all_to_all | solution.py:17
  12.2 2.0 %collective-permute-start = (bf16[1024,512]{1,0:T(8,128)(2,1)}, bf16[1024,512]{1,0:T(8,128)(2,1)S(1)}, u32[]{:S(2)}, u32[]{:S(2)}) collective-permute-start(bf16[1024,512]{1,0:T(8,128)(2,1)} %pool.1), channel_id=1, source_target_pairs={{0,1},{1,0},{2,3},{3,2},{4,5},{5,4},{6,7},{7,6},{8,9},{9,8},{10,11... | collective-permute-start | bytes 3145736 | tf_op jit(solution)/shard_map/ppermute | solution.py:139
  14.2 0.0 copy-start.5
  14.2 0.0 copy-start.6
  14.2 0.6 copy-done.5
  14.9 0.0 copy-done.6
  14.9 0.1 fusion
  15.0 3.0 %all-to-all-done = bf16[8,32,256]{2,1,0:T(8,128)(2,1)S(1)} async-done(((bf16[8,32,256]{2,1,0:T(8,128)(2,1)}), bf16[8,32,256]{2,1,0:T(8,128)(2,1)S(1)}, u32[]{:S(2)}, u32[]{:S(2)}) %all-to-all-start) | async-done | bytes 131104 | tf_op jit(solution)/shard_map/all_to_all | solution.py:17
  18.0 0.1 bitcast_multiply_fusion
  18.1 0.8 broadcast_in_dim.12
  19.0 3.5 %all-to-all-start.2 = ((bf16[4,4,64,256]{3,2,1,0:T(8,128)(2,1)}), bf16[4,4,64,256]{3,2,1,0:T(8,128)(2,1)S(1)}, u32[]{:S(2)}, u32[]{:S(2)}) async-start(bf16[4,4,64,256]{3,2,1,0:T(8,128)(2,1)} %broadcast_in_dim.12), calls=%async_computation.2 | async-start | bytes 1048576 | tf_op jit(solution)/shard_map/all_to_all | solution.py:17
  22.4 0.0 copy-start
  22.5 10.4 %collective-permute-start.1 = (bf16[4,64,256]{2,1,0:T(8,128)(2,1)S(1)}, bf16[4,64,256]{2,1,0:T(8,128)(2,1)S(1)}, u32[]{:S(2)}, u32[]{:S(2)}) collective-permute-start(bf16[4,64,256]{2,1,0:T(8,128)(2,1)S(1)} %bitcast_multiply_fusion), channel_id=1, source_target_pairs={{12,0},{13,1},{38,2},{39,3},{88,4},{89,5},{114,6},{115,7},{138,8},... | collective-permute-start | bytes 393224 | tf_op jit(solution)/shard_map/ppermute | solution.py:147
  32.8 1.9 %collective-permute-done.1 = bf16[4,64,256]{2,1,0:T(8,128)(2,1)S(1)} collective-permute-done((bf16[4,64,256]{2,1,0:T(8,128)(2,1)S(1)}, bf16[4,64,256]{2,1,0:T(8,128)(2,1)S(1)}, u32[]{:S(2)}, u32[]{:S(2)}) %collective-permute-start.1) | collective-permute-done | bytes 131104 | tf_op jit(solution)/shard_map/ppermute | solution.py:147
  34.7 0.0 all-to-all-done.2
  34.8 12.0 %all_to_all.35.strip = bf16[4,4,64,256]{3,2,1,0:T(8,128)(2,1)S(1)} all-to-all(bf16[4,4,64,256]{3,2,1,0:T(8,128)(2,1)S(1)} %broadcast_in_dim.11), channel_id=1, replica_groups=mesh['x'=4,'zh'=4,'zl'=4,'y'=4,'core'=2] {'x'}, dimensions={0} | all-to-all | bytes 1048576 | tf_op jit(solution)/shard_map/all_to_all | solution.py:17
  46.8 0.0 collective-permute-done.sibling
  46.8 0.0 copy-done
  46.8 2.2 %shard_map.102 = (f32[512,128]{1,0:T(8,128)S(1)}, f32[256,256]{1,0:T(8,128)S(1)}, f32[256,256]{1,0:T(8,128)S(1)}, f32[256,256]{1,0:T(8,128)S(1)}, f32[256,256]{1,0:T(8,128)S(1)}) custom-call(bf16[1024,512]{1,0:T(8,128)(2,1)S(1)} %copy-done, bf16[1024,512]{1,0:T(8,128)(2,1)S(1)} %collective-permute-done.sibling, ...), custom_call_target="tpu_custom_call" | custom-call | tf_op jit(solution)/shard_map/pallas_call | solution.py:120
  49.0 0.0 copy-start.3
  49.0 0.7 copy-done.3
  49.7 13.4 %all_to_all.36 = f32[16,32,128]{2,1,0:T(8,128)S(1)} all-to-all(f32[16,32,128]{2,1,0:T(8,128)S(1)} %bitcast.14), channel_id=1, replica_groups=mesh['x'=4,'zh'=4,'zl'=4,'y'=4,'core'=2] {'x','y'}, dimensions={0} | all-to-all | bytes 524288 | tf_op jit(solution)/shard_map/all_to_all | solution.py:17
  63.1 0.0 copy-start.4
  63.1 0.7 broadcast_in_dim.14
  63.7 14.2 %all-to-all-start.4 = ((f32[16,16,128]{2,1,0:T(8,128)}), f32[16,16,128]{2,1,0:T(8,128)S(1)}, u32[]{:S(2)}, u32[]{:S(2)}) async-start(f32[16,16,128]{2,1,0:T(8,128)} %bitcast.7), calls=%async_computation.4 | async-start | bytes 262144 | tf_op jit(solution)/shard_map/all_to_all | solution.py:17
  77.9 0.0 copy-done.4
  78.0 2.0 %collective-permute-start.2 = (f32[256,256]{1,0:T(8,128)S(1)}, f32[256,256]{1,0:T(8,128)S(1)}, u32[]{:S(2)}, u32[]{:S(2)}) collective-permute-start(f32[256,256]{1,0:T(8,128)S(1)} %copy-done.4), channel_id=1, source_target_pairs={{0,2},{2,4},{4,6},{6,0},{1,3},{3,5},{5,7},{7,1},{8,10},{10,12},{12... | collective-permute-start | bytes 786440 | tf_op jit(solution)/shard_map/ppermute | solution.py:26
  80.0 3.6 %collective-permute-start.3 = (f32[256,256]{1,0:T(8,128)S(1)}, f32[256,256]{1,0:T(8,128)S(1)}, u32[]{:S(2)}, u32[]{:S(2)}) collective-permute-start(f32[256,256]{1,0:T(8,128)S(1)} %get-tuple-element.14), channel_id=1, source_target_pairs={{0,4},{2,6},{4,0},{6,2},{1,5},{3,7},{5,1},{7,3},{8,12},{10,14},{12... | collective-permute-start | bytes 786440 | tf_op jit(solution)/shard_map/ppermute | solution.py:26
  83.6 3.4 %collective-permute-start.4 = (f32[256,256]{1,0:T(8,128)S(1)}, f32[256,256]{1,0:T(8,128)S(1)}, u32[]{:S(2)}, u32[]{:S(2)}) collective-permute-start(f32[256,256]{1,0:T(8,128)S(1)} %get-tuple-element.15), channel_id=1, source_target_pairs={{0,6},{2,0},{4,2},{6,4},{1,7},{3,1},{5,3},{7,5},{8,14},{10,8},{12,... | collective-permute-start | bytes 786440 | tf_op jit(solution)/shard_map/ppermute | solution.py:26
  87.0 2.9 %all-to-all-done.4 = f32[16,16,128]{2,1,0:T(8,128)S(1)} async-done(((f32[16,16,128]{2,1,0:T(8,128)}), f32[16,16,128]{2,1,0:T(8,128)S(1)}, u32[]{:S(2)}, u32[]{:S(2)}) %all-to-all-start.4) | async-done | bytes 131104 | tf_op jit(solution)/shard_map/all_to_all | solution.py:17
  89.9 0.0 collective-permute-done.2.in1
  89.9 0.2 collective-permute-done.3.in2
  90.2 2.4 %collective-permute-done.4.in3 = f32[256,256]{1,0:T(8,128)S(1)} collective-permute-done((f32[256,256]{1,0:T(8,128)S(1)}, f32[256,256]{1,0:T(8,128)S(1)}, u32[]{:S(2)}, u32[]{:S(2)}) %collective-permute-start.4) | collective-permute-done | bytes 262176 | tf_op jit(solution)/shard_map/ppermute | solution.py:26
  92.5 0.1 shard_map.103
  92.6 10.5 %all_to_all.37.parts = f32[4,136,128]{2,1,0:T(8,128)S(1)} all-to-all(f32[4,136,128]{2,1,0:T(8,128)S(1)} %shard_map.103), channel_id=1, replica_groups=mesh['x'=4,'zh'=4,'zl'=4,'y'=4,'core'=2] {'zl'}, dimensions={0} | all-to-all | bytes 557056 | tf_op jit(solution)/shard_map/all_to_all | solution.py:17
  103.1 0.6 shard_map.104
  103.7 11.5 %all_to_all.38 = f32[16,32,128]{2,1,0:T(8,128)S(1)} all-to-all(f32[16,32,128]{2,1,0:T(8,128)S(1)} %get-tuple-element.17), channel_id=1, replica_groups=mesh['x'=4,'zh'=4,'zl'=4,'y'=4,'core'=2] {'x','y'}, dimensions={0} | all-to-all | bytes 524288 | tf_op jit(solution)/shard_map/all_to_all | solution.py:17
  115.2 0.0 copy-start.1
  115.2 0.0 copy-start.2
  115.2 10.6 %collective-permute-start.5 = (f32[576,128]{1,0:T(8,128)S(1)}, f32[576,128]{1,0:T(8,128)S(1)}, u32[]{:S(2)}, u32[]{:S(2)}) collective-permute-start(f32[576,128]{1,0:T(8,128)S(1)} %pad_maximum_fusion), channel_id=1, source_target_pairs={{0,1},{1,0},{2,3},{3,2},{4,5},{5,4},{6,7},{7,6},{8,9},{9,8},{10,11... | collective-permute-start | bytes 884744 | tf_op jit(solution)/shard_map/ppermute | solution.py:171
  125.8 1.2 collective-permute-done.5.swapped
  127.0 0.0 copy-done.1
  127.0 0.0 copy-done.2
  127.0 0.9 shard_map.105
  (5 shorter events, 0.1 us)
Async XLA Ops:
  2.0 16.0 %all-to-all-start = ((bf16[8,32,256]{2,1,0:T(8,128)(2,1)}), bf16[8,32,256]{2,1,0:T(8,128)(2,1)S(1)}, u32[]{:S(2)}, u32[]{:S(2)}) async-start(bf16[8,32,256]{2,1,0:T(8,128)(2,1)} %bitcast.2), calls=%async_computation | async-start | bytes 262144 | tf_op jit(solution)/shard_map/all_to_all | solution.py:17
  12.2 34.6 %collective-permute-start = (bf16[1024,512]{1,0:T(8,128)(2,1)}, bf16[1024,512]{1,0:T(8,128)(2,1)S(1)}, u32[]{:S(2)}, u32[]{:S(2)}) collective-permute-start(bf16[1024,512]{1,0:T(8,128)(2,1)} %pool.1), channel_id=1, source_target_pairs={{0,1},{1,0},{2,3},{3,2},{4,5},{5,4},{6,7},{7,6},{8,9},{9,8},{10,11... | collective-permute-start | bytes 3145736 | tf_op jit(solution)/shard_map/ppermute | solution.py:139
  14.2 0.7 copy-start.5
  14.2 0.7 copy-start.6
  19.0 15.8 %all-to-all-start.2 = ((bf16[4,4,64,256]{3,2,1,0:T(8,128)(2,1)}), bf16[4,4,64,256]{3,2,1,0:T(8,128)(2,1)S(1)}, u32[]{:S(2)}, u32[]{:S(2)}) async-start(bf16[4,4,64,256]{3,2,1,0:T(8,128)(2,1)} %broadcast_in_dim.12), calls=%async_computation.2 | async-start | bytes 1048576 | tf_op jit(solution)/shard_map/all_to_all | solution.py:17
  22.4 24.3 %copy-start = (bf16[1024,512]{1,0:T(8,128)(2,1)S(1)}, bf16[1024,512]{1,0:T(8,128)(2,1)}, u32[]{:S(2)}) copy-start(bf16[1024,512]{1,0:T(8,128)(2,1)} %pool.1) | copy-start | bytes 3145732
  22.5 12.3 %collective-permute-start.1 = (bf16[4,64,256]{2,1,0:T(8,128)(2,1)S(1)}, bf16[4,64,256]{2,1,0:T(8,128)(2,1)S(1)}, u32[]{:S(2)}, u32[]{:S(2)}) collective-permute-start(bf16[4,64,256]{2,1,0:T(8,128)(2,1)S(1)} %bitcast_multiply_fusion), channel_id=1, source_target_pairs={{12,0},{13,1},{38,2},{39,3},{88,4},{89,5},{114,6},{115,7},{138,8},... | collective-permute-start | bytes 393224 | tf_op jit(solution)/shard_map/ppermute | solution.py:147
  49.0 0.7 copy-start.3
  63.1 14.9 %copy-start.4 = (f32[256,256]{1,0:T(8,128)S(1)}, f32[256,256]{1,0:T(8,128)}, u32[]{:S(2)}) copy-start(f32[256,256]{1,0:T(8,128)} %copy-done.3) | copy-start | bytes 786436
  63.7 26.2 %all-to-all-start.4 = ((f32[16,16,128]{2,1,0:T(8,128)}), f32[16,16,128]{2,1,0:T(8,128)S(1)}, u32[]{:S(2)}, u32[]{:S(2)}) async-start(f32[16,16,128]{2,1,0:T(8,128)} %bitcast.7), calls=%async_computation.4 | async-start | bytes 262144 | tf_op jit(solution)/shard_map/all_to_all | solution.py:17
  78.0 12.0 %collective-permute-start.2 = (f32[256,256]{1,0:T(8,128)S(1)}, f32[256,256]{1,0:T(8,128)S(1)}, u32[]{:S(2)}, u32[]{:S(2)}) collective-permute-start(f32[256,256]{1,0:T(8,128)S(1)} %copy-done.4), channel_id=1, source_target_pairs={{0,2},{2,4},{4,6},{6,0},{1,3},{3,5},{5,7},{7,1},{8,10},{10,12},{12... | collective-permute-start | bytes 786440 | tf_op jit(solution)/shard_map/ppermute | solution.py:26
  80.0 10.2 %collective-permute-start.3 = (f32[256,256]{1,0:T(8,128)S(1)}, f32[256,256]{1,0:T(8,128)S(1)}, u32[]{:S(2)}, u32[]{:S(2)}) collective-permute-start(f32[256,256]{1,0:T(8,128)S(1)} %get-tuple-element.14), channel_id=1, source_target_pairs={{0,4},{2,6},{4,0},{6,2},{1,5},{3,7},{5,1},{7,3},{8,12},{10,14},{12... | collective-permute-start | bytes 786440 | tf_op jit(solution)/shard_map/ppermute | solution.py:26
  83.6 8.9 %collective-permute-start.4 = (f32[256,256]{1,0:T(8,128)S(1)}, f32[256,256]{1,0:T(8,128)S(1)}, u32[]{:S(2)}, u32[]{:S(2)}) collective-permute-start(f32[256,256]{1,0:T(8,128)S(1)} %get-tuple-element.15), channel_id=1, source_target_pairs={{0,6},{2,0},{4,2},{6,4},{1,7},{3,1},{5,3},{7,5},{8,14},{10,8},{12,... | collective-permute-start | bytes 786440 | tf_op jit(solution)/shard_map/ppermute | solution.py:26
  115.2 11.8 %copy-start.1 = (f32[256,256]{1,0:T(8,128)S(1)}, f32[256,256]{1,0:T(8,128)}, u32[]{:S(2)}) copy-start(f32[256,256]{1,0:T(8,128)} %inv_one.1) | copy-start | bytes 786436
  115.2 11.8 %copy-start.2 = (f32[256,256]{1,0:T(8,128)S(1)}, f32[256,256]{1,0:T(8,128)}, u32[]{:S(2)}) copy-start(f32[256,256]{1,0:T(8,128)} %inv_two.1) | copy-start | bytes 786436
  115.2 11.8 %collective-permute-start.5 = (f32[576,128]{1,0:T(8,128)S(1)}, f32[576,128]{1,0:T(8,128)S(1)}, u32[]{:S(2)}, u32[]{:S(2)}) collective-permute-start(f32[576,128]{1,0:T(8,128)S(1)} %pad_maximum_fusion), channel_id=1, source_target_pairs={{0,1},{1,0},{2,3},{3,2},{4,5},{5,4},{6,7},{7,6},{8,9},{9,8},{10,11... | collective-permute-start | bytes 884744 | tf_op jit(solution)/shard_map/ppermute | solution.py:171

commit v12 on v9

--- a/solution.py
+++ b/solution.py
@@ -46,7 +46,7 @@
 ]
 
 
-def multiply_kernel(pool, sibling, strip, rows, diag, out0, out1, out2, out3, rhs, full):
+def multiply_kernel(pool, sibling, strip, rows0, rows1, rows2, rows3, diag, out0, out1, out2, out3, rhs, full):
     core, y = lax.axis_index("core"), lax.axis_index("y")
     shift = lax.axis_index("zl") - y + 2
     depth = rhs.shape[0] // 2
@@ -63,8 +63,8 @@
         for j in range(4):
             full[j, z * 64 : (z + 1) * 64] = block[j * 64 : (j + 1) * 64]
     term = jnp.zeros((256, 256), jnp.float32)
-    for j in range(4):
-        left, rest = rows[j], full[j]
+    for hop, rows in enumerate((rows0, rows1, rows2, rows3)):
+        left, rest = rows[...], full[(y - hop) & 3]
         for _ in range(3):
             piece = rest.astype(jnp.bfloat16)
             rest = rest - piece.astype(jnp.float32)
@@ -143,14 +143,16 @@
     rows = exchange(both, ("zl", "core")).reshape(4, 2 * row_count, width)
     rows = rows * mask.astype(jnp.bfloat16)[:, None, None]
     rows = lax.optimization_barrier(rows)
-    strip = gather(lax.ppermute(rows, AXES, TURN), "x", 4)
-    around = gather(rows, "y", 4).reshape(4, 256, width)
+    turned, rows = lax.optimization_barrier((lax.ppermute(rows, AXES, TURN), rows))
+    strip = gather(turned, "x", 4)
+    flat = rows.reshape(256, width)
+    around = rotate([flat] * 4, "y")
 
     quarter = jax.ShapeDtypeStruct((256, width), f32)
     diag, *parts = call(
         multiply_kernel,
         [jax.ShapeDtypeStruct((384, 128), f32)] + [quarter] * 4,
-        (inverse_pool, sibling_pool, strip, around),
+        (inverse_pool, sibling_pool, strip, *around),
         [pltpu.VMEM((1024, width), jnp.bfloat16), pltpu.VMEM((4, 256, width), f32)],
     )
     shard = jnp.sum(exchange(diag.reshape(16, 24, 128), ("x", "y")), axis=0)

time: 119 us -> 125 us (1.050)
  blocking collectives: 25 us -> 12.7 us
  starting transfers between devices: 71.1 us -> 82.5 us
  waiting for transfers between devices: 11.7 us -> 17.7 us
    all_to_all x2 -> x1, blocking collectives: 25 us -> 12.7 us  [exchange(): return lax.all_to_all(parts, axes, 0, 0)]
    ppermute x6 -> x9, starting transfers between devices: 18.9 us -> 30.1 us  [rotate(): lax.ppermute(parts[s], axis, [(i, (i + s) % 4) for i in range(4)])]
    ppermute x6 -> x9, waiting for transfers between devices: 2.4 us -> 8.04 us  [rotate(): lax.ppermute(parts[s], axis, [(i, (i + s) % 4) for i in range(4)])]
  transfers between devices with their start and end apart: 13 -> 16, of which waited for: 6 -> 8; matrix products, arithmetic and copies ran while one was open for 2% -> 1% of each run, Pallas kernels for 1% -> 1%
where the time goes in v12:
time: 125 us; the launch traced here: 124 us
  starting transfers between devices  82.5 us (66%)
  waiting for transfers between devices  17.7 us (14%)
  blocking collectives  12.7 us (10%)
  local copies, waits for them, and re-layouts  5.04 us (4%)
  Pallas kernels  3.76 us (3%)
    all_to_all x4, starting transfers between devices, exchange(): return lax.all_to_all(parts, axes, 0, 0)  32.2 us
    ppermute x9, starting transfers between devices, rotate(): lax.ppermute(parts[s], axis, [(i, (i + s) % 4) for i in range(4)])  30.1 us
    all_to_all x1, blocking collectives, exchange(): return lax.all_to_all(parts, axes, 0, 0)  12.7 us
    ppermute x1, starting transfers between devices, per_device(): lax.ppermute(rows, AXES, TURN)  9.54 us
    ppermute x1, starting transfers between devices, per_device(): swapped = lax.ppermute(jnp.concatenate([total, leave]), 'core', SWAP)  8.52 us
    ppermute x9, waiting for transfers between devices, rotate(): lax.ppermute(parts[s], axis, [(i, (i + s) % 4) for i in range(4)])  8.04 us
    all_to_all x4, waiting for transfers between devices, exchange(): return lax.all_to_all(parts, axes, 0, 0)  6.63 us
    pallas_call x4, Pallas kernels, call(): pl.pallas_call(kernel, out_shape=outs, in_specs=[SMEM] * scalars + [VMEM]...  3.76 us
  transfers between devices with their start and end apart: 16, of which 8 were waited for; matrix products, arithmetic and copies ran while one was open for 1% of the time, Pallas kernels for 1%

profile of v12, /device:TPU:1, one launch (start us, length us, event | category | flops | bytes accessed | tf_op | source)
XLA Modules:
  0.0 123.6 jit_solution(6883485726426016787)
XLA Ops:
  0.6 0.7 pad_maximum_fusion.1
  1.4 0.7 broadcast_in_dim.8
  2.0 0.0 copy-start.9
  2.0 0.0 copy-start.10
  2.0 10.3 %all-to-all-start = ((bf16[8,32,256]{2,1,0:T(8,128)(2,1)}), bf16[8,32,256]{2,1,0:T(8,128)(2,1)S(1)}, u32[]{:S(2)}, u32[]{:S(2)}) async-start(bf16[8,32,256]{2,1,0:T(8,128)(2,1)} %bitcast.2), calls=%async_computation | async-start | bytes 262144 | tf_op jit(solution)/shard_map/all_to_all | solution.py:17
  12.3 2.2 %collective-permute-start = (bf16[1024,512]{1,0:T(8,128)(2,1)}, bf16[1024,512]{1,0:T(8,128)(2,1)S(1)}, u32[]{:S(2)}, u32[]{:S(2)}) collective-permute-start(bf16[1024,512]{1,0:T(8,128)(2,1)} %pool.1), channel_id=1, source_target_pairs={{0,1},{1,0},{2,3},{3,2},{4,5},{5,4},{6,7},{7,6},{8,9},{9,8},{10,11... | collective-permute-start | bytes 3145736 | tf_op jit(solution)/shard_map/ppermute | solution.py:138
  14.5 0.0 copy-done.9
  14.5 0.0 copy-done.10
  14.5 0.1 fusion
  14.6 3.5 %all-to-all-done = bf16[8,32,256]{2,1,0:T(8,128)(2,1)S(1)} async-done(((bf16[8,32,256]{2,1,0:T(8,128)(2,1)}), bf16[8,32,256]{2,1,0:T(8,128)(2,1)S(1)}, u32[]{:S(2)}, u32[]{:S(2)}) %all-to-all-start) | async-done | bytes 131104 | tf_op jit(solution)/shard_map/all_to_all | solution.py:17
  18.2 0.1 bitcast_multiply_fusion
  18.2 9.5 %collective-permute-start.1 = (bf16[4,64,256]{2,1,0:T(8,128)(2,1)S(1)}, bf16[4,64,256]{2,1,0:T(8,128)(2,1)S(1)}, u32[]{:S(2)}, u32[]{:S(2)}) collective-permute-start(bf16[4,64,256]{2,1,0:T(8,128)(2,1)S(1)} %bitcast_multiply_fusion), channel_id=1, source_target_pairs={{12,0},{13,1},{38,2},{39,3},{88,4},{89,5},{114,6},{115,7},{138,8},... | collective-permute-start | bytes 393224 | tf_op jit(solution)/shard_map/ppermute | solution.py:146
  27.8 1.9 %collective-permute-done.1 = bf16[4,64,256]{2,1,0:T(8,128)(2,1)S(1)} collective-permute-done((bf16[4,64,256]{2,1,0:T(8,128)(2,1)S(1)}, bf16[4,64,256]{2,1,0:T(8,128)(2,1)S(1)}, u32[]{:S(2)}, u32[]{:S(2)}) %collective-permute-start.1) | collective-permute-done | bytes 131104 | tf_op jit(solution)/shard_map/ppermute | solution.py:146
  29.7 0.9 broadcast_in_dim.9
  30.6 4.7 %all-to-all-start.1 = ((bf16[4,4,64,256]{3,2,1,0:T(8,128)(2,1)}), bf16[4,4,64,256]{3,2,1,0:T(8,128)(2,1)S(1)}, u32[]{:S(2)}, u32[]{:S(2)}) async-start(bf16[4,4,64,256]{3,2,1,0:T(8,128)(2,1)} %broadcast_in_dim.9), calls=%async_computation.1 | async-start | bytes 1048576 | tf_op jit(solution)/shard_map/all_to_all | solution.py:17
  35.3 6.7 %collective-permute-start.4 = (bf16[256,256]{1,0:T(8,128)(2,1)S(1)}, bf16[256,256]{1,0:T(8,128)(2,1)S(1)}, u32[]{:S(2)}, u32[]{:S(2)}) collective-permute-start(bf16[256,256]{1,0:T(8,128)(2,1)S(1)} %bitcast.11), channel_id=1, source_target_pairs={{0,6},{2,0},{4,2},{6,4},{1,7},{3,1},{5,3},{7,5},{8,14},{10,8},{12,... | collective-permute-start | bytes 393224 | tf_op jit(solution)/shard_map/ppermute | solution.py:26
  42.0 1.9 %collective-permute-start.3 = (bf16[256,256]{1,0:T(8,128)(2,1)S(1)}, bf16[256,256]{1,0:T(8,128)(2,1)S(1)}, u32[]{:S(2)}, u32[]{:S(2)}) collective-permute-start(bf16[256,256]{1,0:T(8,128)(2,1)S(1)} %bitcast.12), channel_id=1, source_target_pairs={{0,4},{2,6},{4,0},{6,2},{1,5},{3,7},{5,1},{7,3},{8,12},{10,14},{12... | collective-permute-start | bytes 393224 | tf_op jit(solution)/shard_map/ppermute | solution.py:26
  43.9 2.5 %collective-permute-start.2 = (bf16[256,256]{1,0:T(8,128)(2,1)S(1)}, bf16[256,256]{1,0:T(8,128)(2,1)S(1)}, u32[]{:S(2)}, u32[]{:S(2)}) collective-permute-start(bf16[256,256]{1,0:T(8,128)(2,1)S(1)} %bitcast.13), channel_id=1, source_target_pairs={{0,2},{2,4},{4,6},{6,0},{1,3},{3,5},{5,7},{7,1},{8,10},{10,12},{12... | collective-permute-start | bytes 393224 | tf_op jit(solution)/shard_map/ppermute | solution.py:26
  46.4 0.0 collective-permute-done.4.rows3
  46.4 2.8 %collective-permute-done.3.rows2 = bf16[256,256]{1,0:T(8,128)(2,1)S(1)} collective-permute-done((bf16[256,256]{1,0:T(8,128)(2,1)S(1)}, bf16[256,256]{1,0:T(8,128)(2,1)S(1)}, u32[]{:S(2)}, u32[]{:S(2)}) %collective-permute-start.3) | collective-permute-done | bytes 131104 | tf_op jit(solution)/shard_map/ppermute | solution.py:26
  49.2 2.6 %collective-permute-done.2.rows1 = bf16[256,256]{1,0:T(8,128)(2,1)S(1)} collective-permute-done((bf16[256,256]{1,0:T(8,128)(2,1)S(1)}, bf16[256,256]{1,0:T(8,128)(2,1)S(1)}, u32[]{:S(2)}, u32[]{:S(2)}) %collective-permute-start.2) | collective-permute-done | bytes 131104 | tf_op jit(solution)/shard_map/ppermute | solution.py:26
  51.8 0.0 all-to-all-done.1.strip
  51.8 0.0 collective-permute-done.sibling
  51.8 0.0 copy-done
  51.8 2.2 %shard_map.102 = (f32[384,128]{1,0:T(8,128)S(1)}, f32[256,256]{1,0:T(8,128)S(1)}, f32[256,256]{1,0:T(8,128)S(1)}, f32[256,256]{1,0:T(8,128)S(1)}, f32[256,256]{1,0:T(8,128)S(1)}) custom-call(bf16[1024,512]{1,0:T(8,128)(2,1)S(1)} %copy-done, bf16[1024,512]{1,0:T(8,128)(2,1)S(1)} %collective-permute-done.sibling, ...), custom_call_target="tpu_custom_call" | custom-call | tf_op jit(solution)/shard_map/pallas_call | solution.py:119
  54.0 0.0 copy-start.3
  54.0 0.7 copy-done.3
  54.7 0.0 copy-start.5
  54.7 0.7 copy-done.5
  55.4 0.0 copy-start.7
  55.4 0.7 copy-done.7
  56.1 12.7 %all_to_all.25 = f32[16,24,128]{2,1,0:T(8,128)S(1)} all-to-all(f32[16,24,128]{2,1,0:T(8,128)S(1)} %bitcast.15), channel_id=1, replica_groups=mesh['x'=4,'zh'=4,'zl'=4,'y'=4,'core'=2] {'x','y'}, dimensions={0} | all-to-all | bytes 393216 | tf_op jit(solution)/shard_map/all_to_all | solution.py:17
  68.8 0.0 copy-start.8
  68.8 0.0 copy-start.6
  68.8 0.0 copy-start.4
  68.9 0.7 broadcast_in_dim.10
  69.5 13.5 %all-to-all-start.3 = ((f32[16,24,128]{2,1,0:T(8,128)}), f32[16,24,128]{2,1,0:T(8,128)S(1)}, u32[]{:S(2)}, u32[]{:S(2)}) async-start(f32[16,24,128]{2,1,0:T(8,128)} %broadcast_in_dim.10), calls=%async_computation.3 | async-start | bytes 393216 | tf_op jit(solution)/shard_map/all_to_all | solution.py:17
  83.1 0.0 copy-done.8
  83.1 2.2 %collective-permute-start.5 = (f32[256,256]{1,0:T(8,128)S(1)}, f32[256,256]{1,0:T(8,128)S(1)}, u32[]{:S(2)}, u32[]{:S(2)}) collective-permute-start(f32[256,256]{1,0:T(8,128)S(1)} %copy-done.8), channel_id=1, source_target_pairs={{0,2},{2,4},{4,6},{6,0},{1,3},{3,5},{5,7},{7,1},{8,10},{10,12},{12... | collective-permute-start | bytes 786440 | tf_op jit(solution)/shard_map/ppermute | solution.py:26
  85.3 0.0 copy-done.6
  85.3 3.7 %collective-permute-start.6 = (f32[256,256]{1,0:T(8,128)S(1)}, f32[256,256]{1,0:T(8,128)S(1)}, u32[]{:S(2)}, u32[]{:S(2)}) collective-permute-start(f32[256,256]{1,0:T(8,128)S(1)} %copy-done.6), channel_id=1, source_target_pairs={{0,4},{2,6},{4,0},{6,2},{1,5},{3,7},{5,1},{7,3},{8,12},{10,14},{12... | collective-permute-start | bytes 786440 | tf_op jit(solution)/shard_map/ppermute | solution.py:26
  89.0 0.0 copy-done.4
  89.1 3.3 %collective-permute-start.7 = (f32[256,256]{1,0:T(8,128)S(1)}, f32[256,256]{1,0:T(8,128)S(1)}, u32[]{:S(2)}, u32[]{:S(2)}) collective-permute-start(f32[256,256]{1,0:T(8,128)S(1)} %copy-done.4), channel_id=1, source_target_pairs={{0,6},{2,0},{4,2},{6,4},{1,7},{3,1},{5,3},{7,5},{8,14},{10,8},{12,... | collective-permute-start | bytes 786440 | tf_op jit(solution)/shard_map/ppermute | solution.py:26
  92.4 3.1 %all-to-all-done.3 = f32[16,24,128]{2,1,0:T(8,128)S(1)} async-done(((f32[16,24,128]{2,1,0:T(8,128)}), f32[16,24,128]{2,1,0:T(8,128)S(1)}, u32[]{:S(2)}, u32[]{:S(2)}) %all-to-all-start.3) | async-done | bytes 196640 | tf_op jit(solution)/shard_map/all_to_all | solution.py:17
  95.5 0.7 broadcast_in_dim.11
  96.2 3.7 %all-to-all-start.4 = ((f32[16,24,128]{2,1,0:T(8,128)}), f32[16,24,128]{2,1,0:T(8,128)S(1)}, u32[]{:S(2)}, u32[]{:S(2)}) async-start(f32[16,24,128]{2,1,0:T(8,128)} %broadcast_in_dim.11), calls=%async_computation.4 | async-start | bytes 393216 | tf_op jit(solution)/shard_map/all_to_all | solution.py:17
  99.9 0.0 collective-permute-done.5.in1
  99.9 0.0 collective-permute-done.6.in2
  99.9 0.0 collective-permute-done.7.in3
  99.9 0.1 shard_map.103
  100.0 3.4 %collective-permute-start.8 = (f32[64,256]{1,0:T(8,128)S(1)}, f32[64,256]{1,0:T(8,128)S(1)}, u32[]{:S(2)}, u32[]{:S(2)}) collective-permute-start(f32[64,256]{1,0:T(8,128)S(1)} %get-tuple-element.25), channel_id=1, source_target_pairs={{0,8},{8,16},{16,24},{24,0},{1,9},{9,17},{17,25},{25,1},{2,10},{10... | collective-permute-start | bytes 196616 | tf_op jit(solution)/shard_map/ppermute | solution.py:26
  103.4 3.8 %collective-permute-start.9 = (f32[64,256]{1,0:T(8,128)S(1)}, f32[64,256]{1,0:T(8,128)S(1)}, u32[]{:S(2)}, u32[]{:S(2)}) collective-permute-start(f32[64,256]{1,0:T(8,128)S(1)} %get-tuple-element.26), channel_id=1, source_target_pairs={{0,16},{8,24},{16,0},{24,8},{1,17},{9,25},{17,1},{25,9},{2,18},{10... | collective-permute-start | bytes 196616 | tf_op jit(solution)/shard_map/ppermute | solution.py:26
  107.2 2.6 %collective-permute-start.10 = (f32[64,256]{1,0:T(8,128)S(1)}, f32[64,256]{1,0:T(8,128)S(1)}, u32[]{:S(2)}, u32[]{:S(2)}) collective-permute-start(f32[64,256]{1,0:T(8,128)S(1)} %get-tuple-element.27), channel_id=1, source_target_pairs={{0,24},{8,0},{16,8},{24,16},{1,25},{9,1},{17,9},{25,17},{2,26},{10... | collective-permute-start | bytes 196616 | tf_op jit(solution)/shard_map/ppermute | solution.py:26
  109.8 0.0 collective-permute-done.8.in1
  109.8 0.2 collective-permute-done.9.in2
  110.0 2.5 %collective-permute-done.10.in3 = f32[64,256]{1,0:T(8,128)S(1)} collective-permute-done((f32[64,256]{1,0:T(8,128)S(1)}, f32[64,256]{1,0:T(8,128)S(1)}, u32[]{:S(2)}, u32[]{:S(2)}) %collective-permute-start.10) | collective-permute-done | bytes 65568 | tf_op jit(solution)/shard_map/ppermute | solution.py:26
  112.5 0.6 shard_map.104
  113.0 0.0 copy-start.1
  113.0 0.0 all-to-all-done.4
  113.1 8.5 %collective-permute-start.11 = (f32[448,128]{1,0:T(8,128)S(1)}, f32[448,128]{1,0:T(8,128)S(1)}, u32[]{:S(2)}, u32[]{:S(2)}) collective-permute-start(f32[448,128]{1,0:T(8,128)S(1)} %pad_maximum_fusion), channel_id=1, source_target_pairs={{0,1},{1,0},{2,3},{3,2},{4,5},{5,4},{6,7},{7,6},{8,9},{9,8},{10,11... | collective-permute-start | bytes 688136 | tf_op jit(solution)/shard_map/ppermute | solution.py:171
  121.6 1.1 collective-permute-done.11.swapped
  122.7 0.0 copy-done.2
  122.7 0.0 copy-done.1
  122.7 0.9 shard_map.105
  (6 shorter events, 0.1 us)
Async XLA Ops:
  2.0 12.5 %copy-start.9 = (s32[64]{0:T(128)S(1)}, s32[64]{0:T(128)}, u32[]{:S(2)}) copy-start(s32[64]{0:T(128)} %param.12) | copy-start | bytes 772
  2.0 12.5 %copy-start.10 = (s32[64]{0:T(128)S(1)}, s32[64]{0:T(128)}, u32[]{:S(2)}) copy-start(s32[64]{0:T(128)} %param.13) | copy-start | bytes 772
  2.0 16.1 %all-to-all-start = ((bf16[8,32,256]{2,1,0:T(8,128)(2,1)}), bf16[8,32,256]{2,1,0:T(8,128)(2,1)S(1)}, u32[]{:S(2)}, u32[]{:S(2)}) async-start(bf16[8,32,256]{2,1,0:T(8,128)(2,1)} %bitcast.2), calls=%async_computation | async-start | bytes 262144 | tf_op jit(solution)/shard_map/all_to_all | solution.py:17
  12.3 39.5 %copy-start = (bf16[1024,512]{1,0:T(8,128)(2,1)S(1)}, bf16[1024,512]{1,0:T(8,128)(2,1)}, u32[]{:S(2)}) copy-start(bf16[1024,512]{1,0:T(8,128)(2,1)} %pool.1) | copy-start | bytes 3145732
  12.3 39.5 %collective-permute-start = (bf16[1024,512]{1,0:T(8,128)(2,1)}, bf16[1024,512]{1,0:T(8,128)(2,1)S(1)}, u32[]{:S(2)}, u32[]{:S(2)}) collective-permute-start(bf16[1024,512]{1,0:T(8,128)(2,1)} %pool.1), channel_id=1, source_target_pairs={{0,1},{1,0},{2,3},{3,2},{4,5},{5,4},{6,7},{7,6},{8,9},{9,8},{10,11... | collective-permute-start | bytes 3145736 | tf_op jit(solution)/shard_map/ppermute | solution.py:138
  18.2 11.5 %collective-permute-start.1 = (bf16[4,64,256]{2,1,0:T(8,128)(2,1)S(1)}, bf16[4,64,256]{2,1,0:T(8,128)(2,1)S(1)}, u32[]{:S(2)}, u32[]{:S(2)}) collective-permute-start(bf16[4,64,256]{2,1,0:T(8,128)(2,1)S(1)} %bitcast_multiply_fusion), channel_id=1, source_target_pairs={{12,0},{13,1},{38,2},{39,3},{88,4},{89,5},{114,6},{115,7},{138,8},... | collective-permute-start | bytes 393224 | tf_op jit(solution)/shard_map/ppermute | solution.py:146
  30.6 21.2 %all-to-all-start.1 = ((bf16[4,4,64,256]{3,2,1,0:T(8,128)(2,1)}), bf16[4,4,64,256]{3,2,1,0:T(8,128)(2,1)S(1)}, u32[]{:S(2)}, u32[]{:S(2)}) async-start(bf16[4,4,64,256]{3,2,1,0:T(8,128)(2,1)} %broadcast_in_dim.9), calls=%async_computation.1 | async-start | bytes 1048576 | tf_op jit(solution)/shard_map/all_to_all | solution.py:17
  35.3 11.1 %collective-permute-start.4 = (bf16[256,256]{1,0:T(8,128)(2,1)S(1)}, bf16[256,256]{1,0:T(8,128)(2,1)S(1)}, u32[]{:S(2)}, u32[]{:S(2)}) collective-permute-start(bf16[256,256]{1,0:T(8,128)(2,1)S(1)} %bitcast.11), channel_id=1, source_target_pairs={{0,6},{2,0},{4,2},{6,4},{1,7},{3,1},{5,3},{7,5},{8,14},{10,8},{12,... | collective-permute-start | bytes 393224 | tf_op jit(solution)/shard_map/ppermute | solution.py:26
  42.0 7.2 %collective-permute-start.3 = (bf16[256,256]{1,0:T(8,128)(2,1)S(1)}, bf16[256,256]{1,0:T(8,128)(2,1)S(1)}, u32[]{:S(2)}, u32[]{:S(2)}) collective-permute-start(bf16[256,256]{1,0:T(8,128)(2,1)S(1)} %bitcast.12), channel_id=1, source_target_pairs={{0,4},{2,6},{4,0},{6,2},{1,5},{3,7},{5,1},{7,3},{8,12},{10,14},{12... | collective-permute-start | bytes 393224 | tf_op jit(solution)/shard_map/ppermute | solution.py:26
  43.9 7.9 %collective-permute-start.2 = (bf16[256,256]{1,0:T(8,128)(2,1)S(1)}, bf16[256,256]{1,0:T(8,128)(2,1)S(1)}, u32[]{:S(2)}, u32[]{:S(2)}) collective-permute-start(bf16[256,256]{1,0:T(8,128)(2,1)S(1)} %bitcast.13), channel_id=1, source_target_pairs={{0,2},{2,4},{4,6},{6,0},{1,3},{3,5},{5,7},{7,1},{8,10},{10,12},{12... | collective-permute-start | bytes 393224 | tf_op jit(solution)/shard_map/ppermute | solution.py:26
  54.0 0.7 copy-start.3
  54.7 0.7 copy-start.5
  55.4 0.7 copy-start.7
  68.8 14.3 %copy-start.8 = (f32[256,256]{1,0:T(8,128)S(1)}, f32[256,256]{1,0:T(8,128)}, u32[]{:S(2)}) copy-start(f32[256,256]{1,0:T(8,128)} %copy-done.7) | copy-start | bytes 786436
  68.8 16.5 %copy-start.6 = (f32[256,256]{1,0:T(8,128)S(1)}, f32[256,256]{1,0:T(8,128)}, u32[]{:S(2)}) copy-start(f32[256,256]{1,0:T(8,128)} %copy-done.5) | copy-start | bytes 786436
  68.8 20.2 %copy-start.4 = (f32[256,256]{1,0:T(8,128)S(1)}, f32[256,256]{1,0:T(8,128)}, u32[]{:S(2)}) copy-start(f32[256,256]{1,0:T(8,128)} %copy-done.3) | copy-start | bytes 786436
  69.5 25.9 %all-to-all-start.3 = ((f32[16,24,128]{2,1,0:T(8,128)}), f32[16,24,128]{2,1,0:T(8,128)S(1)}, u32[]{:S(2)}, u32[]{:S(2)}) async-start(f32[16,24,128]{2,1,0:T(8,128)} %broadcast_in_dim.10), calls=%async_computation.3 | async-start | bytes 393216 | tf_op jit(solution)/shard_map/all_to_all | solution.py:17
  83.1 16.8 %collective-permute-start.5 = (f32[256,256]{1,0:T(8,128)S(1)}, f32[256,256]{1,0:T(8,128)S(1)}, u32[]{:S(2)}, u32[]{:S(2)}) collective-permute-start(f32[256,256]{1,0:T(8,128)S(1)} %copy-done.8), channel_id=1, source_target_pairs={{0,2},{2,4},{4,6},{6,0},{1,3},{3,5},{5,7},{7,1},{8,10},{10,12},{12... | collective-permute-start | bytes 786440 | tf_op jit(solution)/shard_map/ppermute | solution.py:26
  85.3 14.6 %collective-permute-start.6 = (f32[256,256]{1,0:T(8,128)S(1)}, f32[256,256]{1,0:T(8,128)S(1)}, u32[]{:S(2)}, u32[]{:S(2)}) collective-permute-start(f32[256,256]{1,0:T(8,128)S(1)} %copy-done.6), channel_id=1, source_target_pairs={{0,4},{2,6},{4,0},{6,2},{1,5},{3,7},{5,1},{7,3},{8,12},{10,14},{12... | collective-permute-start | bytes 786440 | tf_op jit(solution)/shard_map/ppermute | solution.py:26
  89.1 10.8 %collective-permute-start.7 = (f32[256,256]{1,0:T(8,128)S(1)}, f32[256,256]{1,0:T(8,128)S(1)}, u32[]{:S(2)}, u32[]{:S(2)}) collective-permute-start(f32[256,256]{1,0:T(8,128)S(1)} %copy-done.4), channel_id=1, source_target_pairs={{0,6},{2,0},{4,2},{6,4},{1,7},{3,1},{5,3},{7,5},{8,14},{10,8},{12,... | collective-permute-start | bytes 786440 | tf_op jit(solution)/shard_map/ppermute | solution.py:26
  96.2 16.9 %all-to-all-start.4 = ((f32[16,24,128]{2,1,0:T(8,128)}), f32[16,24,128]{2,1,0:T(8,128)S(1)}, u32[]{:S(2)}, u32[]{:S(2)}) async-start(f32[16,24,128]{2,1,0:T(8,128)} %broadcast_in_dim.11), calls=%async_computation.4 | async-start | bytes 393216 | tf_op jit(solution)/shard_map/all_to_all | solution.py:17
  100.0 9.8 %collective-permute-start.8 = (f32[64,256]{1,0:T(8,128)S(1)}, f32[64,256]{1,0:T(8,128)S(1)}, u32[]{:S(2)}, u32[]{:S(2)}) collective-permute-start(f32[64,256]{1,0:T(8,128)S(1)} %get-tuple-element.25), channel_id=1, source_target_pairs={{0,8},{8,16},{16,24},{24,0},{1,9},{9,17},{17,25},{25,1},{2,10},{10... | collective-permute-start | bytes 196616 | tf_op jit(solution)/shard_map/ppermute | solution.py:26
  103.4 6.6 %collective-permute-start.9 = (f32[64,256]{1,0:T(8,128)S(1)}, f32[64,256]{1,0:T(8,128)S(1)}, u32[]{:S(2)}, u32[]{:S(2)}) collective-permute-start(f32[64,256]{1,0:T(8,128)S(1)} %get-tuple-element.26), channel_id=1, source_target_pairs={{0,16},{8,24},{16,0},{24,8},{1,17},{9,25},{17,1},{25,9},{2,18},{10... | collective-permute-start | bytes 196616 | tf_op jit(solution)/shard_map/ppermute | solution.py:26
  107.2 5.3 %collective-permute-start.10 = (f32[64,256]{1,0:T(8,128)S(1)}, f32[64,256]{1,0:T(8,128)S(1)}, u32[]{:S(2)}, u32[]{:S(2)}) collective-permute-start(f32[64,256]{1,0:T(8,128)S(1)} %get-tuple-element.27), channel_id=1, source_target_pairs={{0,24},{8,0},{16,8},{24,16},{1,25},{9,1},{17,9},{25,17},{2,26},{10... | collective-permute-start | bytes 196616 | tf_op jit(solution)/shard_map/ppermute | solution.py:26
  112.5 10.2 %copy-start.2 = (f32[256,256]{1,0:T(8,128)S(1)}, f32[256,256]{1,0:T(8,128)}, u32[]{:S(2)}) copy-start(f32[256,256]{1,0:T(8,128)} %inv_two.1) | copy-start | bytes 786436
  113.0 9.7 %copy-start.1 = (f32[256,256]{1,0:T(8,128)S(1)}, f32[256,256]{1,0:T(8,128)}, u32[]{:S(2)}) copy-start(f32[256,256]{1,0:T(8,128)} %inv_one.1) | copy-start | bytes 786436
  113.1 9.6 %collective-permute-start.11 = (f32[448,128]{1,0:T(8,128)S(1)}, f32[448,128]{1,0:T(8,128)S(1)}, u32[]{:S(2)}, u32[]{:S(2)}) collective-permute-start(f32[448,128]{1,0:T(8,128)S(1)} %pad_maximum_fusion), channel_id=1, source_target_pairs={{0,1},{1,0},{2,3},{3,2},{4,5},{5,4},{6,7},{7,6},{8,9},{9,8},{10,11... | collective-permute-start | bytes 688136 | tf_op jit(solution)/shard_map/ppermute | solution.py:171

commit v13 on v9

--- a/solution.py
+++ b/solution.py
@@ -143,8 +143,10 @@
     rows = exchange(both, ("zl", "core")).reshape(4, 2 * row_count, width)
     rows = rows * mask.astype(jnp.bfloat16)[:, None, None]
     rows = lax.optimization_barrier(rows)
-    strip = gather(lax.ppermute(rows, AXES, TURN), "x", 4)
-    around = gather(rows, "y", 4).reshape(4, 256, width)
+    turned = lax.ppermute(rows, AXES, TURN)
+    around = lax.all_gather(rows.reshape(256, width), "y")
+    turned, around = lax.optimization_barrier((turned, around))
+    strip = gather(turned, "x", 4)
 
     quarter = jax.ShapeDtypeStruct((256, width), f32)
     diag, *parts = call(

time: 119 us -> 115 us (0.966)
  starting transfers between devices: 71.1 us -> 63.3 us
  blocking collectives: 25 us -> 31.6 us
  local copies, waits for them, and re-layouts: 4.33 us -> 2.77 us
  waiting for transfers between devices: 11.7 us -> 10.5 us
    all_gather x0 -> x1, blocking collectives: none -> 10.4 us  [per_device(): around = lax.all_gather(rows.reshape(256, width), 'y')]
    all_to_all x4 -> x3, starting transfers between devices: 31.2 us -> 24.7 us  [exchange(): return lax.all_to_all(parts, axes, 0, 0)]
    all_to_all x2, blocking collectives: 25 us -> 21.2 us  [exchange(): return lax.all_to_all(parts, axes, 0, 0)]
    ppermute x1, waiting for transfers between devices: 1.93 us -> 0.01 us  [per_device(): turned = lax.ppermute(rows, AXES, TURN)]
    all_to_all x4 -> x3, waiting for transfers between devices: 6.25 us -> 6.46 us  [exchange(): return lax.all_to_all(parts, axes, 0, 0)]
  transfers between devices with their start and end apart: 13 -> 12, of which waited for: 6 -> 5; matrix products, arithmetic and copies ran while one was open for 2% -> 1% of each run, Pallas kernels for 1% -> 1%
where the time goes in v13:
time: 115 us; the launch traced here: 114 us
  starting transfers between devices  63.3 us (55%)
  blocking collectives  31.6 us (27%)
  waiting for transfers between devices  10.5 us (9%)
  Pallas kernels  3.72 us (3%)
  local copies, waits for them, and re-layouts  2.77 us (2%)
    all_to_all x3, starting transfers between devices, exchange(): return lax.all_to_all(parts, axes, 0, 0)  24.7 us
    all_to_all x2, blocking collectives, exchange(): return lax.all_to_all(parts, axes, 0, 0)  21.2 us
    ppermute x6, starting transfers between devices, rotate(): lax.ppermute(parts[s], axis, [(i, (i + s) % 4) for i in range(4)])  18.6 us
    all_gather x1, blocking collectives, per_device(): around = lax.all_gather(rows.reshape(256, width), 'y')  10.4 us
    ppermute x1, starting transfers between devices, per_device(): turned = lax.ppermute(rows, AXES, TURN)  9.54 us
    ppermute x1, starting transfers between devices, per_device(): swapped = lax.ppermute(jnp.concatenate([total, leave]), 'core', SWAP)  8.43 us
    all_to_all x3, waiting for transfers between devices, exchange(): return lax.all_to_all(parts, axes, 0, 0)  6.46 us
    pallas_call x4, Pallas kernels, call(): pl.pallas_call(kernel, out_shape=outs, in_specs=[SMEM] * scalars + [VMEM]...  3.72 us
  transfers between devices with their start and end apart: 12, of which 5 were waited for; matrix products, arithmetic and copies ran while one was open for 1% of the time, Pallas kernels for 1%

profile of v13, /device:TPU:1, one launch (start us, length us, event | category | flops | bytes accessed | tf_op | source)
XLA Modules:
  0.0 113.7 jit_solution(1069622480305139042)
XLA Ops:
  0.6 0.7 pad_maximum_fusion.1
  1.4 0.7 broadcast_in_dim.8
  2.0 10.2 %all-to-all-start = ((bf16[8,32,256]{2,1,0:T(8,128)(2,1)}), bf16[8,32,256]{2,1,0:T(8,128)(2,1)S(1)}, u32[]{:S(2)}, u32[]{:S(2)}) async-start(bf16[8,32,256]{2,1,0:T(8,128)(2,1)} %bitcast.2), calls=%async_computation | async-start | bytes 262144 | tf_op jit(solution)/shard_map/all_to_all | solution.py:17
  12.2 2.0 %collective-permute-start = (bf16[1024,512]{1,0:T(8,128)(2,1)}, bf16[1024,512]{1,0:T(8,128)(2,1)S(1)}, u32[]{:S(2)}, u32[]{:S(2)}) collective-permute-start(bf16[1024,512]{1,0:T(8,128)(2,1)} %pool.1), channel_id=1, source_target_pairs={{0,1},{1,0},{2,3},{3,2},{4,5},{5,4},{6,7},{7,6},{8,9},{9,8},{10,11... | collective-permute-start | bytes 3145736 | tf_op jit(solution)/shard_map/ppermute | solution.py:138
  14.2 0.0 copy-start.3
  14.2 0.0 copy-start.4
  14.2 0.6 copy-done.3
  14.9 0.0 copy-done.4
  14.9 0.1 fusion
  15.0 3.0 %all-to-all-done = bf16[8,32,256]{2,1,0:T(8,128)(2,1)S(1)} async-done(((bf16[8,32,256]{2,1,0:T(8,128)(2,1)}), bf16[8,32,256]{2,1,0:T(8,128)(2,1)S(1)}, u32[]{:S(2)}, u32[]{:S(2)}) %all-to-all-start) | async-done | bytes 131104 | tf_op jit(solution)/shard_map/all_to_all | solution.py:17
  18.0 0.1 bitcast_multiply_fusion
  18.1 9.5 %collective-permute-start.1 = (bf16[4,64,256]{2,1,0:T(8,128)(2,1)S(1)}, bf16[4,64,256]{2,1,0:T(8,128)(2,1)S(1)}, u32[]{:S(2)}, u32[]{:S(2)}) collective-permute-start(bf16[4,64,256]{2,1,0:T(8,128)(2,1)S(1)} %bitcast_multiply_fusion), channel_id=1, source_target_pairs={{12,0},{13,1},{38,2},{39,3},{88,4},{89,5},{114,6},{115,7},{138,8},... | collective-permute-start | bytes 393224 | tf_op jit(solution)/shard_map/ppermute | solution.py:146
  27.7 0.0 copy-start
  27.7 10.4 %all_gather.3.rows = bf16[4,256,256]{2,1,0:T(8,128)(2,1)S(1)} all-gather(bf16[1,256,256]{2,1,0:T(8,128)(2,1)S(1)} %bitcast.12), channel_id=1, replica_groups=mesh['x'=4,'zh'=4,'zl'=4,'y'=4,'core'=2] {'y'}, dimensions={0}, use_global_device_ids=true | all-gather | bytes 655360 | tf_op jit(solution)/shard_map/all_gather | solution.py:147
  38.1 0.0 collective-permute-done.1
  38.2 11.0 %all_to_all.25.strip = bf16[4,4,64,256]{3,2,1,0:T(8,128)(2,1)S(1)} all-to-all(bf16[4,4,64,256]{3,2,1,0:T(8,128)(2,1)S(1)} %broadcast_in_dim.9), channel_id=1, replica_groups=mesh['x'=4,'zh'=4,'zl'=4,'y'=4,'core'=2] {'x'}, dimensions={0} | all-to-all | bytes 1048576 | tf_op jit(solution)/shard_map/all_to_all | solution.py:17
  49.2 0.0 collective-permute-done.sibling
  49.2 0.0 copy-done
  49.2 2.2 %shard_map.102 = (f32[384,128]{1,0:T(8,128)S(1)}, f32[256,256]{1,0:T(8,128)S(1)}, f32[256,256]{1,0:T(8,128)S(1)}, f32[256,256]{1,0:T(8,128)S(1)}, f32[256,256]{1,0:T(8,128)S(1)}) custom-call(bf16[1024,512]{1,0:T(8,128)(2,1)S(1)} %copy-done, bf16[1024,512]{1,0:T(8,128)(2,1)S(1)} %collective-permute-done.sibling, ...), custom_call_target="tpu_custom_call" | custom-call | tf_op jit(solution)/shard_map/pallas_call | solution.py:119
  51.4 10.1 %all_to_all.26 = f32[16,24,128]{2,1,0:T(8,128)S(1)} all-to-all(f32[16,24,128]{2,1,0:T(8,128)S(1)} %bitcast.11), channel_id=1, replica_groups=mesh['x'=4,'zh'=4,'zl'=4,'y'=4,'core'=2] {'x','y'}, dimensions={0} | all-to-all | bytes 393216 | tf_op jit(solution)/shard_map/all_to_all | solution.py:17
  61.5 0.7 broadcast_in_dim.10
  62.2 11.0 %all-to-all-start.3 = ((f32[16,24,128]{2,1,0:T(8,128)}), f32[16,24,128]{2,1,0:T(8,128)S(1)}, u32[]{:S(2)}, u32[]{:S(2)}) async-start(f32[16,24,128]{2,1,0:T(8,128)} %broadcast_in_dim.10), calls=%async_computation.3 | async-start | bytes 393216 | tf_op jit(solution)/shard_map/all_to_all | solution.py:17
  73.3 1.9 %collective-permute-start.2 = (f32[256,256]{1,0:T(8,128)S(1)}, f32[256,256]{1,0:T(8,128)S(1)}, u32[]{:S(2)}, u32[]{:S(2)}) collective-permute-start(f32[256,256]{1,0:T(8,128)S(1)} %get-tuple-element.21), channel_id=1, source_target_pairs={{0,2},{2,4},{4,6},{6,0},{1,3},{3,5},{5,7},{7,1},{8,10},{10,12},{12... | collective-permute-start | bytes 786440 | tf_op jit(solution)/shard_map/ppermute | solution.py:26
  75.2 3.9 %collective-permute-start.3 = (f32[256,256]{1,0:T(8,128)S(1)}, f32[256,256]{1,0:T(8,128)S(1)}, u32[]{:S(2)}, u32[]{:S(2)}) collective-permute-start(f32[256,256]{1,0:T(8,128)S(1)} %get-tuple-element.22), channel_id=1, source_target_pairs={{0,4},{2,6},{4,0},{6,2},{1,5},{3,7},{5,1},{7,3},{8,12},{10,14},{12... | collective-permute-start | bytes 786440 | tf_op jit(solution)/shard_map/ppermute | solution.py:26
  79.1 3.1 %collective-permute-start.4 = (f32[256,256]{1,0:T(8,128)S(1)}, f32[256,256]{1,0:T(8,128)S(1)}, u32[]{:S(2)}, u32[]{:S(2)}) collective-permute-start(f32[256,256]{1,0:T(8,128)S(1)} %get-tuple-element.23), channel_id=1, source_target_pairs={{0,6},{2,0},{4,2},{6,4},{1,7},{3,1},{5,3},{7,5},{8,14},{10,8},{12,... | collective-permute-start | bytes 786440 | tf_op jit(solution)/shard_map/ppermute | solution.py:26
  82.2 3.4 %all-to-all-done.3 = f32[16,24,128]{2,1,0:T(8,128)S(1)} async-done(((f32[16,24,128]{2,1,0:T(8,128)}), f32[16,24,128]{2,1,0:T(8,128)S(1)}, u32[]{:S(2)}, u32[]{:S(2)}) %all-to-all-start.3) | async-done | bytes 196640 | tf_op jit(solution)/shard_map/all_to_all | solution.py:17
  85.6 0.7 broadcast_in_dim.11
  86.3 3.5 %all-to-all-start.4 = ((f32[16,24,128]{2,1,0:T(8,128)}), f32[16,24,128]{2,1,0:T(8,128)S(1)}, u32[]{:S(2)}, u32[]{:S(2)}) async-start(f32[16,24,128]{2,1,0:T(8,128)} %broadcast_in_dim.11), calls=%async_computation.4 | async-start | bytes 393216 | tf_op jit(solution)/shard_map/all_to_all | solution.py:17
  89.8 0.0 collective-permute-done.2.in1
  89.9 0.0 collective-permute-done.3.in2
  89.9 0.0 collective-permute-done.4.in3
  89.9 0.1 shard_map.103
  90.0 3.4 %collective-permute-start.5 = (f32[64,256]{1,0:T(8,128)S(1)}, f32[64,256]{1,0:T(8,128)S(1)}, u32[]{:S(2)}, u32[]{:S(2)}) collective-permute-start(f32[64,256]{1,0:T(8,128)S(1)} %get-tuple-element.25), channel_id=1, source_target_pairs={{0,8},{8,16},{16,24},{24,0},{1,9},{9,17},{17,25},{25,1},{2,10},{10... | collective-permute-start | bytes 196616 | tf_op jit(solution)/shard_map/ppermute | solution.py:26
  93.4 4.0 %collective-permute-start.6 = (f32[64,256]{1,0:T(8,128)S(1)}, f32[64,256]{1,0:T(8,128)S(1)}, u32[]{:S(2)}, u32[]{:S(2)}) collective-permute-start(f32[64,256]{1,0:T(8,128)S(1)} %get-tuple-element.26), channel_id=1, source_target_pairs={{0,16},{8,24},{16,0},{24,8},{1,17},{9,25},{17,1},{25,9},{2,18},{10... | collective-permute-start | bytes 196616 | tf_op jit(solution)/shard_map/ppermute | solution.py:26
  97.4 2.4 %collective-permute-start.7 = (f32[64,256]{1,0:T(8,128)S(1)}, f32[64,256]{1,0:T(8,128)S(1)}, u32[]{:S(2)}, u32[]{:S(2)}) collective-permute-start(f32[64,256]{1,0:T(8,128)S(1)} %get-tuple-element.27), channel_id=1, source_target_pairs={{0,24},{8,0},{16,8},{24,16},{1,25},{9,1},{17,9},{25,17},{2,26},{10... | collective-permute-start | bytes 196616 | tf_op jit(solution)/shard_map/ppermute | solution.py:26
  99.7 0.0 collective-permute-done.5.in1
  99.7 0.2 collective-permute-done.6.in2
  100.0 2.7 %collective-permute-done.7.in3 = f32[64,256]{1,0:T(8,128)S(1)} collective-permute-done((f32[64,256]{1,0:T(8,128)S(1)}, f32[64,256]{1,0:T(8,128)S(1)}, u32[]{:S(2)}, u32[]{:S(2)}) %collective-permute-start.7) | collective-permute-done | bytes 65568 | tf_op jit(solution)/shard_map/ppermute | solution.py:26
  102.7 0.0 copy-start.2
  102.7 0.6 shard_map.104
  103.2 0.0 copy-start.1
  103.3 0.0 all-to-all-done.4
  103.3 8.4 %collective-permute-start.8 = (f32[448,128]{1,0:T(8,128)S(1)}, f32[448,128]{1,0:T(8,128)S(1)}, u32[]{:S(2)}, u32[]{:S(2)}) collective-permute-start(f32[448,128]{1,0:T(8,128)S(1)} %pad_maximum_fusion), channel_id=1, source_target_pairs={{0,1},{1,0},{2,3},{3,2},{4,5},{5,4},{6,7},{7,6},{8,9},{9,8},{10,11... | collective-permute-start | bytes 688136 | tf_op jit(solution)/shard_map/ppermute | solution.py:171
  111.7 1.1 collective-permute-done.8.swapped
  112.8 0.0 copy-done.2
  112.8 0.0 copy-done.1
  112.8 0.9 shard_map.105
  (5 shorter events, 0.1 us)
Async XLA Ops:
  2.0 16.0 %all-to-all-start = ((bf16[8,32,256]{2,1,0:T(8,128)(2,1)}), bf16[8,32,256]{2,1,0:T(8,128)(2,1)S(1)}, u32[]{:S(2)}, u32[]{:S(2)}) async-start(bf16[8,32,256]{2,1,0:T(8,128)(2,1)} %bitcast.2), calls=%async_computation | async-start | bytes 262144 | tf_op jit(solution)/shard_map/all_to_all | solution.py:17
  12.2 37.0 %collective-permute-start = (bf16[1024,512]{1,0:T(8,128)(2,1)}, bf16[1024,512]{1,0:T(8,128)(2,1)S(1)}, u32[]{:S(2)}, u32[]{:S(2)}) collective-permute-start(bf16[1024,512]{1,0:T(8,128)(2,1)} %pool.1), channel_id=1, source_target_pairs={{0,1},{1,0},{2,3},{3,2},{4,5},{5,4},{6,7},{7,6},{8,9},{9,8},{10,11... | collective-permute-start | bytes 3145736 | tf_op jit(solution)/shard_map/ppermute | solution.py:138
  14.2 0.7 copy-start.3
  14.2 0.7 copy-start.4
  18.1 20.0 %collective-permute-start.1 = (bf16[4,64,256]{2,1,0:T(8,128)(2,1)S(1)}, bf16[4,64,256]{2,1,0:T(8,128)(2,1)S(1)}, u32[]{:S(2)}, u32[]{:S(2)}) collective-permute-start(bf16[4,64,256]{2,1,0:T(8,128)(2,1)S(1)} %bitcast_multiply_fusion), channel_id=1, source_target_pairs={{12,0},{13,1},{38,2},{39,3},{88,4},{89,5},{114,6},{115,7},{138,8},... | collective-permute-start | bytes 393224 | tf_op jit(solution)/shard_map/ppermute | solution.py:146
  27.7 21.5 %copy-start = (bf16[1024,512]{1,0:T(8,128)(2,1)S(1)}, bf16[1024,512]{1,0:T(8,128)(2,1)}, u32[]{:S(2)}) copy-start(bf16[1024,512]{1,0:T(8,128)(2,1)} %pool.1) | copy-start | bytes 3145732
  62.2 23.4 %all-to-all-start.3 = ((f32[16,24,128]{2,1,0:T(8,128)}), f32[16,24,128]{2,1,0:T(8,128)S(1)}, u32[]{:S(2)}, u32[]{:S(2)}) async-start(f32[16,24,128]{2,1,0:T(8,128)} %broadcast_in_dim.10), calls=%async_computation.3 | async-start | bytes 393216 | tf_op jit(solution)/shard_map/all_to_all | solution.py:17
  73.3 16.6 %collective-permute-start.2 = (f32[256,256]{1,0:T(8,128)S(1)}, f32[256,256]{1,0:T(8,128)S(1)}, u32[]{:S(2)}, u32[]{:S(2)}) collective-permute-start(f32[256,256]{1,0:T(8,128)S(1)} %get-tuple-element.21), channel_id=1, source_target_pairs={{0,2},{2,4},{4,6},{6,0},{1,3},{3,5},{5,7},{7,1},{8,10},{10,12},{12... | collective-permute-start | bytes 786440 | tf_op jit(solution)/shard_map/ppermute | solution.py:26
  75.2 14.7 %collective-permute-start.3 = (f32[256,256]{1,0:T(8,128)S(1)}, f32[256,256]{1,0:T(8,128)S(1)}, u32[]{:S(2)}, u32[]{:S(2)}) collective-permute-start(f32[256,256]{1,0:T(8,128)S(1)} %get-tuple-element.22), channel_id=1, source_target_pairs={{0,4},{2,6},{4,0},{6,2},{1,5},{3,7},{5,1},{7,3},{8,12},{10,14},{12... | collective-permute-start | bytes 786440 | tf_op jit(solution)/shard_map/ppermute | solution.py:26
  79.1 10.8 %collective-permute-start.4 = (f32[256,256]{1,0:T(8,128)S(1)}, f32[256,256]{1,0:T(8,128)S(1)}, u32[]{:S(2)}, u32[]{:S(2)}) collective-permute-start(f32[256,256]{1,0:T(8,128)S(1)} %get-tuple-element.23), channel_id=1, source_target_pairs={{0,6},{2,0},{4,2},{6,4},{1,7},{3,1},{5,3},{7,5},{8,14},{10,8},{12,... | collective-permute-start | bytes 786440 | tf_op jit(solution)/shard_map/ppermute | solution.py:26
  86.3 17.0 %all-to-all-start.4 = ((f32[16,24,128]{2,1,0:T(8,128)}), f32[16,24,128]{2,1,0:T(8,128)S(1)}, u32[]{:S(2)}, u32[]{:S(2)}) async-start(f32[16,24,128]{2,1,0:T(8,128)} %broadcast_in_dim.11), calls=%async_computation.4 | async-start | bytes 393216 | tf_op jit(solution)/shard_map/all_to_all | solution.py:17
  90.0 9.8 %collective-permute-start.5 = (f32[64,256]{1,0:T(8,128)S(1)}, f32[64,256]{1,0:T(8,128)S(1)}, u32[]{:S(2)}, u32[]{:S(2)}) collective-permute-start(f32[64,256]{1,0:T(8,128)S(1)} %get-tuple-element.25), channel_id=1, source_target_pairs={{0,8},{8,16},{16,24},{24,0},{1,9},{9,17},{17,25},{25,1},{2,10},{10... | collective-permute-start | bytes 196616 | tf_op jit(solution)/shard_map/ppermute | solution.py:26
  93.4 6.6 %collective-permute-start.6 = (f32[64,256]{1,0:T(8,128)S(1)}, f32[64,256]{1,0:T(8,128)S(1)}, u32[]{:S(2)}, u32[]{:S(2)}) collective-permute-start(f32[64,256]{1,0:T(8,128)S(1)} %get-tuple-element.26), channel_id=1, source_target_pairs={{0,16},{8,24},{16,0},{24,8},{1,17},{9,25},{17,1},{25,9},{2,18},{10... | collective-permute-start | bytes 196616 | tf_op jit(solution)/shard_map/ppermute | solution.py:26
  97.4 5.3 %collective-permute-start.7 = (f32[64,256]{1,0:T(8,128)S(1)}, f32[64,256]{1,0:T(8,128)S(1)}, u32[]{:S(2)}, u32[]{:S(2)}) collective-permute-start(f32[64,256]{1,0:T(8,128)S(1)} %get-tuple-element.27), channel_id=1, source_target_pairs={{0,24},{8,0},{16,8},{24,16},{1,25},{9,1},{17,9},{25,17},{2,26},{10... | collective-permute-start | bytes 196616 | tf_op jit(solution)/shard_map/ppermute | solution.py:26
  102.7 10.2 %copy-start.2 = (f32[256,256]{1,0:T(8,128)S(1)}, f32[256,256]{1,0:T(8,128)}, u32[]{:S(2)}) copy-start(f32[256,256]{1,0:T(8,128)} %inv_two.1) | copy-start | bytes 786436
  103.2 9.6 %copy-start.1 = (f32[256,256]{1,0:T(8,128)S(1)}, f32[256,256]{1,0:T(8,128)}, u32[]{:S(2)}) copy-start(f32[256,256]{1,0:T(8,128)} %inv_one.1) | copy-start | bytes 786436
  103.3 9.5 %collective-permute-start.8 = (f32[448,128]{1,0:T(8,128)S(1)}, f32[448,128]{1,0:T(8,128)S(1)}, u32[]{:S(2)}, u32[]{:S(2)}) collective-permute-start(f32[448,128]{1,0:T(8,128)S(1)} %pad_maximum_fusion), channel_id=1, source_target_pairs={{0,1},{1,0},{2,3},{3,2},{4,5},{5,4},{6,7},{7,6},{8,9},{9,8},{10,11... | collective-permute-start | bytes 688136 | tf_op jit(solution)/shard_map/ppermute | solution.py:171

commit v14 on v13

--- a/solution.py
+++ b/solution.py
@@ -9,6 +9,7 @@
 SIZES = (4, 4, 4, 4, 2)
 SWAP = [(0, 1), (1, 0)]
 VMEM = pl.BlockSpec(memory_space=pltpu.VMEM)
+ANY = pl.BlockSpec(memory_space=pl.ANY)
 SMEM = pl.BlockSpec(memory_space=pltpu.SMEM)
 PARAMS = pltpu.CompilerParams(vmem_limit_bytes=32 * 1024 * 1024)
 
@@ -44,6 +45,18 @@
     for d in range(4)
     for k in range(2)
 ]
+
+
+def spread_kernel(one, two, out, sems):
+    copies = [
+        pltpu.make_async_copy(source, out.at[2 * z + k], sems.at[2 * z + k])
+        for z in range(4)
+        for k, source in enumerate((one, two))
+    ]
+    for copy in copies:
+        copy.start()
+    for copy in copies:
+        copy.wait()
 
 
 def multiply_kernel(pool, sibling, strip, rows, diag, out0, out1, out2, out3, rhs, full):
@@ -62,15 +75,19 @@
         ) + jnp.dot(sibling[take], rhs[depth:], preferred_element_type=jnp.float32)
         for j in range(4):
             full[j, z * 64 : (z + 1) * 64] = block[j * 64 : (j + 1) * 64]
-    term = jnp.zeros((256, 256), jnp.float32)
+    terms = jnp.zeros((256, 768), jnp.float32)
     for j in range(4):
-        left, rest = rows[j], full[j]
+        pieces, rest = [], full[j]
         for _ in range(3):
-            piece = rest.astype(jnp.bfloat16)
-            rest = rest - piece.astype(jnp.float32)
-            term = term + lax.dot_general(
-                left, piece, (((0,), (0,)), ((), ())), preferred_element_type=jnp.float32
-            )
+            pieces.append(rest.astype(jnp.bfloat16))
+            rest = rest - pieces[-1].astype(jnp.float32)
+        terms = terms + lax.dot_general(
+            rows[j],
+            jnp.concatenate(pieces, axis=1),
+            (((0,), (0,)), ((), ())),
+            preferred_element_type=jnp.float32,
+        )
+    term = terms[:, :256] + terms[:, 256:512] + terms[:, 512:]
     diag[0:128] = term[:128, :128]
     diag[128:256] = term[:128, 128:]
     diag[256:384] = term[128:, 128:]
@@ -137,9 +154,13 @@
     mask = lax.dynamic_slice_in_dim(struct, lax.axis_index(("x", "zh")) * 4, 4)
     sibling_pool = lax.ppermute(inverse_pool, "core", SWAP)
 
-    both = jnp.broadcast_to(
-        jnp.stack([factor_one, factor_two])[None], (4, 2, row_count, width)
-    ).reshape(8, row_count, width)
+    both = pl.pallas_call(
+        spread_kernel,
+        out_shape=jax.ShapeDtypeStruct((8, row_count, width), factor_one.dtype),
+        in_specs=[ANY, ANY],
+        out_specs=ANY,
+        scratch_shapes=[pltpu.SemaphoreType.DMA((8,))],
+    )(factor_one, factor_two)
     rows = exchange(both, ("zl", "core")).reshape(4, 2 * row_count, width)
     rows = rows * mask.astype(jnp.bfloat16)[:, None, None]
     rows = lax.optimization_barrier(rows)

time: 115 us -> 118 us (1.026)
  Pallas kernels: 3.72 us -> 8.9 us
    pallas_call x0 -> x1, Pallas kernels: none -> 5.14 us  [per_device(): pl.pallas_call(spread_kernel, out_shape=jax.ShapeDtypeStruct((8, row_coun...]
where the time goes in v14:
time: 118 us
  starting transfers between devices  63.3 us (54%)
  blocking collectives  31.6 us (27%)
  waiting for transfers between devices  10.5 us (9%)
  Pallas kernels  8.9 us (8%)
  local copies, waits for them, and re-layouts  2.1 us (2%)
    all_to_all x3, starting transfers between devices, exchange(): return lax.all_to_all(parts, axes, 0, 0)  24.7 us
    all_to_all x2, blocking collectives, exchange(): return lax.all_to_all(parts, axes, 0, 0)  21.2 us
    ppermute x6, starting transfers between devices, rotate(): lax.ppermute(parts[s], axis, [(i, (i + s) % 4) for i in range(4)])  18.6 us
    all_gather x1, blocking collectives, per_device(): around = lax.all_gather(rows.reshape(256, width), 'y')  10.4 us
    ppermute x1, starting transfers between devices, per_device(): turned = lax.ppermute(rows, AXES, TURN)  9.54 us
    ppermute x1, starting transfers between devices, per_device(): swapped = lax.ppermute(jnp.concatenate([total, leave]), 'core', SWAP)  8.42 us
    all_to_all x3, waiting for transfers between devices, exchange(): return lax.all_to_all(parts, axes, 0, 0)  6.46 us
    pallas_call x1, Pallas kernels, per_device(): pl.pallas_call(spread_kernel, out_shape=jax.ShapeDtypeStruct((8, row_coun...  5.14 us
  transfers between devices with their start and end apart: 12, of which 5 were waited for; matrix products, arithmetic and copies ran while one was open for 1% of the time, Pallas kernels for 1%

profile of v14, /device:TPU:1, one launch (start us, length us, event | category | flops | bytes accessed | tf_op | source)
XLA Modules:
  0.0 117.5 jit_solution(473229484858083060)
XLA Ops:
  0.6 5.1 %shard_map.102 = bf16[8,32,256]{2,1,0:T(8,128)(2,1)} custom-call(bf16[32,256]{1,0:T(8,128)(2,1)} %one.1, bf16[32,256]{1,0:T(8,128)(2,1)} %two.1), custom_call_target="tpu_custom_call" | custom-call | tf_op jit(solution)/shard_map/pallas_call | solution.py:157
  5.8 10.2 %all-to-all-start = ((bf16[8,32,256]{2,1,0:T(8,128)(2,1)}), bf16[8,32,256]{2,1,0:T(8,128)(2,1)S(1)}, u32[]{:S(2)}, u32[]{:S(2)}) async-start(bf16[8,32,256]{2,1,0:T(8,128)(2,1)} %shard_map.102), calls=%async_computation | async-start | bytes 262144 | tf_op jit(solution)/shard_map/all_to_all | solution.py:18
  15.9 2.0 %collective-permute-start = (bf16[1024,512]{1,0:T(8,128)(2,1)}, bf16[1024,512]{1,0:T(8,128)(2,1)S(1)}, u32[]{:S(2)}, u32[]{:S(2)}) collective-permute-start(bf16[1024,512]{1,0:T(8,128)(2,1)} %pool.1), channel_id=1, source_target_pairs={{0,1},{1,0},{2,3},{3,2},{4,5},{5,4},{6,7},{7,6},{8,9},{9,8},{10,11... | collective-permute-start | bytes 3145736 | tf_op jit(solution)/shard_map/ppermute | solution.py:155
  18.0 0.0 copy-start.3
  18.0 0.0 copy-start.4
  18.0 0.6 copy-done.3
  18.6 0.0 copy-done.4
  18.7 0.1 fusion
  18.7 3.0 %all-to-all-done = bf16[8,32,256]{2,1,0:T(8,128)(2,1)S(1)} async-done(((bf16[8,32,256]{2,1,0:T(8,128)(2,1)}), bf16[8,32,256]{2,1,0:T(8,128)(2,1)S(1)}, u32[]{:S(2)}, u32[]{:S(2)}) %all-to-all-start) | async-done | bytes 131104 | tf_op jit(solution)/shard_map/all_to_all | solution.py:18
  21.8 0.1 bitcast_multiply_fusion
  21.9 9.5 %collective-permute-start.1 = (bf16[4,64,256]{2,1,0:T(8,128)(2,1)S(1)}, bf16[4,64,256]{2,1,0:T(8,128)(2,1)S(1)}, u32[]{:S(2)}, u32[]{:S(2)}) collective-permute-start(bf16[4,64,256]{2,1,0:T(8,128)(2,1)S(1)} %bitcast_multiply_fusion), channel_id=1, source_target_pairs={{12,0},{13,1},{38,2},{39,3},{88,4},{89,5},{114,6},{115,7},{138,8},... | collective-permute-start | bytes 393224 | tf_op jit(solution)/shard_map/ppermute | solution.py:167
  31.4 0.0 copy-start
  31.4 10.4 %all_gather.3.rows = bf16[4,256,256]{2,1,0:T(8,128)(2,1)S(1)} all-gather(bf16[1,256,256]{2,1,0:T(8,128)(2,1)S(1)} %bitcast.9), channel_id=1, replica_groups=mesh['x'=4,'zh'=4,'zl'=4,'y'=4,'core'=2] {'y'}, dimensions={0}, use_global_device_ids=true | all-gather | bytes 655360 | tf_op jit(solution)/shard_map/all_gather | solution.py:168
  41.9 0.0 collective-permute-done.1
  41.9 11.0 %all_to_all.25.strip = bf16[4,4,64,256]{3,2,1,0:T(8,128)(2,1)S(1)} all-to-all(bf16[4,4,64,256]{3,2,1,0:T(8,128)(2,1)S(1)} %broadcast_in_dim.6), channel_id=1, replica_groups=mesh['x'=4,'zh'=4,'zl'=4,'y'=4,'core'=2] {'x'}, dimensions={0} | all-to-all | bytes 1048576 | tf_op jit(solution)/shard_map/all_to_all | solution.py:18
  52.9 0.0 collective-permute-done.sibling
  52.9 0.0 copy-done
  52.9 2.2 %shard_map.103 = (f32[384,128]{1,0:T(8,128)S(1)}, f32[256,256]{1,0:T(8,128)S(1)}, f32[256,256]{1,0:T(8,128)S(1)}, f32[256,256]{1,0:T(8,128)S(1)}, f32[256,256]{1,0:T(8,128)S(1)}) custom-call(bf16[1024,512]{1,0:T(8,128)(2,1)S(1)} %copy-done, bf16[1024,512]{1,0:T(8,128)(2,1)S(1)} %collective-permute-done.sibling, ...), custom_call_target="tpu_custom_call" | custom-call | tf_op jit(solution)/shard_map/pallas_call | solution.py:136
  55.2 10.1 %all_to_all.26 = f32[16,24,128]{2,1,0:T(8,128)S(1)} all-to-all(f32[16,24,128]{2,1,0:T(8,128)S(1)} %bitcast.8), channel_id=1, replica_groups=mesh['x'=4,'zh'=4,'zl'=4,'y'=4,'core'=2] {'x','y'}, dimensions={0} | all-to-all | bytes 393216 | tf_op jit(solution)/shard_map/all_to_all | solution.py:18
  65.3 0.7 broadcast_in_dim.7
  66.0 11.0 %all-to-all-start.3 = ((f32[16,24,128]{2,1,0:T(8,128)}), f32[16,24,128]{2,1,0:T(8,128)S(1)}, u32[]{:S(2)}, u32[]{:S(2)}) async-start(f32[16,24,128]{2,1,0:T(8,128)} %broadcast_in_dim.7), calls=%async_computation.3 | async-start | bytes 393216 | tf_op jit(solution)/shard_map/all_to_all | solution.py:18
  77.0 1.9 %collective-permute-start.2 = (f32[256,256]{1,0:T(8,128)S(1)}, f32[256,256]{1,0:T(8,128)S(1)}, u32[]{:S(2)}, u32[]{:S(2)}) collective-permute-start(f32[256,256]{1,0:T(8,128)S(1)} %get-tuple-element.21), channel_id=1, source_target_pairs={{0,2},{2,4},{4,6},{6,0},{1,3},{3,5},{5,7},{7,1},{8,10},{10,12},{12... | collective-permute-start | bytes 786440 | tf_op jit(solution)/shard_map/ppermute | solution.py:27
  79.0 3.8 %collective-permute-start.3 = (f32[256,256]{1,0:T(8,128)S(1)}, f32[256,256]{1,0:T(8,128)S(1)}, u32[]{:S(2)}, u32[]{:S(2)}) collective-permute-start(f32[256,256]{1,0:T(8,128)S(1)} %get-tuple-element.22), channel_id=1, source_target_pairs={{0,4},{2,6},{4,0},{6,2},{1,5},{3,7},{5,1},{7,3},{8,12},{10,14},{12... | collective-permute-start | bytes 786440 | tf_op jit(solution)/shard_map/ppermute | solution.py:27
  82.8 3.2 %collective-permute-start.4 = (f32[256,256]{1,0:T(8,128)S(1)}, f32[256,256]{1,0:T(8,128)S(1)}, u32[]{:S(2)}, u32[]{:S(2)}) collective-permute-start(f32[256,256]{1,0:T(8,128)S(1)} %get-tuple-element.23), channel_id=1, source_target_pairs={{0,6},{2,0},{4,2},{6,4},{1,7},{3,1},{5,3},{7,5},{8,14},{10,8},{12,... | collective-permute-start | bytes 786440 | tf_op jit(solution)/shard_map/ppermute | solution.py:27
  86.0 3.4 %all-to-all-done.3 = f32[16,24,128]{2,1,0:T(8,128)S(1)} async-done(((f32[16,24,128]{2,1,0:T(8,128)}), f32[16,24,128]{2,1,0:T(8,128)S(1)}, u32[]{:S(2)}, u32[]{:S(2)}) %all-to-all-start.3) | async-done | bytes 196640 | tf_op jit(solution)/shard_map/all_to_all | solution.py:18
  89.4 0.7 broadcast_in_dim.8
  90.1 3.5 %all-to-all-start.4 = ((f32[16,24,128]{2,1,0:T(8,128)}), f32[16,24,128]{2,1,0:T(8,128)S(1)}, u32[]{:S(2)}, u32[]{:S(2)}) async-start(f32[16,24,128]{2,1,0:T(8,128)} %broadcast_in_dim.8), calls=%async_computation.4 | async-start | bytes 393216 | tf_op jit(solution)/shard_map/all_to_all | solution.py:18
  93.6 0.0 collective-permute-done.2.in1
  93.6 0.0 collective-permute-done.3.in2
  93.7 0.0 collective-permute-done.4.in3
  93.7 0.1 shard_map.104
  93.8 3.4 %collective-permute-start.5 = (f32[64,256]{1,0:T(8,128)S(1)}, f32[64,256]{1,0:T(8,128)S(1)}, u32[]{:S(2)}, u32[]{:S(2)}) collective-permute-start(f32[64,256]{1,0:T(8,128)S(1)} %get-tuple-element.25), channel_id=1, source_target_pairs={{0,8},{8,16},{16,24},{24,0},{1,9},{9,17},{17,25},{25,1},{2,10},{10... | collective-permute-start | bytes 196616 | tf_op jit(solution)/shard_map/ppermute | solution.py:27
  97.1 4.0 %collective-permute-start.6 = (f32[64,256]{1,0:T(8,128)S(1)}, f32[64,256]{1,0:T(8,128)S(1)}, u32[]{:S(2)}, u32[]{:S(2)}) collective-permute-start(f32[64,256]{1,0:T(8,128)S(1)} %get-tuple-element.26), channel_id=1, source_target_pairs={{0,16},{8,24},{16,0},{24,8},{1,17},{9,25},{17,1},{25,9},{2,18},{10... | collective-permute-start | bytes 196616 | tf_op jit(solution)/shard_map/ppermute | solution.py:27
  101.2 2.4 %collective-permute-start.7 = (f32[64,256]{1,0:T(8,128)S(1)}, f32[64,256]{1,0:T(8,128)S(1)}, u32[]{:S(2)}, u32[]{:S(2)}) collective-permute-start(f32[64,256]{1,0:T(8,128)S(1)} %get-tuple-element.27), channel_id=1, source_target_pairs={{0,24},{8,0},{16,8},{24,16},{1,25},{9,1},{17,9},{25,17},{2,26},{10... | collective-permute-start | bytes 196616 | tf_op jit(solution)/shard_map/ppermute | solution.py:27
  103.5 0.0 collective-permute-done.5.in1
  103.5 0.2 collective-permute-done.6.in2
  103.8 2.7 %collective-permute-done.7.in3 = f32[64,256]{1,0:T(8,128)S(1)} collective-permute-done((f32[64,256]{1,0:T(8,128)S(1)}, f32[64,256]{1,0:T(8,128)S(1)}, u32[]{:S(2)}, u32[]{:S(2)}) %collective-permute-start.7) | collective-permute-done | bytes 65568 | tf_op jit(solution)/shard_map/ppermute | solution.py:27
  106.5 0.0 copy-start.2
  106.5 0.6 shard_map.105
  107.0 0.0 copy-start.1
  107.0 0.0 all-to-all-done.4
  107.1 8.4 %collective-permute-start.8 = (f32[448,128]{1,0:T(8,128)S(1)}, f32[448,128]{1,0:T(8,128)S(1)}, u32[]{:S(2)}, u32[]{:S(2)}) collective-permute-start(f32[448,128]{1,0:T(8,128)S(1)} %pad_maximum_fusion), channel_id=1, source_target_pairs={{0,1},{1,0},{2,3},{3,2},{4,5},{5,4},{6,7},{7,6},{8,9},{9,8},{10,11... | collective-permute-start | bytes 688136 | tf_op jit(solution)/shard_map/ppermute | solution.py:192
  115.5 1.1 collective-permute-done.8.swapped
  116.6 0.0 copy-done.2
  116.6 0.0 copy-done.1
  116.6 0.9 shard_map.106
  (5 shorter events, 0.1 us)
Async XLA Ops:
  5.8 16.0 %all-to-all-start = ((bf16[8,32,256]{2,1,0:T(8,128)(2,1)}), bf16[8,32,256]{2,1,0:T(8,128)(2,1)S(1)}, u32[]{:S(2)}, u32[]{:S(2)}) async-start(bf16[8,32,256]{2,1,0:T(8,128)(2,1)} %shard_map.102), calls=%async_computation | async-start | bytes 262144 | tf_op jit(solution)/shard_map/all_to_all | solution.py:18
  15.9 37.0 %collective-permute-start = (bf16[1024,512]{1,0:T(8,128)(2,1)}, bf16[1024,512]{1,0:T(8,128)(2,1)S(1)}, u32[]{:S(2)}, u32[]{:S(2)}) collective-permute-start(bf16[1024,512]{1,0:T(8,128)(2,1)} %pool.1), channel_id=1, source_target_pairs={{0,1},{1,0},{2,3},{3,2},{4,5},{5,4},{6,7},{7,6},{8,9},{9,8},{10,11... | collective-permute-start | bytes 3145736 | tf_op jit(solution)/shard_map/ppermute | solution.py:155
  18.0 0.7 copy-start.3
  18.0 0.7 copy-start.4
  21.9 20.0 %collective-permute-start.1 = (bf16[4,64,256]{2,1,0:T(8,128)(2,1)S(1)}, bf16[4,64,256]{2,1,0:T(8,128)(2,1)S(1)}, u32[]{:S(2)}, u32[]{:S(2)}) collective-permute-start(bf16[4,64,256]{2,1,0:T(8,128)(2,1)S(1)} %bitcast_multiply_fusion), channel_id=1, source_target_pairs={{12,0},{13,1},{38,2},{39,3},{88,4},{89,5},{114,6},{115,7},{138,8},... | collective-permute-start | bytes 393224 | tf_op jit(solution)/shard_map/ppermute | solution.py:167
  31.4 21.5 %copy-start = (bf16[1024,512]{1,0:T(8,128)(2,1)S(1)}, bf16[1024,512]{1,0:T(8,128)(2,1)}, u32[]{:S(2)}) copy-start(bf16[1024,512]{1,0:T(8,128)(2,1)} %pool.1) | copy-start | bytes 3145732
  66.0 23.4 %all-to-all-start.3 = ((f32[16,24,128]{2,1,0:T(8,128)}), f32[16,24,128]{2,1,0:T(8,128)S(1)}, u32[]{:S(2)}, u32[]{:S(2)}) async-start(f32[16,24,128]{2,1,0:T(8,128)} %broadcast_in_dim.7), calls=%async_computation.3 | async-start | bytes 393216 | tf_op jit(solution)/shard_map/all_to_all | solution.py:18
  77.0 16.6 %collective-permute-start.2 = (f32[256,256]{1,0:T(8,128)S(1)}, f32[256,256]{1,0:T(8,128)S(1)}, u32[]{:S(2)}, u32[]{:S(2)}) collective-permute-start(f32[256,256]{1,0:T(8,128)S(1)} %get-tuple-element.21), channel_id=1, source_target_pairs={{0,2},{2,4},{4,6},{6,0},{1,3},{3,5},{5,7},{7,1},{8,10},{10,12},{12... | collective-permute-start | bytes 786440 | tf_op jit(solution)/shard_map/ppermute | solution.py:27
  79.0 14.7 %collective-permute-start.3 = (f32[256,256]{1,0:T(8,128)S(1)}, f32[256,256]{1,0:T(8,128)S(1)}, u32[]{:S(2)}, u32[]{:S(2)}) collective-permute-start(f32[256,256]{1,0:T(8,128)S(1)} %get-tuple-element.22), channel_id=1, source_target_pairs={{0,4},{2,6},{4,0},{6,2},{1,5},{3,7},{5,1},{7,3},{8,12},{10,14},{12... | collective-permute-start | bytes 786440 | tf_op jit(solution)/shard_map/ppermute | solution.py:27
  82.8 10.9 %collective-permute-start.4 = (f32[256,256]{1,0:T(8,128)S(1)}, f32[256,256]{1,0:T(8,128)S(1)}, u32[]{:S(2)}, u32[]{:S(2)}) collective-permute-start(f32[256,256]{1,0:T(8,128)S(1)} %get-tuple-element.23), channel_id=1, source_target_pairs={{0,6},{2,0},{4,2},{6,4},{1,7},{3,1},{5,3},{7,5},{8,14},{10,8},{12,... | collective-permute-start | bytes 786440 | tf_op jit(solution)/shard_map/ppermute | solution.py:27
  90.1 17.0 %all-to-all-start.4 = ((f32[16,24,128]{2,1,0:T(8,128)}), f32[16,24,128]{2,1,0:T(8,128)S(1)}, u32[]{:S(2)}, u32[]{:S(2)}) async-start(f32[16,24,128]{2,1,0:T(8,128)} %broadcast_in_dim.8), calls=%async_computation.4 | async-start | bytes 393216 | tf_op jit(solution)/shard_map/all_to_all | solution.py:18
  93.8 9.8 %collective-permute-start.5 = (f32[64,256]{1,0:T(8,128)S(1)}, f32[64,256]{1,0:T(8,128)S(1)}, u32[]{:S(2)}, u32[]{:S(2)}) collective-permute-start(f32[64,256]{1,0:T(8,128)S(1)} %get-tuple-element.25), channel_id=1, source_target_pairs={{0,8},{8,16},{16,24},{24,0},{1,9},{9,17},{17,25},{25,1},{2,10},{10... | collective-permute-start | bytes 196616 | tf_op jit(solution)/shard_map/ppermute | solution.py:27
  97.1 6.6 %collective-permute-start.6 = (f32[64,256]{1,0:T(8,128)S(1)}, f32[64,256]{1,0:T(8,128)S(1)}, u32[]{:S(2)}, u32[]{:S(2)}) collective-permute-start(f32[64,256]{1,0:T(8,128)S(1)} %get-tuple-element.26), channel_id=1, source_target_pairs={{0,16},{8,24},{16,0},{24,8},{1,17},{9,25},{17,1},{25,9},{2,18},{10... | collective-permute-start | bytes 196616 | tf_op jit(solution)/shard_map/ppermute | solution.py:27
  101.2 5.3 %collective-permute-start.7 = (f32[64,256]{1,0:T(8,128)S(1)}, f32[64,256]{1,0:T(8,128)S(1)}, u32[]{:S(2)}, u32[]{:S(2)}) collective-permute-start(f32[64,256]{1,0:T(8,128)S(1)} %get-tuple-element.27), channel_id=1, source_target_pairs={{0,24},{8,0},{16,8},{24,16},{1,25},{9,1},{17,9},{25,17},{2,26},{10... | collective-permute-start | bytes 196616 | tf_op jit(solution)/shard_map/ppermute | solution.py:27
  106.5 10.1 %copy-start.2 = (f32[256,256]{1,0:T(8,128)S(1)}, f32[256,256]{1,0:T(8,128)}, u32[]{:S(2)}) copy-start(f32[256,256]{1,0:T(8,128)} %inv_two.1) | copy-start | bytes 786436
  107.0 9.6 %copy-start.1 = (f32[256,256]{1,0:T(8,128)S(1)}, f32[256,256]{1,0:T(8,128)}, u32[]{:S(2)}) copy-start(f32[256,256]{1,0:T(8,128)} %inv_one.1) | copy-start | bytes 786436
  107.1 9.5 %collective-permute-start.8 = (f32[448,128]{1,0:T(8,128)S(1)}, f32[448,128]{1,0:T(8,128)S(1)}, u32[]{:S(2)}, u32[]{:S(2)}) collective-permute-start(f32[448,128]{1,0:T(8,128)S(1)} %pad_maximum_fusion), channel_id=1, source_target_pairs={{0,1},{1,0},{2,3},{3,2},{4,5},{5,4},{6,7},{7,6},{8,9},{9,8},{10,11... | collective-permute-start | bytes 688136 | tf_op jit(solution)/shard_map/ppermute | solution.py:192

commit v15 on v13

--- a/solution.py
+++ b/solution.py
@@ -95,17 +95,14 @@
     leave[...] = jnp.where(core == 0, high, low)
 
 
-def finish_kernel(total, stay, swapped, inv_one, inv_two, column_one, column_two, diag_one, diag_two):
+def finish_kernel(finals, stay, inv_one, inv_two, column_one, column_two, diag_one, diag_two):
     first = lax.axis_index("core") == 0
-    own, other = total[...], swapped[0:384]
-    own_column, other_column = stay[...], swapped[384:448]
-    for swap, inv, diag, column in (
-        (False, inv_one, diag_one, column_one),
-        (True, inv_two, diag_two, column_two),
+    for k, inv, diag, column in (
+        (0, inv_one, diag_one, column_one),
+        (1, inv_two, diag_two, column_two),
     ):
-        pick = first != swap
-        t = jnp.where(pick, own, other)
-        c = jnp.where(pick, own_column, other_column).astype(jnp.bfloat16)
+        t = finals[k, 0:384]
+        c = jnp.where(first == (k == 0), stay[...], finals[k, 384:448]).astype(jnp.bfloat16)
         diag[0:128, 0:128] = inv[0:128, 0:128] + t[0:128]
         diag[0:128, 128:256] = inv[0:128, 128:256] + t[128:256]
         diag[128:256, 0:128] = inv[128:256, 0:128] + t[128:256].T
@@ -168,14 +165,14 @@
     half = jax.ShapeDtypeStruct((2 * row_count, 128), f32)
     stay, leave = call(split_kernel, [half, half], (mask, *parts), scalars=1)
     total = gather(shard, ("x", "y"), 16).reshape(384, 128)
-    swapped = lax.ppermute(jnp.concatenate([total, leave]), "core", SWAP)
+    finals = lax.all_gather(jnp.concatenate([total, leave]), "core")
     wide = jax.ShapeDtypeStruct((row_count, width), jnp.bfloat16)
     square = jax.ShapeDtypeStruct((width, width), f32)
     return tuple(
         call(
             finish_kernel,
             [wide, wide, square, square],
-            (total, stay, swapped, diag_inv_one, diag_inv_two),
+            (finals, stay, diag_inv_one, diag_inv_two),
         )
     )
 

time: 115 us -> 113 us (0.983)
  starting transfers between devices: 63.3 us -> 54.9 us
  blocking collectives: 31.6 us -> 39.9 us
    ppermute x1 -> x0, starting transfers between devices: 8.43 us -> none  [per_device(): swapped = lax.ppermute(jnp.concatenate([total, leave]), 'core', SWAP)]
    all_gather x0 -> x1, blocking collectives: none -> 8.28 us  [per_device(): finals = lax.all_gather(jnp.concatenate([total, leave]), 'core')]
  transfers between devices with their start and end apart: 12 -> 11, of which waited for: 5 -> 4; matrix products, arithmetic and copies ran while one was open for 1% -> 1% of each run, Pallas kernels for 1% -> 1%
where the time goes in v15:
time: 113 us; the launch traced here: 112 us
  starting transfers between devices  54.9 us (49%)
  blocking collectives  39.9 us (35%)
  waiting for transfers between devices  9.4 us (8%)
  Pallas kernels  3.71 us (3%)
  local copies, waits for them, and re-layouts  2.77 us (2%)
    all_to_all x3, starting transfers between devices, exchange(): return lax.all_to_all(parts, axes, 0, 0)  24.7 us
    all_to_all x2, blocking collectives, exchange(): return lax.all_to_all(parts, axes, 0, 0)  21.2 us
    ppermute x6, starting transfers between devices, rotate(): lax.ppermute(parts[s], axis, [(i, (i + s) % 4) for i in range(4)])  18.6 us
    all_gather x1, blocking collectives, per_device(): around = lax.all_gather(rows.reshape(256, width), 'y')  10.4 us
    ppermute x1, starting transfers between devices, per_device(): turned = lax.ppermute(rows, AXES, TURN)  9.54 us
    all_gather x1, blocking collectives, per_device(): finals = lax.all_gather(jnp.concatenate([total, leave]), 'core')  8.28 us
    all_to_all x3, waiting for transfers between devices, exchange(): return lax.all_to_all(parts, axes, 0, 0)  6.46 us
    pallas_call x4, Pallas kernels, call(): pl.pallas_call(kernel, out_shape=outs, in_specs=[SMEM] * scalars + [VMEM]...  3.71 us
  transfers between devices with their start and end apart: 11, of which 4 were waited for; matrix products, arithmetic and copies ran while one was open for 1% of the time, Pallas kernels for 1%

profile of v15, /device:TPU:1, one launch (start us, length us, event | category | flops | bytes accessed | tf_op | source)
XLA Modules:
  0.0 112.5 jit_solution(13621443042813324656)
XLA Ops:
  0.6 0.7 pad_maximum_fusion.1
  1.4 0.7 broadcast_in_dim.8
  2.0 10.2 %all-to-all-start = ((bf16[8,32,256]{2,1,0:T(8,128)(2,1)}), bf16[8,32,256]{2,1,0:T(8,128)(2,1)S(1)}, u32[]{:S(2)}, u32[]{:S(2)}) async-start(bf16[8,32,256]{2,1,0:T(8,128)(2,1)} %bitcast.2), calls=%async_computation | async-start | bytes 262144 | tf_op jit(solution)/shard_map/all_to_all | solution.py:17
  12.2 2.0 %collective-permute-start = (bf16[1024,512]{1,0:T(8,128)(2,1)}, bf16[1024,512]{1,0:T(8,128)(2,1)S(1)}, u32[]{:S(2)}, u32[]{:S(2)}) collective-permute-start(bf16[1024,512]{1,0:T(8,128)(2,1)} %pool.1), channel_id=1, source_target_pairs={{0,1},{1,0},{2,3},{3,2},{4,5},{5,4},{6,7},{7,6},{8,9},{9,8},{10,11... | collective-permute-start | bytes 3145736 | tf_op jit(solution)/shard_map/ppermute | solution.py:135
  14.2 0.0 copy-start.3
  14.2 0.0 copy-start.4
  14.2 0.6 copy-done.3
  14.9 0.0 copy-done.4
  14.9 0.1 fusion
  15.0 3.0 %all-to-all-done = bf16[8,32,256]{2,1,0:T(8,128)(2,1)S(1)} async-done(((bf16[8,32,256]{2,1,0:T(8,128)(2,1)}), bf16[8,32,256]{2,1,0:T(8,128)(2,1)S(1)}, u32[]{:S(2)}, u32[]{:S(2)}) %all-to-all-start) | async-done | bytes 131104 | tf_op jit(solution)/shard_map/all_to_all | solution.py:17
  18.0 0.1 bitcast_multiply_fusion
  18.1 9.5 %collective-permute-start.1 = (bf16[4,64,256]{2,1,0:T(8,128)(2,1)S(1)}, bf16[4,64,256]{2,1,0:T(8,128)(2,1)S(1)}, u32[]{:S(2)}, u32[]{:S(2)}) collective-permute-start(bf16[4,64,256]{2,1,0:T(8,128)(2,1)S(1)} %bitcast_multiply_fusion), channel_id=1, source_target_pairs={{12,0},{13,1},{38,2},{39,3},{88,4},{89,5},{114,6},{115,7},{138,8},... | collective-permute-start | bytes 393224 | tf_op jit(solution)/shard_map/ppermute | solution.py:143
  27.7 0.0 copy-start
  27.7 10.4 %all_gather.9.rows = bf16[4,256,256]{2,1,0:T(8,128)(2,1)S(1)} all-gather(bf16[1,256,256]{2,1,0:T(8,128)(2,1)S(1)} %bitcast.13), channel_id=1, replica_groups=mesh['x'=4,'zh'=4,'zl'=4,'y'=4,'core'=2] {'y'}, dimensions={0}, use_global_device_ids=true | all-gather | bytes 655360 | tf_op jit(solution)/shard_map/all_gather | solution.py:144
  38.1 0.0 collective-permute-done.1
  38.2 11.0 %all_to_all.25.strip = bf16[4,4,64,256]{3,2,1,0:T(8,128)(2,1)S(1)} all-to-all(bf16[4,4,64,256]{3,2,1,0:T(8,128)(2,1)S(1)} %broadcast_in_dim.9), channel_id=1, replica_groups=mesh['x'=4,'zh'=4,'zl'=4,'y'=4,'core'=2] {'x'}, dimensions={0} | all-to-all | bytes 1048576 | tf_op jit(solution)/shard_map/all_to_all | solution.py:17
  49.2 0.0 collective-permute-done.sibling
  49.2 0.0 copy-done
  49.2 2.2 %shard_map.102 = (f32[384,128]{1,0:T(8,128)S(1)}, f32[256,256]{1,0:T(8,128)S(1)}, f32[256,256]{1,0:T(8,128)S(1)}, f32[256,256]{1,0:T(8,128)S(1)}, f32[256,256]{1,0:T(8,128)S(1)}) custom-call(bf16[1024,512]{1,0:T(8,128)(2,1)S(1)} %copy-done, bf16[1024,512]{1,0:T(8,128)(2,1)S(1)} %collective-permute-done.sibling, ...), custom_call_target="tpu_custom_call" | custom-call | tf_op jit(solution)/shard_map/pallas_call | solution.py:116
  51.4 10.1 %all_to_all.26 = f32[16,24,128]{2,1,0:T(8,128)S(1)} all-to-all(f32[16,24,128]{2,1,0:T(8,128)S(1)} %bitcast.11), channel_id=1, replica_groups=mesh['x'=4,'zh'=4,'zl'=4,'y'=4,'core'=2] {'x','y'}, dimensions={0} | all-to-all | bytes 393216 | tf_op jit(solution)/shard_map/all_to_all | solution.py:17
  61.5 0.7 broadcast_in_dim.10
  62.2 11.0 %all-to-all-start.3 = ((f32[16,24,128]{2,1,0:T(8,128)}), f32[16,24,128]{2,1,0:T(8,128)S(1)}, u32[]{:S(2)}, u32[]{:S(2)}) async-start(f32[16,24,128]{2,1,0:T(8,128)} %broadcast_in_dim.10), calls=%async_computation.3 | async-start | bytes 393216 | tf_op jit(solution)/shard_map/all_to_all | solution.py:17
  73.3 1.9 %collective-permute-start.2 = (f32[256,256]{1,0:T(8,128)S(1)}, f32[256,256]{1,0:T(8,128)S(1)}, u32[]{:S(2)}, u32[]{:S(2)}) collective-permute-start(f32[256,256]{1,0:T(8,128)S(1)} %get-tuple-element.21), channel_id=1, source_target_pairs={{0,2},{2,4},{4,6},{6,0},{1,3},{3,5},{5,7},{7,1},{8,10},{10,12},{12... | collective-permute-start | bytes 786440 | tf_op jit(solution)/shard_map/ppermute | solution.py:26
  75.2 3.9 %collective-permute-start.3 = (f32[256,256]{1,0:T(8,128)S(1)}, f32[256,256]{1,0:T(8,128)S(1)}, u32[]{:S(2)}, u32[]{:S(2)}) collective-permute-start(f32[256,256]{1,0:T(8,128)S(1)} %get-tuple-element.22), channel_id=1, source_target_pairs={{0,4},{2,6},{4,0},{6,2},{1,5},{3,7},{5,1},{7,3},{8,12},{10,14},{12... | collective-permute-start | bytes 786440 | tf_op jit(solution)/shard_map/ppermute | solution.py:26
  79.1 3.1 %collective-permute-start.4 = (f32[256,256]{1,0:T(8,128)S(1)}, f32[256,256]{1,0:T(8,128)S(1)}, u32[]{:S(2)}, u32[]{:S(2)}) collective-permute-start(f32[256,256]{1,0:T(8,128)S(1)} %get-tuple-element.23), channel_id=1, source_target_pairs={{0,6},{2,0},{4,2},{6,4},{1,7},{3,1},{5,3},{7,5},{8,14},{10,8},{12,... | collective-permute-start | bytes 786440 | tf_op jit(solution)/shard_map/ppermute | solution.py:26
  82.2 3.4 %all-to-all-done.3 = f32[16,24,128]{2,1,0:T(8,128)S(1)} async-done(((f32[16,24,128]{2,1,0:T(8,128)}), f32[16,24,128]{2,1,0:T(8,128)S(1)}, u32[]{:S(2)}, u32[]{:S(2)}) %all-to-all-start.3) | async-done | bytes 196640 | tf_op jit(solution)/shard_map/all_to_all | solution.py:17
  85.6 0.7 broadcast_in_dim.11
  86.3 3.5 %all-to-all-start.4 = ((f32[16,24,128]{2,1,0:T(8,128)}), f32[16,24,128]{2,1,0:T(8,128)S(1)}, u32[]{:S(2)}, u32[]{:S(2)}) async-start(f32[16,24,128]{2,1,0:T(8,128)} %broadcast_in_dim.11), calls=%async_computation.4 | async-start | bytes 393216 | tf_op jit(solution)/shard_map/all_to_all | solution.py:17
  89.8 0.0 collective-permute-done.2.in1
  89.9 0.0 collective-permute-done.3.in2
  89.9 0.0 collective-permute-done.4.in3
  89.9 0.1 shard_map.103
  90.0 3.4 %collective-permute-start.5 = (f32[64,256]{1,0:T(8,128)S(1)}, f32[64,256]{1,0:T(8,128)S(1)}, u32[]{:S(2)}, u32[]{:S(2)}) collective-permute-start(f32[64,256]{1,0:T(8,128)S(1)} %get-tuple-element.25), channel_id=1, source_target_pairs={{0,8},{8,16},{16,24},{24,0},{1,9},{9,17},{17,25},{25,1},{2,10},{10... | collective-permute-start | bytes 196616 | tf_op jit(solution)/shard_map/ppermute | solution.py:26
  93.4 4.0 %collective-permute-start.6 = (f32[64,256]{1,0:T(8,128)S(1)}, f32[64,256]{1,0:T(8,128)S(1)}, u32[]{:S(2)}, u32[]{:S(2)}) collective-permute-start(f32[64,256]{1,0:T(8,128)S(1)} %get-tuple-element.26), channel_id=1, source_target_pairs={{0,16},{8,24},{16,0},{24,8},{1,17},{9,25},{17,1},{25,9},{2,18},{10... | collective-permute-start | bytes 196616 | tf_op jit(solution)/shard_map/ppermute | solution.py:26
  97.4 2.4 %collective-permute-start.7 = (f32[64,256]{1,0:T(8,128)S(1)}, f32[64,256]{1,0:T(8,128)S(1)}, u32[]{:S(2)}, u32[]{:S(2)}) collective-permute-start(f32[64,256]{1,0:T(8,128)S(1)} %get-tuple-element.27), channel_id=1, source_target_pairs={{0,24},{8,0},{16,8},{24,16},{1,25},{9,1},{17,9},{25,17},{2,26},{10... | collective-permute-start | bytes 196616 | tf_op jit(solution)/shard_map/ppermute | solution.py:26
  99.7 0.0 collective-permute-done.5.in1
  99.7 0.2 collective-permute-done.6.in2
  100.0 2.7 %collective-permute-done.7.in3 = f32[64,256]{1,0:T(8,128)S(1)} collective-permute-done((f32[64,256]{1,0:T(8,128)S(1)}, f32[64,256]{1,0:T(8,128)S(1)}, u32[]{:S(2)}, u32[]{:S(2)}) %collective-permute-start.7) | collective-permute-done | bytes 65568 | tf_op jit(solution)/shard_map/ppermute | solution.py:26
  102.7 0.6 shard_map.104
  103.2 0.0 all-to-all-done.4
  103.3 0.0 copy-start.1
  103.3 0.0 copy-start.2
  103.3 8.3 %all-gather = f32[896,128]{1,0:T(8,128)S(1)} all-gather(f32[448,128]{1,0:T(8,128)S(1)} %pad_maximum_fusion), channel_id=2, replica_groups=mesh['x'=4,'zh'=4,'zl'=4,'y'=4,'core'=2] {'core'}, dimensions={0}, use_global_device_ids=true | all-gather | bytes 688128 | tf_op jit(solution)/shard_map/all_gather | solution.py:168
  111.6 0.0 copy-done.1
  111.6 0.0 copy-done.2
  111.6 0.9 shard_map.105
  (5 shorter events, 0.1 us)
Async XLA Ops:
  2.0 16.0 %all-to-all-start = ((bf16[8,32,256]{2,1,0:T(8,128)(2,1)}), bf16[8,32,256]{2,1,0:T(8,128)(2,1)S(1)}, u32[]{:S(2)}, u32[]{:S(2)}) async-start(bf16[8,32,256]{2,1,0:T(8,128)(2,1)} %bitcast.2), calls=%async_computation | async-start | bytes 262144 | tf_op jit(solution)/shard_map/all_to_all | solution.py:17
  12.2 37.0 %collective-permute-start = (bf16[1024,512]{1,0:T(8,128)(2,1)}, bf16[1024,512]{1,0:T(8,128)(2,1)S(1)}, u32[]{:S(2)}, u32[]{:S(2)}) collective-permute-start(bf16[1024,512]{1,0:T(8,128)(2,1)} %pool.1), channel_id=1, source_target_pairs={{0,1},{1,0},{2,3},{3,2},{4,5},{5,4},{6,7},{7,6},{8,9},{9,8},{10,11... | collective-permute-start | bytes 3145736 | tf_op jit(solution)/shard_map/ppermute | solution.py:135
  14.2 0.7 copy-start.3
  14.2 0.7 copy-start.4
  18.1 20.0 %collective-permute-start.1 = (bf16[4,64,256]{2,1,0:T(8,128)(2,1)S(1)}, bf16[4,64,256]{2,1,0:T(8,128)(2,1)S(1)}, u32[]{:S(2)}, u32[]{:S(2)}) collective-permute-start(bf16[4,64,256]{2,1,0:T(8,128)(2,1)S(1)} %bitcast_multiply_fusion), channel_id=1, source_target_pairs={{12,0},{13,1},{38,2},{39,3},{88,4},{89,5},{114,6},{115,7},{138,8},... | collective-permute-start | bytes 393224 | tf_op jit(solution)/shard_map/ppermute | solution.py:143
  27.7 21.5 %copy-start = (bf16[1024,512]{1,0:T(8,128)(2,1)S(1)}, bf16[1024,512]{1,0:T(8,128)(2,1)}, u32[]{:S(2)}) copy-start(bf16[1024,512]{1,0:T(8,128)(2,1)} %pool.1) | copy-start | bytes 3145732
  62.2 23.4 %all-to-all-start.3 = ((f32[16,24,128]{2,1,0:T(8,128)}), f32[16,24,128]{2,1,0:T(8,128)S(1)}, u32[]{:S(2)}, u32[]{:S(2)}) async-start(f32[16,24,128]{2,1,0:T(8,128)} %broadcast_in_dim.10), calls=%async_computation.3 | async-start | bytes 393216 | tf_op jit(solution)/shard_map/all_to_all | solution.py:17
  73.3 16.6 %collective-permute-start.2 = (f32[256,256]{1,0:T(8,128)S(1)}, f32[256,256]{1,0:T(8,128)S(1)}, u32[]{:S(2)}, u32[]{:S(2)}) collective-permute-start(f32[256,256]{1,0:T(8,128)S(1)} %get-tuple-element.21), channel_id=1, source_target_pairs={{0,2},{2,4},{4,6},{6,0},{1,3},{3,5},{5,7},{7,1},{8,10},{10,12},{12... | collective-permute-start | bytes 786440 | tf_op jit(solution)/shard_map/ppermute | solution.py:26
  75.2 14.7 %collective-permute-start.3 = (f32[256,256]{1,0:T(8,128)S(1)}, f32[256,256]{1,0:T(8,128)S(1)}, u32[]{:S(2)}, u32[]{:S(2)}) collective-permute-start(f32[256,256]{1,0:T(8,128)S(1)} %get-tuple-element.22), channel_id=1, source_target_pairs={{0,4},{2,6},{4,0},{6,2},{1,5},{3,7},{5,1},{7,3},{8,12},{10,14},{12... | collective-permute-start | bytes 786440 | tf_op jit(solution)/shard_map/ppermute | solution.py:26
  79.1 10.8 %collective-permute-start.4 = (f32[256,256]{1,0:T(8,128)S(1)}, f32[256,256]{1,0:T(8,128)S(1)}, u32[]{:S(2)}, u32[]{:S(2)}) collective-permute-start(f32[256,256]{1,0:T(8,128)S(1)} %get-tuple-element.23), channel_id=1, source_target_pairs={{0,6},{2,0},{4,2},{6,4},{1,7},{3,1},{5,3},{7,5},{8,14},{10,8},{12,... | collective-permute-start | bytes 786440 | tf_op jit(solution)/shard_map/ppermute | solution.py:26
  86.3 16.9 %all-to-all-start.4 = ((f32[16,24,128]{2,1,0:T(8,128)}), f32[16,24,128]{2,1,0:T(8,128)S(1)}, u32[]{:S(2)}, u32[]{:S(2)}) async-start(f32[16,24,128]{2,1,0:T(8,128)} %broadcast_in_dim.11), calls=%async_computation.4 | async-start | bytes 393216 | tf_op jit(solution)/shard_map/all_to_all | solution.py:17
  90.0 9.8 %collective-permute-start.5 = (f32[64,256]{1,0:T(8,128)S(1)}, f32[64,256]{1,0:T(8,128)S(1)}, u32[]{:S(2)}, u32[]{:S(2)}) collective-permute-start(f32[64,256]{1,0:T(8,128)S(1)} %get-tuple-element.25), channel_id=1, source_target_pairs={{0,8},{8,16},{16,24},{24,0},{1,9},{9,17},{17,25},{25,1},{2,10},{10... | collective-permute-start | bytes 196616 | tf_op jit(solution)/shard_map/ppermute | solution.py:26
  93.4 6.6 %collective-permute-start.6 = (f32[64,256]{1,0:T(8,128)S(1)}, f32[64,256]{1,0:T(8,128)S(1)}, u32[]{:S(2)}, u32[]{:S(2)}) collective-permute-start(f32[64,256]{1,0:T(8,128)S(1)} %get-tuple-element.26), channel_id=1, source_target_pairs={{0,16},{8,24},{16,0},{24,8},{1,17},{9,25},{17,1},{25,9},{2,18},{10... | collective-permute-start | bytes 196616 | tf_op jit(solution)/shard_map/ppermute | solution.py:26
  97.4 5.3 %collective-permute-start.7 = (f32[64,256]{1,0:T(8,128)S(1)}, f32[64,256]{1,0:T(8,128)S(1)}, u32[]{:S(2)}, u32[]{:S(2)}) collective-permute-start(f32[64,256]{1,0:T(8,128)S(1)} %get-tuple-element.27), channel_id=1, source_target_pairs={{0,24},{8,0},{16,8},{24,16},{1,25},{9,1},{17,9},{25,17},{2,26},{10... | collective-permute-start | bytes 196616 | tf_op jit(solution)/shard_map/ppermute | solution.py:26
  103.3 8.3 %copy-start.1 = (f32[256,256]{1,0:T(8,128)S(1)}, f32[256,256]{1,0:T(8,128)}, u32[]{:S(2)}) copy-start(f32[256,256]{1,0:T(8,128)} %inv_one.1) | copy-start | bytes 786436
  103.3 8.3 %copy-start.2 = (f32[256,256]{1,0:T(8,128)S(1)}, f32[256,256]{1,0:T(8,128)}, u32[]{:S(2)}) copy-start(f32[256,256]{1,0:T(8,128)} %inv_two.1) | copy-start | bytes 786436

commit v16 on v15

--- a/solution.py
+++ b/solution.py
@@ -5,12 +5,17 @@
 from jax.experimental.pallas import tpu as pltpu
 from jax.sharding import Mesh, PartitionSpec as P
 
-AXES = ("x", "zh", "zl", "y", "core")
-SIZES = (4, 4, 4, 4, 2)
+AXES = ("x", "zh", "zl", "yh", "yl", "core")
+SIZES = (4, 4, 4, 2, 2, 2)
+Y = ("yh", "yl")
 SWAP = [(0, 1), (1, 0)]
 VMEM = pl.BlockSpec(memory_space=pltpu.VMEM)
 SMEM = pl.BlockSpec(memory_space=pltpu.SMEM)
 PARAMS = pltpu.CompilerParams(vmem_limit_bytes=32 * 1024 * 1024)
+
+
+def y_index():
+    return lax.axis_index("yh") * 2 + lax.axis_index("yl")
 
 
 def exchange(parts, axes):
@@ -47,7 +52,7 @@
 
 
 def multiply_kernel(pool, sibling, strip, rows, diag, out0, out1, out2, out3, rhs, full):
-    core, y = lax.axis_index("core"), lax.axis_index("y")
+    core, y = lax.axis_index("core"), y_index()
     shift = lax.axis_index("zl") - y + 2
     depth = rhs.shape[0] // 2
     for side, which in ((0, core), (1, 1 - core)):
@@ -64,7 +69,7 @@
             full[j, z * 64 : (z + 1) * 64] = block[j * 64 : (j + 1) * 64]
     term = jnp.zeros((256, 256), jnp.float32)
     for j in range(4):
-        left, rest = rows[j], full[j]
+        left, rest = rows[(j & 1) * 2 + (j >> 1)], full[j]
         for _ in range(3):
             piece = rest.astype(jnp.bfloat16)
             rest = rest - piece.astype(jnp.float32)
@@ -141,7 +146,8 @@
     rows = rows * mask.astype(jnp.bfloat16)[:, None, None]
     rows = lax.optimization_barrier(rows)
     turned = lax.ppermute(rows, AXES, TURN)
-    around = lax.all_gather(rows.reshape(256, width), "y")
+    around = lax.all_gather(rows.reshape(256, width), "yh")
+    around = lax.all_gather(around, "yl").reshape(4, 256, width)
     turned, around = lax.optimization_barrier((turned, around))
     strip = gather(turned, "x", 4)
 
@@ -152,8 +158,8 @@
         (inverse_pool, sibling_pool, strip, around),
         [pltpu.VMEM((1024, width), jnp.bfloat16), pltpu.VMEM((4, 256, width), f32)],
     )
-    shard = jnp.sum(exchange(diag.reshape(16, 24, 128), ("x", "y")), axis=0)
-    parts = rotate(parts, "y")
+    shard = jnp.sum(exchange(diag.reshape(16, 24, 128), ("x", *Y)), axis=0)
+    parts = rotate(parts, Y)
     shard = jnp.sum(gather(shard, ("zh", "zl"), 16), axis=0)
     parts = call(
         turn_kernel,
@@ -164,7 +170,7 @@
     parts = rotate(parts, "zl")
     half = jax.ShapeDtypeStruct((2 * row_count, 128), f32)
     stay, leave = call(split_kernel, [half, half], (mask, *parts), scalars=1)
-    total = gather(shard, ("x", "y"), 16).reshape(384, 128)
+    total = gather(shard, ("x", *Y), 16).reshape(384, 128)
     finals = lax.all_gather(jnp.concatenate([total, leave]), "core")
     wide = jax.ShapeDtypeStruct((row_count, width), jnp.bfloat16)
     square = jax.ShapeDtypeStruct((width, width), f32)
@@ -180,7 +186,7 @@
 def solution(mesh):
     fine = Mesh(mesh.devices.reshape(SIZES), AXES)
     rows = P(AXES, None)
-    in_specs = (P(("x", "zh"), ("zl", "y", "core")), rows, rows, P(), P(), P(), P())
+    in_specs = (P(("x", "zh"), ("zl", *Y, "core")), rows, rows, P(), P(), P(), P())
     out_specs = (rows, rows, P(), P())
     return jax.shard_map(
         per_device, mesh=fine, in_specs=in_specs, out_specs=out_specs, check_vma=False

time: 113 us -> 116 us (1.027)
  blocking collectives: 39.9 us -> 44.8 us
  starting transfers between devices: 54.9 us -> 52.3 us
    all_to_all x2, blocking collectives: 21.2 us -> 25.1 us  [exchange(): return lax.all_to_all(parts, axes, 0, 0)]
    all_to_all x3, starting transfers between devices: 24.7 us -> 22 us  [exchange(): return lax.all_to_all(parts, axes, 0, 0)]
    all_gather x1 -> x2, blocking collectives: 10.4 us -> 11.9 us  [the longest x1 6 us: per_device(): around = lax.all_gather(rows.reshape(256, width), 'yh')]
where the time goes in v16:
time: 116 us; the launch traced here: 115 us
  starting transfers between devices  52.3 us (45%)
  blocking collectives  44.8 us (39%)
  waiting for transfers between devices  9.56 us (8%)
  Pallas kernels  3.71 us (3%)
  local copies, waits for them, and re-layouts  2.76 us (2%)
    all_to_all x2, blocking collectives, exchange(): return lax.all_to_all(parts, axes, 0, 0)  25.1 us
    all_to_all x3, starting transfers between devices, exchange(): return lax.all_to_all(parts, axes, 0, 0)  22 us
    ppermute x6, starting transfers between devices, rotate(): lax.ppermute(parts[s], axis, [(i, (i + s) % 4) for i in range(4)])  18.7 us
    ppermute x1, starting transfers between devices, per_device(): turned = lax.ppermute(rows, AXES, TURN)  9.54 us
    all_gather x1, blocking collectives, per_device(): finals = lax.all_gather(jnp.concatenate([total, leave]), 'core')  7.85 us
    all_to_all x3, waiting for transfers between devices, exchange(): return lax.all_to_all(parts, axes, 0, 0)  6.38 us
    all_gather x1, blocking collectives, per_device(): around = lax.all_gather(rows.reshape(256, width), 'yh')  6 us
    all_gather x1, blocking collectives, per_device(): around = lax.all_gather(around, 'yl').reshape(4, 256, width)  5.89 us
  transfers between devices with their start and end apart: 11, of which 4 were waited for; matrix products, arithmetic and copies ran while one was open for 1% of the time, Pallas kernels for 1%

profile of v16, /device:TPU:1, one launch (start us, length us, event | category | flops | bytes accessed | tf_op | source)
XLA Modules:
  0.0 115.0 jit_solution(6446591603134657850)
XLA Ops:
  0.6 0.7 pad_maximum_fusion.1
  1.4 0.7 broadcast_in_dim.8
  2.0 10.2 %all-to-all-start = ((bf16[8,32,256]{2,1,0:T(8,128)(2,1)}), bf16[8,32,256]{2,1,0:T(8,128)(2,1)S(1)}, u32[]{:S(2)}, u32[]{:S(2)}) async-start(bf16[8,32,256]{2,1,0:T(8,128)(2,1)} %bitcast.2), calls=%async_computation | async-start | bytes 262144 | tf_op jit(solution)/shard_map/all_to_all | solution.py:22
  12.2 2.0 %collective-permute-start = (bf16[1024,512]{1,0:T(8,128)(2,1)}, bf16[1024,512]{1,0:T(8,128)(2,1)S(1)}, u32[]{:S(2)}, u32[]{:S(2)}) collective-permute-start(bf16[1024,512]{1,0:T(8,128)(2,1)} %pool.1), channel_id=1, source_target_pairs={{0,1},{1,0},{2,3},{3,2},{4,5},{5,4},{6,7},{7,6},{8,9},{9,8},{10,11... | collective-permute-start | bytes 3145736 | tf_op jit(solution)/shard_map/ppermute | solution.py:140
  14.2 0.0 copy-start.3
  14.2 0.0 copy-start.4
  14.2 0.6 copy-done.3
  14.9 0.0 copy-done.4
  14.9 0.1 fusion
  15.0 3.0 %all-to-all-done = bf16[8,32,256]{2,1,0:T(8,128)(2,1)S(1)} async-done(((bf16[8,32,256]{2,1,0:T(8,128)(2,1)}), bf16[8,32,256]{2,1,0:T(8,128)(2,1)S(1)}, u32[]{:S(2)}, u32[]{:S(2)}) %all-to-all-start) | async-done | bytes 131104 | tf_op jit(solution)/shard_map/all_to_all | solution.py:22
  18.0 0.1 bitcast_multiply_fusion
  18.1 9.5 %collective-permute-start.1 = (bf16[4,64,256]{2,1,0:T(8,128)(2,1)S(1)}, bf16[4,64,256]{2,1,0:T(8,128)(2,1)S(1)}, u32[]{:S(2)}, u32[]{:S(2)}) collective-permute-start(bf16[4,64,256]{2,1,0:T(8,128)(2,1)S(1)} %bitcast_multiply_fusion), channel_id=1, source_target_pairs={{12,0},{13,1},{38,2},{39,3},{88,4},{89,5},{114,6},{115,7},{138,8},... | collective-permute-start | bytes 393224 | tf_op jit(solution)/shard_map/ppermute | solution.py:148
  27.7 6.0 %all_gather.15 = bf16[2,256,256]{2,1,0:T(8,128)(2,1)S(1)} all-gather(bf16[1,256,256]{2,1,0:T(8,128)(2,1)S(1)} %bitcast.13), channel_id=1, replica_groups=mesh['x'=4,'zh'=4,'zl'=4,'yh'=2,'yl'=2,'core'=2] {'yh'}, dimensions={0}, use_global_device_ids=true | all-gather | bytes 393216 | tf_op jit(solution)/shard_map/all_gather | solution.py:149
  33.7 5.9 %all-gather.rows = bf16[4,256,256]{2,1,0:T(8,128)(2,1)S(1)} all-gather(bf16[2,256,256]{2,1,0:T(8,128)(2,1)S(1)} %all_gather.15), channel_id=2, replica_groups=mesh['x'=4,'zh'=4,'zl'=4,'yh'=2,'yl'=2,'core'=2] {'yl'}, dimensions={0}, use_global_device_ids=true | all-gather | bytes 786432 | tf_op jit(solution)/shard_map/all_gather | solution.py:150
  39.6 0.0 copy-start
  39.6 0.0 collective-permute-done.1
  39.6 15.3 %all_to_all.25.strip = bf16[4,4,64,256]{3,2,1,0:T(8,128)(2,1)S(1)} all-to-all(bf16[4,4,64,256]{3,2,1,0:T(8,128)(2,1)S(1)} %broadcast_in_dim.9), channel_id=1, replica_groups=mesh['x'=4,'zh'=4,'zl'=4,'yh'=2,'yl'=2,'core'=2] {'x'}, dimensions={0} | all-to-all | bytes 1048576 | tf_op jit(solution)/shard_map/all_to_all | solution.py:22
  54.9 0.0 collective-permute-done.sibling
  54.9 0.0 copy-done
  54.9 2.2 %shard_map.102 = (f32[384,128]{1,0:T(8,128)S(1)}, f32[256,256]{1,0:T(8,128)S(1)}, f32[256,256]{1,0:T(8,128)S(1)}, f32[256,256]{1,0:T(8,128)S(1)}, f32[256,256]{1,0:T(8,128)S(1)}) custom-call(bf16[1024,512]{1,0:T(8,128)(2,1)S(1)} %copy-done, bf16[1024,512]{1,0:T(8,128)(2,1)S(1)} %collective-permute-done.sibling, ...), custom_call_target="tpu_custom_call" | custom-call | tf_op jit(solution)/shard_map/pallas_call | solution.py:121
  57.1 9.8 %all_to_all.26 = f32[16,24,128]{2,1,0:T(8,128)S(1)} all-to-all(f32[16,24,128]{2,1,0:T(8,128)S(1)} %bitcast.11), channel_id=1, replica_groups=mesh['x'=4,'zh'=4,'zl'=4,'yh'=2,'yl'=2,'core'=2] {'x','yh','yl'}, dimensions={0} | all-to-all | bytes 393216 | tf_op jit(solution)/shard_map/all_to_all | solution.py:22
  66.9 0.7 broadcast_in_dim.10
  67.6 8.2 %all-to-all-start.3 = ((f32[16,24,128]{2,1,0:T(8,128)}), f32[16,24,128]{2,1,0:T(8,128)S(1)}, u32[]{:S(2)}, u32[]{:S(2)}) async-start(f32[16,24,128]{2,1,0:T(8,128)} %broadcast_in_dim.10), calls=%async_computation.3 | async-start | bytes 393216 | tf_op jit(solution)/shard_map/all_to_all | solution.py:22
  75.8 2.1 %collective-permute-start.2 = (f32[256,256]{1,0:T(8,128)S(1)}, f32[256,256]{1,0:T(8,128)S(1)}, u32[]{:S(2)}, u32[]{:S(2)}) collective-permute-start(f32[256,256]{1,0:T(8,128)S(1)} %get-tuple-element.21), channel_id=1, source_target_pairs={{0,2},{2,4},{4,6},{6,0},{1,3},{3,5},{5,7},{7,1},{8,10},{10,12},{12... | collective-permute-start | bytes 786440 | tf_op jit(solution)/shard_map/ppermute | solution.py:31
  77.9 3.7 %collective-permute-start.3 = (f32[256,256]{1,0:T(8,128)S(1)}, f32[256,256]{1,0:T(8,128)S(1)}, u32[]{:S(2)}, u32[]{:S(2)}) collective-permute-start(f32[256,256]{1,0:T(8,128)S(1)} %get-tuple-element.22), channel_id=1, source_target_pairs={{0,4},{2,6},{4,0},{6,2},{1,5},{3,7},{5,1},{7,3},{8,12},{10,14},{12... | collective-permute-start | bytes 786440 | tf_op jit(solution)/shard_map/ppermute | solution.py:31
  81.6 3.2 %collective-permute-start.4 = (f32[256,256]{1,0:T(8,128)S(1)}, f32[256,256]{1,0:T(8,128)S(1)}, u32[]{:S(2)}, u32[]{:S(2)}) collective-permute-start(f32[256,256]{1,0:T(8,128)S(1)} %get-tuple-element.23), channel_id=1, source_target_pairs={{0,6},{2,0},{4,2},{6,4},{1,7},{3,1},{5,3},{7,5},{8,14},{10,8},{12,... | collective-permute-start | bytes 786440 | tf_op jit(solution)/shard_map/ppermute | solution.py:31
  84.8 3.3 %all-to-all-done.3 = f32[16,24,128]{2,1,0:T(8,128)S(1)} async-done(((f32[16,24,128]{2,1,0:T(8,128)}), f32[16,24,128]{2,1,0:T(8,128)S(1)}, u32[]{:S(2)}, u32[]{:S(2)}) %all-to-all-start.3) | async-done | bytes 196640 | tf_op jit(solution)/shard_map/all_to_all | solution.py:22
  88.2 0.7 broadcast_in_dim.11
  88.9 3.7 %all-to-all-start.4 = ((f32[16,24,128]{2,1,0:T(8,128)}), f32[16,24,128]{2,1,0:T(8,128)S(1)}, u32[]{:S(2)}, u32[]{:S(2)}) async-start(f32[16,24,128]{2,1,0:T(8,128)} %broadcast_in_dim.11), calls=%async_computation.4 | async-start | bytes 393216 | tf_op jit(solution)/shard_map/all_to_all | solution.py:22
  92.5 0.0 collective-permute-done.2.in1
  92.5 0.0 collective-permute-done.3.in2
  92.6 0.0 collective-permute-done.4.in3
  92.6 0.1 shard_map.103
  92.7 3.4 %collective-permute-start.5 = (f32[64,256]{1,0:T(8,128)S(1)}, f32[64,256]{1,0:T(8,128)S(1)}, u32[]{:S(2)}, u32[]{:S(2)}) collective-permute-start(f32[64,256]{1,0:T(8,128)S(1)} %get-tuple-element.25), channel_id=1, source_target_pairs={{0,8},{8,16},{16,24},{24,0},{1,9},{9,17},{17,25},{25,1},{2,10},{10... | collective-permute-start | bytes 196616 | tf_op jit(solution)/shard_map/ppermute | solution.py:31
  96.0 4.2 %collective-permute-start.6 = (f32[64,256]{1,0:T(8,128)S(1)}, f32[64,256]{1,0:T(8,128)S(1)}, u32[]{:S(2)}, u32[]{:S(2)}) collective-permute-start(f32[64,256]{1,0:T(8,128)S(1)} %get-tuple-element.26), channel_id=1, source_target_pairs={{0,16},{8,24},{16,0},{24,8},{1,17},{9,25},{17,1},{25,9},{2,18},{10... | collective-permute-start | bytes 196616 | tf_op jit(solution)/shard_map/ppermute | solution.py:31
  100.3 2.1 %collective-permute-start.7 = (f32[64,256]{1,0:T(8,128)S(1)}, f32[64,256]{1,0:T(8,128)S(1)}, u32[]{:S(2)}, u32[]{:S(2)}) collective-permute-start(f32[64,256]{1,0:T(8,128)S(1)} %get-tuple-element.27), channel_id=1, source_target_pairs={{0,24},{8,0},{16,8},{24,16},{1,25},{9,1},{17,9},{25,17},{2,26},{10... | collective-permute-start | bytes 196616 | tf_op jit(solution)/shard_map/ppermute | solution.py:31
  102.4 0.0 collective-permute-done.5.in1
  102.4 0.2 collective-permute-done.6.in2
  102.7 2.9 %collective-permute-done.7.in3 = f32[64,256]{1,0:T(8,128)S(1)} collective-permute-done((f32[64,256]{1,0:T(8,128)S(1)}, f32[64,256]{1,0:T(8,128)S(1)}, u32[]{:S(2)}, u32[]{:S(2)}) %collective-permute-start.7) | collective-permute-done | bytes 65568 | tf_op jit(solution)/shard_map/ppermute | solution.py:31
  105.6 0.6 shard_map.104
  106.1 0.0 all-to-all-done.4
  106.2 0.0 copy-start.1
  106.2 0.0 copy-start.2
  106.2 7.8 %all-gather.1 = f32[896,128]{1,0:T(8,128)S(1)} all-gather(f32[448,128]{1,0:T(8,128)S(1)} %pad_maximum_fusion), channel_id=3, replica_groups=mesh['x'=4,'zh'=4,'zl'=4,'yh'=2,'yl'=2,'core'=2] {'core'}, dimensions={0}, use_global_device_ids=true | all-gather | bytes 688128 | tf_op jit(solution)/shard_map/all_gather | solution.py:174
  114.1 0.0 copy-done.1
  114.1 0.0 copy-done.2
  114.1 0.9 shard_map.105
  (5 shorter events, 0.1 us)
Async XLA Ops:
  2.0 16.0 %all-to-all-start = ((bf16[8,32,256]{2,1,0:T(8,128)(2,1)}), bf16[8,32,256]{2,1,0:T(8,128)(2,1)S(1)}, u32[]{:S(2)}, u32[]{:S(2)}) async-start(bf16[8,32,256]{2,1,0:T(8,128)(2,1)} %bitcast.2), calls=%async_computation | async-start | bytes 262144 | tf_op jit(solution)/shard_map/all_to_all | solution.py:22
  12.2 42.7 %collective-permute-start = (bf16[1024,512]{1,0:T(8,128)(2,1)}, bf16[1024,512]{1,0:T(8,128)(2,1)S(1)}, u32[]{:S(2)}, u32[]{:S(2)}) collective-permute-start(bf16[1024,512]{1,0:T(8,128)(2,1)} %pool.1), channel_id=1, source_target_pairs={{0,1},{1,0},{2,3},{3,2},{4,5},{5,4},{6,7},{7,6},{8,9},{9,8},{10,11... | collective-permute-start | bytes 3145736 | tf_op jit(solution)/shard_map/ppermute | solution.py:140
  14.2 0.7 copy-start.3
  14.2 0.7 copy-start.4
  18.1 21.4 %collective-permute-start.1 = (bf16[4,64,256]{2,1,0:T(8,128)(2,1)S(1)}, bf16[4,64,256]{2,1,0:T(8,128)(2,1)S(1)}, u32[]{:S(2)}, u32[]{:S(2)}) collective-permute-start(bf16[4,64,256]{2,1,0:T(8,128)(2,1)S(1)} %bitcast_multiply_fusion), channel_id=1, source_target_pairs={{12,0},{13,1},{38,2},{39,3},{88,4},{89,5},{114,6},{115,7},{138,8},... | collective-permute-start | bytes 393224 | tf_op jit(solution)/shard_map/ppermute | solution.py:148
  39.6 15.4 %copy-start = (bf16[1024,512]{1,0:T(8,128)(2,1)S(1)}, bf16[1024,512]{1,0:T(8,128)(2,1)}, u32[]{:S(2)}) copy-start(bf16[1024,512]{1,0:T(8,128)(2,1)} %pool.1) | copy-start | bytes 3145732
  67.6 20.6 %all-to-all-start.3 = ((f32[16,24,128]{2,1,0:T(8,128)}), f32[16,24,128]{2,1,0:T(8,128)S(1)}, u32[]{:S(2)}, u32[]{:S(2)}) async-start(f32[16,24,128]{2,1,0:T(8,128)} %broadcast_in_dim.10), calls=%async_computation.3 | async-start | bytes 393216 | tf_op jit(solution)/shard_map/all_to_all | solution.py:22
  75.8 16.7 %collective-permute-start.2 = (f32[256,256]{1,0:T(8,128)S(1)}, f32[256,256]{1,0:T(8,128)S(1)}, u32[]{:S(2)}, u32[]{:S(2)}) collective-permute-start(f32[256,256]{1,0:T(8,128)S(1)} %get-tuple-element.21), channel_id=1, source_target_pairs={{0,2},{2,4},{4,6},{6,0},{1,3},{3,5},{5,7},{7,1},{8,10},{10,12},{12... | collective-permute-start | bytes 786440 | tf_op jit(solution)/shard_map/ppermute | solution.py:31
  77.9 14.6 %collective-permute-start.3 = (f32[256,256]{1,0:T(8,128)S(1)}, f32[256,256]{1,0:T(8,128)S(1)}, u32[]{:S(2)}, u32[]{:S(2)}) collective-permute-start(f32[256,256]{1,0:T(8,128)S(1)} %get-tuple-element.22), channel_id=1, source_target_pairs={{0,4},{2,6},{4,0},{6,2},{1,5},{3,7},{5,1},{7,3},{8,12},{10,14},{12... | collective-permute-start | bytes 786440 | tf_op jit(solution)/shard_map/ppermute | solution.py:31
  81.6 10.9 %collective-permute-start.4 = (f32[256,256]{1,0:T(8,128)S(1)}, f32[256,256]{1,0:T(8,128)S(1)}, u32[]{:S(2)}, u32[]{:S(2)}) collective-permute-start(f32[256,256]{1,0:T(8,128)S(1)} %get-tuple-element.23), channel_id=1, source_target_pairs={{0,6},{2,0},{4,2},{6,4},{1,7},{3,1},{5,3},{7,5},{8,14},{10,8},{12,... | collective-permute-start | bytes 786440 | tf_op jit(solution)/shard_map/ppermute | solution.py:31
  88.9 17.3 %all-to-all-start.4 = ((f32[16,24,128]{2,1,0:T(8,128)}), f32[16,24,128]{2,1,0:T(8,128)S(1)}, u32[]{:S(2)}, u32[]{:S(2)}) async-start(f32[16,24,128]{2,1,0:T(8,128)} %broadcast_in_dim.11), calls=%async_computation.4 | async-start | bytes 393216 | tf_op jit(solution)/shard_map/all_to_all | solution.py:22
  92.7 9.7 %collective-permute-start.5 = (f32[64,256]{1,0:T(8,128)S(1)}, f32[64,256]{1,0:T(8,128)S(1)}, u32[]{:S(2)}, u32[]{:S(2)}) collective-permute-start(f32[64,256]{1,0:T(8,128)S(1)} %get-tuple-element.25), channel_id=1, source_target_pairs={{0,8},{8,16},{16,24},{24,0},{1,9},{9,17},{17,25},{25,1},{2,10},{10... | collective-permute-start | bytes 196616 | tf_op jit(solution)/shard_map/ppermute | solution.py:31
  96.0 6.6 %collective-permute-start.6 = (f32[64,256]{1,0:T(8,128)S(1)}, f32[64,256]{1,0:T(8,128)S(1)}, u32[]{:S(2)}, u32[]{:S(2)}) collective-permute-start(f32[64,256]{1,0:T(8,128)S(1)} %get-tuple-element.26), channel_id=1, source_target_pairs={{0,16},{8,24},{16,0},{24,8},{1,17},{9,25},{17,1},{25,9},{2,18},{10... | collective-permute-start | bytes 196616 | tf_op jit(solution)/shard_map/ppermute | solution.py:31
  100.3 5.3 %collective-permute-start.7 = (f32[64,256]{1,0:T(8,128)S(1)}, f32[64,256]{1,0:T(8,128)S(1)}, u32[]{:S(2)}, u32[]{:S(2)}) collective-permute-start(f32[64,256]{1,0:T(8,128)S(1)} %get-tuple-element.27), channel_id=1, source_target_pairs={{0,24},{8,0},{16,8},{24,16},{1,25},{9,1},{17,9},{25,17},{2,26},{10... | collective-permute-start | bytes 196616 | tf_op jit(solution)/shard_map/ppermute | solution.py:31
  106.2 7.9 %copy-start.1 = (f32[256,256]{1,0:T(8,128)S(1)}, f32[256,256]{1,0:T(8,128)}, u32[]{:S(2)}) copy-start(f32[256,256]{1,0:T(8,128)} %inv_one.1) | copy-start | bytes 786436
  106.2 7.9 %copy-start.2 = (f32[256,256]{1,0:T(8,128)S(1)}, f32[256,256]{1,0:T(8,128)}, u32[]{:S(2)}) copy-start(f32[256,256]{1,0:T(8,128)} %inv_two.1) | copy-start | bytes 786436

commit v17 on v15

--- a/solution.py
+++ b/solution.py
@@ -23,7 +23,7 @@
 
 def rotate(parts, axis):
     return [parts[0]] + [
-        lax.ppermute(parts[s], axis, [(i, (i + s) % 4) for i in range(4)]) for s in (1, 2, 3)
+        lax.ppermute(parts[s], axis, [(i, i ^ s) for i in range(4)]) for s in (1, 2, 3)
     ]
 
 
@@ -75,14 +75,14 @@
     diag[128:256] = term[:128, 128:]
     diag[256:384] = term[128:, 128:]
     for hop, out in enumerate((out0, out1, out2, out3)):
-        out[...] = full[(y + hop) & 3]
+        out[...] = full[y ^ hop]
 
 
 def turn_kernel(in0, in1, in2, in3, out0, out1, out2, out3, full):
     zl = lax.axis_index("zl")
     full[...] = in0[...] + in1[...] + in2[...] + in3[...]
     for hop, out in enumerate((out0, out1, out2, out3)):
-        out[...] = full[pl.ds(pl.multiple_of(((zl + hop) & 3) * 64, 64), 64)]
+        out[...] = full[pl.ds(pl.multiple_of((zl ^ hop) * 64, 64), 64)]
 
 
 def split_kernel(mask, in0, in1, in2, in3, stay, leave):

time: 113 us -> 115 us (1.018)
  waiting for transfers between devices: 9.4 us -> 12.3 us
  blocking collectives: 39.9 us -> 38 us
    ppermute x6, waiting for transfers between devices: 2.94 us -> 6.5 us  [rotate(): lax.ppermute(parts[s], axis, [(i, i ^ s) for i in range(4)])]
    all_gather x1, blocking collectives: 8.28 us -> 6.43 us  [per_device(): finals = lax.all_gather(jnp.concatenate([total, leave]), 'core')]
  transfers between devices with their start and end apart: 11 -> 11, of which waited for: 4 -> 5; matrix products, arithmetic and copies ran while one was open for 1% -> 1% of each run, Pallas kernels for 1% -> 1%
where the time goes in v17:
time: 115 us; the launch traced here: 114 us
  starting transfers between devices  55.1 us (48%)
  blocking collectives  38 us (33%)
  waiting for transfers between devices  12.3 us (11%)
  Pallas kernels  3.69 us (3%)
  local copies, waits for them, and re-layouts  2.77 us (2%)
    all_to_all x3, starting transfers between devices, exchange(): return lax.all_to_all(parts, axes, 0, 0)  24.7 us
    all_to_all x2, blocking collectives, exchange(): return lax.all_to_all(parts, axes, 0, 0)  21.2 us
    ppermute x6, starting transfers between devices, rotate(): lax.ppermute(parts[s], axis, [(i, i ^ s) for i in range(4)])  18.9 us
    all_gather x1, blocking collectives, per_device(): around = lax.all_gather(rows.reshape(256, width), 'y')  10.4 us
    ppermute x1, starting transfers between devices, per_device(): turned = lax.ppermute(rows, AXES, TURN)  9.54 us
    ppermute x6, waiting for transfers between devices, rotate(): lax.ppermute(parts[s], axis, [(i, i ^ s) for i in range(4)])  6.5 us
    all_gather x1, blocking collectives, per_device(): finals = lax.all_gather(jnp.concatenate([total, leave]), 'core')  6.43 us
    all_to_all x3, waiting for transfers between devices, exchange(): return lax.all_to_all(parts, axes, 0, 0)  5.78 us
  transfers between devices with their start and end apart: 11, of which 5 were waited for; matrix products, arithmetic and copies ran while one was open for 1% of the time, Pallas kernels for 1%

profile of v17, /device:TPU:1, one launch (start us, length us, event | category | flops | bytes accessed | tf_op | source)
XLA Modules:
  0.0 113.7 jit_solution(16757843528485326529)
XLA Ops:
  0.6 0.7 pad_maximum_fusion.1
  1.4 0.7 broadcast_in_dim.8
  2.0 10.2 %all-to-all-start = ((bf16[8,32,256]{2,1,0:T(8,128)(2,1)}), bf16[8,32,256]{2,1,0:T(8,128)(2,1)S(1)}, u32[]{:S(2)}, u32[]{:S(2)}) async-start(bf16[8,32,256]{2,1,0:T(8,128)(2,1)} %bitcast.2), calls=%async_computation | async-start | bytes 262144 | tf_op jit(solution)/shard_map/all_to_all | solution.py:17
  12.2 2.0 %collective-permute-start = (bf16[1024,512]{1,0:T(8,128)(2,1)}, bf16[1024,512]{1,0:T(8,128)(2,1)S(1)}, u32[]{:S(2)}, u32[]{:S(2)}) collective-permute-start(bf16[1024,512]{1,0:T(8,128)(2,1)} %pool.1), channel_id=1, source_target_pairs={{0,1},{1,0},{2,3},{3,2},{4,5},{5,4},{6,7},{7,6},{8,9},{9,8},{10,11... | collective-permute-start | bytes 3145736 | tf_op jit(solution)/shard_map/ppermute | solution.py:135
  14.2 0.0 copy-start.3
  14.2 0.0 copy-start.4
  14.2 0.6 copy-done.3
  14.9 0.0 copy-done.4
  14.9 0.1 fusion
  15.0 3.0 %all-to-all-done = bf16[8,32,256]{2,1,0:T(8,128)(2,1)S(1)} async-done(((bf16[8,32,256]{2,1,0:T(8,128)(2,1)}), bf16[8,32,256]{2,1,0:T(8,128)(2,1)S(1)}, u32[]{:S(2)}, u32[]{:S(2)}) %all-to-all-start) | async-done | bytes 131104 | tf_op jit(solution)/shard_map/all_to_all | solution.py:17
  18.0 0.1 bitcast_multiply_fusion
  18.1 9.5 %collective-permute-start.1 = (bf16[4,64,256]{2,1,0:T(8,128)(2,1)S(1)}, bf16[4,64,256]{2,1,0:T(8,128)(2,1)S(1)}, u32[]{:S(2)}, u32[]{:S(2)}) collective-permute-start(bf16[4,64,256]{2,1,0:T(8,128)(2,1)S(1)} %bitcast_multiply_fusion), channel_id=1, source_target_pairs={{12,0},{13,1},{38,2},{39,3},{88,4},{89,5},{114,6},{115,7},{138,8},... | collective-permute-start | bytes 393224 | tf_op jit(solution)/shard_map/ppermute | solution.py:143
  27.7 0.0 copy-start
  27.7 10.4 %all_gather.9.rows = bf16[4,256,256]{2,1,0:T(8,128)(2,1)S(1)} all-gather(bf16[1,256,256]{2,1,0:T(8,128)(2,1)S(1)} %bitcast.13), channel_id=1, replica_groups=mesh['x'=4,'zh'=4,'zl'=4,'y'=4,'core'=2] {'y'}, dimensions={0}, use_global_device_ids=true | all-gather | bytes 655360 | tf_op jit(solution)/shard_map/all_gather | solution.py:144
  38.1 0.0 collective-permute-done.1
  38.2 11.0 %all_to_all.25.strip = bf16[4,4,64,256]{3,2,1,0:T(8,128)(2,1)S(1)} all-to-all(bf16[4,4,64,256]{3,2,1,0:T(8,128)(2,1)S(1)} %broadcast_in_dim.9), channel_id=1, replica_groups=mesh['x'=4,'zh'=4,'zl'=4,'y'=4,'core'=2] {'x'}, dimensions={0} | all-to-all | bytes 1048576 | tf_op jit(solution)/shard_map/all_to_all | solution.py:17
  49.2 0.0 collective-permute-done.sibling
  49.2 0.0 copy-done
  49.2 2.2 %shard_map.102 = (f32[384,128]{1,0:T(8,128)S(1)}, f32[256,256]{1,0:T(8,128)S(1)}, f32[256,256]{1,0:T(8,128)S(1)}, f32[256,256]{1,0:T(8,128)S(1)}, f32[256,256]{1,0:T(8,128)S(1)}) custom-call(bf16[1024,512]{1,0:T(8,128)(2,1)S(1)} %copy-done, bf16[1024,512]{1,0:T(8,128)(2,1)S(1)} %collective-permute-done.sibling, ...), custom_call_target="tpu_custom_call" | custom-call | tf_op jit(solution)/shard_map/pallas_call | solution.py:116
  51.4 10.1 %all_to_all.26 = f32[16,24,128]{2,1,0:T(8,128)S(1)} all-to-all(f32[16,24,128]{2,1,0:T(8,128)S(1)} %bitcast.11), channel_id=1, replica_groups=mesh['x'=4,'zh'=4,'zl'=4,'y'=4,'core'=2] {'x','y'}, dimensions={0} | all-to-all | bytes 393216 | tf_op jit(solution)/shard_map/all_to_all | solution.py:17
  61.5 0.7 broadcast_in_dim.10
  62.2 11.0 %all-to-all-start.3 = ((f32[16,24,128]{2,1,0:T(8,128)}), f32[16,24,128]{2,1,0:T(8,128)S(1)}, u32[]{:S(2)}, u32[]{:S(2)}) async-start(f32[16,24,128]{2,1,0:T(8,128)} %broadcast_in_dim.10), calls=%async_computation.3 | async-start | bytes 393216 | tf_op jit(solution)/shard_map/all_to_all | solution.py:17
  73.2 1.9 %collective-permute-start.2 = (f32[256,256]{1,0:T(8,128)S(1)}, f32[256,256]{1,0:T(8,128)S(1)}, u32[]{:S(2)}, u32[]{:S(2)}) collective-permute-start(f32[256,256]{1,0:T(8,128)S(1)} %get-tuple-element.21), channel_id=1, source_target_pairs={{0,2},{2,0},{4,6},{6,4},{1,3},{3,1},{5,7},{7,5},{8,10},{10,8},{12,... | collective-permute-start | bytes 786440 | tf_op jit(solution)/shard_map/ppermute | solution.py:26
  75.2 3.8 %collective-permute-start.3 = (f32[256,256]{1,0:T(8,128)S(1)}, f32[256,256]{1,0:T(8,128)S(1)}, u32[]{:S(2)}, u32[]{:S(2)}) collective-permute-start(f32[256,256]{1,0:T(8,128)S(1)} %get-tuple-element.22), channel_id=1, source_target_pairs={{0,4},{2,6},{4,0},{6,2},{1,5},{3,7},{5,1},{7,3},{8,12},{10,14},{12... | collective-permute-start | bytes 786440 | tf_op jit(solution)/shard_map/ppermute | solution.py:26
  79.0 3.9 %collective-permute-start.4 = (f32[256,256]{1,0:T(8,128)S(1)}, f32[256,256]{1,0:T(8,128)S(1)}, u32[]{:S(2)}, u32[]{:S(2)}) collective-permute-start(f32[256,256]{1,0:T(8,128)S(1)} %get-tuple-element.23), channel_id=1, source_target_pairs={{0,6},{2,4},{4,2},{6,0},{1,7},{3,5},{5,3},{7,1},{8,14},{10,12},{12... | collective-permute-start | bytes 786440 | tf_op jit(solution)/shard_map/ppermute | solution.py:26
  82.8 2.7 %all-to-all-done.3 = f32[16,24,128]{2,1,0:T(8,128)S(1)} async-done(((f32[16,24,128]{2,1,0:T(8,128)}), f32[16,24,128]{2,1,0:T(8,128)S(1)}, u32[]{:S(2)}, u32[]{:S(2)}) %all-to-all-start.3) | async-done | bytes 196640 | tf_op jit(solution)/shard_map/all_to_all | solution.py:17
  85.6 0.7 broadcast_in_dim.11
  86.3 3.5 %all-to-all-start.4 = ((f32[16,24,128]{2,1,0:T(8,128)}), f32[16,24,128]{2,1,0:T(8,128)S(1)}, u32[]{:S(2)}, u32[]{:S(2)}) async-start(f32[16,24,128]{2,1,0:T(8,128)} %broadcast_in_dim.11), calls=%async_computation.4 | async-start | bytes 393216 | tf_op jit(solution)/shard_map/all_to_all | solution.py:17
  89.8 0.0 collective-permute-done.2.in1
  89.8 0.0 collective-permute-done.3.in2
  89.8 2.0 %collective-permute-done.4.in3 = f32[256,256]{1,0:T(8,128)S(1)} collective-permute-done((f32[256,256]{1,0:T(8,128)S(1)}, f32[256,256]{1,0:T(8,128)S(1)}, u32[]{:S(2)}, u32[]{:S(2)}) %collective-permute-start.4) | collective-permute-done | bytes 262176 | tf_op jit(solution)/shard_map/ppermute | solution.py:26
  91.8 0.1 shard_map.103
  91.9 2.9 %collective-permute-start.5 = (f32[64,256]{1,0:T(8,128)S(1)}, f32[64,256]{1,0:T(8,128)S(1)}, u32[]{:S(2)}, u32[]{:S(2)}) collective-permute-start(f32[64,256]{1,0:T(8,128)S(1)} %get-tuple-element.25), channel_id=1, source_target_pairs={{0,8},{8,0},{16,24},{24,16},{1,9},{9,1},{17,25},{25,17},{2,10},{10... | collective-permute-start | bytes 196616 | tf_op jit(solution)/shard_map/ppermute | solution.py:26
  94.8 4.0 %collective-permute-start.6 = (f32[64,256]{1,0:T(8,128)S(1)}, f32[64,256]{1,0:T(8,128)S(1)}, u32[]{:S(2)}, u32[]{:S(2)}) collective-permute-start(f32[64,256]{1,0:T(8,128)S(1)} %get-tuple-element.26), channel_id=1, source_target_pairs={{0,16},{8,24},{16,0},{24,8},{1,17},{9,25},{17,1},{25,9},{2,18},{10... | collective-permute-start | bytes 196616 | tf_op jit(solution)/shard_map/ppermute | solution.py:26
  98.8 2.4 %collective-permute-start.7 = (f32[64,256]{1,0:T(8,128)S(1)}, f32[64,256]{1,0:T(8,128)S(1)}, u32[]{:S(2)}, u32[]{:S(2)}) collective-permute-start(f32[64,256]{1,0:T(8,128)S(1)} %get-tuple-element.27), channel_id=1, source_target_pairs={{0,24},{8,16},{16,8},{24,0},{1,25},{9,17},{17,9},{25,1},{2,26},{10... | collective-permute-start | bytes 196616 | tf_op jit(solution)/shard_map/ppermute | solution.py:26
  101.2 0.0 collective-permute-done.5.in1
  101.2 0.5 collective-permute-done.6.in2
  101.7 4.0 %collective-permute-done.7.in3 = f32[64,256]{1,0:T(8,128)S(1)} collective-permute-done((f32[64,256]{1,0:T(8,128)S(1)}, f32[64,256]{1,0:T(8,128)S(1)}, u32[]{:S(2)}, u32[]{:S(2)}) %collective-permute-start.7) | collective-permute-done | bytes 65568 | tf_op jit(solution)/shard_map/ppermute | solution.py:26
  105.7 0.6 shard_map.104
  106.3 0.0 all-to-all-done.4
  106.3 0.0 copy-start.1
  106.3 0.0 copy-start.2
  106.4 6.4 %all-gather = f32[896,128]{1,0:T(8,128)S(1)} all-gather(f32[448,128]{1,0:T(8,128)S(1)} %pad_maximum_fusion), channel_id=2, replica_groups=mesh['x'=4,'zh'=4,'zl'=4,'y'=4,'core'=2] {'core'}, dimensions={0}, use_global_device_ids=true | all-gather | bytes 688128 | tf_op jit(solution)/shard_map/all_gather | solution.py:168
  112.8 0.0 copy-done.1
  112.8 0.0 copy-done.2
  112.8 0.9 shard_map.105
  (5 shorter events, 0.1 us)
Async XLA Ops:
  2.0 16.0 %all-to-all-start = ((bf16[8,32,256]{2,1,0:T(8,128)(2,1)}), bf16[8,32,256]{2,1,0:T(8,128)(2,1)S(1)}, u32[]{:S(2)}, u32[]{:S(2)}) async-start(bf16[8,32,256]{2,1,0:T(8,128)(2,1)} %bitcast.2), calls=%async_computation | async-start | bytes 262144 | tf_op jit(solution)/shard_map/all_to_all | solution.py:17
  12.2 37.0 %collective-permute-start = (bf16[1024,512]{1,0:T(8,128)(2,1)}, bf16[1024,512]{1,0:T(8,128)(2,1)S(1)}, u32[]{:S(2)}, u32[]{:S(2)}) collective-permute-start(bf16[1024,512]{1,0:T(8,128)(2,1)} %pool.1), channel_id=1, source_target_pairs={{0,1},{1,0},{2,3},{3,2},{4,5},{5,4},{6,7},{7,6},{8,9},{9,8},{10,11... | collective-permute-start | bytes 3145736 | tf_op jit(solution)/shard_map/ppermute | solution.py:135
  14.2 0.7 copy-start.3
  14.2 0.7 copy-start.4
  18.1 20.0 %collective-permute-start.1 = (bf16[4,64,256]{2,1,0:T(8,128)(2,1)S(1)}, bf16[4,64,256]{2,1,0:T(8,128)(2,1)S(1)}, u32[]{:S(2)}, u32[]{:S(2)}) collective-permute-start(bf16[4,64,256]{2,1,0:T(8,128)(2,1)S(1)} %bitcast_multiply_fusion), channel_id=1, source_target_pairs={{12,0},{13,1},{38,2},{39,3},{88,4},{89,5},{114,6},{115,7},{138,8},... | collective-permute-start | bytes 393224 | tf_op jit(solution)/shard_map/ppermute | solution.py:143
  27.7 21.5 %copy-start = (bf16[1024,512]{1,0:T(8,128)(2,1)S(1)}, bf16[1024,512]{1,0:T(8,128)(2,1)}, u32[]{:S(2)}) copy-start(bf16[1024,512]{1,0:T(8,128)(2,1)} %pool.1) | copy-start | bytes 3145732
  62.2 23.4 %all-to-all-start.3 = ((f32[16,24,128]{2,1,0:T(8,128)}), f32[16,24,128]{2,1,0:T(8,128)S(1)}, u32[]{:S(2)}, u32[]{:S(2)}) async-start(f32[16,24,128]{2,1,0:T(8,128)} %broadcast_in_dim.10), calls=%async_computation.3 | async-start | bytes 393216 | tf_op jit(solution)/shard_map/all_to_all | solution.py:17
  73.2 16.6 %collective-permute-start.2 = (f32[256,256]{1,0:T(8,128)S(1)}, f32[256,256]{1,0:T(8,128)S(1)}, u32[]{:S(2)}, u32[]{:S(2)}) collective-permute-start(f32[256,256]{1,0:T(8,128)S(1)} %get-tuple-element.21), channel_id=1, source_target_pairs={{0,2},{2,0},{4,6},{6,4},{1,3},{3,1},{5,7},{7,5},{8,10},{10,8},{12,... | collective-permute-start | bytes 786440 | tf_op jit(solution)/shard_map/ppermute | solution.py:26
  75.2 14.7 %collective-permute-start.3 = (f32[256,256]{1,0:T(8,128)S(1)}, f32[256,256]{1,0:T(8,128)S(1)}, u32[]{:S(2)}, u32[]{:S(2)}) collective-permute-start(f32[256,256]{1,0:T(8,128)S(1)} %get-tuple-element.22), channel_id=1, source_target_pairs={{0,4},{2,6},{4,0},{6,2},{1,5},{3,7},{5,1},{7,3},{8,12},{10,14},{12... | collective-permute-start | bytes 786440 | tf_op jit(solution)/shard_map/ppermute | solution.py:26
  79.0 12.8 %collective-permute-start.4 = (f32[256,256]{1,0:T(8,128)S(1)}, f32[256,256]{1,0:T(8,128)S(1)}, u32[]{:S(2)}, u32[]{:S(2)}) collective-permute-start(f32[256,256]{1,0:T(8,128)S(1)} %get-tuple-element.23), channel_id=1, source_target_pairs={{0,6},{2,4},{4,2},{6,0},{1,7},{3,5},{5,3},{7,1},{8,14},{10,12},{12... | collective-permute-start | bytes 786440 | tf_op jit(solution)/shard_map/ppermute | solution.py:26
  86.3 20.0 %all-to-all-start.4 = ((f32[16,24,128]{2,1,0:T(8,128)}), f32[16,24,128]{2,1,0:T(8,128)S(1)}, u32[]{:S(2)}, u32[]{:S(2)}) async-start(f32[16,24,128]{2,1,0:T(8,128)} %broadcast_in_dim.11), calls=%async_computation.4 | async-start | bytes 393216 | tf_op jit(solution)/shard_map/all_to_all | solution.py:17
  91.9 9.3 %collective-permute-start.5 = (f32[64,256]{1,0:T(8,128)S(1)}, f32[64,256]{1,0:T(8,128)S(1)}, u32[]{:S(2)}, u32[]{:S(2)}) collective-permute-start(f32[64,256]{1,0:T(8,128)S(1)} %get-tuple-element.25), channel_id=1, source_target_pairs={{0,8},{8,0},{16,24},{24,16},{1,9},{9,1},{17,25},{25,17},{2,10},{10... | collective-permute-start | bytes 196616 | tf_op jit(solution)/shard_map/ppermute | solution.py:26
  94.8 6.9 %collective-permute-start.6 = (f32[64,256]{1,0:T(8,128)S(1)}, f32[64,256]{1,0:T(8,128)S(1)}, u32[]{:S(2)}, u32[]{:S(2)}) collective-permute-start(f32[64,256]{1,0:T(8,128)S(1)} %get-tuple-element.26), channel_id=1, source_target_pairs={{0,16},{8,24},{16,0},{24,8},{1,17},{9,25},{17,1},{25,9},{2,18},{10... | collective-permute-start | bytes 196616 | tf_op jit(solution)/shard_map/ppermute | solution.py:26
  98.8 6.9 %collective-permute-start.7 = (f32[64,256]{1,0:T(8,128)S(1)}, f32[64,256]{1,0:T(8,128)S(1)}, u32[]{:S(2)}, u32[]{:S(2)}) collective-permute-start(f32[64,256]{1,0:T(8,128)S(1)} %get-tuple-element.27), channel_id=1, source_target_pairs={{0,24},{8,16},{16,8},{24,0},{1,25},{9,17},{17,9},{25,1},{2,26},{10... | collective-permute-start | bytes 196616 | tf_op jit(solution)/shard_map/ppermute | solution.py:26
  106.3 6.5 %copy-start.1 = (f32[256,256]{1,0:T(8,128)S(1)}, f32[256,256]{1,0:T(8,128)}, u32[]{:S(2)}) copy-start(f32[256,256]{1,0:T(8,128)} %inv_one.1) | copy-start | bytes 786436
  106.3 6.5 %copy-start.2 = (f32[256,256]{1,0:T(8,128)S(1)}, f32[256,256]{1,0:T(8,128)}, u32[]{:S(2)}) copy-start(f32[256,256]{1,0:T(8,128)} %inv_two.1) | copy-start | bytes 786436

commit v18 on v15

--- a/solution.py
+++ b/solution.py
@@ -82,7 +82,7 @@
     zl = lax.axis_index("zl")
     full[...] = in0[...] + in1[...] + in2[...] + in3[...]
     for hop, out in enumerate((out0, out1, out2, out3)):
-        out[...] = full[pl.ds(pl.multiple_of(((zl + hop) & 3) * 64, 64), 64)]
+        out[...] = full[pl.ds(pl.multiple_of((zl ^ hop) * 64, 64), 64)]
 
 
 def split_kernel(mask, in0, in1, in2, in3, stay, leave):
@@ -161,7 +161,9 @@
         parts,
         [pltpu.VMEM((256, width), f32)],
     )
-    parts = rotate(parts, "zl")
+    parts = [parts[0]] + [
+        lax.ppermute(parts[s], "zl", [(i, i ^ s) for i in range(4)]) for s in (1, 2, 3)
+    ]
     half = jax.ShapeDtypeStruct((2 * row_count, 128), f32)
     stay, leave = call(split_kernel, [half, half], (mask, *parts), scalars=1)
     total = gather(shard, ("x", "y"), 16).reshape(384, 128)

time: 113 us -> 115 us (1.018)
  waiting for transfers between devices: 9.4 us -> 11.4 us
    ppermute x6 -> x3, starting transfers between devices: 18.6 us -> 8.9 us  [rotate(): lax.ppermute(parts[s], axis, [(i, (i + s) % 4) for i in range(4)])]
    ppermute x0 -> x3, starting transfers between devices: none -> 9.3 us  [per_device(): lax.ppermute(parts[s], 'zl', [(i, i ^ s) for i in range(4)])]
    ppermute x0 -> x3, waiting for transfers between devices: none -> 4.95 us  [per_device(): lax.ppermute(parts[s], 'zl', [(i, i ^ s) for i in range(4)])]
    ppermute x6 -> x3, waiting for transfers between devices: 2.94 us -> 0.01 us  [rotate(): lax.ppermute(parts[s], axis, [(i, (i + s) % 4) for i in range(4)])]
where the time goes in v18:
time: 115 us; the launch traced here: 114 us
  starting transfers between devices  54.5 us (47%)
  blocking collectives  39.5 us (34%)
  waiting for transfers between devices  11.4 us (10%)
  Pallas kernels  3.71 us (3%)
  local copies, waits for them, and re-layouts  2.77 us (2%)
    all_to_all x3, starting transfers between devices, exchange(): return lax.all_to_all(parts, axes, 0, 0)  24.7 us
    all_to_all x2, blocking collectives, exchange(): return lax.all_to_all(parts, axes, 0, 0)  21.2 us
    all_gather x1, blocking collectives, per_device(): around = lax.all_gather(rows.reshape(256, width), 'y')  10.4 us
    ppermute x1, starting transfers between devices, per_device(): turned = lax.ppermute(rows, AXES, TURN)  9.54 us
    ppermute x3, starting transfers between devices, per_device(): lax.ppermute(parts[s], 'zl', [(i, i ^ s) for i in range(4)])  9.3 us
    ppermute x3, starting transfers between devices, rotate(): lax.ppermute(parts[s], axis, [(i, (i + s) % 4) for i in range(4)])  8.9 us
    all_gather x1, blocking collectives, per_device(): finals = lax.all_gather(jnp.concatenate([total, leave]), 'core')  7.93 us
    all_to_all x3, waiting for transfers between devices, exchange(): return lax.all_to_all(parts, axes, 0, 0)  6.46 us
  transfers between devices with their start and end apart: 11, of which 4 were waited for; matrix products, arithmetic and copies ran while one was open for 1% of the time, Pallas kernels for 1%

profile of v18, /device:TPU:1, one launch (start us, length us, event | category | flops | bytes accessed | tf_op | source)
XLA Modules:
  0.0 113.7 jit_solution(2014021006249051434)
XLA Ops:
  0.6 0.7 pad_maximum_fusion.1
  1.4 0.7 broadcast_in_dim.8
  2.0 10.2 %all-to-all-start = ((bf16[8,32,256]{2,1,0:T(8,128)(2,1)}), bf16[8,32,256]{2,1,0:T(8,128)(2,1)S(1)}, u32[]{:S(2)}, u32[]{:S(2)}) async-start(bf16[8,32,256]{2,1,0:T(8,128)(2,1)} %bitcast.2), calls=%async_computation | async-start | bytes 262144 | tf_op jit(solution)/shard_map/all_to_all | solution.py:17
  12.2 2.0 %collective-permute-start = (bf16[1024,512]{1,0:T(8,128)(2,1)}, bf16[1024,512]{1,0:T(8,128)(2,1)S(1)}, u32[]{:S(2)}, u32[]{:S(2)}) collective-permute-start(bf16[1024,512]{1,0:T(8,128)(2,1)} %pool.1), channel_id=1, source_target_pairs={{0,1},{1,0},{2,3},{3,2},{4,5},{5,4},{6,7},{7,6},{8,9},{9,8},{10,11... | collective-permute-start | bytes 3145736 | tf_op jit(solution)/shard_map/ppermute | solution.py:135
  14.2 0.0 copy-start.3
  14.2 0.0 copy-start.4
  14.2 0.6 copy-done.3
  14.9 0.0 copy-done.4
  14.9 0.1 fusion
  15.0 3.0 %all-to-all-done = bf16[8,32,256]{2,1,0:T(8,128)(2,1)S(1)} async-done(((bf16[8,32,256]{2,1,0:T(8,128)(2,1)}), bf16[8,32,256]{2,1,0:T(8,128)(2,1)S(1)}, u32[]{:S(2)}, u32[]{:S(2)}) %all-to-all-start) | async-done | bytes 131104 | tf_op jit(solution)/shard_map/all_to_all | solution.py:17
  18.0 0.1 bitcast_multiply_fusion
  18.1 9.5 %collective-permute-start.1 = (bf16[4,64,256]{2,1,0:T(8,128)(2,1)S(1)}, bf16[4,64,256]{2,1,0:T(8,128)(2,1)S(1)}, u32[]{:S(2)}, u32[]{:S(2)}) collective-permute-start(bf16[4,64,256]{2,1,0:T(8,128)(2,1)S(1)} %bitcast_multiply_fusion), channel_id=1, source_target_pairs={{12,0},{13,1},{38,2},{39,3},{88,4},{89,5},{114,6},{115,7},{138,8},... | collective-permute-start | bytes 393224 | tf_op jit(solution)/shard_map/ppermute | solution.py:143
  27.7 0.0 copy-start
  27.7 10.4 %all_gather.9.rows = bf16[4,256,256]{2,1,0:T(8,128)(2,1)S(1)} all-gather(bf16[1,256,256]{2,1,0:T(8,128)(2,1)S(1)} %bitcast.13), channel_id=1, replica_groups=mesh['x'=4,'zh'=4,'zl'=4,'y'=4,'core'=2] {'y'}, dimensions={0}, use_global_device_ids=true | all-gather | bytes 655360 | tf_op jit(solution)/shard_map/all_gather | solution.py:144
  38.1 0.0 collective-permute-done.1
  38.2 11.0 %all_to_all.25.strip = bf16[4,4,64,256]{3,2,1,0:T(8,128)(2,1)S(1)} all-to-all(bf16[4,4,64,256]{3,2,1,0:T(8,128)(2,1)S(1)} %broadcast_in_dim.9), channel_id=1, replica_groups=mesh['x'=4,'zh'=4,'zl'=4,'y'=4,'core'=2] {'x'}, dimensions={0} | all-to-all | bytes 1048576 | tf_op jit(solution)/shard_map/all_to_all | solution.py:17
  49.2 0.0 collective-permute-done.sibling
  49.2 0.0 copy-done
  49.2 2.2 %shard_map.102 = (f32[384,128]{1,0:T(8,128)S(1)}, f32[256,256]{1,0:T(8,128)S(1)}, f32[256,256]{1,0:T(8,128)S(1)}, f32[256,256]{1,0:T(8,128)S(1)}, f32[256,256]{1,0:T(8,128)S(1)}) custom-call(bf16[1024,512]{1,0:T(8,128)(2,1)S(1)} %copy-done, bf16[1024,512]{1,0:T(8,128)(2,1)S(1)} %collective-permute-done.sibling, ...), custom_call_target="tpu_custom_call" | custom-call | tf_op jit(solution)/shard_map/pallas_call | solution.py:116
  51.4 10.1 %all_to_all.26 = f32[16,24,128]{2,1,0:T(8,128)S(1)} all-to-all(f32[16,24,128]{2,1,0:T(8,128)S(1)} %bitcast.11), channel_id=1, replica_groups=mesh['x'=4,'zh'=4,'zl'=4,'y'=4,'core'=2] {'x','y'}, dimensions={0} | all-to-all | bytes 393216 | tf_op jit(solution)/shard_map/all_to_all | solution.py:17
  61.5 0.7 broadcast_in_dim.10
  62.2 11.0 %all-to-all-start.3 = ((f32[16,24,128]{2,1,0:T(8,128)}), f32[16,24,128]{2,1,0:T(8,128)S(1)}, u32[]{:S(2)}, u32[]{:S(2)}) async-start(f32[16,24,128]{2,1,0:T(8,128)} %broadcast_in_dim.10), calls=%async_computation.3 | async-start | bytes 393216 | tf_op jit(solution)/shard_map/all_to_all | solution.py:17
  73.3 1.9 %collective-permute-start.2 = (f32[256,256]{1,0:T(8,128)S(1)}, f32[256,256]{1,0:T(8,128)S(1)}, u32[]{:S(2)}, u32[]{:S(2)}) collective-permute-start(f32[256,256]{1,0:T(8,128)S(1)} %get-tuple-element.21), channel_id=1, source_target_pairs={{0,2},{2,4},{4,6},{6,0},{1,3},{3,5},{5,7},{7,1},{8,10},{10,12},{12... | collective-permute-start | bytes 786440 | tf_op jit(solution)/shard_map/ppermute | solution.py:26
  75.2 3.9 %collective-permute-start.3 = (f32[256,256]{1,0:T(8,128)S(1)}, f32[256,256]{1,0:T(8,128)S(1)}, u32[]{:S(2)}, u32[]{:S(2)}) collective-permute-start(f32[256,256]{1,0:T(8,128)S(1)} %get-tuple-element.22), channel_id=1, source_target_pairs={{0,4},{2,6},{4,0},{6,2},{1,5},{3,7},{5,1},{7,3},{8,12},{10,14},{12... | collective-permute-start | bytes 786440 | tf_op jit(solution)/shard_map/ppermute | solution.py:26
  79.1 3.1 %collective-permute-start.4 = (f32[256,256]{1,0:T(8,128)S(1)}, f32[256,256]{1,0:T(8,128)S(1)}, u32[]{:S(2)}, u32[]{:S(2)}) collective-permute-start(f32[256,256]{1,0:T(8,128)S(1)} %get-tuple-element.23), channel_id=1, source_target_pairs={{0,6},{2,0},{4,2},{6,4},{1,7},{3,1},{5,3},{7,5},{8,14},{10,8},{12,... | collective-permute-start | bytes 786440 | tf_op jit(solution)/shard_map/ppermute | solution.py:26
  82.2 3.4 %all-to-all-done.3 = f32[16,24,128]{2,1,0:T(8,128)S(1)} async-done(((f32[16,24,128]{2,1,0:T(8,128)}), f32[16,24,128]{2,1,0:T(8,128)S(1)}, u32[]{:S(2)}, u32[]{:S(2)}) %all-to-all-start.3) | async-done | bytes 196640 | tf_op jit(solution)/shard_map/all_to_all | solution.py:17
  85.6 0.7 broadcast_in_dim.11
  86.3 3.5 %all-to-all-start.4 = ((f32[16,24,128]{2,1,0:T(8,128)}), f32[16,24,128]{2,1,0:T(8,128)S(1)}, u32[]{:S(2)}, u32[]{:S(2)}) async-start(f32[16,24,128]{2,1,0:T(8,128)} %broadcast_in_dim.11), calls=%async_computation.4 | async-start | bytes 393216 | tf_op jit(solution)/shard_map/all_to_all | solution.py:17
  89.8 0.0 collective-permute-done.2.in1
  89.9 0.0 collective-permute-done.3.in2
  89.9 0.0 collective-permute-done.4.in3
  89.9 0.1 shard_map.103
  90.0 3.4 %collective-permute-start.5 = (f32[64,256]{1,0:T(8,128)S(1)}, f32[64,256]{1,0:T(8,128)S(1)}, u32[]{:S(2)}, u32[]{:S(2)}) collective-permute-start(f32[64,256]{1,0:T(8,128)S(1)} %get-tuple-element.25), channel_id=1, source_target_pairs={{0,8},{8,0},{16,24},{24,16},{1,9},{9,1},{17,25},{25,17},{2,10},{10... | collective-permute-start | bytes 196616 | tf_op jit(solution)/shard_map/ppermute | solution.py:165
  93.4 4.0 %collective-permute-start.6 = (f32[64,256]{1,0:T(8,128)S(1)}, f32[64,256]{1,0:T(8,128)S(1)}, u32[]{:S(2)}, u32[]{:S(2)}) collective-permute-start(f32[64,256]{1,0:T(8,128)S(1)} %get-tuple-element.26), channel_id=1, source_target_pairs={{0,16},{8,24},{16,0},{24,8},{1,17},{9,25},{17,1},{25,9},{2,18},{10... | collective-permute-start | bytes 196616 | tf_op jit(solution)/shard_map/ppermute | solution.py:165
  97.4 1.9 %collective-permute-start.7 = (f32[64,256]{1,0:T(8,128)S(1)}, f32[64,256]{1,0:T(8,128)S(1)}, u32[]{:S(2)}, u32[]{:S(2)}) collective-permute-start(f32[64,256]{1,0:T(8,128)S(1)} %get-tuple-element.27), channel_id=1, source_target_pairs={{0,24},{8,16},{16,8},{24,0},{1,25},{9,17},{17,9},{25,1},{2,26},{10... | collective-permute-start | bytes 196616 | tf_op jit(solution)/shard_map/ppermute | solution.py:165
  99.3 0.0 collective-permute-done.5.in1
  99.3 0.4 collective-permute-done.6.in2
  99.7 4.5 %collective-permute-done.7.in3 = f32[64,256]{1,0:T(8,128)S(1)} collective-permute-done((f32[64,256]{1,0:T(8,128)S(1)}, f32[64,256]{1,0:T(8,128)S(1)}, u32[]{:S(2)}, u32[]{:S(2)}) %collective-permute-start.7) | collective-permute-done | bytes 65568 | tf_op jit(solution)/shard_map/ppermute | solution.py:165
  104.3 0.6 shard_map.104
  104.8 0.0 all-to-all-done.4
  104.9 0.0 copy-start.1
  104.9 0.0 copy-start.2
  104.9 7.9 %all-gather = f32[896,128]{1,0:T(8,128)S(1)} all-gather(f32[448,128]{1,0:T(8,128)S(1)} %pad_maximum_fusion), channel_id=2, replica_groups=mesh['x'=4,'zh'=4,'zl'=4,'y'=4,'core'=2] {'core'}, dimensions={0}, use_global_device_ids=true | all-gather | bytes 688128 | tf_op jit(solution)/shard_map/all_gather | solution.py:170
  112.8 0.0 copy-done.1
  112.8 0.0 copy-done.2
  112.8 0.9 shard_map.105
  (5 shorter events, 0.1 us)
Async XLA Ops:
  2.0 16.0 %all-to-all-start = ((bf16[8,32,256]{2,1,0:T(8,128)(2,1)}), bf16[8,32,256]{2,1,0:T(8,128)(2,1)S(1)}, u32[]{:S(2)}, u32[]{:S(2)}) async-start(bf16[8,32,256]{2,1,0:T(8,128)(2,1)} %bitcast.2), calls=%async_computation | async-start | bytes 262144 | tf_op jit(solution)/shard_map/all_to_all | solution.py:17
  12.2 37.0 %collective-permute-start = (bf16[1024,512]{1,0:T(8,128)(2,1)}, bf16[1024,512]{1,0:T(8,128)(2,1)S(1)}, u32[]{:S(2)}, u32[]{:S(2)}) collective-permute-start(bf16[1024,512]{1,0:T(8,128)(2,1)} %pool.1), channel_id=1, source_target_pairs={{0,1},{1,0},{2,3},{3,2},{4,5},{5,4},{6,7},{7,6},{8,9},{9,8},{10,11... | collective-permute-start | bytes 3145736 | tf_op jit(solution)/shard_map/ppermute | solution.py:135
  14.2 0.7 copy-start.3
  14.2 0.7 copy-start.4
  18.1 20.0 %collective-permute-start.1 = (bf16[4,64,256]{2,1,0:T(8,128)(2,1)S(1)}, bf16[4,64,256]{2,1,0:T(8,128)(2,1)S(1)}, u32[]{:S(2)}, u32[]{:S(2)}) collective-permute-start(bf16[4,64,256]{2,1,0:T(8,128)(2,1)S(1)} %bitcast_multiply_fusion), channel_id=1, source_target_pairs={{12,0},{13,1},{38,2},{39,3},{88,4},{89,5},{114,6},{115,7},{138,8},... | collective-permute-start | bytes 393224 | tf_op jit(solution)/shard_map/ppermute | solution.py:143
  27.7 21.5 %copy-start = (bf16[1024,512]{1,0:T(8,128)(2,1)S(1)}, bf16[1024,512]{1,0:T(8,128)(2,1)}, u32[]{:S(2)}) copy-start(bf16[1024,512]{1,0:T(8,128)(2,1)} %pool.1) | copy-start | bytes 3145732
  62.2 23.4 %all-to-all-start.3 = ((f32[16,24,128]{2,1,0:T(8,128)}), f32[16,24,128]{2,1,0:T(8,128)S(1)}, u32[]{:S(2)}, u32[]{:S(2)}) async-start(f32[16,24,128]{2,1,0:T(8,128)} %broadcast_in_dim.10), calls=%async_computation.3 | async-start | bytes 393216 | tf_op jit(solution)/shard_map/all_to_all | solution.py:17
  73.3 16.6 %collective-permute-start.2 = (f32[256,256]{1,0:T(8,128)S(1)}, f32[256,256]{1,0:T(8,128)S(1)}, u32[]{:S(2)}, u32[]{:S(2)}) collective-permute-start(f32[256,256]{1,0:T(8,128)S(1)} %get-tuple-element.21), channel_id=1, source_target_pairs={{0,2},{2,4},{4,6},{6,0},{1,3},{3,5},{5,7},{7,1},{8,10},{10,12},{12... | collective-permute-start | bytes 786440 | tf_op jit(solution)/shard_map/ppermute | solution.py:26
  75.2 14.7 %collective-permute-start.3 = (f32[256,256]{1,0:T(8,128)S(1)}, f32[256,256]{1,0:T(8,128)S(1)}, u32[]{:S(2)}, u32[]{:S(2)}) collective-permute-start(f32[256,256]{1,0:T(8,128)S(1)} %get-tuple-element.22), channel_id=1, source_target_pairs={{0,4},{2,6},{4,0},{6,2},{1,5},{3,7},{5,1},{7,3},{8,12},{10,14},{12... | collective-permute-start | bytes 786440 | tf_op jit(solution)/shard_map/ppermute | solution.py:26
  79.1 10.8 %collective-permute-start.4 = (f32[256,256]{1,0:T(8,128)S(1)}, f32[256,256]{1,0:T(8,128)S(1)}, u32[]{:S(2)}, u32[]{:S(2)}) collective-permute-start(f32[256,256]{1,0:T(8,128)S(1)} %get-tuple-element.23), channel_id=1, source_target_pairs={{0,6},{2,0},{4,2},{6,4},{1,7},{3,1},{5,3},{7,5},{8,14},{10,8},{12,... | collective-permute-start | bytes 786440 | tf_op jit(solution)/shard_map/ppermute | solution.py:26
  86.3 18.5 %all-to-all-start.4 = ((f32[16,24,128]{2,1,0:T(8,128)}), f32[16,24,128]{2,1,0:T(8,128)S(1)}, u32[]{:S(2)}, u32[]{:S(2)}) async-start(f32[16,24,128]{2,1,0:T(8,128)} %broadcast_in_dim.11), calls=%async_computation.4 | async-start | bytes 393216 | tf_op jit(solution)/shard_map/all_to_all | solution.py:17
  90.0 9.3 %collective-permute-start.5 = (f32[64,256]{1,0:T(8,128)S(1)}, f32[64,256]{1,0:T(8,128)S(1)}, u32[]{:S(2)}, u32[]{:S(2)}) collective-permute-start(f32[64,256]{1,0:T(8,128)S(1)} %get-tuple-element.25), channel_id=1, source_target_pairs={{0,8},{8,0},{16,24},{24,16},{1,9},{9,1},{17,25},{25,17},{2,10},{10... | collective-permute-start | bytes 196616 | tf_op jit(solution)/shard_map/ppermute | solution.py:165
  93.4 6.3 %collective-permute-start.6 = (f32[64,256]{1,0:T(8,128)S(1)}, f32[64,256]{1,0:T(8,128)S(1)}, u32[]{:S(2)}, u32[]{:S(2)}) collective-permute-start(f32[64,256]{1,0:T(8,128)S(1)} %get-tuple-element.26), channel_id=1, source_target_pairs={{0,16},{8,24},{16,0},{24,8},{1,17},{9,25},{17,1},{25,9},{2,18},{10... | collective-permute-start | bytes 196616 | tf_op jit(solution)/shard_map/ppermute | solution.py:165
  97.4 6.9 %collective-permute-start.7 = (f32[64,256]{1,0:T(8,128)S(1)}, f32[64,256]{1,0:T(8,128)S(1)}, u32[]{:S(2)}, u32[]{:S(2)}) collective-permute-start(f32[64,256]{1,0:T(8,128)S(1)} %get-tuple-element.27), channel_id=1, source_target_pairs={{0,24},{8,16},{16,8},{24,0},{1,25},{9,17},{17,9},{25,1},{2,26},{10... | collective-permute-start | bytes 196616 | tf_op jit(solution)/shard_map/ppermute | solution.py:165
  104.9 8.0 %copy-start.1 = (f32[256,256]{1,0:T(8,128)S(1)}, f32[256,256]{1,0:T(8,128)}, u32[]{:S(2)}) copy-start(f32[256,256]{1,0:T(8,128)} %inv_one.1) | copy-start | bytes 786436
  104.9 8.0 %copy-start.2 = (f32[256,256]{1,0:T(8,128)S(1)}, f32[256,256]{1,0:T(8,128)}, u32[]{:S(2)}) copy-start(f32[256,256]{1,0:T(8,128)} %inv_two.1) | copy-start | bytes 786436
